TPU v7x, 32 devices: a whole 2x2x4 slice. The times are simulated.
32 devices in a mesh: nodes: 16 (over z, y, x), stream: 2 (over core).
Axes of the slice: x: 2, y: 2, z: 4, core: 2. Of those that a mesh axis runs over, the one named last changes fastest.
Arguments:
- features: bfloat16 [5120, 1024], P('nodes'), may hold values from -6 to 6
- neighbours: int32 [5120, 50], P('nodes', 'stream'), may hold values from 0 to 5119, as said below
- present: int32 [5120, 50], P('nodes', 'stream'), may hold values from 0 to 1, as said below
- importance: int32 [5120, 50], P('nodes', 'stream'), may hold values from 1 to 64
- q_weight: bfloat16 [1024, 1024], replicated, may hold values from -0.1875 to 0.1875
- q_bias: float32 [1024], replicated, may hold values from -3 to 3
- w_weight: bfloat16 [2048, 1024], P('stream'), may hold values from -0.1875 to 0.1875
- w_bias: float32 [1024], replicated, may hold values from -3 to 3
- cotangent: bfloat16 [5120, 1024], P('nodes'), may hold values from -6 to 6
Outputs:
- embeddings: float32 [5120, 1024], P('nodes')
- feature_grad: float32 [5120, 1024], P('nodes', 'stream')
- q_weight_grad: float32 [1024, 1024], replicated
- q_bias_grad: float32 [1024], replicated
- w_weight_grad: float32 [2048, 1024], P('stream')
- w_bias_grad: float32 [1024], replicated
Inputs may be any that keep to these rules, and one draw needn't show every extreme that they name: `neighbours`: number a device's nodes' slots of one half of the 50 slots node by node, j = local node * 25 + slot within the half; slot j names a row of the block of 320 rows of device j % 16 of nodes, so that each device's block is named exactly 500 times by each device and half; a row may be named several times. Each node has between 5 and 50 present slots.
All inputs are finite; a program needn't handle non-finite values.
Results may differ from a plain program's by a relative error of at most 0.014.
The roundings to bfloat16 on the way count: a program that leaves them out, or rounds other values in their place, can miss the bound.
Values may be sent and summed in bfloat16 or wider, within the bound.
No kernel may reach another device: no remote copies, remote signals or barrier semaphores. Data moves between devices by JAX's collectives and lax.ppermute only.
A program may use at most 128 MiB of HBM per device.

v0:
```python
import jax
import jax.numpy as jnp
from jax import lax
from jax.sharding import PartitionSpec as P


def spread(value, axis, source):
    kept = jnp.where(lax.axis_index(axis) == source, value, 0).astype(value.dtype)
    return lax.psum(kept, axis)


def one_hot_rows(row_ids, count):
    return (row_ids[..., None] == jnp.arange(count, dtype=jnp.int32)).astype(jnp.bfloat16)


def on_device(
    features, neighbours, present, importance, q_weight, q_bias, w_weight, w_bias, cotangent
):
    node_rows, feature_dim = features.shape
    slot_count = neighbours.shape[1]
    owners_count = lax.axis_size("nodes")
    stream_index = lax.axis_index("stream")
    slot_total = node_rows * slot_count
    capacity = slot_total // owners_count
    local_row = neighbours.reshape(slot_total) % node_rows
    requests = local_row.reshape(capacity, owners_count).T
    shard_rows = lax.all_gather(features, "nodes", axis=0, tiled=True)
    shards = shard_rows.shape[0] // node_rows
    blocks_of = shard_rows.reshape(shards, node_rows, feature_dim)
    picked = jnp.einsum(
        "scr,srd->scd",
        one_hot_rows(requests, node_rows),
        blocks_of,
        preferred_element_type=jnp.float32,
    ).astype(jnp.bfloat16)
    slot_rows = jnp.transpose(picked, (1, 0, 2)).reshape(slot_total, feature_dim)
    weights = (present * importance).astype(jnp.float32)
    weight_half = jnp.sum(weights, axis=1)
    block_nodes = 32
    steps_count = node_rows // block_nodes
    row_blocks = slot_rows.reshape(steps_count, block_nodes * slot_count, feature_dim)
    weight_blocks = weights.reshape(steps_count, block_nodes, slot_count)

    def hidden_of(collected_rows):
        return jnp.dot(collected_rows, q_weight, preferred_element_type=jnp.float32) + q_bias

    def forward_block(inputs):
        collected_rows, importance_block_weights = inputs
        hidden_pre = hidden_of(collected_rows)
        hidden_state = jax.nn.relu(hidden_pre).reshape(block_nodes, slot_count, feature_dim)
        return jnp.einsum(
            "gk,gkd->gd", importance_block_weights, hidden_state, precision=lax.Precision.HIGHEST
        )

    weighted_numerator = lax.map(forward_block, (row_blocks, weight_blocks)).reshape(
        node_rows, feature_dim
    )
    weighted_numerator, weight_sum = lax.psum((weighted_numerator, weight_half), "stream")
    aggregate = (weighted_numerator / weight_sum[:, None]).astype(jnp.bfloat16)
    stream_input = jnp.where(stream_index == 0, features, aggregate)
    partial_value = jnp.dot(stream_input, w_weight, preferred_element_type=jnp.float32)
    linear = lax.psum(partial_value, "stream") + w_bias
    relu_out = jax.nn.relu(linear)
    norm_scale = lax.rsqrt(jnp.mean(relu_out * relu_out, axis=1, keepdims=True) + 1e-06)
    embeddings = relu_out * norm_scale
    grad_out = cotangent.astype(jnp.float32)
    grad_relu = norm_scale * grad_out - relu_out * (
        norm_scale * norm_scale * norm_scale
    ) * jnp.mean(relu_out * grad_out, axis=1, keepdims=True)
    grad_linear = jnp.where(linear > 0, grad_relu, 0.0).astype(jnp.bfloat16)
    w_grad_local = lax.dot_general(
        stream_input, grad_linear, (((0,), (0,)), ((), ())), preferred_element_type=jnp.float32
    )
    w_bias_local = jnp.sum(grad_linear.astype(jnp.float32), axis=0)
    back_rows = lax.dot_general(
        grad_linear, w_weight, (((1,), (1,)), ((), ())), preferred_element_type=jnp.float32
    )
    grad_aggregate = spread(back_rows, "stream", 1)
    self_grad = jnp.where(stream_index == 0, back_rows, 0.0)
    grad_sum = grad_aggregate / weight_sum[:, None]
    grad_blocks = grad_sum.reshape(steps_count, block_nodes, feature_dim)

    def backward_block(totals, inputs):
        q_total, bias_total = totals
        collected_rows, importance_block_weights, grad_block = inputs
        hidden_pre = hidden_of(collected_rows)
        grad_hidden = (importance_block_weights[:, :, None] * grad_block[:, None, :]).reshape(
            block_nodes * slot_count, feature_dim
        )
        grad_hidden = jnp.where(hidden_pre > 0, grad_hidden, 0.0).astype(jnp.bfloat16)
        q_total = q_total + lax.dot_general(
            collected_rows,
            grad_hidden,
            (((0,), (0,)), ((), ())),
            preferred_element_type=jnp.float32,
        )
        bias_total = bias_total + jnp.sum(grad_hidden.astype(jnp.float32), axis=0)
        grad_rows = lax.dot_general(
            grad_hidden, q_weight, (((1,), (1,)), ((), ())), preferred_element_type=jnp.float32
        ).astype(jnp.bfloat16)
        return ((q_total, bias_total), grad_rows)

    start_totals = (
        jnp.zeros((feature_dim, feature_dim), jnp.float32),
        jnp.zeros((feature_dim,), jnp.float32),
    )
    (q_grad_local, q_bias_local), grad_rows = lax.scan(
        backward_block, start_totals, (row_blocks, weight_blocks, grad_blocks)
    )
    grad_buffer = jnp.transpose(grad_rows.reshape(capacity, owners_count, feature_dim), (1, 0, 2))
    asked_rows, returned = (
        lax.all_to_all(requests, "nodes", split_axis=0, concat_axis=0, tiled=True),
        lax.all_to_all(grad_buffer, "nodes", split_axis=0, concat_axis=0, tiled=True),
    )
    neighbour_grad = lax.dot_general(
        one_hot_rows(asked_rows.reshape(-1), node_rows),
        returned.reshape(-1, feature_dim),
        (((0,), (0,)), ((), ())),
        preferred_element_type=jnp.float32,
    )
    feature_grad = lax.psum_scatter(
        self_grad + neighbour_grad, "stream", scatter_dimension=1, tiled=True
    )
    w_grad, w_bias_grad, q_grad, q_bias_grad = lax.psum(
        (w_grad_local, w_bias_local, q_grad_local, q_bias_local), "nodes"
    )
    q_grad, q_bias_grad = lax.psum((q_grad, q_bias_grad), "stream")
    return (embeddings, feature_grad, q_grad, q_bias_grad, w_grad, w_bias_grad)


def solution(mesh):
    in_specs = (
        P("nodes", None),
        P("nodes", "stream"),
        P("nodes", "stream"),
        P("nodes", "stream"),
        P(),
        P(),
        P("stream", None),
        P(),
        P("nodes", None),
    )
    out_specs = (P("nodes", None), P("nodes", "stream"), P(), P(), P("stream", None), P())
    return jax.shard_map(
        on_device, mesh=mesh, in_specs=in_specs, out_specs=out_specs, check_vma=False
    )
```

profile of v0, /device:TPU:1, one launch (start us, length us, event | category | flops | bytes accessed | tf_op | source)
XLA Modules:
  0.0 1334.6 jit_solution(5990324770737478218)
XLA Ops:
  10.2 134.5 %all-gather.2.cloned.1.call-done = bf16[5120,1024]{1,0:T(8,128)(2,1)} async-done(((bf16[320,1024]{1,0:T(8,128)(2,1)}), bf16[5120,1024]{1,0:T(8,128)(2,1)}) %all-gather.2.cloned.1.call-update) | async-done | bytes 10485776 | tf_op jit(solution)/shard_map/all_gather | solution.py:27
  144.6 16.2 %convert_bitcast_fusion = bf16[500,16,1024]{2,0,1:T(8,128)(2,1)} fusion(bf16[16,320,1024]{2,1,0:T(8,128)(2,1)} %bitcast.85, s32[16,500]{1,0:T(8,128)S(1)} %copy.35), kind=kOutput, calls=%fused_computation.22 | convolution fusion | flops 5253632000 | bytes 26901760 | tf_op jit(solution)/shard_map/scr,srd->scd/dot_general | solution.py:30
  160.9 15.5 %copy.36 = bf16[500,16,1024]{2,1,0:T(8,128)(2,1)} copy(bf16[500,16,1024]{2,0,1:T(8,128)(2,1)} %convert_bitcast_fusion) | data formatting | bytes 32768000 | tf_op jit(solution)/shard_map/convert_element_type | solution.py:35
  176.4 143.1 %while.25 = (s32[]{:T(128)}, f32[10,32,1024]{2,1,0:T(8,128)}, f32[10,32,25]{2,1,0:T(8,128)S(1)}, bf16[10,800,1024]{2,1,0:T(8,128)(2,1)}, bf16[1024,1024]{1,0:T(8,128)(2,1)}, /*index=5*/f32[1024]{0:T(1024)S(1)}, s32[]{:T(128)}) while((s32[]{:T(128)}, f32[10,32,1024]{2,1,0:T(8,128)}, f32[10,32,25]{2,1,0:T(8,128)S(1)}, ...), condition=%wide.region_1.2_spmd, body=%wide.region_0.1_spmd.sunk | while | flops 1689190400 | bytes 17250768 | solution.py:55
  176.4 5.7 add_maximum_fusion.3
  185.8 4.3 fusion.56
  190.8 5.7 add_maximum_fusion.3
  205.1 5.7 add_maximum_fusion.3
  219.4 5.7 add_maximum_fusion.3
  233.7 5.7 add_maximum_fusion.3
  248.0 5.7 add_maximum_fusion.3
  262.3 5.7 add_maximum_fusion.3
  276.6 5.7 add_maximum_fusion.3
  290.9 5.7 add_maximum_fusion.3
  305.2 5.7 add_maximum_fusion.3
  322.8 15.8 %all-reduce.8.cloned.1.call-done = f32[320,1024]{1,0:T(8,128)} async-done(((f32[320,1024]{1,0:T(8,128)}), f32[320,1024]{1,0:T(8,128)}) %all-reduce.8.cloned.1.call-update) | async-done | bytes 1310736 | tf_op jit(solution)/shard_map/psum | solution.py:58
  342.4 21.1 %all-reduce.10.cloned.1.call-done = f32[320,1024]{1,0:T(8,128)} async-done(((f32[320,1024]{1,0:T(8,128)}), f32[320,1024]{1,0:T(8,128)}) %all-reduce.10.cloned.1.call-update) | async-done | bytes 1310736 | tf_op jit(solution)/shard_map/psum | solution.py:62
  371.1 6.6 all-to-all-start
  377.7 13.1 all-reduce.12.cloned.1.call-done
  392.2 239.1 %while.26 = (s32[]{:T(128)}, f32[1024,1024]{1,0:T(8,128)}, f32[1024]{0:T(1024)S(1)}, bf16[10,800,1024]{2,1,0:T(8,128)(2,1)}, bf16[10,800,1024]{2,1,0:T(8,128)(2,...) while((s32[]{:T(128)}, f32[1024,1024]{1,0:T(8,128)}, ...), condition=%wide.region_11.12_spmd.clone, body=%wide.region_9.11_spmd.clone.sunk | while | flops 5041816576 | bytes 50894132 | solution.py:107
  399.2 5.2 convert_reduce_fusion.3
  408.7 6.3 select_add_fusion.4
  422.0 5.2 convert_reduce_fusion.3
  431.4 7.6 select_add_fusion.4
  446.0 5.2 convert_reduce_fusion.3
  455.5 7.6 select_add_fusion.4
  470.1 5.2 convert_reduce_fusion.3
  479.5 7.6 select_add_fusion.4
  494.1 5.2 convert_reduce_fusion.3
  503.5 7.6 select_add_fusion.4
  518.1 5.2 convert_reduce_fusion.3
  527.6 7.6 select_add_fusion.4
  542.2 5.2 convert_reduce_fusion.3
  551.7 7.6 select_add_fusion.4
  566.2 5.2 convert_reduce_fusion.3
  575.7 7.6 select_add_fusion.4
  590.2 5.2 convert_reduce_fusion.3
  599.7 7.6 select_add_fusion.4
  614.3 5.2 convert_reduce_fusion.3
  623.7 7.6 select_add_fusion.4
  631.3 15.5 %copy.43 = bf16[500,16,1024]{2,0,1:T(8,128)(2,1)} copy(bf16[500,16,1024]{2,1,0:T(8,128)(2,1)} %bitcast.14) | data formatting | bytes 32768000 | tf_op jit(solution)/shard_map/reshape | solution.py:110
  646.8 6.6 all-to-all-start.1
  656.9 592.3 %all-reduce.16.cloned.1.call-done = (f32[1024,1024]{1,0:T(8,128)}, f32[1024,1024]{1,0:T(8,128)}) async-done(((f32[1024,1024]{1,0:T(8,128)}, f32[1024,1024]{1,0:T(8,128)}), (f32[1024,1024]{1,0:T(8,128)}, f32[1024,1024]{1,0:T(8,128)})) %all-reduce.16.cloned.1.call-update) | async-done | bytes 8388624 | tf_op jit(solution)/shard_map/psum | solution.py:124
  1249.7 15.0 %reshape.78 = bf16[8000,1024]{1,0:T(8,128)(2,1)} reshape(bf16[16,500,1024]{2,1,0:T(8,128)(2,1)} %all-to-all-done.1) | data formatting | bytes 32768000 | tf_op jit(solution)/shard_map/reshape | solution.py:117
  1264.7 10.4 fusion.13
  1275.2 34.1 %all-reduce = (f32[1024]{0:T(1024)S(1)}, f32[1024]{0:T(1024)}) all-reduce(f32[1024]{0:T(1024)S(1)} %get-tuple-element.90, f32[1024]{0:T(1024)S(1)} %get-tuple-element.157), channel_id=1, replica_groups=mesh['nodes'=16,'stream'=2] {'nodes'}, use_global_device_ids=true, to_apply=%region_15.16 | all-reduce | flops 2048 | bytes 16384 | tf_op jit(solution)/shard_map/psum | solution.py:124
  1309.3 10.4 psum.77
  1319.7 4.9 copy.72
  (217 shorter events, 220.1 us)
Async XLA Ops:
  7.2 333.1 %copy-start = (bf16[1024,1024]{1,0:T(8,128)(2,1)S(1)}, bf16[1024,1024]{1,0:T(8,128)(2,1)}, u32[]{:S(2)}) copy-start(bf16[1024,1024]{1,0:T(8,128)(2,1)} %param.19) | copy-start | bytes 6291460
  7.2 2.8 copy-start.9
  7.2 2.8 copy-start.10
  7.2 137.4 %all-gather.2.cloned.1.call-start = ((), (), s32[]{:S(2)}) async-start(), calls=%async_computation.3 | async-start | bytes 11141120 | tf_op jit(solution)/shard_map/all_gather | solution.py:27
  7.9 330.7 %all-reduce.8.cloned.1.call-start = ((), (), s32[]{:S(2)}) async-start(), calls=%async_computation.4 | async-start | bytes 2621440 | tf_op jit(solution)/shard_map/psum | solution.py:58
  160.9 15.5 %copy-start.13 = (f32[1024]{0:T(1024)S(1)}, f32[1024]{0:T(1024)}, u32[]{:S(2)}) copy-start(f32[1024]{0:T(1024)} %param.18) | copy-start | bytes 12292
  176.4 162.2 %copy-start.4 = (bf16[320,1024]{1,0:T(8,128)(2,1)S(1)}, bf16[320,1024]{1,0:T(8,128)(2,1)}, u32[]{:S(2)}) copy-start(bf16[320,1024]{1,0:T(8,128)(2,1)} %param.13) | copy-start | bytes 1966084
  319.5 3.3 copy-start.8
  319.5 44.0 %all-reduce.10.cloned.1.call-start = ((), (), s32[]{:S(2)}) async-start(), calls=%async_computation.5 | async-start | bytes 2621440 | tf_op jit(solution)/shard_map/psum | solution.py:62
  340.2 23.3 %copy-start.5 = (bf16[320,1024]{1,0:T(8,128)(2,1)S(1)}, bf16[320,1024]{1,0:T(8,128)(2,1)}, u32[]{:S(2)}) copy-start(bf16[320,1024]{1,0:T(8,128)(2,1)} %param.21) | copy-start | bytes 1966084
  340.3 23.3 %copy-start.11 = (f32[1024]{0:T(1024)S(1)}, f32[1024]{0:T(1024)}, u32[]{:S(2)}) copy-start(f32[1024]{0:T(1024)} %param.20) | copy-start | bytes 12292
  342.2 48.5 %all-reduce.12.cloned.1.call-start = ((), (), s32[]{:S(2)}) async-start(), calls=%async_computation.6 | async-start | bytes 2621440 | tf_op jit(solution)/shard_map/psum | solution.py:9
  363.5 1.9 copy-start.2
  363.5 1.9 copy-start.6
  371.1 275.8 %all-to-all-start = ((s32[16,1,500]{2,1,0:T(1,128)}), s32[16,1,500]{2,1,0:T(1,128)S(1)}, u32[]{:S(2)}, u32[]{:S(2)}) async-start(s32[16,1,500]{2,1,0:T(1,128)} %copy.37), calls=%async_computation | async-start | bytes 65536 | tf_op jit(solution)/shard_map/all_to_all | solution.py:112
  399.2 6.4 copy-start.12
  404.4 1.2 copy-start.14
  422.0 6.4 copy-start.12
  427.2 1.2 copy-start.14
  446.0 6.4 copy-start.12
  451.2 1.2 copy-start.14
  470.0 6.4 copy-start.12
  475.3 1.2 copy-start.14
  494.0 6.4 copy-start.12
  499.3 1.2 copy-start.14
  518.1 6.4 copy-start.12
  523.3 1.2 copy-start.14
  542.1 6.4 copy-start.12
  547.4 1.2 copy-start.14
  566.2 6.4 copy-start.12
  571.4 1.2 copy-start.14
  590.2 6.4 copy-start.12
  595.4 1.2 copy-start.14
  614.2 6.4 copy-start.12
  619.5 1.2 copy-start.14
  646.8 602.9 %all-to-all-start.1 = ((bf16[16,500,1024]{2,1,0:T(8,128)(2,1)}), bf16[16,500,1024]{2,1,0:T(8,128)(2,1)}, u32[]{:S(2)}, u32[]{:S(2)}) async-start(bf16[16,500,1024]{2,1,0:T(8,128)(2,1)} %bitcast.80), calls=%async_computation.1 | async-start | bytes 33030144 | tf_op jit(solution)/shard_map/all_to_all | solution.py:113
  653.5 595.8 %all-reduce.16.cloned.1.call-start = ((), (), s32[]{:S(2)}) async-start(), calls=%async_computation.9 | async-start | bytes 16777216 | tf_op jit(solution)/shard_map/psum | solution.py:124
  656.8 662.8 %all-reduce.14.cloned.1.call-start = ((), (), s32[]{:S(2)}) async-start(), calls=%async_computation.8 | async-start | bytes 8388608 | tf_op jit(solution)/shard_map/psum | solution.py:127
  1249.3 70.4 %reduce-scatter.2.cloned.1.call-start = ((), (), s32[]{:S(2)}) async-start(), calls=%async_computation.7 | async-start | bytes 1966080 | tf_op jit(solution)/shard_map/reduce_scatter | solution.py:121
  1249.7 15.0 %copy-start.7 = (f32[320,1024]{1,0:T(8,128)S(1)}, f32[320,1024]{1,0:T(8,128)}, u32[]{:S(2)}) copy-start(f32[320,1024]{1,0:T(8,128)} %get-tuple-element.169) | copy-start | bytes 3932164
  1319.7 4.9 copy-start.3
  1324.6 3.1 copy-start.1
Sparse Core Ops, SparseCore 0:
  10.7 133.8 all-gather.1
  319.6 18.9 all-reduce.7
  342.3 21.1 all-reduce.9
  369.5 21.1 all-reduce.11
  661.9 587.3 all-reduce.15
  1251.7 27.7 all-reduce.13
  1282.4 9.9 reduce-scatter.1
where the time goes:
time: 1340 us; the launch traced here: 1330 us
  waiting for transfers between devices  778 us (58%)
  matrix products  291 us (22%)
  local copies, waits for them, and re-layouts  181 us (14%)
  blocking collectives  47.7 us (4%)
  between operations  14.3 us (1%)
  starting transfers between devices  13.9 us (1%)
    psum x1, waiting for transfers between devices, on_device(): lax.psum((w_grad_local, w_bias_local, q_grad_local, q_bias_local), 'nodes')  592 us
    all_gather x1, waiting for transfers between devices, on_device(): shard_rows = lax.all_gather(features, 'nodes', axis=0, tiled=True)  134 us
    dot_general x20, matrix products, hidden_of(): jnp.dot(collected_rows, q_weight, preferred_element_type=jnp.float32)  109 us
    dot_general x10, matrix products, backward_block(): lax.dot_general(collected_rows, grad_hidden, (((0,), (0,)), ((), ())), pr...  74.6 us
    mul x40, local copies, waits for them, and re-layouts, backward_block(): importance_block_weights[:, :, None] * grad_block[:, None, :]  62.3 us
    dot_general x10, matrix products, forward_block(): jnp.einsum('gk,gkd->gd', importance_block_weights, hidden_state, precisio...  42.9 us
    reshape x10, local copies, waits for them, and re-layouts, forward_block(): jax.nn.relu(hidden_pre).reshape(block_nodes, slot_count, feature_dim)  36.6 us
    psum x1, blocking collectives, on_device(): lax.psum((w_grad_local, w_bias_local, q_grad_local, q_bias_local), 'nodes')  34.1 us
  transfers between devices with their start and end apart: 9, of which 5 were waited for; matrix products, arithmetic and copies ran while one was open for 21% of the time, Pallas kernels for 0%

commit v1 on v0

v1 whole, which is shorter than its diff:
```python
import jax
import jax.numpy as jnp
from jax import lax
from jax.experimental import pallas as pl
from jax.experimental.pallas import tpu as pltpu
from jax.sharding import PartitionSpec as P

PLANE = 4
TILE = 16


def slot_matrix_kernel(lists_ref, out_ref):
    turns, width = lists_ref.shape[1], out_ref.shape[1]
    ids = [lists_ref[0, turn : turn + 1, :] >> 7 for turn in range(turns)]
    weights = [(lists_ref[0, turn : turn + 1, :] & 127).astype(jnp.float32) for turn in range(turns)]

    @pl.loop(0, out_ref.shape[0] // TILE)
    def _(step):
        row_at = lax.broadcasted_iota(jnp.int32, (TILE, width), 0) + step * TILE
        total = jnp.zeros((TILE, width), jnp.float32)
        for listed, weight in zip(ids, weights):
            total = total + jnp.where(listed == row_at, weight, 0.0)
        out_ref[pl.ds(pl.multiple_of(step * TILE, TILE), TILE), :] = total.astype(jnp.bfloat16)


def slot_matrix(lists, rows):
    lines, turns, width = lists.shape
    return pl.pallas_call(
        slot_matrix_kernel,
        name="slot_matrix",
        out_shape=jax.ShapeDtypeStruct((lines * rows, width), jnp.bfloat16),
        grid=(lines,),
        in_specs=[pl.BlockSpec((1, turns, width), lambda line: (line, 0, 0))],
        out_specs=pl.BlockSpec((rows, width), lambda line: (line, 0)),
        cost_estimate=pl.CostEstimate(
            flops=3 * turns * lines * rows * width,
            bytes_accessed=2 * lines * rows * width,
            transcendentals=0,
        ),
    )(lists)


def on_device(
    features, neighbours, present, importance, q_weight, q_bias, w_weight, w_bias, cotangent
):
    rows, dim = features.shape
    slots = neighbours.shape[1]
    count = lax.axis_size("nodes")
    lines = count // PLANE
    node = lax.axis_index("nodes")
    core = lax.axis_index("stream")
    half_rows, half_dim = rows // 2, dim // 2
    f32, bf16 = jnp.float32, jnp.bfloat16

    def swap(value, bit):
        return lax.ppermute(value, "nodes", [(i, i ^ bit) for i in range(count)])

    def trade(value):
        return lax.ppermute(value, "stream", [(0, 1), (1, 0)])

    def own_half(value, axis):
        size = value.shape[axis] // 2
        return lax.dynamic_slice_in_dim(value, core * size, size, axis)

    def joined(mine, other, axis):
        return jnp.where(
            core == 0,
            jnp.concatenate([mine, other], axis),
            jnp.concatenate([other, mine], axis),
        )

    mine = own_half(features, 0)
    parts = {0: mine}
    bit = lines // 2
    while bit:
        for at in list(parts):
            parts[at ^ bit] = swap(parts[at], bit * PLANE)
        bit //= 2
    line_rows = [features] + [joined(parts[at], trade(parts[at]), 0) for at in range(1, lines)]

    per_block = -(-slots // count)
    packed = ((neighbours % rows) * 128 + present * importance).T
    block_at = jnp.arange(count, dtype=jnp.int32)[:, None]
    node_at = jnp.arange(rows, dtype=jnp.int32)[None, :]
    first = (block_at - slots * node_at) % count
    chosen = []
    for turn in range(per_block):
        slot = first + count * turn
        chosen.append(
            jnp.sum(
                jnp.where(
                    slot[None] == jnp.arange(slots, dtype=jnp.int32)[:, None, None],
                    packed[:, None, :],
                    0,
                ),
                axis=0,
            )
        )
    chosen = jnp.stack(chosen)
    chosen = jnp.concatenate([chosen, trade(chosen)], 0)
    weight_sum = jnp.sum((chosen & 127), axis=(0, 1)).astype(f32)
    named = {0: chosen}
    for bit in (2, 1):
        for at in list(named):
            named[at ^ bit] = swap(named[at], bit)
    lists = jnp.stack([named[at] for at in range(PLANE)])
    lists = lists.reshape(PLANE, 2 * per_block, lines, PLANE, rows)
    lists = lax.dynamic_index_in_dim(lists, node % PLANE, 3, False)
    order = (node // PLANE) ^ jnp.arange(lines)
    lists = jnp.take(lists, order, axis=2)
    lists = jnp.transpose(lists, (2, 1, 0, 3)).reshape(lines, 2 * per_block, PLANE * rows)
    matrix = slot_matrix(lists, rows)

    w_other = trade(w_weight)
    w_self = jnp.where(core == 0, w_weight, w_other)
    w_near = jnp.where(core == 0, w_other, w_weight)
    q_half = own_half(q_weight, 1)
    bias_half = own_half(q_bias, 0)

    high, low = [], []
    for shard in line_rows:
        hidden = jax.nn.relu(jnp.dot(shard, q_half, preferred_element_type=f32) + bias_half)
        top = lax.reduce_precision(hidden, 8, 7)
        high.append(top.astype(bf16))
        low.append((hidden - top).astype(bf16))
    high = jnp.concatenate(high, 0)
    low = jnp.concatenate(low, 0)

    def across(lhs, rhs):
        return lax.dot_general(lhs, rhs, (((0,), (0,)), ((), ())), preferred_element_type=f32)

    def times_t(lhs, rhs):
        return lax.dot_general(lhs, rhs, (((1,), (1,)), ((), ())), preferred_element_type=f32)

    partial = (across(matrix, high) + across(matrix, low)).reshape(PLANE, rows, half_dim)
    quarter = half_dim // 2
    left, right = partial[:, :, :quarter], partial[:, :, quarter:]
    got_x = swap(jnp.stack([left[1], left[3]]), 1)
    got_y = swap(jnp.stack([right[2], right[3]]), 2)
    last_y = swap(left[2] + got_x[1], 2)
    last_x = swap(right[1] + got_y[1], 1)
    numerator = jnp.concatenate(
        [left[0] + got_x[0] + last_y, right[0] + got_y[0] + last_x], axis=1
    )
    mean_half = (numerator / weight_sum[:, None]).astype(bf16)
    aggregate = joined(mean_half, trade(mean_half), 1)

    linear = (
        jnp.dot(features, w_self, preferred_element_type=f32)
        + jnp.dot(aggregate, w_near, preferred_element_type=f32)
        + w_bias
    )
    relu_out = jax.nn.relu(linear)
    scale = lax.rsqrt(jnp.mean(relu_out * relu_out, axis=1, keepdims=True) + 1e-06)
    embeddings = relu_out * scale
    grad_out = cotangent.astype(f32)
    grad_relu = scale * grad_out - relu_out * (scale * scale * scale) * jnp.mean(
        relu_out * grad_out, axis=1, keepdims=True
    )
    grad_linear = jnp.where(linear > 0, grad_relu, 0.0).astype(bf16)

    near_half = own_half(w_near, 0)
    grad_sum = (times_t(grad_linear, near_half) / weight_sum[:, None]).astype(bf16)
    from_x = swap(grad_sum, 1)
    from_y = swap(grad_sum, 2)
    diagonal = jnp.concatenate(
        [swap(from_x[:half_rows], 2), swap(from_y[half_rows:], 1)], axis=0
    )
    plane_grad = jnp.concatenate([grad_sum, from_x, from_y, diagonal], axis=0)

    def halves(value):
        middle = value.shape[-1] // 2
        return value[..., :middle], value[..., middle:]

    def summed(value):
        height, width = value.shape
        blocks = value.astype(bf16).reshape(count, height // count, width)
        order = node ^ jnp.arange(count)
        blocks = jnp.take(blocks, order, axis=0).reshape(lines, PLANE, height // count, width)

        def plus(one, two):
            return (one.astype(f32) + two.astype(f32)).astype(bf16)

        one, two = halves(blocks)
        got_one = swap(one[:, 1::2], 1)
        got_two = swap(two[:, 2:], 2)
        one = plus(one[:, 0::2], got_one)
        two = plus(two[:, :2], got_two)
        got_one = swap(one[:, 1], 2)
        got_two = swap(two[:, 1], 1)
        piece = jnp.concatenate([plus(one[:, 0], got_one), plus(two[:, 0], got_two)], -1)
        piece = {at: piece[at] for at in range(lines)}
        bit = 1
        while bit < lines:
            for at in sorted(piece, reverse=True):
                if at & bit:
                    piece[at ^ bit] = plus(piece[at ^ bit], swap(piece.pop(at), bit * PLANE))
            bit *= 2
        bit = lines // 2
        while bit:
            for at in list(piece):
                piece[at ^ bit] = swap(piece[at], bit * PLANE)
            bit //= 2
        piece = jnp.stack([piece[at] for at in range(lines)])
        one, two = halves(piece)
        one_y = swap(one, 2)
        two_x = swap(two, 1)
        one = jnp.stack([one, one_y], 1)
        two = jnp.stack([two, two_x], 1)
        one_x = swap(one, 1)
        two_y = swap(two, 2)
        one = jnp.stack([one[:, 0], one_x[:, 0], one[:, 1], one_x[:, 1]], 1)
        two = jnp.concatenate([two, two_y], 1)
        whole = jnp.concatenate([one, two], -1).reshape(count, height // count, width)
        return jnp.take(whole, order, axis=0).reshape(height, width).astype(f32)

    def summed_row(value):
        bit = 1
        while bit < count:
            value = value + swap(value, bit)
            bit *= 2
        return value

    stream_input = jnp.where(core == 0, features, aggregate)
    w_grad = summed(across(stream_input, grad_linear))
    w_bias_local = jnp.sum(grad_linear.astype(f32), axis=0)

    grad_rows = jnp.where(
        high > 0, jnp.dot(matrix, plane_grad, preferred_element_type=f32), 0.0
    )
    q_bias_half = jnp.sum(grad_rows, axis=0)
    grad_rows = grad_rows.astype(bf16)
    q_half_grad = summed(across(jnp.concatenate(line_rows, 0), grad_rows))
    biases = summed_row(jnp.stack([w_bias_local[:half_dim], w_bias_local[half_dim:], q_bias_half]))
    w_bias_grad = biases[:2].reshape(dim)
    q_bias_grad = joined(biases[2], trade(biases[2]), 0)
    q_grad = joined(q_half_grad, trade(q_half_grad), 1)

    owned = {at: grad_rows[at * rows : (at + 1) * rows] for at in range(lines)}
    bit = 1
    while bit < lines:
        for at in sorted(owned, reverse=True):
            if at & bit:
                came = swap(owned.pop(at), bit * PLANE)
                owned[at ^ bit] = (owned[at ^ bit].astype(f32) + came.astype(f32)).astype(bf16)
        bit *= 2
    row_half = owned[0]
    row_grad = joined(row_half, trade(row_half), 1)
    feature_grad = times_t(grad_linear, own_half(w_self, 0)) + times_t(
        row_grad, own_half(q_weight, 0)
    )
    return (embeddings, feature_grad, q_grad, q_bias_grad, w_grad, w_bias_grad)


def solution(mesh):
    in_specs = (
        P("nodes", None),
        P("nodes", "stream"),
        P("nodes", "stream"),
        P("nodes", "stream"),
        P(),
        P(),
        P("stream", None),
        P(),
        P("nodes", None),
    )
    out_specs = (P("nodes", None), P("nodes", "stream"), P(), P(), P("stream", None), P())
    return jax.shard_map(
        on_device, mesh=mesh, in_specs=in_specs, out_specs=out_specs, check_vma=False
    )
```

time: 1340 us -> 247 us (0.18)
  waiting for transfers between devices: 778 us -> 78.3 us
  matrix products: 291 us -> 20.7 us
  local copies, waits for them, and re-layouts: 181 us -> 25.2 us
  starting transfers between devices: 13.9 us -> 79 us
  blocking collectives: 47.7 us -> 0 us
  other arithmetic: 8.3 us -> 33.9 us
    psum x5 -> x0, waiting for transfers between devices: 642 us -> none  [the longest x1 592 us: on_device(): lax.psum((w_grad_local, w_bias_local, q_grad_local, q_bias_local), 'nodes')]
    dot_general x55 -> x14, matrix products: 291 us -> 20.7 us  [the longest x4 9.02 us: across(): lax.dot_general(lhs, rhs, (((0,), (0,)), ((), ())), preferred_element_typ...]
    all_gather x1 -> x0, waiting for transfers between devices: 134 us -> none  [on_device(): shard_rows = lax.all_gather(features, 'nodes', axis=0, tiled=True)]
    ppermute x0 -> x58, starting transfers between devices: none -> 79 us  [the longest x49 52.6 us: swap(): return lax.ppermute(value, 'nodes', [(i, i ^ bit) for i in range(count)])]
    ppermute x0 -> x58, waiting for transfers between devices: none -> 78.3 us  [the longest x49 78.3 us: swap(): return lax.ppermute(value, 'nodes', [(i, i ^ bit) for i in range(count)])]
    reshape x12 -> x1, local copies, waits for them, and re-layouts: 67.1 us -> 0.77 us  [on_device(): jnp.transpose(lists, (2, 1, 0, 3))]
    mul x40 -> x0, local copies, waits for them, and re-layouts: 62.3 us -> none  [backward_block(): importance_block_weights[:, :, None] * grad_block[:, None, :]]
    psum x3 -> x0, blocking collectives: 47.7 us -> none  [the longest x1 34.1 us: on_device(): lax.psum((w_grad_local, w_bias_local, q_grad_local, q_bias_local), 'nodes')]
  transfers between devices with their start and end apart: 9 -> 58, of which waited for: 5 -> 26; matrix products, arithmetic and copies ran while one was open for 21% -> 26% of each run, Pallas kernels for 0% -> 2%
where the time goes in v1:
time: 247 us; the launch traced here: 245 us
  starting transfers between devices  79 us (32%)
  waiting for transfers between devices  78.3 us (32%)
  other arithmetic  33.9 us (14%)
  local copies, waits for them, and re-layouts  25.2 us (10%)
  matrix products  20.7 us (8%)
  Pallas kernels  5.86 us (2%)
    ppermute x49, waiting for transfers between devices, swap(): return lax.ppermute(value, 'nodes', [(i, i ^ bit) for i in range(count)])  78.3 us
    ppermute x49, starting transfers between devices, swap(): return lax.ppermute(value, 'nodes', [(i, i ^ bit) for i in range(count)])  52.6 us
    ppermute x9, starting transfers between devices, trade(): return lax.ppermute(value, 'stream', [(0, 1), (1, 0)])  26.4 us
    select_n x5, other arithmetic, joined(): jnp.where(core == 0, jnp.concatenate([mine, other], axis), jnp.concatenat...  11.6 us
    dot_general x4, matrix products, across(): lax.dot_general(lhs, rhs, (((0,), (0,)), ((), ())), preferred_element_typ...  9.02 us
    pallas_call x1, Pallas kernels, slot_matrix(): pl.pallas_call(slot_matrix_kernel, name='slot_matrix', out_shape=jax.Shap...  5.86 us
    gather x2, local copies, waits for them, and re-layouts, summed(): jnp.take(blocks, order, axis=0)  5.45 us
    gather x2, local copies, waits for them, and re-layouts, summed(): return jnp.take(whole, order, axis=0).reshape(height, width).astype(f32)  5.42 us
  transfers between devices with their start and end apart: 58, of which 26 were waited for; matrix products, arithmetic and copies ran while one was open for 26% of the time, Pallas kernels for 2%

profile of v1, /device:TPU:1, one launch (start us, length us, event | category | flops | bytes accessed | tf_op | source)
XLA Modules:
  0.0 244.7 jit_solution(15003918487735087143)
XLA Ops:
  1.8 3.2 %collective-permute-start.7 = (bf16[160,1024]{1,0:T(8,128)(2,1)S(1)}, bf16[160,1024]{1,0:T(8,128)(2,1)S(1)}, u32[]{:S(2)}, u32[]{:S(2)}) collective-permute-start(bf16[160,1024]{1,0:T(8,128)(2,1)S(1)} %constant_dynamic-slice_fusion), channel_id=1, source_target_pairs={{0,16},{2,18},{4,20},{6,22},{8,24},{10,26},{12,28},{14,30},{16,0},... | collective-permute-start | bytes 983048 | tf_op jit(solution)/shard_map/ppermute | solution.py:56
  9.5 2.5 %fusion.38 = (bf16[320,512]{1,0:T(8,128)(2,1)}, bf16[320,512]{1,0:T(8,128)(2,1)}) fusion(f32[512]{0:T(512)S(1)} %dynamic_slice.24, bf16[320,1024]{1,0:T(8,128)(2,1)} %param.13, bf16[1024,1024]{1,0:T(8,128)(2,1)S(1)} %copy-done, s32[]{:T(128)S(6)} %select_n.166), kind=kOutput, calls=%fused_computation.84 | convolution fusion | flops 336527360 | bytes 2361348 | tf_op jit(solution)/shard_map/dot_general | solution.py:122
  14.6 1.5 collective-permute-done.3
  17.5 2.5 %collective-permute-done.4 = s32[4,16,320]{2,1,0:T(8,128)S(1)} collective-permute-done((s32[4,16,320]{2,1,0:T(8,128)S(1)}, s32[4,16,320]{2,1,0:T(8,128)S(1)}, u32[]{:S(2)}, u32[]{:S(2)}) %collective-permute-start.4) | collective-permute-done | bytes 81952 | tf_op jit(solution)/shard_map/ppermute | solution.py:56
  20.6 1.9 collective-permute-start.8
  24.1 5.9 %slot_matrix.1 = bf16[1280,1280]{1,0:T(8,128)(2,1)} custom-call(s32[4,4,1280]{2,1,0:T(4,128)} %reshape.189.lists_ref), custom_call_target="tpu_custom_call" | custom-call | flops 19660800 | bytes 3276800 | tf_op jit(solution)/shard_map/slot_matrix/pallas_call | solution.py:28
  30.5 1.5 maximum_select_fusion.2
  34.6 1.5 maximum_select_fusion.3
  36.9 1.9 fusion.63
  38.9 1.9 convolution_add_fusion
  43.5 13.8 %collective-permute-done.11 = f32[2,320,256]{2,1,0:T(8,128)S(1)} collective-permute-done((f32[2,320,256]{2,1,0:T(8,128)S(1)}, f32[2,320,256]{2,1,0:T(8,128)S(1)}, u32[]{:S(2)}, u32[]{:S(2)}) %collective-permute-start.11) | collective-permute-done | bytes 655392 | tf_op jit(solution)/shard_map/ppermute | solution.py:56
  60.0 6.4 %collective-permute-done.12 = f32[320,256]{1,0:T(8,128)S(1)} collective-permute-done((f32[320,256]{1,0:T(8,128)S(1)}, f32[320,256]{1,0:T(8,128)S(1)}, u32[]{:S(2)}, u32[]{:S(2)}) %collective-permute-start.12) | collective-permute-done | bytes 327712 | tf_op jit(solution)/shard_map/ppermute | solution.py:56
  67.6 2.4 collective-permute-start.15
  70.0 2.1 broadcast_select_fusion.3
  75.4 1.6 convert_reduce_fusion
  79.0 2.6 %convolution_convert_fusion = bf16[1024,1024]{1,0:T(8,128)(2,1)} fusion(bf16[320,1024]{1,0:T(8,128)(2,1)S(1)} %get-tuple-element.13, bf16[320,1024]{1,0:T(8,128)(2,1)S(1)} %copy-done.19, pred[]{:T(512)S(6)} %eq.19, bf16[320,512]{1,0:T(8,128)(2,1)S(1)} %collective-permute-done.15, bf16[320,512]{1,0:T(8,128)(2,1)S(1)} %fusion.42), kind=kOutput, calls=%fused_computation.22 | convolution fusion | flops 675414016 | bytes 4063233 | tf_op jit(solution)/shard_map/dot_general | solution.py:130
  81.6 3.6 %gather_fusion.3 = bf16[16,64,1024]{2,1,0:T(8,128)(2,1)} fusion(bf16[16,64,1024]{2,1,0:T(8,128)(2,1)} %bitcast.161, s32[1024]{0:T(1024)S(1)} %pad_clamp_fusion), kind=kCustom, calls=%fused_computation.1.clone | custom fusion | bytes 4194368 | tf_op jit(solution)/shard_map/jit(_take)/gather | solution.py:179
  85.2 1.8 broadcast_select_fusion
  93.4 14.2 %collective-permute-done.18 = bf16[160,512]{1,0:T(8,128)(2,1)S(1)} collective-permute-done((bf16[160,512]{1,0:T(8,128)(2,1)S(1)}, bf16[160,512]{1,0:T(8,128)(2,1)S(1)}, u32[]{:S(2)}, u32[]{:S(2)}) %collective-permute-start.18) | collective-permute-done | bytes 163872 | tf_op jit(solution)/shard_map/ppermute | solution.py:56
  107.8 2.2 fusion.110
  110.5 2.6 %fusion.8 = bf16[1024,512]{1,0:T(8,128)(2,1)} fusion(bf16[1280,512]{1,0:T(8,128)(2,1)S(1)} %get-tuple-element.17, bf16[320,1024]{1,0:T(8,128)(2,1)S(1)} %copy-done.17, bf16[320,1024]{1,0:T(8,128)(2,1)S(1)} %maximum_select_fusion.2, bf16[320,1024]{1,0:T(8,128)(2,1)S(1)} %copy-done.15, bf16[320,1024]{1,0:T(8,128)(2,1)S(1)} %copy-done.20), kind=kOutput, calls=%fused_computation.25 | convolution fusion | flops 1353187328 | bytes 4980736 | tf_op jit(solution)/shard_map/dot_general | solution.py:130
  113.1 1.8 gather_fusion.1
  121.3 2.3 collective-permute-start.42
  123.7 7.2 %collective-permute-done.42 = f32[3,512]{1,0:T(4,128)S(1)} collective-permute-done((f32[3,512]{1,0:T(4,128)S(1)}, f32[3,512]{1,0:T(4,128)S(1)}, u32[]{:S(2)}, u32[]{:S(2)}) %collective-permute-start.42) | collective-permute-done | bytes 6176 | tf_op jit(solution)/shard_map/ppermute | solution.py:56
  139.1 1.7 collective-permute-done.45
  141.3 2.7 %collective-permute-done.47 = bf16[4,64,512]{2,1,0:T(8,128)(2,1)S(1)} collective-permute-done((bf16[4,64,512]{2,1,0:T(8,128)(2,1)S(1)}, bf16[4,64,512]{2,1,0:T(8,128)(2,1)S(1)}, u32[]{:S(2)}, u32[]{:S(2)}) %collective-permute-start.47) | collective-permute-done | bytes 262176 | tf_op jit(solution)/shard_map/ppermute | solution.py:56
  145.4 4.3 %collective-permute-start.29 = (bf16[64,512]{1,0:T(8,128)(2,1)S(1)}, bf16[64,512]{1,0:T(8,128)(2,1)S(1)}, u32[]{:S(2)}, u32[]{:S(2)}) collective-permute-start(bf16[64,512]{1,0:T(8,128)(2,1)S(1)} %get-tuple-element.54), channel_id=1, source_target_pairs={{0,8},{2,10},{4,12},{6,14},{8,0},{10,2},{12,4},{14,6},{16,24},{18,... | collective-permute-start | bytes 196616 | tf_op jit(solution)/shard_map/ppermute | solution.py:56
  149.9 1.5 collective-permute-start.48
  151.7 1.5 collective-permute-start.28
  153.7 2.1 collective-permute-done.28
  156.2 1.5 collective-permute-done.30
  158.9 11.0 %collective-permute-start.43 = (f32[512]{0:T(512)S(1)}, f32[512]{0:T(512)S(1)}, u32[]{:S(2)}, u32[]{:S(2)}) collective-permute-start(f32[512]{0:T(512)S(1)} %bitcast.192), channel_id=1, source_target_pairs={{0,1},{1,0},{2,3},{3,2},{4,5},{5,4},{6,7},{7,6},{8,9},{9,8},{10,11... | collective-permute-start | bytes 6152 | tf_op jit(solution)/shard_map/ppermute | solution.py:59
  169.9 1.5 collective-permute-start.33
  171.4 1.6 collective-permute-done.31
  173.0 3.1 %collective-permute-start.52 = (bf16[64,1024]{1,0:T(8,128)(2,1)S(1)}, bf16[64,1024]{1,0:T(8,128)(2,1)S(1)}, u32[]{:S(2)}, u32[]{:S(2)}) collective-permute-start(bf16[64,1024]{1,0:T(8,128)(2,1)S(1)} %add_convert_fusion.7), channel_id=1, source_target_pairs={{0,16},{2,18},{4,20},{6,22},{8,24},{10,26},{12,28},{14,30},{16,0},... | collective-permute-start | bytes 393224 | tf_op jit(solution)/shard_map/ppermute | solution.py:56
  182.4 2.3 collective-permute-done.51
  187.2 1.9 collective-permute-start.35
  190.1 3.1 %collective-permute-done.35 = bf16[4,2,64,256]{3,2,0,1:T(8,128)(2,1)S(1)} collective-permute-done((bf16[4,2,64,256]{3,2,0,1:T(8,128)(2,1)S(1)}, bf16[4,2,64,256]{3,2,0,1:T(8,128)(2,1)S(1)}, u32[]{:S(2)}, u32[]{:S(2)}) %collective-permute-start.35) | collective-permute-done | bytes 262176 | tf_op jit(solution)/shard_map/ppermute | solution.py:56
  193.2 1.5 collective-permute-start.56
  197.2 1.8 gather_fusion.2
  199.2 1.7 bitcast_convert_fusion.1
  200.9 9.2 %collective-permute-start.38 = (f32[1024,512]{1,0:T(8,128)}, f32[1024,512]{1,0:T(8,128)}, u32[]{:S(2)}, u32[]{:S(2)}) collective-permute-start(f32[1024,512]{1,0:T(8,128)} %bitcast_convert_fusion.1), channel_id=1, source_target_pairs={{0,1},{1,0},{2,3},{3,2},{4,5},{5,4},{6,7},{7,6},{8,9},{9,8},{10,11... | collective-permute-start | bytes 6291464 | tf_op jit(solution)/shard_map/ppermute | solution.py:59
  217.6 8.6 %collective-permute-done.55 = bf16[4,2,64,512]{3,2,0,1:T(8,128)(2,1)S(1)} collective-permute-done((bf16[4,2,64,512]{3,2,0,1:T(8,128)(2,1)S(1)}, bf16[4,2,64,512]{3,2,0,1:T(8,128)(2,1)S(1)}, u32[]{:S(2)}, u32[]{:S(2)}) %collective-permute-start.55) | collective-permute-done | bytes 524320 | tf_op jit(solution)/shard_map/ppermute | solution.py:56
  228.5 1.5 copy.47
  230.0 3.6 %gather_fusion.4 = bf16[16,64,1024]{2,1,0:T(8,128)(2,1)} fusion(bf16[16,64,1024]{2,1,0:T(8,128)(2,1)} %bitcast.152, s32[1024]{0:T(1024)S(1)} %pad_clamp_fusion), kind=kCustom, calls=%fused_computation.3.clone | custom fusion | bytes 4194368 | tf_op jit(solution)/shard_map/jit(_take)/gather | solution.py:215
  233.6 1.8 broadcast_select_fusion.1
  235.4 2.6 %bitcast_convert_fusion = f32[1024,1024]{1,0:T(8,128)} fusion(bf16[16,64,1024]{2,1,0:T(8,128)(2,1)S(1)} %broadcast_select_fusion.1), kind=kLoop, calls=%fused_computation.17 | loop fusion | flops 1048576 | bytes 6291456 | tf_op jit(solution)/shard_map/convert_element_type | solution.py:215
  238.1 6.6 %maximum_select_fusion = f32[1024,1024]{1,0:T(8,128)} fusion(f32[1024,512]{1,0:T(8,128)} %collective-permute-done.38, f32[1024,512]{1,0:T(8,128)} %bitcast_convert_fusion.1, pred[]{:T(512)S(6)} %eq.19), kind=kLoop, calls=%fused_computation.5 | loop fusion | flops 3145728 | bytes 8388609 | tf_op jit(solution)/shard_map/jit(_where)/select_n | solution.py:66
  (255 shorter events, 75.1 us)
Async XLA Ops:
  1.8 18.2 %collective-permute-start.7 = (bf16[160,1024]{1,0:T(8,128)(2,1)S(1)}, bf16[160,1024]{1,0:T(8,128)(2,1)S(1)}, u32[]{:S(2)}, u32[]{:S(2)}) collective-permute-start(bf16[160,1024]{1,0:T(8,128)(2,1)S(1)} %constant_dynamic-slice_fusion), channel_id=1, source_target_pairs={{0,16},{2,18},{4,20},{6,22},{8,24},{10,26},{12,28},{14,30},{16,0},... | collective-permute-start | bytes 983048 | tf_op jit(solution)/shard_map/ppermute | solution.py:56
  5.0 24.9 %collective-permute-start.5 = (bf16[160,1024]{1,0:T(8,128)(2,1)S(1)}, bf16[160,1024]{1,0:T(8,128)(2,1)}, u32[]{:S(2)}, u32[]{:S(2)}) collective-permute-start(bf16[160,1024]{1,0:T(8,128)(2,1)S(1)} %constant_dynamic-slice_fusion), channel_id=1, source_target_pairs={{0,8},{2,10},{4,12},{6,14},{8,0},{10,2},{12,4},{14,6},{16,24},{18,... | collective-permute-start | bytes 983048 | tf_op jit(solution)/shard_map/ppermute | solution.py:56
  6.3 63.7 %collective-permute-start = (bf16[1024,1024]{1,0:T(8,128)(2,1)}, bf16[1024,1024]{1,0:T(8,128)(2,1)}, u32[]{:S(2)}, u32[]{:S(2)}) collective-permute-start(bf16[1024,1024]{1,0:T(8,128)(2,1)} %param.19), channel_id=1, source_target_pairs={{0,1},{1,0},{2,3},{3,2},{4,5},{5,4},{6,7},{7,6},{8,9},{9,8},{10,11... | collective-permute-start | bytes 6291464 | tf_op jit(solution)/shard_map/ppermute | solution.py:59
  12.1 4.1 %collective-permute-start.3 = (s32[4,16,320]{2,1,0:T(8,128)S(1)}, s32[4,16,320]{2,1,0:T(8,128)S(1)}, u32[]{:S(2)}, u32[]{:S(2)}) collective-permute-start(s32[4,16,320]{2,1,0:T(8,128)S(1)} %get-tuple-element.56), channel_id=1, source_target_pairs={{0,4},{2,6},{4,0},{6,2},{8,12},{10,14},{12,8},{14,10},{16,20},{18,... | collective-permute-start | bytes 245768 | tf_op jit(solution)/shard_map/ppermute | solution.py:56
  13.4 4.1 %collective-permute-start.2 = (s32[4,16,320]{2,1,0:T(8,128)S(1)}, s32[4,16,320]{2,1,0:T(8,128)S(1)}, u32[]{:S(2)}, u32[]{:S(2)}) collective-permute-start(s32[4,16,320]{2,1,0:T(8,128)S(1)} %get-tuple-element.56), channel_id=1, source_target_pairs={{0,2},{2,0},{4,6},{6,4},{8,10},{10,8},{12,14},{14,12},{16,18},{18,... | collective-permute-start | bytes 245768 | tf_op jit(solution)/shard_map/ppermute | solution.py:56
  20.1 9.9 %collective-permute-start.9 = (bf16[160,1024]{1,0:T(8,128)(2,1)S(1)}, bf16[160,1024]{1,0:T(8,128)(2,1)}, u32[]{:S(2)}, u32[]{:S(2)}) collective-permute-start(bf16[160,1024]{1,0:T(8,128)(2,1)S(1)} %collective-permute-done.7), channel_id=1, source_target_pairs={{0,8},{2,10},{4,12},{6,14},{8,0},{10,2},{12,4},{14,6},{16,24},{18,... | collective-permute-start | bytes 983048 | tf_op jit(solution)/shard_map/ppermute | solution.py:56
  20.6 9.8 %collective-permute-start.8 = (bf16[160,1024]{1,0:T(8,128)(2,1)S(1)}, bf16[160,1024]{1,0:T(8,128)(2,1)}, u32[]{:S(2)}, u32[]{:S(2)}) collective-permute-start(bf16[160,1024]{1,0:T(8,128)(2,1)S(1)} %collective-permute-done.7), channel_id=1, source_target_pairs={{0,1},{1,0},{2,3},{3,2},{4,5},{5,4},{6,7},{7,6},{8,9},{9,8},{10,11... | collective-permute-start | bytes 983048 | tf_op jit(solution)/shard_map/ppermute | solution.py:59
  30.0 4.6 %collective-permute-start.10 = (bf16[160,1024]{1,0:T(8,128)(2,1)}, bf16[160,1024]{1,0:T(8,128)(2,1)S(1)}, u32[]{:S(2)}, u32[]{:S(2)}) collective-permute-start(bf16[160,1024]{1,0:T(8,128)(2,1)} %collective-permute-done.9), channel_id=1, source_target_pairs={{0,1},{1,0},{2,3},{3,2},{4,5},{5,4},{6,7},{7,6},{8,9},{9,8},{10,11... | collective-permute-start | bytes 983048 | tf_op jit(solution)/shard_map/ppermute | solution.py:59
  40.9 16.4 %collective-permute-start.11 = (f32[2,320,256]{2,1,0:T(8,128)S(1)}, f32[2,320,256]{2,1,0:T(8,128)S(1)}, u32[]{:S(2)}, u32[]{:S(2)}) collective-permute-start(f32[2,320,256]{2,1,0:T(8,128)S(1)} %pad_maximum_fusion.1), channel_id=1, source_target_pairs={{0,2},{2,0},{4,6},{6,4},{8,10},{10,8},{12,14},{14,12},{16,18},{18,... | collective-permute-start | bytes 1966088 | tf_op jit(solution)/shard_map/ppermute | solution.py:56
  42.2 16.0 %collective-permute-start.13 = (f32[2,320,256]{2,1,0:T(8,128)S(1)}, f32[2,320,256]{2,1,0:T(8,128)S(1)}, u32[]{:S(2)}, u32[]{:S(2)}) collective-permute-start(f32[2,320,256]{2,1,0:T(8,128)S(1)} %stack.149), channel_id=1, source_target_pairs={{0,4},{2,6},{4,0},{6,2},{8,12},{10,14},{12,8},{14,10},{16,20},{18,... | collective-permute-start | bytes 1966088 | tf_op jit(solution)/shard_map/ppermute | solution.py:56
  58.3 8.1 %collective-permute-start.12 = (f32[320,256]{1,0:T(8,128)S(1)}, f32[320,256]{1,0:T(8,128)S(1)}, u32[]{:S(2)}, u32[]{:S(2)}) collective-permute-start(f32[320,256]{1,0:T(8,128)S(1)} %get-tuple-element.20), channel_id=1, source_target_pairs={{0,4},{2,6},{4,0},{6,2},{8,12},{10,14},{12,8},{14,10},{16,20},{18,... | collective-permute-start | bytes 983048 | tf_op jit(solution)/shard_map/ppermute | solution.py:56
  59.6 7.7 %collective-permute-start.14 = (f32[320,256]{1,0:T(8,128)S(1)}, f32[320,256]{1,0:T(8,128)S(1)}, u32[]{:S(2)}, u32[]{:S(2)}) collective-permute-start(f32[320,256]{1,0:T(8,128)S(1)} %get-tuple-element.21), channel_id=1, source_target_pairs={{0,2},{2,0},{4,6},{6,4},{8,10},{10,8},{12,14},{14,12},{16,18},{18,... | collective-permute-start | bytes 983048 | tf_op jit(solution)/shard_map/ppermute | solution.py:56
  67.6 4.6 %collective-permute-start.15 = (bf16[320,512]{1,0:T(8,128)(2,1)S(1)}, bf16[320,512]{1,0:T(8,128)(2,1)S(1)}, u32[]{:S(2)}, u32[]{:S(2)}) collective-permute-start(bf16[320,512]{1,0:T(8,128)(2,1)S(1)} %fusion.42), channel_id=1, source_target_pairs={{0,1},{1,0},{2,3},{3,2},{4,5},{5,4},{6,7},{7,6},{8,9},{9,8},{10,11... | collective-permute-start | bytes 983048 | tf_op jit(solution)/shard_map/ppermute | solution.py:59
  78.4 14.2 %collective-permute-start.16 = (bf16[320,512]{1,0:T(8,128)(2,1)}, bf16[320,512]{1,0:T(8,128)(2,1)S(1)}, u32[]{:S(2)}, u32[]{:S(2)}) collective-permute-start(bf16[320,512]{1,0:T(8,128)(2,1)} %get-tuple-element.65), channel_id=1, source_target_pairs={{0,2},{2,0},{4,6},{6,4},{8,10},{10,8},{12,14},{14,12},{16,18},{18,... | collective-permute-start | bytes 983048 | tf_op jit(solution)/shard_map/ppermute | solution.py:56
  78.7 14.2 %collective-permute-start.17 = (bf16[320,512]{1,0:T(8,128)(2,1)}, bf16[320,512]{1,0:T(8,128)(2,1)S(1)}, u32[]{:S(2)}, u32[]{:S(2)}) collective-permute-start(bf16[320,512]{1,0:T(8,128)(2,1)} %get-tuple-element.65), channel_id=1, source_target_pairs={{0,4},{2,6},{4,0},{6,2},{8,12},{10,14},{12,8},{14,10},{16,20},{18,... | collective-permute-start | bytes 983048 | tf_op jit(solution)/shard_map/ppermute | solution.py:56
  90.3 41.7 %collective-permute-start.44 = (bf16[4,2,64,512]{3,2,0,1:T(8,128)(2,1)}, bf16[4,2,64,512]{3,2,0,1:T(8,128)(2,1)}, u32[]{:S(2)}, u32[]{:S(2)}) collective-permute-start(bf16[4,2,64,512]{3,2,0,1:T(8,128)(2,1)} %copy.54), channel_id=1, source_target_pairs={{0,2},{2,0},{4,6},{6,4},{8,10},{10,8},{12,14},{14,12},{16,18},{18,... | collective-permute-start | bytes 1572872 | tf_op jit(solution)/shard_map/ppermute | solution.py:56
  91.4 43.1 %collective-permute-start.46 = (bf16[4,2,64,512]{3,2,1,0:T(8,128)(2,1)}, bf16[4,2,64,512]{3,2,1,0:T(8,128)(2,1)}, u32[]{:S(2)}, u32[]{:S(2)}) collective-permute-start(bf16[4,2,64,512]{3,2,1,0:T(8,128)(2,1)} %slice.284), channel_id=1, source_target_pairs={{0,4},{2,6},{4,0},{6,2},{8,12},{10,14},{12,8},{14,10},{16,20},{18,... | collective-permute-start | bytes 1572872 | tf_op jit(solution)/shard_map/ppermute | solution.py:56
  92.7 15.0 %collective-permute-start.18 = (bf16[160,512]{1,0:T(8,128)(2,1)S(1)}, bf16[160,512]{1,0:T(8,128)(2,1)S(1)}, u32[]{:S(2)}, u32[]{:S(2)}) collective-permute-start(bf16[160,512]{1,0:T(8,128)(2,1)S(1)} %slice.256), channel_id=1, source_target_pairs={{0,4},{2,6},{4,0},{6,2},{8,12},{10,14},{12,8},{14,10},{16,20},{18,... | collective-permute-start | bytes 491528 | tf_op jit(solution)/shard_map/ppermute | solution.py:56
  93.0 14.7 %collective-permute-start.19 = (bf16[160,512]{1,0:T(8,128)(2,1)S(1)}, bf16[160,512]{1,0:T(8,128)(2,1)S(1)}, u32[]{:S(2)}, u32[]{:S(2)}) collective-permute-start(bf16[160,512]{1,0:T(8,128)(2,1)S(1)} %slice.257), channel_id=1, source_target_pairs={{0,2},{2,0},{4,6},{6,4},{8,10},{10,8},{12,14},{14,12},{16,18},{18,... | collective-permute-start | bytes 491528 | tf_op jit(solution)/shard_map/ppermute | solution.py:56
  110.1 4.9 %collective-permute-start.39 = (f32[3,512]{1,0:T(4,128)S(1)}, f32[3,512]{1,0:T(4,128)S(1)}, u32[]{:S(2)}, u32[]{:S(2)}) collective-permute-start(f32[3,512]{1,0:T(4,128)S(1)} %pad_maximum_fusion.11), channel_id=1, source_target_pairs={{0,2},{2,0},{4,6},{6,4},{8,10},{10,8},{12,14},{14,12},{16,18},{18,... | collective-permute-start | bytes 18440 | tf_op jit(solution)/shard_map/ppermute | solution.py:56
  119.7 57.5 %collective-permute-start.21 = (bf16[320,512]{1,0:T(8,128)(2,1)S(1)}, bf16[320,512]{1,0:T(8,128)(2,1)S(1)}, u32[]{:S(2)}, u32[]{:S(2)}) collective-permute-start(bf16[320,512]{1,0:T(8,128)(2,1)S(1)} %get-tuple-element.26), channel_id=1, source_target_pairs={{0,8},{2,10},{4,12},{6,14},{8,0},{10,2},{12,4},{14,6},{16,24},{18,... | collective-permute-start | bytes 983048 | tf_op jit(solution)/shard_map/ppermute | solution.py:56
  120.0 80.9 %collective-permute-start.20 = (bf16[320,512]{1,0:T(8,128)(2,1)}, bf16[320,512]{1,0:T(8,128)(2,1)}, u32[]{:S(2)}, u32[]{:S(2)}) collective-permute-start(bf16[320,512]{1,0:T(8,128)(2,1)} %get-tuple-element.25), channel_id=1, source_target_pairs={{0,8},{2,10},{4,12},{6,14},{8,0},{10,2},{12,4},{14,6},{16,24},{18,... | collective-permute-start | bytes 983048 | tf_op jit(solution)/shard_map/ppermute | solution.py:56
  121.3 9.6 %collective-permute-start.42 = (f32[3,512]{1,0:T(4,128)S(1)}, f32[3,512]{1,0:T(4,128)S(1)}, u32[]{:S(2)}, u32[]{:S(2)}) collective-permute-start(f32[3,512]{1,0:T(4,128)S(1)} %add.270), channel_id=1, source_target_pairs={{0,16},{2,18},{4,20},{6,22},{8,24},{10,26},{12,28},{14,30},{16,0},... | collective-permute-start | bytes 18440 | tf_op jit(solution)/shard_map/ppermute | solution.py:56
  130.9 5.6 %collective-permute-start.24 = (bf16[4,2,64,256]{3,2,0,1:T(8,128)(2,1)S(1)}, bf16[4,2,64,256]{3,2,0,1:T(8,128)(2,1)S(1)}, u32[]{:S(2)}, u32[]{:S(2)}) collective-permute-start(bf16[4,2,64,256]{3,2,0,1:T(8,128)(2,1)S(1)} %copy.50), channel_id=1, source_target_pairs={{0,2},{2,0},{4,6},{6,4},{8,10},{10,8},{12,14},{14,12},{16,18},{18,... | collective-permute-start | bytes 786440 | tf_op jit(solution)/shard_map/ppermute | solution.py:56
  132.0 5.7 %collective-permute-start.26 = (bf16[4,2,64,256]{3,2,1,0:T(8,128)(2,1)S(1)}, bf16[4,2,64,256]{3,2,1,0:T(8,128)(2,1)S(1)}, u32[]{:S(2)}, u32[]{:S(2)}) collective-permute-start(bf16[4,2,64,256]{3,2,1,0:T(8,128)(2,1)S(1)} %slice.266), channel_id=1, source_target_pairs={{0,4},{2,6},{4,0},{6,2},{8,12},{10,14},{12,8},{14,10},{16,20},{18,... | collective-permute-start | bytes 786440 | tf_op jit(solution)/shard_map/ppermute | solution.py:56
  134.5 6.3 %collective-permute-start.45 = (bf16[4,64,512]{2,1,0:T(8,128)(2,1)S(1)}, bf16[4,64,512]{2,1,0:T(8,128)(2,1)S(1)}, u32[]{:S(2)}, u32[]{:S(2)}) collective-permute-start(bf16[4,64,512]{2,1,0:T(8,128)(2,1)S(1)} %slice_bitcast_fusion.2), channel_id=1, source_target_pairs={{0,4},{2,6},{4,0},{6,2},{8,12},{10,14},{12,8},{14,10},{16,20},{18,... | collective-permute-start | bytes 786440 | tf_op jit(solution)/shard_map/ppermute | solution.py:56
  136.5 7.5 %collective-permute-start.47 = (bf16[4,64,512]{2,1,0:T(8,128)(2,1)S(1)}, bf16[4,64,512]{2,1,0:T(8,128)(2,1)S(1)}, u32[]{:S(2)}, u32[]{:S(2)}) collective-permute-start(bf16[4,64,512]{2,1,0:T(8,128)(2,1)S(1)} %slice_bitcast_fusion), channel_id=1, source_target_pairs={{0,2},{2,0},{4,6},{6,4},{8,10},{10,8},{12,14},{14,12},{16,18},{18,... | collective-permute-start | bytes 786440 | tf_op jit(solution)/shard_map/ppermute | solution.py:56
  137.7 6.4 %collective-permute-start.25 = (bf16[4,64,256]{2,1,0:T(8,128)(2,1)S(1)}, bf16[4,64,256]{2,1,0:T(8,128)(2,1)S(1)}, u32[]{:S(2)}, u32[]{:S(2)}) collective-permute-start(bf16[4,64,256]{2,1,0:T(8,128)(2,1)S(1)} %slice_bitcast_fusion.6), channel_id=1, source_target_pairs={{0,4},{2,6},{4,0},{6,2},{8,12},{10,14},{12,8},{14,10},{16,20},{18,... | collective-permute-start | bytes 393224 | tf_op jit(solution)/shard_map/ppermute | solution.py:56
  140.8 4.6 %collective-permute-start.27 = (bf16[4,64,256]{2,1,0:T(8,128)(2,1)S(1)}, bf16[4,64,256]{2,1,0:T(8,128)(2,1)S(1)}, u32[]{:S(2)}, u32[]{:S(2)}) collective-permute-start(bf16[4,64,256]{2,1,0:T(8,128)(2,1)S(1)} %slice_bitcast_fusion.4), channel_id=1, source_target_pairs={{0,2},{2,0},{4,6},{6,4},{8,10},{10,8},{12,14},{14,12},{16,18},{18,... | collective-permute-start | bytes 393224 | tf_op jit(solution)/shard_map/ppermute | solution.py:56
  145.4 6.3 %collective-permute-start.29 = (bf16[64,512]{1,0:T(8,128)(2,1)S(1)}, bf16[64,512]{1,0:T(8,128)(2,1)S(1)}, u32[]{:S(2)}, u32[]{:S(2)}) collective-permute-start(bf16[64,512]{1,0:T(8,128)(2,1)S(1)} %get-tuple-element.54), channel_id=1, source_target_pairs={{0,8},{2,10},{4,12},{6,14},{8,0},{10,2},{12,4},{14,6},{16,24},{18,... | collective-permute-start | bytes 196616 | tf_op jit(solution)/shard_map/ppermute | solution.py:56
  149.9 9.0 %collective-permute-start.48 = (bf16[64,1024]{1,0:T(8,128)(2,1)S(1)}, bf16[64,1024]{1,0:T(8,128)(2,1)S(1)}, u32[]{:S(2)}, u32[]{:S(2)}) collective-permute-start(bf16[64,1024]{1,0:T(8,128)(2,1)S(1)} %get-tuple-element.43), channel_id=1, source_target_pairs={{0,8},{2,10},{4,12},{6,14},{8,0},{10,2},{12,4},{14,6},{16,24},{18,... | collective-permute-start | bytes 393224 | tf_op jit(solution)/shard_map/ppermute | solution.py:56
  151.7 4.1 %collective-permute-start.28 = (bf16[64,512]{1,0:T(8,128)(2,1)S(1)}, bf16[64,512]{1,0:T(8,128)(2,1)S(1)}, u32[]{:S(2)}, u32[]{:S(2)}) collective-permute-start(bf16[64,512]{1,0:T(8,128)(2,1)S(1)} %get-tuple-element.53), channel_id=1, source_target_pairs={{0,8},{2,10},{4,12},{6,14},{8,0},{10,2},{12,4},{14,6},{16,24},{18,... | collective-permute-start | bytes 196616 | tf_op jit(solution)/shard_map/ppermute | solution.py:56
  155.8 14.1 %collective-permute-start.50 = (bf16[64,1024]{1,0:T(8,128)(2,1)S(1)}, bf16[64,1024]{1,0:T(8,128)(2,1)S(1)}, u32[]{:S(2)}, u32[]{:S(2)}) collective-permute-start(bf16[64,1024]{1,0:T(8,128)(2,1)S(1)} %fusion.59), channel_id=1, source_target_pairs={{0,16},{2,18},{4,20},{6,22},{8,24},{10,26},{12,28},{14,30},{16,0},... | collective-permute-start | bytes 393224 | tf_op jit(solution)/shard_map/ppermute | solution.py:56
  157.8 12.1 %collective-permute-start.32 = (bf16[64,512]{1,0:T(8,128)(2,1)S(1)}, bf16[64,512]{1,0:T(8,128)(2,1)S(1)}, u32[]{:S(2)}, u32[]{:S(2)}) collective-permute-start(bf16[64,512]{1,0:T(8,128)(2,1)S(1)} %add_convert_fusion.8), channel_id=1, source_target_pairs={{0,16},{2,18},{4,20},{6,22},{8,24},{10,26},{12,28},{14,30},{16,0},... | collective-permute-start | bytes 196616 | tf_op jit(solution)/shard_map/ppermute | solution.py:56
  158.9 52.6 %collective-permute-start.43 = (f32[512]{0:T(512)S(1)}, f32[512]{0:T(512)S(1)}, u32[]{:S(2)}, u32[]{:S(2)}) collective-permute-start(f32[512]{0:T(512)S(1)} %bitcast.192), channel_id=1, source_target_pairs={{0,1},{1,0},{2,3},{3,2},{4,5},{5,4},{6,7},{7,6},{8,9},{9,8},{10,11... | collective-permute-start | bytes 6152 | tf_op jit(solution)/shard_map/ppermute | solution.py:59
  169.9 6.3 %collective-permute-start.33 = (bf16[64,512]{1,0:T(8,128)(2,1)S(1)}, bf16[64,512]{1,0:T(8,128)(2,1)S(1)}, u32[]{:S(2)}, u32[]{:S(2)}) collective-permute-start(bf16[64,512]{1,0:T(8,128)(2,1)S(1)} %collective-permute-done.32), channel_id=1, source_target_pairs={{0,8},{2,10},{4,12},{6,14},{8,0},{10,2},{12,4},{14,6},{16,24},{18,... | collective-permute-start | bytes 196616 | tf_op jit(solution)/shard_map/ppermute | solution.py:56
  173.0 6.5 %collective-permute-start.52 = (bf16[64,1024]{1,0:T(8,128)(2,1)S(1)}, bf16[64,1024]{1,0:T(8,128)(2,1)S(1)}, u32[]{:S(2)}, u32[]{:S(2)}) collective-permute-start(bf16[64,1024]{1,0:T(8,128)(2,1)S(1)} %add_convert_fusion.7), channel_id=1, source_target_pairs={{0,16},{2,18},{4,20},{6,22},{8,24},{10,26},{12,28},{14,30},{16,0},... | collective-permute-start | bytes 393224 | tf_op jit(solution)/shard_map/ppermute | solution.py:56
  177.3 4.1 %collective-permute-start.34 = (bf16[4,64,256]{2,1,0:T(8,128)(2,1)S(1)}, bf16[4,64,256]{2,1,0:T(8,128)(2,1)S(1)}, u32[]{:S(2)}, u32[]{:S(2)}) collective-permute-start(bf16[4,64,256]{2,1,0:T(8,128)(2,1)S(1)} %get-tuple-element.52), channel_id=1, source_target_pairs={{0,4},{2,6},{4,0},{6,2},{8,12},{10,14},{12,8},{14,10},{16,20},{18,... | collective-permute-start | bytes 393224 | tf_op jit(solution)/shard_map/ppermute | solution.py:56
  179.5 5.2 %collective-permute-start.51 = (bf16[64,1024]{1,0:T(8,128)(2,1)S(1)}, bf16[64,1024]{1,0:T(8,128)(2,1)S(1)}, u32[]{:S(2)}, u32[]{:S(2)}) collective-permute-start(bf16[64,1024]{1,0:T(8,128)(2,1)S(1)} %add_convert_fusion.7), channel_id=1, source_target_pairs={{0,8},{2,10},{4,12},{6,14},{8,0},{10,2},{12,4},{14,6},{16,24},{18,... | collective-permute-start | bytes 393224 | tf_op jit(solution)/shard_map/ppermute | solution.py:56
  180.1 7.1 %collective-permute-start.53 = (bf16[64,1024]{1,0:T(8,128)(2,1)S(1)}, bf16[64,1024]{1,0:T(8,128)(2,1)S(1)}, u32[]{:S(2)}, u32[]{:S(2)}) collective-permute-start(bf16[64,1024]{1,0:T(8,128)(2,1)S(1)} %collective-permute-done.52), channel_id=1, source_target_pairs={{0,8},{2,10},{4,12},{6,14},{8,0},{10,2},{12,4},{14,6},{16,24},{18,... | collective-permute-start | bytes 393224 | tf_op jit(solution)/shard_map/ppermute | solution.py:56
  181.4 28.7 %collective-permute-start.22 = (bf16[320,512]{1,0:T(8,128)(2,1)}, bf16[320,512]{1,0:T(8,128)(2,1)}, u32[]{:S(2)}, u32[]{:S(2)}) collective-permute-start(bf16[320,512]{1,0:T(8,128)(2,1)} %add_convert_fusion.3), channel_id=1, source_target_pairs={{0,16},{2,18},{4,20},{6,22},{8,24},{10,26},{12,28},{14,30},{16,0},... | collective-permute-start | bytes 983048 | tf_op jit(solution)/shard_map/ppermute | solution.py:56
  184.7 10.0 %collective-permute-start.37 = (bf16[4,2,64,256]{3,2,0,1:T(8,128)(2,1)S(1)}, bf16[4,2,64,256]{3,2,0,1:T(8,128)(2,1)S(1)}, u32[]{:S(2)}, u32[]{:S(2)}) collective-permute-start(bf16[4,2,64,256]{3,2,0,1:T(8,128)(2,1)S(1)} %pad_maximum_fusion.7), channel_id=1, source_target_pairs={{0,4},{2,6},{4,0},{6,2},{8,12},{10,14},{12,8},{14,10},{16,20},{18,... | collective-permute-start | bytes 786440 | tf_op jit(solution)/shard_map/ppermute | solution.py:56
  187.2 6.0 %collective-permute-start.35 = (bf16[4,2,64,256]{3,2,0,1:T(8,128)(2,1)S(1)}, bf16[4,2,64,256]{3,2,0,1:T(8,128)(2,1)S(1)}, u32[]{:S(2)}, u32[]{:S(2)}) collective-permute-start(bf16[4,2,64,256]{3,2,0,1:T(8,128)(2,1)S(1)} %pad_maximum_fusion.6), channel_id=1, source_target_pairs={{0,2},{2,0},{4,6},{6,4},{8,10},{10,8},{12,14},{14,12},{16,18},{18,... | collective-permute-start | bytes 786440 | tf_op jit(solution)/shard_map/ppermute | solution.py:56
  193.2 20.2 %collective-permute-start.56 = (bf16[4,64,512]{2,1,0:T(8,128)(2,1)}, bf16[4,64,512]{2,1,0:T(8,128)(2,1)}, u32[]{:S(2)}, u32[]{:S(2)}) collective-permute-start(bf16[4,64,512]{2,1,0:T(8,128)(2,1)} %get-tuple-element.41), channel_id=1, source_target_pairs={{0,2},{2,0},{4,6},{6,4},{8,10},{10,8},{12,14},{14,12},{16,18},{18,... | collective-permute-start | bytes 786440 | tf_op jit(solution)/shard_map/ppermute | solution.py:56
  194.7 17.3 %collective-permute-start.54 = (bf16[4,64,512]{2,1,0:T(8,128)(2,1)}, bf16[4,64,512]{2,1,0:T(8,128)(2,1)}, u32[]{:S(2)}, u32[]{:S(2)}) collective-permute-start(bf16[4,64,512]{2,1,0:T(8,128)(2,1)} %get-tuple-element.42), channel_id=1, source_target_pairs={{0,4},{2,6},{4,0},{6,2},{8,12},{10,14},{12,8},{14,10},{16,20},{18,... | collective-permute-start | bytes 786440 | tf_op jit(solution)/shard_map/ppermute | solution.py:56
  200.9 37.2 %collective-permute-start.38 = (f32[1024,512]{1,0:T(8,128)}, f32[1024,512]{1,0:T(8,128)}, u32[]{:S(2)}, u32[]{:S(2)}) collective-permute-start(f32[1024,512]{1,0:T(8,128)} %bitcast_convert_fusion.1), channel_id=1, source_target_pairs={{0,1},{1,0},{2,3},{3,2},{4,5},{5,4},{6,7},{7,6},{8,9},{9,8},{10,11... | collective-permute-start | bytes 6291464 | tf_op jit(solution)/shard_map/ppermute | solution.py:59
  213.1 13.1 %collective-permute-start.55 = (bf16[4,2,64,512]{3,2,0,1:T(8,128)(2,1)S(1)}, bf16[4,2,64,512]{3,2,0,1:T(8,128)(2,1)S(1)}, u32[]{:S(2)}, u32[]{:S(2)}) collective-permute-start(bf16[4,2,64,512]{3,2,0,1:T(8,128)(2,1)S(1)} %pad_maximum_fusion.3), channel_id=1, source_target_pairs={{0,2},{2,0},{4,6},{6,4},{8,10},{10,8},{12,14},{14,12},{16,18},{18,... | collective-permute-start | bytes 1572872 | tf_op jit(solution)/shard_map/ppermute | solution.py:56
  214.5 12.8 %collective-permute-start.57 = (bf16[4,2,64,512]{3,2,0,1:T(8,128)(2,1)S(1)}, bf16[4,2,64,512]{3,2,0,1:T(8,128)(2,1)S(1)}, u32[]{:S(2)}, u32[]{:S(2)}) collective-permute-start(bf16[4,2,64,512]{3,2,0,1:T(8,128)(2,1)S(1)} %pad_maximum_fusion.4), channel_id=1, source_target_pairs={{0,4},{2,6},{4,0},{6,2},{8,12},{10,14},{12,8},{14,10},{16,20},{18,... | collective-permute-start | bytes 1572872 | tf_op jit(solution)/shard_map/ppermute | solution.py:56
  (42 other events, 245.1 us)

commit v2 on v0

v2 whole, which is shorter than its diff:
```python
import jax
import jax.numpy as jnp
from jax import lax
from jax.experimental import pallas as pl
from jax.experimental.pallas import tpu as pltpu
from jax.sharding import PartitionSpec as P

PLANE = 4
TILE = 16
PIECES = 2 * PLANE - 1
VMEM_BYTES = 48 * 1024 * 1024
ALL_VMEM = 60 * 1024 * 1024
F32, BF16, I32 = jnp.float32, jnp.bfloat16, jnp.int32


def across(lhs, rhs):
    return lax.dot_general(lhs, rhs, (((0,), (0,)), ((), ())), preferred_element_type=F32)


def times_t(lhs, rhs):
    return lax.dot_general(lhs, rhs, (((1,), (1,)), ((), ())), preferred_element_type=F32)


def aligned(start, size):
    start = start if isinstance(start, int) else pl.multiple_of(start, size)
    return pl.ds(start, size)


def spaced(space, arrays):
    return [pl.BlockSpec(memory_space=space) for _ in arrays]


def array(shape, dtype):
    return jax.ShapeDtypeStruct(shape, dtype)


def call(kernel, name, outs, place, near, far=(), scratch=(), flops=0, far_outs=0,
         limit=VMEM_BYTES, light=False):
    operands = list(near) + list(far)
    moved = sum(a.size * a.dtype.itemsize for a in operands + list(outs))
    if light:
        flops, moved = 1, 1
    return pl.pallas_call(
        kernel,
        name=name,
        out_shape=list(outs),
        in_specs=spaced(pltpu.SMEM, [place]) + spaced(pltpu.VMEM, near) + spaced(pltpu.HBM, far),
        out_specs=spaced(pltpu.VMEM, outs[: len(outs) - far_outs])
        + spaced(pltpu.HBM, outs[len(outs) - far_outs :]),
        scratch_shapes=list(scratch),
        compiler_params=pltpu.CompilerParams(vmem_limit_bytes=limit),
        cost_estimate=pl.CostEstimate(
            flops=int(flops), bytes_accessed=int(moved), transcendentals=0
        ),
    )(place, *operands)


def reversed_bits(value, bits):
    out = 0
    for bit in range(bits):
        out = out | (((value >> bit) & 1) << (bits - 1 - bit))
    return out


def away(core, slot, bits):
    return jnp.where(core == 0, reversed_bits(slot, bits), slot)


def bits_of(size):
    return size.bit_length() - 1


def bias_rows(value):
    top = value.astype(BF16).astype(F32)
    row_at = lax.broadcasted_iota(I32, (TILE, value.shape[1]), 0)
    return jnp.where(row_at == 0, top, jnp.where(row_at == 1, value - top, 0.0)).astype(BF16)


def stacked(parts, target, sem, first=0):
    copies, at = [], 0
    for index, part in enumerate(parts):
        span = pl.ds(at, part.shape[0])
        copies.append(pltpu.make_async_copy(part, target.at[span, :], sem.at[first + index]))
        at += part.shape[0]
    return copies


def start_all(copies):
    for copy in copies:
        copy.start()


def wait_all(copies):
    for copy in copies:
        copy.wait()


def sort_slots(place, neighbours, present, importance, count):
    rows, slots = neighbours.shape
    turns = -(-slots // count)
    arrays = [neighbours.T, present.T, importance.T]

    def kernel(place_ref, *refs):
        out_ref, neighbours_ref, present_ref, importance_ref, sem = refs[3:]
        copies = [
            pltpu.make_async_copy(part, target, sem.at[index])
            for index, (part, target) in enumerate(zip(refs[:3], refs[4:7]))
        ]
        start_all(copies)
        wait_all(copies)
        slot_at = lax.broadcasted_iota(I32, (slots, rows), 0)
        node_at = lax.broadcasted_iota(I32, (slots, rows), 1)
        block = (node_at * slots + slot_at) & (count - 1)
        row = neighbours_ref[...] - rows * block
        packed = row * 128 + present_ref[...] * importance_ref[...]
        block_at = lax.broadcasted_iota(I32, (count, rows), 0)
        node_at = lax.broadcasted_iota(I32, (count, rows), 1)
        first = (block_at - slots * node_at) & (count - 1)
        for turn in range(turns):
            total = jnp.zeros((count, rows), I32)
            for slot in range(slots):
                at = slot - count * turn
                if 0 <= at < count:
                    total = jnp.where(first == at, packed[slot : slot + 1, :], total)
            out_ref[turn * count : (turn + 1) * count, :] = total

    (out,) = call(
        kernel, "sort_slots", [array((turns * count, rows), I32)], place, [], arrays,
        [pltpu.VMEM((slots, rows), I32)] * 3 + [pltpu.SemaphoreType.DMA((3,))], limit=ALL_VMEM,
    )
    return out


def slot_matrix(place, lists, count):
    tall, rows = lists[0].shape
    lines, width, turns = count // PLANE, PLANE * rows, tall // count

    def kernel(place_ref, own_ref, next_ref, rest_ref, sums_ref, far_ref, out_ref, sem):
        slot_refs = [(own_ref, 0), (next_ref, 0), (rest_ref, 0), (rest_ref, tall)]
        core, spot, line = place_ref[1], place_ref[0] % PLANE, place_ref[0] // PLANE
        sums = [
            jnp.sum((ref[at : at + tall, :] & 127).astype(F32), axis=0, keepdims=True)
            for ref, at in slot_refs
        ]
        sums = jnp.broadcast_to(jnp.concatenate(sums, axis=1), (8, width))
        sums_ref[...] = sums.T
        for at in range(lines):
            block = (line ^ at) * PLANE + spot
            ids, weights = [], []
            for turn in range(turns):
                listed = jnp.concatenate(
                    [ref[pl.ds(at + turn * count + block, 1), :] for ref, at in slot_refs],
                    axis=1,
                )
                ids.append(listed >> 7)
                weights.append((listed & 127).astype(F32))
            shift = core * (rows // 2) if at else 0

            @pl.loop(0, rows // TILE)
            def _(step):
                base = step * TILE + shift
                base = jnp.where(base >= rows, base - rows, base)
                row_at = lax.broadcasted_iota(I32, (TILE, width), 0) + base
                total = jnp.zeros((TILE, width), F32)
                for listed, weight in zip(ids, weights):
                    total = total + jnp.where(listed == row_at, weight, 0.0)
                out_ref[aligned(at * rows + step * TILE, TILE), :] = total.astype(BF16)

            span = pl.ds(at * rows, rows)
            pltpu.make_async_copy(out_ref.at[span, :], far_ref.at[span, :], sem.at[at]).start()
        for at in range(lines):
            span = pl.ds(at * rows, rows)
            pltpu.make_async_copy(out_ref.at[span, :], far_ref.at[span, :], sem.at[at]).wait()

    sums, matrix = call(
        kernel, "slot_matrix", [array((width, 8), F32), array((lines * rows, width), BF16)],
        place, lists,
        scratch=[pltpu.VMEM((lines * rows, width), BF16), pltpu.SemaphoreType.DMA((lines,))],
        flops=3 * turns * lines * rows * width, far_outs=1, limit=ALL_VMEM, light=True,
    )
    return matrix, sums


def hidden_of(rows, q_ref, bias_ref):
    hidden = jnp.maximum(jnp.dot(rows, q_ref[...], preferred_element_type=F32) + bias_ref[...], 0.0)
    top = hidden.astype(BF16)
    return top, (hidden - top.astype(F32)).astype(BF16)


def hidden_rows(place, pieces, q_half, bias_half):
    total, half = sum(piece.shape[0] for piece in pieces), q_half.shape[1]

    def kernel(place_ref, q_ref, bias_ref, *refs):
        parts, (high_out, low_out, high_ref, low_ref, rows_ref, sem) = (
            refs[: len(pieces)], refs[len(pieces) :]
        )
        copies = stacked(parts, rows_ref, sem)
        start_all(copies)
        wait_all(copies)
        high_ref[...], low_ref[...] = hidden_of(rows_ref[...], q_ref, bias_ref)
        copies = [
            pltpu.make_async_copy(high_ref, high_out, sem.at[0]),
            pltpu.make_async_copy(low_ref, low_out, sem.at[1]),
        ]
        start_all(copies)
        wait_all(copies)

    return call(
        kernel, "hidden_rows", [array((total, half), BF16)] * 2, place, [q_half, bias_half], pieces,
        [pltpu.VMEM((total, half), BF16)] * 2 + [
            pltpu.VMEM((total, q_half.shape[0]), BF16),
            pltpu.SemaphoreType.DMA((max(len(pieces), 2),)),
        ],
        flops=2 * total * q_half.size, far_outs=2, limit=ALL_VMEM,
    )


def lane_span(start, size):
    low = start // 128 * 128
    high = -(-(start + size) // 128) * 128
    return low, high - low, start - low


def first_sums(place, pieces, early_high, early_low, q_half, bias_half, matrix):
    early, half = early_high.shape
    late = sum(piece.shape[0] for piece in pieces)
    total, width = matrix.shape
    count, part = len(pieces), width // PLANE
    low, span_width, skip = lane_span(width - part, part)

    def kernel(place_ref, q_ref, bias_ref, *refs):
        (matrix_in, high_in, low_in), refs = refs[:3], refs[3:]
        parts, refs = refs[:count], refs[count:]
        send_ref, high_out, low_out, rows_ref, high_ref, low_ref, matrix_ref, sem = refs
        copies = stacked(parts, rows_ref, sem)
        others = [
            pltpu.make_async_copy(
                matrix_in.at[:, pl.ds(low, span_width)], matrix_ref, sem.at[count]
            )
        ]
        others += stacked([high_in], high_ref, sem, count + 1)
        others += stacked([low_in], low_ref, sem, count + 2)
        start_all(copies + others)
        wait_all(copies)
        high_ref[early:, :], low_ref[early:, :] = hidden_of(rows_ref[...], q_ref, bias_ref)
        span = pl.ds(early, late)
        outs = [
            pltpu.make_async_copy(high_ref.at[span, :], high_out, sem.at[0]),
            pltpu.make_async_copy(low_ref.at[span, :], low_out, sem.at[1]),
        ]
        start_all(outs)
        wait_all(others)
        total_sum = across(matrix_ref[...], high_ref[...]) + across(matrix_ref[...], low_ref[...])
        send_ref[...] = total_sum[skip : skip + part, :]
        wait_all(outs)

    return call(
        kernel, "first_sums",
        [array((part, half), F32)] + [array((late, half), BF16)] * 2,
        place, [q_half, bias_half], [matrix, early_high, early_low] + list(pieces),
        [
            pltpu.VMEM((late, q_half.shape[0]), BF16),
            pltpu.VMEM((total, half), BF16),
            pltpu.VMEM((total, half), BF16),
            pltpu.VMEM((total, span_width), BF16),
            pltpu.SemaphoreType.DMA((count + 3,)),
        ],
        flops=2 * late * q_half.size + 4 * total * part * half, far_outs=2, limit=ALL_VMEM,
    )


def more_sums(place, highs, lows, matrix, first, slots):
    total = matrix.shape[0]
    part = matrix.shape[1] // PLANE
    width = slots * part
    start, span_width, skip = lane_span(first * part, width)
    half, count = highs[0].shape[1], len(highs)

    def kernel(place_ref, matrix_in, *refs):
        keep_ref, high_ref, low_ref, matrix_ref, sem = refs[2 * count :]
        copies = [
            pltpu.make_async_copy(
                matrix_in.at[:, pl.ds(start, span_width)], matrix_ref, sem.at[2 * count]
            )
        ]
        copies += stacked(refs[:count], high_ref, sem)
        copies += stacked(refs[count : 2 * count], low_ref, sem, count)
        start_all(copies)
        wait_all(copies)
        total_sum = across(matrix_ref[...], high_ref[...]) + across(matrix_ref[...], low_ref[...])
        keep_ref[...] = total_sum[skip : skip + width, :]

    (keep,) = call(
        kernel, "more_sums", [array((width, half), F32)], place, [],
        [matrix] + list(highs) + list(lows),
        [
            pltpu.VMEM((total, half), BF16),
            pltpu.VMEM((total, half), BF16),
            pltpu.VMEM((total, span_width), BF16),
            pltpu.SemaphoreType.DMA((2 * count + 1,)),
        ],
        flops=4 * total * width * half, limit=ALL_VMEM,
    )
    return keep


def plane_slices(place, features, mine, other):
    rows, dim = features.shape
    half, width = dim // 2, dim // PLANE

    def kernel(place_ref, features_ref, mine_ref, other_ref, own_ref, next_ref, send_ref):
        core, spot = place_ref[1], place_ref[0] % PLANE
        targets = [own_ref, next_ref, send_ref.at[pl.ds(0, rows), :], send_ref.at[pl.ds(rows, rows), :]]
        for slot, target in enumerate(targets):
            to = spot ^ away(core, slot, 2)

            @pl.when(core == 0)
            def _():
                target[...] = features_ref[:, aligned(to * width, width)]

            within = aligned(to % 2 * width, width)

            @pl.when((core == 1) & (to < 2))
            def _():
                target[...] = other_ref[:, within]

            @pl.when((core == 1) & (to >= 2))
            def _():
                target[...] = mine_ref[:, within]

    outs = [array((rows, width), BF16)] * 2 + [array((2 * rows, width), BF16)]
    return call(kernel, "plane_slices", outs, place, [features, mine, other])


def node_step(place, mine, other, self_part, cotangent, w_weight, w_other):
    rows, half = mine.shape
    dim = 2 * half

    def kernel(
        place_ref, mine_ref, other_ref, self_ref, cotangent_ref, w_in, w_other_in,
        embeddings_ref, grad_ref, half_ref, lhs_ref, linear_ref, near_ref, sem,
    ):
        core = place_ref[1]

        @pl.when(core == 0)
        def _():
            pltpu.make_async_copy(w_other_in, near_ref, sem).start()

        @pl.when(core == 1)
        def _():
            pltpu.make_async_copy(w_in, near_ref, sem).start()

        lhs_ref[:, aligned(core * half, half)] = mine_ref[...]
        lhs_ref[:, aligned((1 - core) * half, half)] = other_ref[...]
        pltpu.make_async_copy(w_in, near_ref, sem).wait()
        linear_ref[...] = self_ref[...] + jnp.dot(
            lhs_ref[...], near_ref[...], preferred_element_type=F32
        )

        @pl.loop(0, rows // TILE, unroll=4)
        def _(step):
            at = aligned(step * TILE, TILE)
            linear = linear_ref[at, :]
            relu_out = jnp.maximum(linear, 0.0)
            scale = lax.rsqrt(jnp.mean(relu_out * relu_out, axis=1, keepdims=True) + 1e-06)
            embeddings_ref[at, :] = relu_out * scale
            grad_out = cotangent_ref[at, :].astype(F32)
            inner = jnp.mean(relu_out * grad_out, axis=1, keepdims=True)
            grad_relu = scale * grad_out - relu_out * (scale * scale * scale) * inner
            grad_ref[at, :] = jnp.where(linear > 0, grad_relu, 0.0).astype(BF16)

        half_ref[...] = grad_ref[aligned(core * (rows // 2), rows // 2), :]

    outs = [
        array((rows, dim), F32), array((rows, dim), BF16), array((rows // 2, dim), BF16),
    ]
    return call(
        kernel, "node_step", outs, place, [mine, other, self_part, cotangent],
        [w_weight, w_other],
        [
            pltpu.VMEM((rows, dim), BF16), pltpu.VMEM((rows, dim), F32),
            pltpu.VMEM((dim, dim), BF16), pltpu.SemaphoreType.DMA(()),
        ],
        flops=2 * rows * dim * dim,
    )


def plane_copies(core, rows, pieces, target, sem):
    own, traded = pieces[0], pieces[PLANE]
    half = rows // 2
    copies = [pltpu.make_async_copy(own, target.at[pl.ds(0, rows), :], sem.at[0])]
    for slot in range(1, PLANE):
        mine = pieces[slot]
        other = traded.at[pl.ds((reversed_bits(slot, 2) - 1) * half, half), :]
        for index, (part, at) in enumerate(((mine, core), (other, 1 - core))):
            spot = pl.multiple_of(slot * rows + at * half, TILE)
            copies.append(
                pltpu.make_async_copy(
                    part, target.at[pl.ds(spot, half), :], sem.at[2 * slot - 1 + index]
                )
            )
    return copies


def self_weight(place, pieces, slices):
    rows, dim = pieces[0].shape
    width = slices[0].shape[1]

    def kernel(place_ref, *refs):
        parts, slots, out_ref = refs[:5], refs[5:9], refs[9]
        grads_ref, lhs_ref, sem, slice_sem = refs[10:]
        copies = plane_copies(place_ref[1], rows, parts, grads_ref, sem)
        own, far, near, last = slots
        spans = [own, last.at[pl.ds(0, rows), :], far.at[pl.ds(0, rows), :], last.at[pl.ds(rows, rows), :]]
        for slot, part in enumerate(spans):
            copies.append(
                pltpu.make_async_copy(part, lhs_ref.at[pl.ds(slot * rows, rows), :], slice_sem.at[slot])
            )
        for copy in copies:
            copy.start()
        for copy in copies:
            copy.wait()
        out_ref[:width, :] = across(lhs_ref[...], grads_ref[...]).astype(BF16)
        bias = jnp.sum(grads_ref[...].astype(F32), axis=0, keepdims=True)
        out_ref[width:, :] = bias_rows(bias)

    (out,) = call(
        kernel, "self_weight", [array((width + TILE, dim), BF16)], place, [],
        list(pieces) + list(slices),
        [
            pltpu.VMEM((PLANE * rows, dim), BF16),
            pltpu.VMEM((PLANE * rows, width), BF16),
            pltpu.SemaphoreType.DMA((PIECES,)),
            pltpu.SemaphoreType.DMA((PLANE,)),
        ],
        flops=2 * PLANE * rows * dim * width,
    )
    return out


def row_grad(place, sums, pieces, near_half, matrix, highs, line_parts, lines):
    rows, dim = pieces[0].shape
    half = near_half.shape[0]
    total, nodes, width = lines * rows, PLANE * rows, dim // PLANE

    def kernel(place_ref, sums_ref, near_ref, *refs):
        parts, refs = refs[:5], refs[5:]
        matrix_in, high_parts, refs = refs[0], refs[1 : 1 + len(highs)], refs[1 + len(highs) :]
        row_parts, refs = refs[: len(line_parts)], refs[len(line_parts) :]
        stay_ref, late_ref, go_ref, keep_ref, send_ref, refs = *refs[:5], refs[5:]
        grads_ref, rows_ref, sum_ref, hidden_ref, matrix_ref, high_ref = refs[:6]
        sem, row_sem, matrix_sem = refs[6:]
        core, spot = place_ref[1], place_ref[0] % PLANE
        copies = plane_copies(core, rows, parts, grads_ref, sem)
        row_copies = stacked(row_parts, rows_ref, row_sem)
        matrix_copies = stacked([matrix_in], matrix_ref, matrix_sem)
        matrix_copies += stacked(high_parts, high_ref, matrix_sem, 1)
        start_all(copies + matrix_copies + row_copies)
        for slot in range(PLANE):
            wait_all(copies[max(2 * slot - 1, 0) : 2 * slot + 1])
            span = slice(slot * rows, (slot + 1) * rows)
            grad = times_t(grads_ref[span, :], near_ref[...])
            sum_ref[span, :] = (grad / sums_ref[span, 0:1]).astype(BF16)
        wait_all(matrix_copies)
        bias = jnp.zeros((1, half), F32)
        for at in range(lines):
            span = slice(at * rows, (at + 1) * rows)
            grad = jnp.dot(matrix_ref[span, :], sum_ref[...], preferred_element_type=F32)
            grad = jnp.where(high_ref[span, :].astype(F32) > 0, grad, 0.0)
            bias = bias + jnp.sum(grad, axis=0, keepdims=True)
            hidden_ref[span, :] = grad.astype(BF16)
        for slot in range(lines):
            at = away(core, slot, bits_of(lines))
            to = slot * rows
            for ref in (stay_ref, late_ref, go_ref):
                if 0 <= to < ref.shape[0]:
                    break
                to -= ref.shape[0]
            ref[to : to + rows, :] = hidden_ref[aligned(at * rows, rows), :]
        wait_all(row_copies)
        for slot in range(PLANE):
            to = spot ^ away(core, slot, 2)
            ref, at = (keep_ref, send_ref)[slot // 2], slot % 2 * width
            ref[at : at + width, :] = across(
                rows_ref[:, aligned(to * width, width)], hidden_ref[...]
            ).astype(BF16)
        for ref in (keep_ref, send_ref):
            ref[2 * width :, :] = bias_rows(bias)

    outs = [array((total // 2, half), BF16)] + [array((total // 4, half), BF16)] * 2
    outs += [array((dim // 2 + TILE, half), BF16)] * 2
    return call(
        kernel, "row_grad", outs, place, [sums, near_half],
        list(pieces) + [matrix] + list(highs) + list(line_parts),
        [
            pltpu.VMEM((nodes, dim), BF16),
            pltpu.VMEM((total, dim), BF16),
            pltpu.VMEM((nodes, half), BF16),
            pltpu.VMEM((total, half), BF16),
            pltpu.VMEM((total, nodes), BF16),
            pltpu.VMEM((total, half), BF16),
            pltpu.SemaphoreType.DMA((PIECES,)),
            pltpu.SemaphoreType.DMA((len(line_parts),)),
            pltpu.SemaphoreType.DMA((1 + len(highs),)),
        ],
        flops=2 * nodes * dim * half + 2 * total * nodes * half + 2 * total * dim * half,
    )


def fold(place, keep, came):
    height, width = keep.shape[0] - TILE, keep.shape[1]
    part = height // 2

    def kernel(place_ref, keep_ref, came_ref, stay_ref, go_ref):
        bias = keep_ref[height:, :].astype(F32) + came_ref[height:, :].astype(F32)
        bias = bias_rows(bias[0:1] + bias[1:2])
        for ref, at in ((stay_ref, 0), (go_ref, part)):
            span = slice(at, at + part)
            ref[:part, :] = (keep_ref[span, :].astype(F32) + came_ref[span, :].astype(F32)).astype(BF16)
            ref[part:, :] = bias

    return call(
        kernel, "fold", [array((part + TILE, width), BF16)] * 2, place, [keep, came]
    )


def merge(place, keep, came):
    height, width = keep.shape[0] - TILE, keep.shape[1]

    def kernel(place_ref, keep_ref, came_ref, out_ref):
        out_ref[...] = (keep_ref[...].astype(F32) + came_ref[...].astype(F32)).astype(BF16)
        bias = keep_ref[height:, :].astype(F32) + came_ref[height:, :].astype(F32)
        out_ref[height:, :] = bias_rows(bias[0:1] + bias[1:2])

    (out,) = call(kernel, "merge", [array(keep.shape, BF16)], place, [keep, came])
    return out


def unpack(place, sides):
    tall, width = sides[0][0].shape
    height = tall // 2

    def kernel(place_ref, *refs):
        out_ref = refs[-1]
        spot = place_ref[0] % PLANE
        for side in range(len(sides)):
            core = place_ref[1] ^ side
            cols = aligned(core * width, width) if len(sides) > 1 else slice(None)
            for slot in range(PLANE):
                block = spot ^ away(core, slot, 2)
                start = slot % 2 * height
                out_ref[aligned(block * height, height), cols] = refs[2 * side + slot // 2][
                    start : start + height, :
                ].astype(F32)

    (out,) = call(
        kernel, "unpack", [array((2 * tall, width * len(sides)), F32)], place,
        [part for side in sides for part in side],
    )
    return out


def on_device(
    features, neighbours, present, importance, q_weight, q_bias, w_weight, w_bias, cotangent
):
    rows, dim = features.shape
    count = lax.axis_size("nodes")
    lines = count // PLANE
    line_bits = bits_of(lines)
    node = lax.axis_index("nodes")
    core = lax.axis_index("stream")
    place = jnp.stack([node, core]).astype(I32)
    half_rows = rows // 2
    fence = lax.optimization_barrier

    def swap(value, bit, other_bit=None):
        bits = (bit, bit if other_bit is None else other_bit)
        pairs = [
            (2 * at + side, 2 * (at ^ bits[side]) + side) for at in range(count) for side in (0, 1)
        ]
        return lax.ppermute(value, ("nodes", "stream"), pairs)

    def plane_swap(value, step):
        return swap(value, 1 << step, 2 >> step)

    def line_swap(value, step):
        return swap(value, PLANE << step, PLANE << (line_bits - 1 - step))

    def trade(value):
        return lax.ppermute(value, "stream", [(0, 1), (1, 0)])

    def own_half(value, axis):
        size = value.shape[axis] // 2
        return lax.dynamic_slice_in_dim(value, core * size, size, axis)

    def joined(mine, other, axis):
        return jnp.where(
            core == 0,
            jnp.concatenate([mine, other], axis),
            jnp.concatenate([other, mine], axis),
        )

    parts = {0: own_half(features, 0)}
    parts[lines // 2] = swap(parts[0], lines // 2 * PLANE)

    lists = sort_slots(place, neighbours, present, importance, count)
    lists = [jnp.concatenate([lists, trade(lists)], 0)]
    lists.append(plane_swap(lists[0], 1))
    lists.append(plane_swap(jnp.concatenate(lists, 0), 0))
    matrix, weight_sums = slot_matrix(place, lists, count)
    matrix, parts[lines // 2] = fence((matrix, parts[lines // 2]))
    bit = lines // 4
    while bit:
        for at in sorted(parts, reverse=True):
            parts[at ^ bit] = swap(parts[at], bit * PLANE)
        bit //= 2
    w_other = trade(w_weight)

    line_parts = [features]
    for at in range(1, lines - 1):
        line_parts += [parts[at], trade(parts[at])]
    q_half = own_half(q_weight, 1)
    bias_half = own_half(q_bias, 0)[None]
    high, low = hidden_rows(place, line_parts, q_half, bias_half)
    matrix, high, low, final = fence((matrix, high, low, parts[lines - 1]))
    line_parts += [final, trade(final)]
    send, *late = first_sums(place, line_parts[-2:], high, low, q_half, bias_half, matrix)
    highs, lows = [high, late[0]], [low, late[1]]

    came = plane_swap(send, 0)
    middle = more_sums(place, highs, lows, matrix, 1, 2)
    came, middle = fence((came, middle))
    last = plane_swap(middle[:rows] + came, 1)
    came_own = plane_swap(middle[rows:], 0)
    keep = more_sums(place, highs, lows, matrix, 0, 1)
    w_self = jnp.where(core == 0, w_weight, w_other)
    w_near = jnp.where(core == 0, w_other, w_weight)
    self_part = jnp.dot(features, w_self, preferred_element_type=F32) + w_bias
    ready = (self_part, own_half(w_near, 0), own_half(w_self, 0), own_half(q_weight, 0), keep)
    last, ready = fence((last, ready))
    self_part, near_half, self_half, q_rows, keep = ready
    mean_half = ((keep + came_own + last) / weight_sums[:rows, 0:1]).astype(BF16)

    mean_other = trade(mean_half)
    own_slice, next_slice, send_slices = plane_slices(place, features, mean_half, mean_other)
    far_slices = plane_swap(send_slices, 0)
    embeddings, grad_linear, grad_half = node_step(
        place, mean_half, mean_other, self_part, cotangent, w_weight, w_other
    )
    grad_half, far_slices = fence((grad_half, far_slices))

    one, two = plane_swap(grad_half, 1), plane_swap(grad_half, 0)
    last_slices = plane_swap(jnp.concatenate([next_slice, far_slices[rows:]], 0), 1)
    one, two = fence((one, two))
    three = plane_swap(one, 0)
    three, last_slices = fence((three, last_slices))
    pieces = [grad_linear, one, two, three, trade(jnp.concatenate([one, two, three], 0))]
    slices = [own_slice, far_slices, next_slice, last_slices]
    w_part = self_weight(place, pieces, slices)
    pieces, w_part = fence((pieces, w_part))

    stay, late, go, q_keep, q_send = row_grad(
        place, weight_sums, pieces, near_half, matrix, highs, line_parts, lines
    )
    w_came = line_swap(w_part, 0)
    stay, late, go, q_keep, q_send, w_came = fence((stay, late, go, q_keep, q_send, w_came))

    def last_sum(keep, came):
        height = keep.shape[0] - TILE
        total = keep.astype(F32) + came.astype(F32)
        return total[:height].astype(BF16), total[height] + total[height + 1]

    def grow(piece, came):
        return jnp.concatenate([piece, came], 0)

    biases = {}

    def steps_of(name, first, line_steps):
        def fold_step(state):
            return fold(place, *state)

        def merge_step(state):
            total = merge(place, *state)
            return total, total

        def last_step(state):
            piece, biases[name] = last_sum(*state)
            return piece, piece

        def grow_step(state):
            piece = grow(*state)
            return piece, piece

        steps = [(fold_step, plane_swap, 1)] if first else []
        steps += [(merge_step, line_swap, step) for step in line_steps]
        return steps + [(last_step, plane_swap, 1), (grow_step, plane_swap, 0)]

    q_steps = steps_of("q", True, range(line_bits))
    w_steps = steps_of("w", False, range(1, line_bits))
    w_steps.insert(line_bits - 1, None)

    q_state, w_state = (q_keep, plane_swap(q_send, 0)), (w_part, w_came)
    last_round = len(q_steps)
    rows_came, row_round = {}, last_round - 2
    for index in range(last_round + 1):
        rows_send = None
        if index == row_round:
            rows_send = go
        if index == row_round + 1:
            rows_send = late
        if index == row_round + 2:
            half = stay.shape[0] // 2
            rows_send = (stay[half:].astype(F32) + rows_came[row_round].astype(F32)).astype(BF16)
        if index:
            kind, exchange, step = q_steps[index - 1]
            keep, send = kind(q_state)
            if rows_send is not None:
                send, rows_send = fence((send, rows_send))
            q_state = (keep, exchange(send, step))
        if rows_send is not None:
            rows_came[index] = line_swap(rows_send, max(index - row_round - 1, 0))
        w_step = w_steps[index] if index < len(w_steps) else None
        if w_step is not None:
            kind, exchange, step = w_step
            keep, send = kind(w_state)
            w_state = (keep, exchange(send, step))
        w_open = index in (line_bits - 2, len(w_steps) - 1)
        if index < last_round and w_open:
            q_state, go, late, rows_came = fence((q_state, go, late, rows_came))
        elif index < last_round:
            q_state, w_state, go, late, rows_came = fence((q_state, w_state, go, late, rows_came))
    w_grad = unpack(place, [list(w_state)])
    q_plane, q_last = q_state
    rows_late, rows_next = rows_came[row_round + 1], rows_came[row_round + 2]
    q_grad = unpack(place, [[q_plane, q_last], [trade(q_plane), trade(q_last)]])
    w_bias_grad, q_bias_half = biases["w"], biases["q"]
    q_bias_grad = joined(q_bias_half, trade(q_bias_half), 0)

    half = stay.shape[0] // 2
    came_sum = rows_late.astype(F32) + rows_next.astype(F32)
    stay = stay[:half]
    for step in range(2, line_bits):
        half = came_sum.shape[0] // 2
        next_came = line_swap((stay[half:].astype(F32) + came_sum[half:]).astype(BF16), step)
        stay, came_sum = stay[:half], came_sum[:half] + next_came.astype(F32)
    came_sum = joined(came_sum[:half_rows], came_sum[half_rows:], 0)
    row_half = (stay.astype(F32) + came_sum).astype(BF16)
    row_full = joined(row_half, trade(row_half), 1)
    feature_grad = times_t(grad_linear, self_half) + times_t(row_full, q_rows)
    return (embeddings, feature_grad, q_grad, q_bias_grad, w_grad, w_bias_grad)


def solution(mesh):
    in_specs = (
        P("nodes", None),
        P("nodes", "stream"),
        P("nodes", "stream"),
        P("nodes", "stream"),
        P(),
        P(),
        P("stream", None),
        P(),
        P("nodes", None),
    )
    out_specs = (P("nodes", None), P("nodes", "stream"), P(), P(), P("stream", None), P())
    return jax.shard_map(
        on_device, mesh=mesh, in_specs=in_specs, out_specs=out_specs, check_vma=False
    )
```

time: 1340 us -> 206 us (0.15)
  waiting for transfers between devices: 778 us -> 81.7 us
  matrix products: 291 us -> 2.81 us
  local copies, waits for them, and re-layouts: 181 us -> 7.1 us
  Pallas kernels: 0 us -> 56.1 us
  blocking collectives: 47.7 us -> 0 us
  starting transfers between devices: 13.9 us -> 45.1 us
    psum x5 -> x0, waiting for transfers between devices: 642 us -> none  [the longest x1 592 us: on_device(): lax.psum((w_grad_local, w_bias_local, q_grad_local, q_bias_local), 'nodes')]
    dot_general x55 -> x3, matrix products: 291 us -> 2.81 us  [the longest x2 1.96 us: times_t(): lax.dot_general(lhs, rhs, (((1,), (1,)), ((), ())), preferred_element_typ...]
    all_gather x1 -> x0, waiting for transfers between devices: 134 us -> none  [on_device(): shard_rows = lax.all_gather(features, 'nodes', axis=0, tiled=True)]
    ppermute x0 -> x37, waiting for transfers between devices: none -> 81.7 us  [the longest x26 75.6 us: swap(): return lax.ppermute(value, ('nodes', 'stream'), pairs)]
    reshape x12 -> x0, local copies, waits for them, and re-layouts: 67.1 us -> none  [the longest x10 36.6 us: forward_block(): jax.nn.relu(hidden_pre).reshape(block_nodes, slot_count, feature_dim)]
    mul x40 -> x0, local copies, waits for them, and re-layouts: 62.3 us -> none  [backward_block(): importance_block_weights[:, :, None] * grad_block[:, None, :]]
    pallas_call x0 -> x16, Pallas kernels: none -> 56.1 us  [call(): pl.pallas_call(kernel, name=name, out_shape=list(outs), in_specs=spaced(p...]
    psum x3 -> x0, blocking collectives: 47.7 us -> none  [the longest x1 34.1 us: on_device(): lax.psum((w_grad_local, w_bias_local, q_grad_local, q_bias_local), 'nodes')]
  transfers between devices with their start and end apart: 9 -> 37, of which waited for: 5 -> 23; matrix products, arithmetic and copies ran while one was open for 21% -> 8% of each run, Pallas kernels for 0% -> 23%
where the time goes in v2:
time: 206 us; the launch traced here: 204 us
  waiting for transfers between devices  81.7 us (40%)
  Pallas kernels  56.1 us (27%)
  starting transfers between devices  45.1 us (22%)
  other arithmetic  10.4 us (5%)
  local copies, waits for them, and re-layouts  7.1 us (3%)
  matrix products  2.81 us (1%)
    ppermute x26, waiting for transfers between devices, swap(): return lax.ppermute(value, ('nodes', 'stream'), pairs)  75.6 us
    pallas_call x16, Pallas kernels, call(): pl.pallas_call(kernel, name=name, out_shape=list(outs), in_specs=spaced(p...  56.1 us
    ppermute x26, starting transfers between devices, swap(): return lax.ppermute(value, ('nodes', 'stream'), pairs)  23.1 us
    ppermute x11, starting transfers between devices, trade(): return lax.ppermute(value, 'stream', [(0, 1), (1, 0)])  22 us
    ppermute x11, waiting for transfers between devices, trade(): return lax.ppermute(value, 'stream', [(0, 1), (1, 0)])  6.11 us
  transfers between devices with their start and end apart: 37, of which 23 were waited for; matrix products, arithmetic and copies ran while one was open for 8% of the time, Pallas kernels for 23%

profile of v2, /device:TPU:1, one launch (start us, length us, event | category | flops | bytes accessed | tf_op | source)
XLA Modules:
  0.0 204.5 jit_solution(11943999682554813582)
XLA Ops:
  1.3 2.2 %sort_slots.1 = s32[32,320]{1,0:T(8,128)} custom-call(s32[2]{0:T(128)} %pad_add_fusion.2.place_ref, s32[25,320]{1,0:T(8,128)} %bitcast.15, s32[25,320]{1,0:T(8,128)} %bitcast.16, s32[25,320]{1,0:T(8,128)} %bitcast.17), custom_call_target="tpu_custom_call" | custom-call | bytes 136960 | tf_op jit(solution)/shard_map/sort_slots/pallas_call | solution.py:43
  3.6 1.4 collective-permute-done
  5.8 2.4 %collective-permute-start.1 = (s32[64,320]{1,0:T(8,128)S(1)}, s32[64,320]{1,0:T(8,128)S(1)}, u32[]{:S(2)}, u32[]{:S(2)}) collective-permute-start(s32[64,320]{1,0:T(8,128)S(1)} %pad_add_fusion.1.own_ref), channel_id=1, source_target_pairs={{0,4},{1,3},{2,6},{3,1},{4,0},{5,7},{6,2},{7,5},{8,12},{9,11},{10,... | collective-permute-start | bytes 245768 | tf_op jit(solution)/shard_map/ppermute | solution.py:581
  9.3 2.4 %collective-permute-start.3 = (bf16[160,1024]{1,0:T(8,128)(2,1)S(1)}, bf16[160,1024]{1,0:T(8,128)(2,1)S(1)}, u32[]{:S(2)}, u32[]{:S(2)}) collective-permute-start(bf16[160,1024]{1,0:T(8,128)(2,1)S(1)} %constant_dynamic-slice_fusion.2), channel_id=1, source_target_pairs={{0,16},{1,17},{2,18},{3,19},{4,20},{5,21},{6,22},{7,23},{8,24},{9,... | collective-permute-start | bytes 983048 | tf_op jit(solution)/shard_map/ppermute | solution.py:581
  11.6 1.3 collective-permute-start.4
  15.3 4.6 %collective-permute-done.2.rest_ref = s32[128,320]{1,0:T(8,128)S(1)} collective-permute-done((s32[128,320]{1,0:T(8,128)S(1)}, s32[128,320]{1,0:T(8,128)S(1)}, u32[]{:S(2)}, u32[]{:S(2)}) %collective-permute-start.2) | collective-permute-done | bytes 163872 | tf_op jit(solution)/shard_map/ppermute | solution.py:581
  20.6 8.0 %slot_matrix.1 = (f32[1280,8]{1,0:T(8,128)}, bf16[1280,1280]{1,0:T(8,128)(2,1)}) custom-call(s32[2]{0:T(128)} %pad_add_fusion.2.place_ref, s32[64,320]{1,0:T(8,128)} %copy-done.20, s32[64,320]{1,0:T(8,128)} %copy-done.21, s32[128,320]{1,0:T(8,128)} %copy-done.22), custom_call_target="tpu_custom_call" | custom-call | flops 1 | bytes 1 | tf_op jit(solution)/shard_map/slot_matrix/pallas_call | solution.py:43
  29.8 1.3 dynamic_slice.19
  33.0 5.3 %hidden_rows.1 = (bf16[960,512]{1,0:T(8,128)(2,1)}, bf16[960,512]{1,0:T(8,128)(2,1)}) custom-call(s32[2]{0:T(128)} %pad_add_fusion.2.place_ref, bf16[1024,512]{1,0:T(8,128)(2,1)} %constant_dynamic-slice_fusion.3.q_ref, f32[1,512]{1,0:T(1,128)} %bitcast.18, bf16[320,1024]{1,0:T(8,128)(2,1)} %refs_8_.1, bf16[160,1024]{1,0:T(8,128)(2,1)} %copy-done.15, ...), custom_call_target="tpu_custom_call" | custom-call | flops 1006632960 | bytes 4982784 | tf_op jit(solution)/shard_map/hidden_rows/pallas_call | solution.py:43
  38.5 1.3 collective-permute-start.8
  39.8 1.3 collective-permute-done.8.refs_4_.refs_14_
  41.8 5.3 %first_sums.1 = (f32[320,512]{1,0:T(8,128)}, bf16[320,512]{1,0:T(8,128)(2,1)}, bf16[320,512]{1,0:T(8,128)(2,1)}) custom-call(s32[2]{0:T(128)} %pad_add_fusion.2.place_ref, bf16[1024,512]{1,0:T(8,128)(2,1)} %constant_dynamic-slice_fusion.3.q_ref, f32[1,512]{1,0:T(1,128)} %bitcast.19, bf16[1280,1280]{1,0:T(8,128)(2,1)} %get-tuple-element.95.refs_0_.matrix_in.refs_5_, ...), custom_call_target="tpu_custom_call" | custom-call | flops 1174405120 | bytes 8259584 | tf_op jit(solution)/shard_map/first_sums/pallas_call | solution.py:43
  48.9 4.7 %more_sums.3 = f32[320,512]{1,0:T(8,128)} custom-call(s32[2]{0:T(128)} %pad_add_fusion.2.place_ref, bf16[1280,1280]{1,0:T(8,128)(2,1)} %get-tuple-element.95.refs_0_.matrix_in.refs_5_, bf16[960,512]{1,0:T(8,128)(2,1)} %get-tuple-element.96.refs_1_.refs_0_.refs_6_, bf16[320,512]{1,0:T(8,128)(2,1)} %get-tuple-element.100.refs_1_.refs_7_, ...), custom_call_target="tpu_custom_call" | custom-call | flops 838860800 | bytes 6553600 | tf_op jit(solution)/shard_map/more_sums/pallas_call | solution.py:43
  53.6 6.2 %more_sums.2 = f32[640,512]{1,0:T(8,128)} custom-call(s32[2]{0:T(128)} %pad_add_fusion.2.place_ref, bf16[1280,1280]{1,0:T(8,128)(2,1)} %get-tuple-element.95.refs_0_.matrix_in.refs_5_, bf16[960,512]{1,0:T(8,128)(2,1)} %get-tuple-element.96.refs_1_.refs_0_.refs_6_, bf16[320,512]{1,0:T(8,128)(2,1)} %get-tuple-element.100.refs_1_.refs_7_, ...), custom_call_target="tpu_custom_call" | custom-call | flops 1677721600 | bytes 7208960 | tf_op jit(solution)/shard_map/more_sums/pallas_call | solution.py:43
  59.9 1.6 fusion.11
  63.7 1.8 broadcast_select_fusion
  65.6 2.7 %dynamic-slice_select_fusion.near_ref = bf16[512,1024]{1,0:T(8,128)(2,1)} fusion(bf16[1024,1024]{1,0:T(8,128)(2,1)S(1)} %copy-done.1, s32[]{:T(128)S(6)} %select_n.46, bf16[1024,1024]{1,0:T(8,128)(2,1)} %collective-permute-done.11.w_other_in, pred[]{:T(512)S(6)} %eq.2), kind=kLoop, calls=%fused_computation.6 | loop fusion | flops 524288 | bytes 3145733 | tf_op jit(solution)/shard_map/jit(_where)/select_n | solution.py:637
  69.2 6.7 %collective-permute-done.10 = f32[320,512]{1,0:T(8,128)S(1)} collective-permute-done((f32[320,512]{1,0:T(8,128)S(1)}, f32[320,512]{1,0:T(8,128)S(1)}, u32[]{:S(2)}, u32[]{:S(2)}) %collective-permute-start.10) | collective-permute-done | bytes 655392 | tf_op jit(solution)/shard_map/ppermute | solution.py:581
  75.9 2.4 %collective-permute-done.12 = f32[320,512]{1,0:T(8,128)S(1)} collective-permute-done((f32[320,512]{1,0:T(8,128)S(1)}, f32[320,512]{1,0:T(8,128)S(1)}, u32[]{:S(2)}, u32[]{:S(2)}) %collective-permute-start.12) | collective-permute-done | bytes 655392 | tf_op jit(solution)/shard_map/ppermute | solution.py:581
  78.5 1.3 collective-permute-start.13
  79.8 1.3 collective-permute-done.13.other_ref
  82.8 3.7 %node_step.1 = (f32[320,1024]{1,0:T(8,128)}, bf16[320,1024]{1,0:T(8,128)(2,1)S(1)}, bf16[160,1024]{1,0:T(8,128)(2,1)S(1)}) custom-call(s32[2]{0:T(128)S(1)} %copy-done.12, bf16[320,512]{1,0:T(8,128)(2,1)S(1)} %divide_convert_fusion.mine_ref, bf16[320,512]{1,0:T(8,128)(2,1)S(1)} %collective-permute-done.13.other_ref, f32[320,1024]{1,0:T(8,128)S(1)} %fusion.self_ref, ...), custom_call_target="tpu_custom_call" | custom-call | flops 671088640 | bytes 9109504 | tf_op jit(solution)/shard_map/node_step/pallas_call | solution.py:43
  86.5 1.5 collective-permute-done.14.refs_6_
  90.6 4.1 %collective-permute-done.15.refs_1_ = bf16[160,1024]{1,0:T(8,128)(2,1)S(1)} collective-permute-done((bf16[160,1024]{1,0:T(8,128)(2,1)S(1)}, bf16[160,1024]{1,0:T(8,128)(2,1)S(1)}, u32[]{:S(2)}, u32[]{:S(2)}) %collective-permute-start.15) | collective-permute-done | bytes 327712 | tf_op jit(solution)/shard_map/ppermute | solution.py:581
  94.7 2.4 %collective-permute-done.16.refs_2_ = bf16[160,1024]{1,0:T(8,128)(2,1)S(1)} collective-permute-done((bf16[160,1024]{1,0:T(8,128)(2,1)S(1)}, bf16[160,1024]{1,0:T(8,128)(2,1)S(1)}, u32[]{:S(2)}, u32[]{:S(2)}) %collective-permute-start.16) | collective-permute-done | bytes 327712 | tf_op jit(solution)/shard_map/ppermute | solution.py:581
  98.0 3.3 %collective-permute-done.18.refs_8_ = bf16[640,256]{1,0:T(8,128)(2,1)S(1)} collective-permute-done((bf16[640,256]{1,0:T(8,128)(2,1)S(1)}, bf16[640,256]{1,0:T(8,128)(2,1)S(1)}, u32[]{:S(2)}, u32[]{:S(2)}) %collective-permute-start.18) | collective-permute-done | bytes 327712 | tf_op jit(solution)/shard_map/ppermute | solution.py:581
  101.3 4.1 %collective-permute-done.17.refs_3_ = bf16[160,1024]{1,0:T(8,128)(2,1)S(1)} collective-permute-done((bf16[160,1024]{1,0:T(8,128)(2,1)S(1)}, bf16[160,1024]{1,0:T(8,128)(2,1)S(1)}, u32[]{:S(2)}, u32[]{:S(2)}) %collective-permute-start.17) | collective-permute-done | bytes 327712 | tf_op jit(solution)/shard_map/ppermute | solution.py:581
  105.4 3.0 %collective-permute-start.19 = (bf16[480,1024]{1,0:T(8,128)(2,1)S(1)}, bf16[480,1024]{1,0:T(8,128)(2,1)S(1)}, u32[]{:S(2)}, u32[]{:S(2)}) collective-permute-start(bf16[480,1024]{1,0:T(8,128)(2,1)S(1)} %pad_maximum_fusion), channel_id=1, source_target_pairs={{0,1},{1,0},{2,3},{3,2},{4,5},{5,4},{6,7},{7,6},{8,9},{9,8},{10,11... | collective-permute-start | bytes 2949128 | tf_op jit(solution)/shard_map/ppermute | solution.py:590
  108.4 2.2 %collective-permute-done.19.refs_4_ = bf16[480,1024]{1,0:T(8,128)(2,1)S(1)} collective-permute-done((bf16[480,1024]{1,0:T(8,128)(2,1)S(1)}, bf16[480,1024]{1,0:T(8,128)(2,1)S(1)}, u32[]{:S(2)}, u32[]{:S(2)}) %collective-permute-start.19) | collective-permute-done | bytes 983072 | tf_op jit(solution)/shard_map/ppermute | solution.py:590
  110.7 3.2 %self_weight.1.keep_ref = bf16[272,1024]{1,0:T(8,128)(2,1)S(1)} custom-call(s32[2]{0:T(128)S(1)} %copy-done.12, bf16[320,1024]{1,0:T(8,128)(2,1)S(1)} %get-tuple-element.122.refs_0_, bf16[160,1024]{1,0:T(8,128)(2,1)S(1)} %collective-permute-done.15.refs_1_, bf16[160,1024]{1,0:T(8,128)(2,1)S(1)} %collective-permute-done.16.refs_2_, ...), custom_call_target="tpu_custom_call" | custom-call | flops 671088640 | bytes 4161536 | tf_op jit(solution)/shard_map/self_weight/pallas_call | solution.py:43
  114.9 8.4 %row_grad.1 = (bf16[640,512]{1,0:T(8,128)(2,1)S(1)}, bf16[320,512]{1,0:T(8,128)(2,1)S(1)}, bf16[320,512]{1,0:T(8,128)(2,1)S(1)}, bf16[528,512]{1,0:T(8,128)(2,1)S(1)}, bf16[528,512]{1,0:T(8,128)(2,1)S(1)}) custom-call(s32[2]{0:T(128)S(1)} %copy-done.12, f32[1280,8]{1,0:T(8,128)} %get-tuple-element.106.sums_ref, ...), custom_call_target="tpu_custom_call" | custom-call | flops 4362076160 | bytes 13312000 | tf_op jit(solution)/shard_map/row_grad/pallas_call | solution.py:43
  123.3 5.8 %collective-permute-done.20.came_ref = bf16[272,1024]{1,0:T(8,128)(2,1)S(1)} collective-permute-done((bf16[272,1024]{1,0:T(8,128)(2,1)S(1)}, bf16[272,1024]{1,0:T(8,128)(2,1)S(1)}, u32[]{:S(2)}, u32[]{:S(2)}) %collective-permute-start.20) | collective-permute-done | bytes 557088 | tf_op jit(solution)/shard_map/ppermute | solution.py:581
  130.5 7.2 %collective-permute-done.21.came_ref = bf16[528,512]{1,0:T(8,128)(2,1)S(1)} collective-permute-done((bf16[528,512]{1,0:T(8,128)(2,1)S(1)}, bf16[528,512]{1,0:T(8,128)(2,1)S(1)}, u32[]{:S(2)}, u32[]{:S(2)}) %collective-permute-start.21) | collective-permute-done | bytes 540704 | tf_op jit(solution)/shard_map/ppermute | solution.py:581
  138.7 4.2 %collective-permute-done.23 = bf16[272,1024]{1,0:T(8,128)(2,1)S(1)} collective-permute-done((bf16[272,1024]{1,0:T(8,128)(2,1)S(1)}, bf16[272,1024]{1,0:T(8,128)(2,1)S(1)}, u32[]{:S(2)}, u32[]{:S(2)}) %collective-permute-start.23) | collective-permute-done | bytes 557088 | tf_op jit(solution)/shard_map/ppermute | solution.py:581
  145.3 1.3 collective-permute-start.24
  146.6 8.1 %collective-permute-done.24.came_ref = bf16[272,512]{1,0:T(8,128)(2,1)S(1)} collective-permute-done((bf16[272,512]{1,0:T(8,128)(2,1)S(1)}, bf16[272,512]{1,0:T(8,128)(2,1)S(1)}, u32[]{:S(2)}, u32[]{:S(2)}) %collective-permute-start.24) | collective-permute-done | bytes 278560 | tf_op jit(solution)/shard_map/ppermute | solution.py:581
  156.5 1.9 collective-permute-start.26
  158.4 7.3 %collective-permute-done.26 = bf16[272,512]{1,0:T(8,128)(2,1)S(1)} collective-permute-done((bf16[272,512]{1,0:T(8,128)(2,1)S(1)}, bf16[272,512]{1,0:T(8,128)(2,1)S(1)}, u32[]{:S(2)}, u32[]{:S(2)}) %collective-permute-start.26) | collective-permute-done | bytes 278560 | tf_op jit(solution)/shard_map/ppermute | solution.py:581
  165.7 2.3 %collective-permute-done.27 = bf16[320,512]{1,0:T(8,128)(2,1)S(1)} collective-permute-done((bf16[320,512]{1,0:T(8,128)(2,1)S(1)}, bf16[320,512]{1,0:T(8,128)(2,1)S(1)}, u32[]{:S(2)}, u32[]{:S(2)}) %collective-permute-start.27) | collective-permute-done | bytes 327712 | tf_op jit(solution)/shard_map/ppermute | solution.py:581
  168.7 1.6 collective-permute-start.28
  170.3 5.1 %collective-permute-done.28 = bf16[256,512]{1,0:T(8,128)(2,1)S(1)} collective-permute-done((bf16[256,512]{1,0:T(8,128)(2,1)S(1)}, bf16[256,512]{1,0:T(8,128)(2,1)S(1)}, u32[]{:S(2)}, u32[]{:S(2)}) %collective-permute-start.28) | collective-permute-done | bytes 262176 | tf_op jit(solution)/shard_map/ppermute | solution.py:581
  175.4 3.8 %collective-permute-done.30 = bf16[320,512]{1,0:T(8,128)(2,1)S(1)} collective-permute-done((bf16[320,512]{1,0:T(8,128)(2,1)S(1)}, bf16[320,512]{1,0:T(8,128)(2,1)S(1)}, u32[]{:S(2)}, u32[]{:S(2)}) %collective-permute-start.30) | collective-permute-done | bytes 327712 | tf_op jit(solution)/shard_map/ppermute | solution.py:581
  179.4 4.9 %collective-permute-start.36 = (f32[512]{0:T(512)S(1)}, f32[512]{0:T(512)S(1)}, u32[]{:S(2)}, u32[]{:S(2)}) collective-permute-start(f32[512]{0:T(512)S(1)} %bitcast.20), channel_id=1, source_target_pairs={{0,1},{1,0},{2,3},{3,2},{4,5},{5,4},{6,7},{7,6},{8,9},{9,8},{10,11... | collective-permute-start | bytes 6152 | tf_op jit(solution)/shard_map/ppermute | solution.py:590
  184.9 1.3 collective-permute-done.31
  186.4 8.6 %collective-permute-start.32 = (bf16[320,512]{1,0:T(8,128)(2,1)S(1)}, bf16[320,512]{1,0:T(8,128)(2,1)S(1)}, u32[]{:S(2)}, u32[]{:S(2)}) collective-permute-start(bf16[320,512]{1,0:T(8,128)(2,1)S(1)} %fusion.2), channel_id=1, source_target_pairs={{0,1},{1,0},{2,3},{3,2},{4,5},{5,4},{6,7},{7,6},{8,9},{9,8},{10,11... | collective-permute-start | bytes 983048 | tf_op jit(solution)/shard_map/ppermute | solution.py:590
  196.3 2.8 %unpack.3 = f32[1024,1024]{1,0:T(8,128)} custom-call(s32[2]{0:T(128)S(1)} %copy-done.12, bf16[512,1024]{1,0:T(8,128)(2,1)S(1)} %constant_dynamic-update-slice_fusion.refs_0_, bf16[512,1024]{1,0:T(8,128)(2,1)S(1)} %collective-permute-done.29.refs_1_), custom_call_target="tpu_custom_call" | custom-call | bytes 6291456 | tf_op jit(solution)/shard_map/unpack/pallas_call | solution.py:43
  200.2 1.4 convolution_add_fusion.1
  201.6 2.8 %unpack.2 = f32[1024,1024]{1,0:T(8,128)} custom-call(s32[2]{0:T(128)S(1)} %copy-done.12, bf16[512,512]{1,0:T(8,128)(2,1)S(1)} %constant_dynamic-update-slice_fusion.2.refs_0_, bf16[512,512]{1,0:T(8,128)(2,1)S(1)} %collective-permute-done.33.refs_1_, bf16[512,512]{1,0:T(8,128)(2,1)S(1)} %collective-permute-done.34.refs_2_, ...), custom_call_target="tpu_custom_call" | custom-call | bytes 6291456 | tf_op jit(solution)/shard_map/unpack/pallas_call | solution.py:43
  (124 shorter events, 31.3 us)
Async XLA Ops:
  0.6 30.5 %copy-start = (bf16[1024,1024]{1,0:T(8,128)(2,1)S(1)}, bf16[1024,1024]{1,0:T(8,128)(2,1)}, u32[]{:S(2)}) copy-start(bf16[1024,1024]{1,0:T(8,128)(2,1)} %param.13) | copy-start | bytes 6291460
  3.5 1.5 collective-permute-start
  5.8 14.1 %copy-start.20 = (s32[64,320]{1,0:T(8,128)}, s32[64,320]{1,0:T(8,128)S(1)}, u32[]{:S(2)}) copy-start(s32[64,320]{1,0:T(8,128)S(1)} %pad_add_fusion.1.own_ref) | copy-start | bytes 245764
  5.8 8.3 %collective-permute-start.1 = (s32[64,320]{1,0:T(8,128)S(1)}, s32[64,320]{1,0:T(8,128)S(1)}, u32[]{:S(2)}, u32[]{:S(2)}) collective-permute-start(s32[64,320]{1,0:T(8,128)S(1)} %pad_add_fusion.1.own_ref), channel_id=1, source_target_pairs={{0,4},{1,3},{2,6},{3,1},{4,0},{5,7},{6,2},{7,5},{8,12},{9,11},{10,... | collective-permute-start | bytes 245768 | tf_op jit(solution)/shard_map/ppermute | solution.py:581
  9.3 19.4 %collective-permute-start.3 = (bf16[160,1024]{1,0:T(8,128)(2,1)S(1)}, bf16[160,1024]{1,0:T(8,128)(2,1)S(1)}, u32[]{:S(2)}, u32[]{:S(2)}) collective-permute-start(bf16[160,1024]{1,0:T(8,128)(2,1)S(1)} %constant_dynamic-slice_fusion.2), channel_id=1, source_target_pairs={{0,16},{1,17},{2,18},{3,19},{4,20},{5,21},{6,22},{7,23},{8,24},{9,... | collective-permute-start | bytes 983048 | tf_op jit(solution)/shard_map/ppermute | solution.py:581
  11.6 17.0 %collective-permute-start.4 = (bf16[160,1024]{1,0:T(8,128)(2,1)S(1)}, bf16[160,1024]{1,0:T(8,128)(2,1)S(1)}, u32[]{:S(2)}, u32[]{:S(2)}) collective-permute-start(bf16[160,1024]{1,0:T(8,128)(2,1)S(1)} %constant_dynamic-slice_fusion.2), channel_id=1, source_target_pairs={{0,8},{1,9},{2,10},{3,11},{4,12},{5,13},{6,14},{7,15},{8,0},{9,1},... | collective-permute-start | bytes 983048 | tf_op jit(solution)/shard_map/ppermute | solution.py:581
  12.9 50.8 %collective-permute-start.11 = (bf16[1024,1024]{1,0:T(8,128)(2,1)}, bf16[1024,1024]{1,0:T(8,128)(2,1)}, u32[]{:S(2)}, u32[]{:S(2)}) collective-permute-start(bf16[1024,1024]{1,0:T(8,128)(2,1)} %w_in.1), channel_id=1, source_target_pairs={{0,1},{1,0},{2,3},{3,2},{4,5},{5,4},{6,7},{7,6},{8,9},{9,8},{10,11... | collective-permute-start | bytes 6291464 | tf_op jit(solution)/shard_map/ppermute | solution.py:590
  14.2 5.7 %copy-start.21 = (s32[64,320]{1,0:T(8,128)}, s32[64,320]{1,0:T(8,128)S(1)}, u32[]{:S(2)}) copy-start(s32[64,320]{1,0:T(8,128)S(1)} %collective-permute-done.1.next_ref) | copy-start | bytes 245764
  15.0 4.9 %collective-permute-start.2 = (s32[128,320]{1,0:T(8,128)S(1)}, s32[128,320]{1,0:T(8,128)S(1)}, u32[]{:S(2)}, u32[]{:S(2)}) collective-permute-start(s32[128,320]{1,0:T(8,128)S(1)} %pad_add_fusion), channel_id=1, source_target_pairs={{0,2},{1,5},{2,0},{3,7},{4,6},{5,1},{6,4},{7,3},{8,10},{9,13},{10,... | collective-permute-start | bytes 491528 | tf_op jit(solution)/shard_map/ppermute | solution.py:581
  28.7 3.6 %collective-permute-start.5 = (bf16[160,1024]{1,0:T(8,128)(2,1)S(1)}, bf16[160,1024]{1,0:T(8,128)(2,1)S(1)}, u32[]{:S(2)}, u32[]{:S(2)}) collective-permute-start(bf16[160,1024]{1,0:T(8,128)(2,1)S(1)} %collective-permute-done.4.refs_1_.refs_9_), channel_id=1, source_target_pairs={{0,1},{1,0},{2,3},{3,2},{4,5},{5,4},{6,7},{7,6},{8,9},{9,8},{10,11... | collective-permute-start | bytes 983048 | tf_op jit(solution)/shard_map/ppermute | solution.py:590
  29.6 2.7 %collective-permute-start.6 = (bf16[160,1024]{1,0:T(8,128)(2,1)S(1)}, bf16[160,1024]{1,0:T(8,128)(2,1)}, u32[]{:S(2)}, u32[]{:S(2)}) collective-permute-start(bf16[160,1024]{1,0:T(8,128)(2,1)S(1)} %collective-permute-done.3.refs_3_.refs_11_), channel_id=1, source_target_pairs={{0,1},{1,0},{2,3},{3,2},{4,5},{5,4},{6,7},{7,6},{8,9},{9,8},{10,11... | collective-permute-start | bytes 983048 | tf_op jit(solution)/shard_map/ppermute | solution.py:590
  29.7 8.9 %collective-permute-start.7 = (bf16[160,1024]{1,0:T(8,128)(2,1)S(1)}, bf16[160,1024]{1,0:T(8,128)(2,1)S(1)}, u32[]{:S(2)}, u32[]{:S(2)}) collective-permute-start(bf16[160,1024]{1,0:T(8,128)(2,1)S(1)} %collective-permute-done.3.refs_3_.refs_11_), channel_id=1, source_target_pairs={{0,8},{1,9},{2,10},{3,11},{4,12},{5,13},{6,14},{7,15},{8,0},{9,1},... | collective-permute-start | bytes 983048 | tf_op jit(solution)/shard_map/ppermute | solution.py:581
  38.5 2.5 %collective-permute-start.8 = (bf16[160,1024]{1,0:T(8,128)(2,1)S(1)}, bf16[160,1024]{1,0:T(8,128)(2,1)S(1)}, u32[]{:S(2)}, u32[]{:S(2)}) collective-permute-start(bf16[160,1024]{1,0:T(8,128)(2,1)S(1)} %collective-permute-done.7.refs_3_.refs_13_), channel_id=1, source_target_pairs={{0,1},{1,0},{2,3},{3,2},{4,5},{5,4},{6,7},{7,6},{8,9},{9,8},{10,11... | collective-permute-start | bytes 983048 | tf_op jit(solution)/shard_map/ppermute | solution.py:590
  47.1 12.7 %collective-permute-start.9 = (f32[320,512]{1,0:T(8,128)}, f32[320,512]{1,0:T(8,128)S(1)}, u32[]{:S(2)}, u32[]{:S(2)}) collective-permute-start(f32[320,512]{1,0:T(8,128)} %get-tuple-element.99), channel_id=1, source_target_pairs={{0,2},{1,5},{2,0},{3,7},{4,6},{5,1},{6,4},{7,3},{8,10},{9,13},{10,... | collective-permute-start | bytes 1966088 | tf_op jit(solution)/shard_map/ppermute | solution.py:581
  61.5 14.4 %collective-permute-start.10 = (f32[320,512]{1,0:T(8,128)S(1)}, f32[320,512]{1,0:T(8,128)S(1)}, u32[]{:S(2)}, u32[]{:S(2)}) collective-permute-start(f32[320,512]{1,0:T(8,128)S(1)} %get-tuple-element.175), channel_id=1, source_target_pairs={{0,4},{1,3},{2,6},{3,1},{4,0},{5,7},{6,2},{7,5},{8,12},{9,11},{10,... | collective-permute-start | bytes 1966088 | tf_op jit(solution)/shard_map/ppermute | solution.py:581
  62.5 15.9 %collective-permute-start.12 = (f32[320,512]{1,0:T(8,128)S(1)}, f32[320,512]{1,0:T(8,128)S(1)}, u32[]{:S(2)}, u32[]{:S(2)}) collective-permute-start(f32[320,512]{1,0:T(8,128)S(1)} %get-tuple-element.174), channel_id=1, source_target_pairs={{0,2},{1,5},{2,0},{3,7},{4,6},{5,1},{6,4},{7,3},{8,10},{9,13},{10,... | collective-permute-start | bytes 1966088 | tf_op jit(solution)/shard_map/ppermute | solution.py:581
  68.3 10.0 %copy-start.19 = (f32[320,512]{1,0:T(8,128)S(1)}, f32[320,512]{1,0:T(8,128)}, u32[]{:S(2)}) copy-start(f32[320,512]{1,0:T(8,128)} %more_sums.3) | copy-start | bytes 1966084
  69.2 11.9 %copy-start.12 = (s32[2]{0:T(128)S(1)}, s32[2]{0:T(128)}, u32[]{:S(2)}) copy-start(s32[2]{0:T(128)} %pad_add_fusion.2.place_ref) | copy-start | bytes 28
  69.2 13.6 %copy-start.7 = (bf16[320,1024]{1,0:T(8,128)(2,1)S(1)}, bf16[320,1024]{1,0:T(8,128)(2,1)}, u32[]{:S(2)}) copy-start(bf16[320,1024]{1,0:T(8,128)(2,1)} %cotangent_ref.1) | copy-start | bytes 1966084
  78.5 2.6 %collective-permute-start.13 = (bf16[320,512]{1,0:T(8,128)(2,1)S(1)}, bf16[320,512]{1,0:T(8,128)(2,1)S(1)}, u32[]{:S(2)}, u32[]{:S(2)}) collective-permute-start(bf16[320,512]{1,0:T(8,128)(2,1)S(1)} %divide_convert_fusion.mine_ref), channel_id=1, source_target_pairs={{0,1},{1,0},{2,3},{3,2},{4,5},{5,4},{6,7},{7,6},{8,9},{9,8},{10,11... | collective-permute-start | bytes 983048 | tf_op jit(solution)/shard_map/ppermute | solution.py:590
  81.8 6.3 %collective-permute-start.14 = (bf16[640,256]{1,0:T(8,128)(2,1)S(1)}, bf16[640,256]{1,0:T(8,128)(2,1)S(1)}, u32[]{:S(2)}, u32[]{:S(2)}) collective-permute-start(bf16[640,256]{1,0:T(8,128)(2,1)S(1)} %get-tuple-element.113), channel_id=1, source_target_pairs={{0,2},{1,5},{2,0},{3,7},{4,6},{5,1},{6,4},{7,3},{8,10},{9,13},{10,... | collective-permute-start | bytes 983048 | tf_op jit(solution)/shard_map/ppermute | solution.py:581
  86.5 27.4 %copy-start.2 = (bf16[320,1024]{1,0:T(8,128)(2,1)}, bf16[320,1024]{1,0:T(8,128)(2,1)S(1)}, u32[]{:S(2)}) copy-start(bf16[320,1024]{1,0:T(8,128)(2,1)S(1)} %get-tuple-element.122.refs_0_) | copy-start | bytes 1966084
  88.0 6.7 %collective-permute-start.15 = (bf16[160,1024]{1,0:T(8,128)(2,1)S(1)}, bf16[160,1024]{1,0:T(8,128)(2,1)S(1)}, u32[]{:S(2)}, u32[]{:S(2)}) collective-permute-start(bf16[160,1024]{1,0:T(8,128)(2,1)S(1)} %get-tuple-element.114), channel_id=1, source_target_pairs={{0,4},{1,3},{2,6},{3,1},{4,0},{5,7},{6,2},{7,5},{8,12},{9,11},{10,... | collective-permute-start | bytes 983048 | tf_op jit(solution)/shard_map/ppermute | solution.py:581
  88.6 8.5 %collective-permute-start.16 = (bf16[160,1024]{1,0:T(8,128)(2,1)S(1)}, bf16[160,1024]{1,0:T(8,128)(2,1)S(1)}, u32[]{:S(2)}, u32[]{:S(2)}) collective-permute-start(bf16[160,1024]{1,0:T(8,128)(2,1)S(1)} %get-tuple-element.114), channel_id=1, source_target_pairs={{0,2},{1,5},{2,0},{3,7},{4,6},{5,1},{6,4},{7,3},{8,10},{9,13},{10,... | collective-permute-start | bytes 983048 | tf_op jit(solution)/shard_map/ppermute | solution.py:581
  89.6 11.7 %collective-permute-start.18 = (bf16[640,256]{1,0:T(8,128)(2,1)S(1)}, bf16[640,256]{1,0:T(8,128)(2,1)S(1)}, u32[]{:S(2)}, u32[]{:S(2)}) collective-permute-start(bf16[640,256]{1,0:T(8,128)(2,1)S(1)} %pad_maximum_fusion.1), channel_id=1, source_target_pairs={{0,4},{1,3},{2,6},{3,1},{4,0},{5,7},{6,2},{7,5},{8,12},{9,11},{10,... | collective-permute-start | bytes 983048 | tf_op jit(solution)/shard_map/ppermute | solution.py:581
  97.1 8.2 %collective-permute-start.17 = (bf16[160,1024]{1,0:T(8,128)(2,1)S(1)}, bf16[160,1024]{1,0:T(8,128)(2,1)S(1)}, u32[]{:S(2)}, u32[]{:S(2)}) collective-permute-start(bf16[160,1024]{1,0:T(8,128)(2,1)S(1)} %collective-permute-done.15.refs_1_), channel_id=1, source_target_pairs={{0,2},{1,5},{2,0},{3,7},{4,6},{5,1},{6,4},{7,3},{8,10},{9,13},{10,... | collective-permute-start | bytes 983048 | tf_op jit(solution)/shard_map/ppermute | solution.py:581
  105.4 5.2 %collective-permute-start.19 = (bf16[480,1024]{1,0:T(8,128)(2,1)S(1)}, bf16[480,1024]{1,0:T(8,128)(2,1)S(1)}, u32[]{:S(2)}, u32[]{:S(2)}) collective-permute-start(bf16[480,1024]{1,0:T(8,128)(2,1)S(1)} %pad_maximum_fusion), channel_id=1, source_target_pairs={{0,1},{1,0},{2,3},{3,2},{4,5},{5,4},{6,7},{7,6},{8,9},{9,8},{10,11... | collective-permute-start | bytes 2949128 | tf_op jit(solution)/shard_map/ppermute | solution.py:590
  110.6 4.2 %copy-start.11 = (bf16[160,1024]{1,0:T(8,128)(2,1)S(1)}, bf16[160,1024]{1,0:T(8,128)(2,1)}, u32[]{:S(2)}) copy-start(bf16[160,1024]{1,0:T(8,128)(2,1)} %copy-done.10) | copy-start | bytes 983044
  110.6 4.2 %copy-start.14 = (bf16[160,1024]{1,0:T(8,128)(2,1)S(1)}, bf16[160,1024]{1,0:T(8,128)(2,1)}, u32[]{:S(2)}) copy-start(bf16[160,1024]{1,0:T(8,128)(2,1)} %copy-done.13) | copy-start | bytes 983044
  110.7 4.2 %copy-start.16 = (bf16[160,1024]{1,0:T(8,128)(2,1)S(1)}, bf16[160,1024]{1,0:T(8,128)(2,1)}, u32[]{:S(2)}) copy-start(bf16[160,1024]{1,0:T(8,128)(2,1)} %copy-done.15) | copy-start | bytes 983044
  110.7 4.2 %copy-start.18 = (bf16[160,1024]{1,0:T(8,128)(2,1)S(1)}, bf16[160,1024]{1,0:T(8,128)(2,1)}, u32[]{:S(2)}) copy-start(bf16[160,1024]{1,0:T(8,128)(2,1)} %copy-done.17) | copy-start | bytes 983044
  113.9 15.2 %collective-permute-start.20 = (bf16[272,1024]{1,0:T(8,128)(2,1)S(1)}, bf16[272,1024]{1,0:T(8,128)(2,1)S(1)}, u32[]{:S(2)}, u32[]{:S(2)}) collective-permute-start(bf16[272,1024]{1,0:T(8,128)(2,1)S(1)} %self_weight.1.keep_ref), channel_id=1, source_target_pairs={{0,8},{1,17},{2,10},{3,19},{4,12},{5,21},{6,14},{7,23},{8,0},{9,25... | collective-permute-start | bytes 1671176 | tf_op jit(solution)/shard_map/ppermute | solution.py:581
  129.2 8.5 %collective-permute-start.21 = (bf16[528,512]{1,0:T(8,128)(2,1)S(1)}, bf16[528,512]{1,0:T(8,128)(2,1)S(1)}, u32[]{:S(2)}, u32[]{:S(2)}) collective-permute-start(bf16[528,512]{1,0:T(8,128)(2,1)S(1)} %get-tuple-element.135), channel_id=1, source_target_pairs={{0,2},{1,5},{2,0},{3,7},{4,6},{5,1},{6,4},{7,3},{8,10},{9,13},{10,... | collective-permute-start | bytes 1622024 | tf_op jit(solution)/shard_map/ppermute | solution.py:581
  130.4 12.4 %collective-permute-start.23 = (bf16[272,1024]{1,0:T(8,128)(2,1)S(1)}, bf16[272,1024]{1,0:T(8,128)(2,1)S(1)}, u32[]{:S(2)}, u32[]{:S(2)}) collective-permute-start(bf16[272,1024]{1,0:T(8,128)(2,1)S(1)} %merge.3), channel_id=1, source_target_pairs={{0,16},{1,9},{2,18},{3,11},{4,20},{5,13},{6,22},{7,15},{8,24},{9,1... | collective-permute-start | bytes 1671176 | tf_op jit(solution)/shard_map/ppermute | solution.py:581
  138.3 5.8 %collective-permute-start.22 = (bf16[272,512]{1,0:T(8,128)(2,1)S(1)}, bf16[272,512]{1,0:T(8,128)(2,1)S(1)}, u32[]{:S(2)}, u32[]{:S(2)}) collective-permute-start(bf16[272,512]{1,0:T(8,128)(2,1)S(1)} %get-tuple-element.141), channel_id=1, source_target_pairs={{0,4},{1,3},{2,6},{3,1},{4,0},{5,7},{6,2},{7,5},{8,12},{9,11},{10,... | collective-permute-start | bytes 835592 | tf_op jit(solution)/shard_map/ppermute | solution.py:581
  144.4 10.4 %collective-permute-start.25 = (bf16[256,1024]{1,0:T(8,128)(2,1)S(1)}, bf16[256,1024]{1,0:T(8,128)(2,1)S(1)}, u32[]{:S(2)}, u32[]{:S(2)}) collective-permute-start(bf16[256,1024]{1,0:T(8,128)(2,1)S(1)} %slice.77), channel_id=1, source_target_pairs={{0,4},{1,3},{2,6},{3,1},{4,0},{5,7},{6,2},{7,5},{8,12},{9,11},{10,... | collective-permute-start | bytes 1572872 | tf_op jit(solution)/shard_map/ppermute | solution.py:581
  145.3 9.5 %collective-permute-start.24 = (bf16[272,512]{1,0:T(8,128)(2,1)S(1)}, bf16[272,512]{1,0:T(8,128)(2,1)S(1)}, u32[]{:S(2)}, u32[]{:S(2)}) collective-permute-start(bf16[272,512]{1,0:T(8,128)(2,1)S(1)} %merge.4.keep_ref), channel_id=1, source_target_pairs={{0,8},{1,17},{2,10},{3,19},{4,12},{5,21},{6,14},{7,23},{8,0},{9,25... | collective-permute-start | bytes 835592 | tf_op jit(solution)/shard_map/ppermute | solution.py:581
  154.9 24.3 %collective-permute-start.29 = (bf16[512,1024]{1,0:T(8,128)(2,1)S(1)}, bf16[512,1024]{1,0:T(8,128)(2,1)S(1)}, u32[]{:S(2)}, u32[]{:S(2)}) collective-permute-start(bf16[512,1024]{1,0:T(8,128)(2,1)S(1)} %constant_dynamic-update-slice_fusion.refs_0_), channel_id=1, source_target_pairs={{0,2},{1,5},{2,0},{3,7},{4,6},{5,1},{6,4},{7,3},{8,10},{9,13},{10,... | collective-permute-start | bytes 3145736 | tf_op jit(solution)/shard_map/ppermute | solution.py:581
  156.4 11.6 %collective-permute-start.27 = (bf16[320,512]{1,0:T(8,128)(2,1)S(1)}, bf16[320,512]{1,0:T(8,128)(2,1)S(1)}, u32[]{:S(2)}, u32[]{:S(2)}) collective-permute-start(bf16[320,512]{1,0:T(8,128)(2,1)S(1)} %get-tuple-element.156), channel_id=1, source_target_pairs={{0,8},{1,17},{2,10},{3,19},{4,12},{5,21},{6,14},{7,23},{8,0},{9,25... | collective-permute-start | bytes 983048 | tf_op jit(solution)/shard_map/ppermute | solution.py:581
  156.5 9.2 %collective-permute-start.26 = (bf16[272,512]{1,0:T(8,128)(2,1)S(1)}, bf16[272,512]{1,0:T(8,128)(2,1)S(1)}, u32[]{:S(2)}, u32[]{:S(2)}) collective-permute-start(bf16[272,512]{1,0:T(8,128)(2,1)S(1)} %merge.5), channel_id=1, source_target_pairs={{0,16},{1,9},{2,18},{3,11},{4,20},{5,13},{6,22},{7,15},{8,24},{9,1... | collective-permute-start | bytes 835592 | tf_op jit(solution)/shard_map/ppermute | solution.py:581
  168.1 11.1 %collective-permute-start.30 = (bf16[320,512]{1,0:T(8,128)(2,1)S(1)}, bf16[320,512]{1,0:T(8,128)(2,1)S(1)}, u32[]{:S(2)}, u32[]{:S(2)}) collective-permute-start(bf16[320,512]{1,0:T(8,128)(2,1)S(1)} %get-tuple-element.164), channel_id=1, source_target_pairs={{0,8},{1,17},{2,10},{3,19},{4,12},{5,21},{6,14},{7,23},{8,0},{9,25... | collective-permute-start | bytes 983048 | tf_op jit(solution)/shard_map/ppermute | solution.py:581
  168.7 6.7 %collective-permute-start.28 = (bf16[256,512]{1,0:T(8,128)(2,1)S(1)}, bf16[256,512]{1,0:T(8,128)(2,1)S(1)}, u32[]{:S(2)}, u32[]{:S(2)}) collective-permute-start(bf16[256,512]{1,0:T(8,128)(2,1)S(1)} %slice.78), channel_id=1, source_target_pairs={{0,4},{1,3},{2,6},{3,1},{4,0},{5,7},{6,2},{7,5},{8,12},{9,11},{10,... | collective-permute-start | bytes 786440 | tf_op jit(solution)/shard_map/ppermute | solution.py:581
  179.3 6.8 %collective-permute-start.31 = (bf16[320,512]{1,0:T(8,128)(2,1)S(1)}, bf16[320,512]{1,0:T(8,128)(2,1)S(1)}, u32[]{:S(2)}, u32[]{:S(2)}) collective-permute-start(bf16[320,512]{1,0:T(8,128)(2,1)S(1)} %add_convert_fusion), channel_id=1, source_target_pairs={{0,16},{1,9},{2,18},{3,11},{4,20},{5,13},{6,22},{7,15},{8,24},{9,1... | collective-permute-start | bytes 983048 | tf_op jit(solution)/shard_map/ppermute | solution.py:581
  179.4 16.3 %collective-permute-start.36 = (f32[512]{0:T(512)S(1)}, f32[512]{0:T(512)S(1)}, u32[]{:S(2)}, u32[]{:S(2)}) collective-permute-start(f32[512]{0:T(512)S(1)} %bitcast.20), channel_id=1, source_target_pairs={{0,1},{1,0},{2,3},{3,2},{4,5},{5,4},{6,7},{7,6},{8,9},{9,8},{10,11... | collective-permute-start | bytes 6152 | tf_op jit(solution)/shard_map/ppermute | solution.py:590
  184.3 14.8 %collective-permute-start.33 = (bf16[512,512]{1,0:T(8,128)(2,1)S(1)}, bf16[512,512]{1,0:T(8,128)(2,1)S(1)}, u32[]{:S(2)}, u32[]{:S(2)}) collective-permute-start(bf16[512,512]{1,0:T(8,128)(2,1)S(1)} %constant_dynamic-update-slice_fusion.2.refs_0_), channel_id=1, source_target_pairs={{0,2},{1,5},{2,0},{3,7},{4,6},{5,1},{6,4},{7,3},{8,10},{9,13},{10,... | collective-permute-start | bytes 1572872 | tf_op jit(solution)/shard_map/ppermute | solution.py:581
  186.4 13.2 %collective-permute-start.32 = (bf16[320,512]{1,0:T(8,128)(2,1)S(1)}, bf16[320,512]{1,0:T(8,128)(2,1)S(1)}, u32[]{:S(2)}, u32[]{:S(2)}) collective-permute-start(bf16[320,512]{1,0:T(8,128)(2,1)S(1)} %fusion.2), channel_id=1, source_target_pairs={{0,1},{1,0},{2,3},{3,2},{4,5},{5,4},{6,7},{7,6},{8,9},{9,8},{10,11... | collective-permute-start | bytes 983048 | tf_op jit(solution)/shard_map/ppermute | solution.py:590
  196.3 5.3 %collective-permute-start.34 = (bf16[512,512]{1,0:T(8,128)(2,1)S(1)}, bf16[512,512]{1,0:T(8,128)(2,1)S(1)}, u32[]{:S(2)}, u32[]{:S(2)}) collective-permute-start(bf16[512,512]{1,0:T(8,128)(2,1)S(1)} %constant_dynamic-update-slice_fusion.2.refs_0_), channel_id=1, source_target_pairs={{0,1},{1,0},{2,3},{3,2},{4,5},{5,4},{6,7},{7,6},{8,9},{9,8},{10,11... | collective-permute-start | bytes 1572872 | tf_op jit(solution)/shard_map/ppermute | solution.py:590
  199.1 2.5 %collective-permute-start.35 = (bf16[512,512]{1,0:T(8,128)(2,1)S(1)}, bf16[512,512]{1,0:T(8,128)(2,1)S(1)}, u32[]{:S(2)}, u32[]{:S(2)}) collective-permute-start(bf16[512,512]{1,0:T(8,128)(2,1)S(1)} %collective-permute-done.33.refs_1_), channel_id=1, source_target_pairs={{0,1},{1,0},{2,3},{3,2},{4,5},{5,4},{6,7},{7,6},{8,9},{9,8},{10,11... | collective-permute-start | bytes 1572872 | tf_op jit(solution)/shard_map/ppermute | solution.py:590
  (13 other events, 34.0 us)

commit v3 on v2

v3 whole, which is shorter than its diff:
```python
import jax
import jax.numpy as jnp
from jax import lax
from jax.experimental import pallas as pl
from jax.experimental.pallas import tpu as pltpu
from jax.sharding import PartitionSpec as P

PLANE = 4
TILE = 16
PIECES = 2 * PLANE - 1
VMEM_BYTES = 48 * 1024 * 1024
ALL_VMEM = 67_000_000
F32, BF16, I32 = jnp.float32, jnp.bfloat16, jnp.int32


def across(lhs, rhs):
    return lax.dot_general(lhs, rhs, (((0,), (0,)), ((), ())), preferred_element_type=F32)


def times_t(lhs, rhs):
    return lax.dot_general(lhs, rhs, (((1,), (1,)), ((), ())), preferred_element_type=F32)


def aligned(start, size):
    start = start if isinstance(start, int) else pl.multiple_of(start, size)
    return pl.ds(start, size)


def spaced(space, arrays):
    return [pl.BlockSpec(memory_space=space) for _ in arrays]


def array(shape, dtype):
    return jax.ShapeDtypeStruct(shape, dtype)


def call(kernel, name, outs, place, near, far=(), scratch=(), flops=0, far_outs=0,
         limit=VMEM_BYTES, light=False):
    operands = list(near) + list(far)
    moved = sum(a.size * a.dtype.itemsize for a in operands + list(outs))
    if light:
        flops, moved = 1, 1
    return pl.pallas_call(
        kernel,
        name=name,
        out_shape=list(outs),
        in_specs=spaced(pltpu.SMEM, [place]) + spaced(pltpu.VMEM, near) + spaced(pltpu.HBM, far),
        out_specs=spaced(pltpu.VMEM, outs[: len(outs) - far_outs])
        + spaced(pltpu.HBM, outs[len(outs) - far_outs :]),
        scratch_shapes=list(scratch),
        compiler_params=pltpu.CompilerParams(vmem_limit_bytes=limit),
        cost_estimate=pl.CostEstimate(
            flops=int(flops), bytes_accessed=int(moved), transcendentals=0
        ),
    )(place, *operands)


def reversed_bits(value, bits):
    out = 0
    for bit in range(bits):
        out = out | (((value >> bit) & 1) << (bits - 1 - bit))
    return out


def away(core, slot, bits):
    return jnp.where(core == 0, reversed_bits(slot, bits), slot)


def bits_of(size):
    return size.bit_length() - 1


def line_side(place_ref, lines):
    line = place_ref[0] // PLANE
    return jnp.where(place_ref[1] == 0, line & 1, line // (lines // 2))


def bias_rows(value):
    top = value.astype(BF16).astype(F32)
    row_at = lax.broadcasted_iota(I32, (TILE, value.shape[1]), 0)
    return jnp.where(row_at == 0, top, jnp.where(row_at == 1, value - top, 0.0)).astype(BF16)


def stacked(parts, target, sem, first=0):
    copies, at = [], 0
    for index, part in enumerate(parts):
        span = pl.ds(at, part.shape[0])
        copies.append(pltpu.make_async_copy(part, target.at[span, :], sem.at[first + index]))
        at += part.shape[0]
    return copies


def line_copies(parts, target, sem):
    own, parts = parts[0], parts[1:]
    mine, other = parts[: len(parts) // 2], parts[len(parts) // 2 :]
    rows, bits = own.shape[0], len(mine)
    half = rows // 2
    copies = [pltpu.make_async_copy(own, target.at[pl.ds(0, rows), :], sem.at[0])]
    for slot in range(1, 1 << bits):
        for index, (stages, at) in enumerate(((mine, slot), (other, reversed_bits(slot, bits)))):
            stage = at.bit_length() - 1
            view = stages[stage].at[pl.ds((at - (1 << stage)) * half, half), :]
            spot = target.at[pl.ds(slot * rows + index * half, half), :]
            copies.append(pltpu.make_async_copy(view, spot, sem.at[2 * slot - 1 + index]))
    return copies


def start_all(copies):
    for copy in copies:
        copy.start()


def wait_all(copies):
    for copy in copies:
        copy.wait()


def sort_slots(place, neighbours, present, importance, count):
    rows, slots = neighbours.shape
    turns = -(-slots // count)
    arrays = [neighbours.T, present.T, importance.T]

    def kernel(place_ref, *refs):
        out_ref, neighbours_ref, present_ref, importance_ref, sem = refs[3:]
        copies = [
            pltpu.make_async_copy(part, target, sem.at[index])
            for index, (part, target) in enumerate(zip(refs[:3], refs[4:7]))
        ]
        start_all(copies)
        wait_all(copies)
        slot_at = lax.broadcasted_iota(I32, (slots, rows), 0)
        node_at = lax.broadcasted_iota(I32, (slots, rows), 1)
        block = (node_at * slots + slot_at) & (count - 1)
        row = neighbours_ref[...] - rows * block
        packed = row * 128 + present_ref[...] * importance_ref[...]
        block_at = lax.broadcasted_iota(I32, (count, rows), 0)
        node_at = lax.broadcasted_iota(I32, (count, rows), 1)
        first = (block_at - slots * node_at) & (count - 1)
        for turn in range(turns):
            total = jnp.zeros((count, rows), I32)
            for slot in range(slots):
                at = slot - count * turn
                if 0 <= at < count:
                    total = jnp.where(first == at, packed[slot : slot + 1, :], total)
            out_ref[turn * count : (turn + 1) * count, :] = total

    (out,) = call(
        kernel, "sort_slots", [array((turns * count, rows), I32)], place, [], arrays,
        [pltpu.VMEM((slots, rows), I32)] * 3 + [pltpu.SemaphoreType.DMA((3,))], limit=ALL_VMEM,
    )
    return out


def slot_matrix(place, lists, count):
    tall, rows = lists[0].shape
    lines, width, turns = count // PLANE, PLANE * rows, tall // count

    def kernel(place_ref, own_ref, next_ref, rest_ref, sums_ref, far_ref, out_ref, sem):
        slot_refs = [(own_ref, 0), (next_ref, 0), (rest_ref, 0), (rest_ref, tall)]
        core, spot, line = place_ref[1], place_ref[0] % PLANE, place_ref[0] // PLANE
        sums = [
            jnp.sum((ref[at : at + tall, :] & 127).astype(F32), axis=0, keepdims=True)
            for ref, at in slot_refs
        ]
        sums = jnp.broadcast_to(jnp.concatenate(sums, axis=1), (8, width))
        sums_ref[...] = sums.T
        for at in range(lines):
            block = (line ^ away(core, at, bits_of(lines))) * PLANE + spot
            ids, weights = [], []
            for turn in range(turns):
                listed = jnp.concatenate(
                    [ref[pl.ds(at + turn * count + block, 1), :] for ref, at in slot_refs],
                    axis=1,
                )
                ids.append(((listed >> 7) - rows // 2).astype(F32).astype(BF16))
                weights.append((listed & 127).astype(F32).astype(BF16))
            shift = core * (rows // 2) if at else 0

            @pl.loop(0, rows // TILE)
            def _(step):
                base = step * TILE + shift
                base = jnp.where(base >= rows, base - rows, base)
                row_at = lax.broadcasted_iota(I32, (TILE, width), 0) + (base - rows // 2)
                row_at = row_at.astype(F32).astype(BF16)
                zero = jnp.zeros((TILE, width), BF16)
                total = zero
                for listed, weight in zip(ids, weights):
                    total = total + jnp.where(listed == row_at, weight, zero)
                out_ref[aligned(at * rows + step * TILE, TILE), :] = total

            span = pl.ds(at * rows, rows)
            pltpu.make_async_copy(out_ref.at[span, :], far_ref.at[span, :], sem.at[at]).start()
        for at in range(lines):
            span = pl.ds(at * rows, rows)
            pltpu.make_async_copy(out_ref.at[span, :], far_ref.at[span, :], sem.at[at]).wait()

    sums, matrix = call(
        kernel, "slot_matrix", [array((width, 8), F32), array((lines * rows, width), BF16)],
        place, lists,
        scratch=[pltpu.VMEM((lines * rows, width), BF16), pltpu.SemaphoreType.DMA((lines,))],
        flops=3 * turns * lines * rows * width, far_outs=1, limit=ALL_VMEM, light=True,
    )
    return matrix, sums


def half_copy(core, q_in, q_ref, sem):
    half = q_ref.shape[1]
    return pltpu.make_async_copy(q_in.at[:, aligned(core * half, half)], q_ref, sem)


def hidden_of(core, rows, q_ref, bias_ref):
    half = q_ref.shape[1]
    bias = bias_ref[:, aligned(core * half, half)]
    hidden = jnp.maximum(jnp.dot(rows, q_ref[...], preferred_element_type=F32) + bias, 0.0)
    top = hidden.astype(BF16)
    return top, (hidden - top.astype(F32)).astype(BF16)


def lane_span(start, size):
    low = start // 128 * 128
    high = -(-(start + size) // 128) * 128
    return low, high - low, start - low


def first_sums(place, line_parts, q_weight, q_bias, matrix):
    rows, dim = line_parts[0].shape
    total, width = matrix.shape
    half, part, count = dim // 2, width // PLANE, len(line_parts)
    lines = total // rows
    low, span_width, skip = lane_span(width - part, part)

    def kernel(place_ref, bias_ref, q_in, matrix_in, *refs):
        parts, refs = refs[:count], refs[count:]
        send_ref, high_out, low_out, rows_ref, high_ref, low_ref, matrix_ref, q_ref = refs[:8]
        row_sem, sem = refs[8:]
        core = place_ref[1]
        q_copy = half_copy(core, q_in, q_ref, sem.at[0])
        matrix_copy = pltpu.make_async_copy(
            matrix_in.at[:, pl.ds(low, span_width)], matrix_ref, sem.at[1]
        )
        copies = line_copies(parts, rows_ref, row_sem)
        start_all([q_copy] + copies + [matrix_copy])
        q_copy.wait()
        for at in range(lines):
            wait_all(copies[max(2 * at - 1, 0) : 2 * at + 1])
            span = slice(at * rows, (at + 1) * rows)
            high_ref[span, :], low_ref[span, :] = hidden_of(
                core, rows_ref[span, :], q_ref, bias_ref
            )
        outs = [
            pltpu.make_async_copy(high_ref, high_out, sem.at[2]),
            pltpu.make_async_copy(low_ref, low_out, sem.at[3]),
        ]
        start_all(outs)
        matrix_copy.wait()
        total_sum = across(matrix_ref[...], high_ref[...]) + across(matrix_ref[...], low_ref[...])
        send_ref[...] = total_sum[skip : skip + part, :]
        wait_all(outs)

    return call(
        kernel, "first_sums",
        [array((part, half), F32)] + [array((total, half), BF16)] * 2,
        place, [q_bias], [q_weight, matrix] + list(line_parts),
        [
            pltpu.VMEM((total, dim), BF16),
            pltpu.VMEM((total, half), BF16),
            pltpu.VMEM((total, half), BF16),
            pltpu.VMEM((total, span_width), BF16),
            pltpu.VMEM((dim, half), BF16),
            pltpu.SemaphoreType.DMA((2 * lines - 1,)),
            pltpu.SemaphoreType.DMA((4,)),
        ],
        flops=2 * total * dim * half + 4 * total * part * half, far_outs=2, limit=ALL_VMEM,
    )


def more_sums(place, highs, lows, matrix, first, slots):
    total = matrix.shape[0]
    part = matrix.shape[1] // PLANE
    width = slots * part
    start, span_width, skip = lane_span(first * part, width)
    half, count = highs[0].shape[1], len(highs)

    def kernel(place_ref, matrix_in, *refs):
        parts, refs = refs[: 2 * count], refs[2 * count :]
        sum_refs, refs = refs[:slots], refs[slots:]
        high_ref, low_ref, matrix_ref, sem = refs
        copies = [
            pltpu.make_async_copy(
                matrix_in.at[:, pl.ds(start, span_width)], matrix_ref, sem.at[2 * count]
            )
        ]
        copies += stacked(parts[:count], high_ref, sem)
        copies += stacked(parts[count:], low_ref, sem, count)
        start_all(copies)
        wait_all(copies)
        total_sum = across(matrix_ref[...], high_ref[...]) + across(matrix_ref[...], low_ref[...])
        for slot, sum_ref in enumerate(sum_refs):
            at = skip + slot * part
            sum_ref[...] = total_sum[at : at + part, :]

    return call(
        kernel, "more_sums", [array((part, half), F32)] * slots, place, [],
        [matrix] + list(highs) + list(lows),
        [
            pltpu.VMEM((total, half), BF16),
            pltpu.VMEM((total, half), BF16),
            pltpu.VMEM((total, span_width), BF16),
            pltpu.SemaphoreType.DMA((2 * count + 1,)),
        ],
        flops=4 * total * width * half, limit=ALL_VMEM,
    )


def pick_copy(core, first, second, target, sem, rows=None):
    views = [ref if rows is None else ref.at[rows, :] for ref in (first, second)]
    for side, view in enumerate(views):

        @pl.when(core == side)
        def _():
            pltpu.make_async_copy(view, target, sem).start()

    return pltpu.make_async_copy(views[0], target, sem)


def self_product(place, features, w_weight, w_other, w_bias):
    rows, dim = features.shape

    def kernel(place_ref, features_ref, bias_ref, w_in, w_other_in, out_ref, w_ref, sem):
        pick_copy(place_ref[1], w_in, w_other_in, w_ref, sem).wait()
        out_ref[...] = bias_ref[...] + jnp.dot(
            features_ref[...], w_ref[...], preferred_element_type=F32
        )

    (out,) = call(
        kernel, "self_product", [array((rows, dim), F32)], place, [features, w_bias],
        [w_weight, w_other], [pltpu.VMEM((dim, dim), BF16), pltpu.SemaphoreType.DMA(())],
        flops=2 * rows * dim * dim,
    )
    return out


def row_sums(place, stay, late, come):
    rows, half = late.shape

    def kernel(place_ref, stay_ref, late_ref, come_ref, out_ref):
        for part in range(2):
            span = slice(part * rows // 2, (part + 1) * rows // 2)
            came = late_ref[span, :].astype(F32) + come_ref[span, :].astype(F32)
            at = aligned((place_ref[1] ^ part) * (rows // 2), rows // 2)
            out_ref[at, :] = (stay_ref[at, :].astype(F32) + came).astype(BF16)

    (out,) = call(kernel, "row_sums", [array((rows, half), BF16)], place, [stay, late, come])
    return out


def feature_step(place, grad_linear, mine, other, w_weight, w_other, q_weight):
    rows, dim = grad_linear.shape
    half = dim // 2

    def kernel(
        place_ref, grad_ref, mine_ref, other_ref, w_in, w_other_in, q_in, out_ref, w_ref, q_ref, sem
    ):
        core = place_ref[1]
        span = aligned(core * half, half)
        q_copy = pltpu.make_async_copy(q_in.at[span, :], q_ref, sem.at[1])
        q_copy.start()
        pick_copy(core, w_in, w_other_in, w_ref, sem.at[0], span).wait()
        total = times_t(grad_ref[...], w_ref[...])
        q_copy.wait()
        total += times_t(mine_ref[...], q_ref[:, span])
        out_ref[...] = total + times_t(other_ref[...], q_ref[:, aligned((1 - core) * half, half)])

    (out,) = call(
        kernel, "feature_step", [array((rows, half), F32)], place, [grad_linear, mine, other],
        [w_weight, w_other, q_weight],
        [pltpu.VMEM((half, dim), BF16)] * 2 + [pltpu.SemaphoreType.DMA((2,))],
        flops=4 * rows * dim * half,
    )
    return out


def plane_slices(place, features, mine, other):
    rows, dim = features.shape
    half, width = dim // 2, dim // PLANE

    def kernel(place_ref, features_ref, mine_ref, other_ref, own_ref, next_ref, send_ref):
        core, spot = place_ref[1], place_ref[0] % PLANE
        targets = [own_ref, next_ref, send_ref.at[pl.ds(0, rows), :], send_ref.at[pl.ds(rows, rows), :]]
        for slot, target in enumerate(targets):
            to = spot ^ away(core, slot, 2)

            @pl.when(core == 0)
            def _():
                target[...] = features_ref[:, aligned(to * width, width)]

            within = aligned(to % 2 * width, width)

            @pl.when((core == 1) & (to < 2))
            def _():
                target[...] = other_ref[:, within]

            @pl.when((core == 1) & (to >= 2))
            def _():
                target[...] = mine_ref[:, within]

    outs = [array((rows, width), BF16)] * 2 + [array((2 * rows, width), BF16)]
    return call(kernel, "plane_slices", outs, place, [features, mine, other])


def node_step(place, mine, other, self_part, cotangent, w_weight, w_other):
    rows, half = mine.shape
    dim = 2 * half

    def kernel(
        place_ref, mine_ref, other_ref, self_ref, cotangent_ref, w_in, w_other_in,
        embeddings_ref, grad_ref, half_ref, lhs_ref, linear_ref, near_ref, sem,
    ):
        core = place_ref[1]
        near_copy = pick_copy(core, w_other_in, w_in, near_ref, sem)
        lhs_ref[:, aligned(core * half, half)] = mine_ref[...]
        lhs_ref[:, aligned((1 - core) * half, half)] = other_ref[...]
        near_copy.wait()
        linear_ref[...] = self_ref[...] + jnp.dot(
            lhs_ref[...], near_ref[...], preferred_element_type=F32
        )

        @pl.loop(0, rows // TILE, unroll=4)
        def _(step):
            at = aligned(step * TILE, TILE)
            linear = linear_ref[at, :]
            relu_out = jnp.maximum(linear, 0.0)
            scale = lax.rsqrt(jnp.mean(relu_out * relu_out, axis=1, keepdims=True) + 1e-06)
            embeddings_ref[at, :] = relu_out * scale
            grad_out = cotangent_ref[at, :].astype(F32)
            inner = jnp.mean(relu_out * grad_out, axis=1, keepdims=True)
            grad_relu = scale * grad_out - relu_out * (scale * scale * scale) * inner
            grad_ref[at, :] = jnp.where(linear > 0, grad_relu, 0.0).astype(BF16)

        half_ref[...] = grad_ref[aligned(core * (rows // 2), rows // 2), :]

    outs = [
        array((rows, dim), F32), array((rows, dim), BF16), array((rows // 2, dim), BF16),
    ]
    return call(
        kernel, "node_step", outs, place, [mine, other, self_part, cotangent],
        [w_weight, w_other],
        [
            pltpu.VMEM((rows, dim), BF16), pltpu.VMEM((rows, dim), F32),
            pltpu.VMEM((dim, dim), BF16), pltpu.SemaphoreType.DMA(()),
        ],
        flops=2 * rows * dim * dim,
    )


def plane_copies(core, rows, pieces, target, sem):
    own = pieces[0]
    half = rows // 2
    copies = [pltpu.make_async_copy(own, target.at[pl.ds(0, rows), :], sem.at[0])]
    for slot in range(1, PLANE):
        mine = pieces[slot]
        other = pieces[PLANE - 1 + reversed_bits(slot, 2)]
        for index, (part, at) in enumerate(((mine, core), (other, 1 - core))):
            spot = pl.multiple_of(slot * rows + at * half, TILE)
            copies.append(
                pltpu.make_async_copy(
                    part, target.at[pl.ds(spot, half), :], sem.at[2 * slot - 1 + index]
                )
            )
    return copies


def self_weight(place, pieces, slices, lines):
    rows, dim = pieces[0].shape
    width = slices[0].shape[1]

    def kernel(place_ref, *refs):
        parts, refs = refs[:PIECES], refs[PIECES:]
        slots, outs = refs[:4], refs[4:6]
        grads_ref, lhs_ref, sum_ref, sem, slice_sem = refs[6:]
        copies = plane_copies(place_ref[1], rows, parts, grads_ref, sem)
        own, far, near, last = slots
        spans = [own, last.at[pl.ds(0, rows), :], far.at[pl.ds(0, rows), :], last.at[pl.ds(rows, rows), :]]
        for slot, part in enumerate(spans):
            copies.append(
                pltpu.make_async_copy(part, lhs_ref.at[pl.ds(slot * rows, rows), :], slice_sem.at[slot])
            )
        for copy in copies:
            copy.start()
        for copy in copies:
            copy.wait()
        sum_ref[...] = across(lhs_ref[...], grads_ref[...])
        bias = bias_rows(jnp.sum(grads_ref[...].astype(F32), axis=0, keepdims=True))
        first = line_side(place_ref, lines)
        for slot, out_ref in enumerate(outs):
            out_ref[: width // 2, :] = sum_ref[
                aligned((first ^ slot) * (width // 2), width // 2), :
            ].astype(BF16)
            out_ref[width // 2 :, :] = bias

    return call(
        kernel, "self_weight", [array((width // 2 + TILE, dim), BF16)] * 2, place, [],
        list(pieces) + list(slices),
        [
            pltpu.VMEM((PLANE * rows, dim), BF16),
            pltpu.VMEM((PLANE * rows, width), BF16),
            pltpu.VMEM((width, dim), F32),
            pltpu.SemaphoreType.DMA((PIECES,)),
            pltpu.SemaphoreType.DMA((PLANE,)),
        ],
        flops=2 * PLANE * rows * dim * width,
    )


def row_grad(place, sums, pieces, w_weight, w_other, matrix, high, line_parts, lines):
    rows, dim = pieces[0].shape
    half = dim // 2
    total, nodes, width = lines * rows, PLANE * rows, dim // PLANE

    def kernel(place_ref, sums_ref, matrix_in, high_in, w_in, w_other_in, *refs):
        parts, refs = refs[:PIECES], refs[PIECES:]
        row_parts, refs = refs[: len(line_parts)], refs[len(line_parts) :]
        stay_ref, late_ref, go_ref, keep_ref, send_ref, refs = *refs[:5], refs[5:]
        grads_ref, rows_ref, sum_ref, hidden_ref, near_ref, matrix_ref, high_ref = refs[:7]
        sem, row_sem, near_sem, line_sem = refs[7:]
        core, spot = place_ref[1], place_ref[0] % PLANE
        copies = plane_copies(core, rows, parts, grads_ref, sem)
        row_copies = line_copies(row_parts, rows_ref, row_sem)
        near_copy = pick_copy(
            core, w_other_in, w_in, near_ref, near_sem, aligned(core * half, half)
        )
        line_sums = [
            pltpu.make_async_copy(matrix_in, matrix_ref, line_sem.at[0]),
            pltpu.make_async_copy(high_in, high_ref, line_sem.at[1]),
        ]
        start_all(copies + line_sums + row_copies)
        near_copy.wait()
        for slot in range(PLANE):
            wait_all(copies[max(2 * slot - 1, 0) : 2 * slot + 1])
            span = slice(slot * rows, (slot + 1) * rows)
            grad = times_t(grads_ref[span, :], near_ref[...])
            sum_ref[span, :] = (grad / sums_ref[span, 0:1]).astype(BF16)
        wait_all(line_sums)
        bias = jnp.zeros((1, half), F32)
        for at in range(lines):
            span = slice(at * rows, (at + 1) * rows)
            grad = jnp.dot(matrix_ref[span, :], sum_ref[...], preferred_element_type=F32)
            grad = jnp.where(high_ref[span, :].astype(F32) > 0, grad, 0.0)
            bias = bias + jnp.sum(grad, axis=0, keepdims=True)
            hidden_ref[span, :] = grad.astype(BF16)
        for slot in range(lines):
            at = to = slot * rows
            for ref in (stay_ref, late_ref, go_ref):
                if 0 <= to < ref.shape[0]:
                    break
                to -= ref.shape[0]
            ref[to : to + rows, :] = hidden_ref[at : at + rows, :]
        wait_all(row_copies)
        for slot in range(PLANE):
            to = spot ^ away(core, slot, 2)
            ref, at = (keep_ref, send_ref)[slot // 2], slot % 2 * width
            ref[at : at + width, :] = across(
                rows_ref[:, aligned(to * width, width)], hidden_ref[...]
            ).astype(BF16)
        for ref in (keep_ref, send_ref):
            ref[2 * width :, :] = bias_rows(bias)

    outs = [array((total // 2, half), BF16)] + [array((total // 4, half), BF16)] * 2
    outs += [array((dim // 2 + TILE, half), BF16)] * 2
    return call(
        kernel, "row_grad", outs, place, [sums],
        [matrix, high, w_weight, w_other] + list(pieces) + list(line_parts),
        [
            pltpu.VMEM((nodes, dim), BF16),
            pltpu.VMEM((total, dim), BF16),
            pltpu.VMEM((nodes, half), BF16),
            pltpu.VMEM((total, half), BF16),
            pltpu.VMEM((half, dim), BF16),
            pltpu.VMEM((total, nodes), BF16),
            pltpu.VMEM((total, half), BF16),
            pltpu.SemaphoreType.DMA((PIECES,)),
            pltpu.SemaphoreType.DMA((2 * lines - 1,)),
            pltpu.SemaphoreType.DMA(()),
            pltpu.SemaphoreType.DMA((2,)),
        ],
        flops=2 * nodes * dim * half + 2 * total * nodes * half + 2 * total * dim * half,
        limit=VMEM_BYTES if lines <= PLANE else ALL_VMEM,
    )


def fold(place, keep, came):
    height, width = keep.shape[0] - TILE, keep.shape[1]
    part = height // 2

    def kernel(place_ref, keep_ref, came_ref, stay_ref, go_ref):
        bias = keep_ref[height:, :].astype(F32) + came_ref[height:, :].astype(F32)
        bias = bias_rows(bias[0:1] + bias[1:2])
        for ref, at in ((stay_ref, 0), (go_ref, part)):
            span = slice(at, at + part)
            ref[:part, :] = (keep_ref[span, :].astype(F32) + came_ref[span, :].astype(F32)).astype(BF16)
            ref[part:, :] = bias

    return call(
        kernel, "fold", [array((part + TILE, width), BF16)] * 2, place, [keep, came]
    )


def merge(place, keep, came):
    height, width = keep.shape[0] - TILE, keep.shape[1]

    def kernel(place_ref, keep_ref, came_ref, out_ref):
        out_ref[...] = (keep_ref[...].astype(F32) + came_ref[...].astype(F32)).astype(BF16)
        bias = keep_ref[height:, :].astype(F32) + came_ref[height:, :].astype(F32)
        out_ref[height:, :] = bias_rows(bias[0:1] + bias[1:2])

    (out,) = call(kernel, "merge", [array(keep.shape, BF16)], place, [keep, came])
    return out


def unpack(place, sides, lines=0):
    parts = 2 if lines else 1
    height, width = sides[0][0].shape
    blocks = [block for side in sides for block in side]
    count = len(blocks)

    def kernel(place_ref, *refs):
        sources, (out_ref, block_ref, wide_ref, sem, out_sem) = refs[:count], refs[count:]
        spot = place_ref[0] % PLANE
        copies = [
            pltpu.make_async_copy(source, block_ref.at[index], sem.at[index])
            for index, source in enumerate(sources)
        ]
        start_all(copies)
        outs = []
        for index, copy in enumerate(copies):
            side, slot, at = index // (PLANE * parts), index // parts % PLANE, index % parts
            core = place_ref[1] ^ side
            row = (spot ^ away(core, slot, 2)) * parts
            if lines:
                row = row + (line_side(place_ref, lines) ^ at)
            cols = aligned(core * width, width) if len(sides) > 1 else pl.ds(0, width)
            copy.wait()
            wide_ref[index] = block_ref[index].astype(F32)
            outs.append(
                pltpu.make_async_copy(
                    wide_ref.at[index], out_ref.at[aligned(row * height, height), cols],
                    out_sem.at[index],
                )
            )
            outs[-1].start()
        wait_all(outs)

    (out,) = call(
        kernel, "unpack", [array((PLANE * parts * height, width * len(sides)), F32)], place, [],
        blocks,
        [
            pltpu.VMEM((count, height, width), BF16), pltpu.VMEM((count, height, width), F32),
            pltpu.SemaphoreType.DMA((count,)), pltpu.SemaphoreType.DMA((count,)),
        ],
        far_outs=1,
    )
    return out


def on_device(
    features, neighbours, present, importance, q_weight, q_bias, w_weight, w_bias, cotangent
):
    rows, dim = features.shape
    count = lax.axis_size("nodes")
    lines = count // PLANE
    line_bits = bits_of(lines)
    node = lax.axis_index("nodes")
    core = lax.axis_index("stream")
    place = jnp.stack([node, core]).astype(I32)
    half_rows = rows // 2
    fence = lax.optimization_barrier

    def swap(value, bit, other_bit=None):
        bits = (bit, bit if other_bit is None else other_bit)
        pairs = [
            (2 * at + side, 2 * (at ^ bits[side]) + side) for at in range(count) for side in (0, 1)
        ]
        return lax.ppermute(value, ("nodes", "stream"), pairs)

    def plane_swap(value, step):
        return swap(value, 1 << step, 2 >> step)

    def line_swap(value, step):
        return swap(value, PLANE << step, PLANE << (line_bits - 1 - step))

    def trade(value):
        return lax.ppermute(value, "stream", [(0, 1), (1, 0)])

    def own_half(value, axis):
        size = value.shape[axis] // 2
        return lax.dynamic_slice_in_dim(value, core * size, size, axis)

    def joined(mine, other, axis):
        return jnp.where(
            core == 0,
            jnp.concatenate([mine, other], axis),
            jnp.concatenate([other, mine], axis),
        )

    mine = own_half(features, 0)
    stages = [line_swap(mine, line_bits - 1)]
    lists = sort_slots(place, neighbours, present, importance, count)
    lists = [jnp.concatenate([lists, trade(lists)], 0)]
    lists.append(plane_swap(lists[0], 1))
    lists[1], stages[0] = fence((lists[1], stages[0]))
    for step in reversed(range(line_bits - 1)):
        stages.append(line_swap(jnp.concatenate([mine] + stages, 0), step))
    lists.append(plane_swap(jnp.concatenate(lists, 0), 0))
    traded = [trade(stage) for stage in stages[:-1]]
    matrix, weight_sums = slot_matrix(place, lists, count)
    matrix, stages[-1] = fence((matrix, stages[-1]))
    line_parts = [features] + stages + traded + [trade(stages[-1])]
    send, high, low = first_sums(place, line_parts, q_weight, q_bias[None], matrix)
    send, w_sent = fence((send, w_weight))
    w_other = trade(w_sent)

    came = plane_swap(send, 0)
    keep, middle, own_send = more_sums(place, [high], [low], matrix, 0, 3)
    came_own = plane_swap(own_send, 0)
    last = plane_swap(middle + came, 1)
    came_own, w_other = fence((came_own, w_other))
    self_part = self_product(place, features, w_weight, w_other, w_bias[None])
    last, self_part, keep = fence((last, self_part, keep))
    mean_half = ((keep + came_own + last) / weight_sums[:rows, 0:1]).astype(BF16)

    mean_other = trade(mean_half)
    own_slice, next_slice, send_slices = plane_slices(place, features, mean_half, mean_other)
    far_slices = plane_swap(send_slices, 0)
    embeddings, grad_linear, grad_half = node_step(
        place, mean_half, mean_other, self_part, cotangent, w_weight, w_other
    )

    one, two = plane_swap(grad_half, 1), plane_swap(grad_half, 0)
    last_slices = plane_swap(jnp.concatenate([next_slice, far_slices[rows:]], 0), 1)
    one, two = fence((one, two))
    three = plane_swap(one, 0)
    three, last_slices = fence((three, last_slices))
    pieces = [grad_linear, one, two, three, trade(one), trade(two), trade(three)]
    slices = [own_slice, far_slices, next_slice, last_slices]
    w_keep, w_send = self_weight(place, pieces, slices, lines)
    pieces, w_keep, w_send = fence((pieces, w_keep, w_send))

    stay, late, go, q_keep, q_send = row_grad(
        place, weight_sums, pieces, w_weight, w_other, matrix, high, line_parts, lines
    )
    w_came = line_swap(w_send, 0)
    stay, late, go, q_keep, q_send, w_keep, w_came = fence(
        (stay, late, go, q_keep, q_send, w_keep, w_came)
    )

    def last_sum(keep, came):
        height = keep.shape[0] - TILE
        total = keep.astype(F32) + came.astype(F32)
        return total[:height].astype(BF16), total[height] + total[height + 1]

    biases = {}

    rows_go, rows_late = line_swap(go, 0), line_swap(late, 0)
    q_came = plane_swap(q_send, 0)
    w_sum = merge(place, w_keep, w_came)
    w_came = line_swap(w_sum, 1)
    q_came = fence(q_came)
    q_keep, q_send = fold(place, q_keep, q_came)
    q_came, w_came, stay, rows_go, rows_late = fence(
        (plane_swap(q_send, 1), w_came, stay, rows_go, rows_late)
    )
    for step in range(2, line_bits):
        w_sum = merge(place, w_sum, w_came)
        w_came = line_swap(w_sum, step)
    q_sum = merge(place, q_keep, q_came)
    q_came = line_swap(q_sum, 0)
    w_near, biases["w"] = last_sum(w_sum, w_came)
    w_far = line_swap(w_near, 0)
    near_one, near_two = plane_swap(w_near, 1), plane_swap(w_near, 0)
    q_came, w_far, near_one, near_two, biases = fence((q_came, w_far, near_one, near_two, biases))
    for step in range(1, line_bits):
        q_sum = merge(place, q_sum, q_came)
        q_came = line_swap(q_sum, step)
    near_three = plane_swap(near_one, 0)
    far_one, far_two = plane_swap(w_far, 1), plane_swap(w_far, 0)
    q_came, near_three, far_one, far_two = fence((q_came, near_three, far_one, far_two))
    q_own, biases["q"] = last_sum(q_sum, q_came)
    half = stay.shape[0] // 2
    upper = (stay[half:].astype(F32) + rows_go.astype(F32)).astype(BF16)
    q_own, upper = fence((q_own, upper))
    rows_next = line_swap(upper, 1)
    q_one, q_two = plane_swap(q_own, 1), plane_swap(q_own, 0)
    far_three = plane_swap(far_one, 0)
    q_one, q_two, far_three, rows_next, biases = fence((q_one, q_two, far_three, rows_next, biases))
    q_three = plane_swap(q_one, 0)
    w_all = [w_near, w_far, near_one, far_one, near_two, far_two, near_three, far_three]
    w_grad = unpack(place, [w_all], lines)
    w_bias_grad, q_bias_half = biases["w"], biases["q"]
    q_bias_grad = joined(q_bias_half, trade(q_bias_half), 0)

    stay = stay[: stay.shape[0] // 2]
    for step in range(2, line_bits):
        half = rows_late.shape[0] // 2
        upper = stay[half:].astype(F32) + rows_late[half:] + rows_next[half:]
        rows_next = (rows_next[:half] + line_swap(upper.astype(BF16), step).astype(F32)).astype(BF16)
        stay, rows_late = stay[:half], rows_late[:half]
    row_half = row_sums(place, stay, rows_late, rows_next)
    row_other = trade(row_half)
    q_mine = [q_own, q_one, q_two]
    q_other = [trade(block) for block in q_mine]
    q_three, q_other, w_grad, q_bias_grad, row_other = fence(
        (q_three, q_other, w_grad, q_bias_grad, row_other)
    )
    feature_grad = feature_step(
        place, grad_linear, row_half, row_other, w_weight, w_other, q_weight
    )
    q_grad = unpack(place, [q_mine + [q_three], q_other + [trade(q_three)]])
    return (embeddings, feature_grad, q_grad, q_bias_grad, w_grad, w_bias_grad)


def solution(mesh):
    in_specs = (
        P("nodes", None),
        P("nodes", "stream"),
        P("nodes", "stream"),
        P("nodes", "stream"),
        P(),
        P(),
        P("stream", None),
        P(),
        P("nodes", None),
    )
    out_specs = (P("nodes", None), P("nodes", "stream"), P(), P(), P("stream", None), P())
    return jax.shard_map(
        on_device, mesh=mesh, in_specs=in_specs, out_specs=out_specs, check_vma=False
    )
```

time: 206 us -> 198 us (0.961)
  waiting for transfers between devices: 81.7 us -> 87.3 us
  other arithmetic: 10.4 us -> 6.44 us
  starting transfers between devices: 45.1 us -> 42.2 us
  matrix products: 2.81 us -> 0 us
  local copies, waits for them, and re-layouts: 7.1 us -> 4.65 us
    ppermute x11 -> x14, starting transfers between devices: 22 us -> 15.4 us  [trade(): return lax.ppermute(value, 'stream', [(0, 1), (1, 0)])]
    ppermute x26 -> x31, waiting for transfers between devices: 75.6 us -> 80.9 us  [swap(): return lax.ppermute(value, ('nodes', 'stream'), pairs)]
    select_n x2 -> x0, other arithmetic: 4.47 us -> none  [the longest x1 2.66 us: on_device(): w_near = jnp.where(core == 0, w_other, w_weight)]
    ppermute x26 -> x31, starting transfers between devices: 23.1 us -> 26.8 us  [swap(): return lax.ppermute(value, ('nodes', 'stream'), pairs)]
    dot_general x3 -> x0, matrix products: 2.81 us -> none  [the longest x2 1.96 us: times_t(): lax.dot_general(lhs, rhs, (((1,), (1,)), ((), ())), preferred_element_typ...]
    ppermute x11 -> x14, waiting for transfers between devices: 6.11 us -> 6.39 us  [trade(): return lax.ppermute(value, 'stream', [(0, 1), (1, 0)])]
    pallas_call x16 -> x17, Pallas kernels: 56.1 us -> 56 us  [call(): pl.pallas_call(kernel, name=name, out_shape=list(outs), in_specs=spaced(p...]
  transfers between devices with their start and end apart: 37 -> 45, of which waited for: 23 -> 27; matrix products, arithmetic and copies ran while one was open for 8% -> 3% of each run, Pallas kernels for 23% -> 19%
where the time goes in v3:
time: 198 us
  waiting for transfers between devices  87.3 us (44%)
  Pallas kernels  56 us (28%)
  starting transfers between devices  42.2 us (21%)
  other arithmetic  6.44 us (3%)
  local copies, waits for them, and re-layouts  4.65 us (2%)
    ppermute x31, waiting for transfers between devices, swap(): return lax.ppermute(value, ('nodes', 'stream'), pairs)  80.9 us
    pallas_call x17, Pallas kernels, call(): pl.pallas_call(kernel, name=name, out_shape=list(outs), in_specs=spaced(p...  56 us
    ppermute x31, starting transfers between devices, swap(): return lax.ppermute(value, ('nodes', 'stream'), pairs)  26.8 us
    ppermute x14, starting transfers between devices, trade(): return lax.ppermute(value, 'stream', [(0, 1), (1, 0)])  15.4 us
    ppermute x14, waiting for transfers between devices, trade(): return lax.ppermute(value, 'stream', [(0, 1), (1, 0)])  6.39 us
  transfers between devices with their start and end apart: 45, of which 27 were waited for; matrix products, arithmetic and copies ran while one was open for 3% of the time, Pallas kernels for 19%

profile of v3, /device:TPU:1, one launch (start us, length us, event | category | flops | bytes accessed | tf_op | source)
XLA Modules:
  0.0 197.7 jit_solution(7939523653704342752)
XLA Ops:
  0.6 1.7 constant_dynamic-slice_fusion
  2.4 2.1 %collective-permute-start.2 = (bf16[160,1024]{1,0:T(8,128)(2,1)}, bf16[160,1024]{1,0:T(8,128)(2,1)}, u32[]{:S(2)}, u32[]{:S(2)}) collective-permute-start(bf16[160,1024]{1,0:T(8,128)(2,1)} %constant_dynamic-slice_fusion), channel_id=1, source_target_pairs={{0,16},{1,9},{2,18},{3,11},{4,20},{5,13},{6,22},{7,15},{8,24},{9,1... | collective-permute-start | bytes 983048 | tf_op jit(solution)/shard_map/ppermute | solution.py:683
  5.1 2.2 %sort_slots.1 = s32[32,320]{1,0:T(8,128)} custom-call(s32[2]{0:T(128)} %pad_add_fusion.2.place_ref, s32[25,320]{1,0:T(8,128)} %bitcast.10, s32[25,320]{1,0:T(8,128)} %bitcast.11, s32[25,320]{1,0:T(8,128)} %bitcast.12), custom_call_target="tpu_custom_call" | custom-call | bytes 136960 | tf_op jit(solution)/shard_map/sort_slots/pallas_call | solution.py:43
  7.3 2.0 %collective-permute-start = (s32[32,320]{1,0:T(8,128)}, s32[32,320]{1,0:T(8,128)S(1)}, u32[]{:S(2)}, u32[]{:S(2)}) collective-permute-start(s32[32,320]{1,0:T(8,128)} %sort_slots.1), channel_id=1, source_target_pairs={{0,1},{1,0},{2,3},{3,2},{4,5},{5,4},{6,7},{7,6},{8,9},{9,8},{10,11... | collective-permute-start | bytes 122888 | tf_op jit(solution)/shard_map/ppermute | solution.py:692
  13.1 2.6 %collective-permute-done.1.next_ref = s32[64,320]{1,0:T(8,128)S(1)} collective-permute-done((s32[64,320]{1,0:T(8,128)S(1)}, s32[64,320]{1,0:T(8,128)S(1)}, u32[]{:S(2)}, u32[]{:S(2)}) %collective-permute-start.1) | collective-permute-done | bytes 81952 | tf_op jit(solution)/shard_map/ppermute | solution.py:683
  15.7 2.0 %pad_maximum_fusion = bf16[320,1024]{1,0:T(8,128)(2,1)} fusion(bf16[160,1024]{1,0:T(8,128)(2,1)} %collective-permute-done.2.refs_1_.refs_8_, bf16[160,1024]{1,0:T(8,128)(2,1)} %constant_dynamic-slice_fusion), kind=kLoop, calls=%fused_computation | loop fusion | flops 1310720 | bytes 1310720 | tf_op jit(solution)/shard_map/concatenate | solution.py:712
  18.4 1.3 collective-permute-start.3
  19.7 3.7 %collective-permute-done.3.rest_ref = s32[128,320]{1,0:T(8,128)} collective-permute-done((s32[128,320]{1,0:T(8,128)S(1)}, s32[128,320]{1,0:T(8,128)}, u32[]{:S(2)}, u32[]{:S(2)}) %collective-permute-start.3) | collective-permute-done | bytes 163872 | tf_op jit(solution)/shard_map/ppermute | solution.py:683
  23.4 6.9 %slot_matrix.1 = (f32[1280,8]{1,0:T(8,128)}, bf16[1280,1280]{1,0:T(8,128)(2,1)}) custom-call(s32[2]{0:T(128)} %pad_add_fusion.2.place_ref, s32[64,320]{1,0:T(8,128)} %copy-done.12, s32[64,320]{1,0:T(8,128)} %copy-done.13, s32[128,320]{1,0:T(8,128)} %collective-permute-done.3.rest_ref), custom_call_target="tpu_custom_call" | custom-call | flops 1 | bytes 1 | tf_op jit(solution)/shard_map/slot_matrix/pallas_call | solution.py:43
  30.3 4.1 %collective-permute-done.4.refs_2_.refs_9_ = bf16[320,1024]{1,0:T(8,128)(2,1)} collective-permute-done((bf16[320,1024]{1,0:T(8,128)(2,1)}, bf16[320,1024]{1,0:T(8,128)(2,1)}, u32[]{:S(2)}, u32[]{:S(2)}) %collective-permute-start.4) | collective-permute-done | bytes 655392 | tf_op jit(solution)/shard_map/ppermute | solution.py:683
  34.4 1.6 collective-permute-start.6
  36.0 2.5 %collective-permute-done.5.refs_3_.refs_10_ = bf16[160,1024]{1,0:T(8,128)(2,1)} collective-permute-done((bf16[160,1024]{1,0:T(8,128)(2,1)}, bf16[160,1024]{1,0:T(8,128)(2,1)}, u32[]{:S(2)}, u32[]{:S(2)}) %collective-permute-start.5) | collective-permute-done | bytes 327712 | tf_op jit(solution)/shard_map/ppermute | solution.py:692
  38.6 7.1 %first_sums.1 = (f32[320,512]{1,0:T(8,128)}, bf16[1280,512]{1,0:T(8,128)(2,1)}, bf16[1280,512]{1,0:T(8,128)(2,1)}) custom-call(s32[2]{0:T(128)} %pad_add_fusion.2.place_ref, f32[1,1024]{1,0:T(1,128)} %bitcast.16, bf16[1024,1024]{1,0:T(8,128)(2,1)} %q_in.3, bf16[1280,1280]{1,0:T(8,128)(2,1)} %get-tuple-element.92.matrix_in, bf16[320,1024]{1,0:T(8,128)(2,1)} %refs_7_.1, ...), custom_call_target="tpu_custom_call" | custom-call | flops 2181038080 | bytes 11276288 | tf_op jit(solution)/shard_map/first_sums/pallas_call | solution.py:43
  47.4 7.2 %more_sums.1 = (f32[320,512]{1,0:T(8,128)}, f32[320,512]{1,0:T(8,128)}, f32[320,512]{1,0:T(8,128)}) custom-call(s32[2]{0:T(128)} %pad_add_fusion.2.place_ref, bf16[1280,1280]{1,0:T(8,128)(2,1)} %get-tuple-element.92.matrix_in, bf16[1280,512]{1,0:T(8,128)(2,1)} %get-tuple-element.94.refs_0_.high_in, bf16[1280,512]{1,0:T(8,128)(2,1)} %get-tuple-element.95.refs_1_), custom_call_target="tpu_custom_call" | custom-call | flops 2516582400 | bytes 7864320 | tf_op jit(solution)/shard_map/more_sums/pallas_call | solution.py:43
  56.2 1.4 add.34
  59.9 7.5 %collective-permute-done.9 = f32[320,512]{1,0:T(8,128)S(1)} collective-permute-done((f32[320,512]{1,0:T(8,128)}, f32[320,512]{1,0:T(8,128)S(1)}, u32[]{:S(2)}, u32[]{:S(2)}) %collective-permute-start.9) | collective-permute-done | bytes 655392 | tf_op jit(solution)/shard_map/ppermute | solution.py:683
  68.6 3.0 %self_product.1.self_ref = f32[320,1024]{1,0:T(8,128)S(1)} custom-call(s32[2]{0:T(128)S(1)} %copy-done.7, bf16[320,1024]{1,0:T(8,128)(2,1)S(1)} %copy-done.2, f32[1,1024]{1,0:T(1,128)S(1)} %bitcast.9, bf16[1024,1024]{1,0:T(8,128)(2,1)S(1)} %copy-done, bf16[1024,1024]{1,0:T(8,128)(2,1)} %collective-permute-done.10.w_other_in), custom_call_target="tpu_custom_call" | custom-call | flops 671088640 | bytes 6164480 | tf_op jit(solution)/shard_map/self_product/pallas_call | solution.py:43
  72.4 1.5 collective-permute-start.11
  75.2 3.5 %node_step.1 = (f32[320,1024]{1,0:T(8,128)}, bf16[320,1024]{1,0:T(8,128)(2,1)S(1)}, bf16[160,1024]{1,0:T(8,128)(2,1)S(1)}) custom-call(s32[2]{0:T(128)S(1)} %copy-done.7, bf16[320,512]{1,0:T(8,128)(2,1)S(1)} %divide_convert_fusion.mine_ref, bf16[320,512]{1,0:T(8,128)(2,1)S(1)} %collective-permute-done.11.other_ref, f32[320,1024]{1,0:T(8,128)S(1)} %self_product.1.self_ref, ...), custom_call_target="tpu_custom_call" | custom-call | flops 671088640 | bytes 9109504 | tf_op jit(solution)/shard_map/node_step/pallas_call | solution.py:43
  78.8 1.3 collective-permute-start.13
  81.2 5.0 %collective-permute-done.13.refs_2_ = bf16[160,1024]{1,0:T(8,128)(2,1)S(1)} collective-permute-done((bf16[160,1024]{1,0:T(8,128)(2,1)S(1)}, bf16[160,1024]{1,0:T(8,128)(2,1)S(1)}, u32[]{:S(2)}, u32[]{:S(2)}) %collective-permute-start.13) | collective-permute-done | bytes 327712 | tf_op jit(solution)/shard_map/ppermute | solution.py:683
  86.2 2.6 %collective-permute-done.12.refs_1_ = bf16[160,1024]{1,0:T(8,128)(2,1)S(1)} collective-permute-done((bf16[160,1024]{1,0:T(8,128)(2,1)S(1)}, bf16[160,1024]{1,0:T(8,128)(2,1)S(1)}, u32[]{:S(2)}, u32[]{:S(2)}) %collective-permute-start.12) | collective-permute-done | bytes 327712 | tf_op jit(solution)/shard_map/ppermute | solution.py:683
  88.8 3.3 %collective-permute-done.15.refs_8_ = bf16[640,256]{1,0:T(8,128)(2,1)S(1)} collective-permute-done((bf16[640,256]{1,0:T(8,128)(2,1)S(1)}, bf16[640,256]{1,0:T(8,128)(2,1)S(1)}, u32[]{:S(2)}, u32[]{:S(2)}) %collective-permute-start.15) | collective-permute-done | bytes 327712 | tf_op jit(solution)/shard_map/ppermute | solution.py:683
  92.2 2.3 %collective-permute-start.17 = (bf16[160,1024]{1,0:T(8,128)(2,1)S(1)}, bf16[160,1024]{1,0:T(8,128)(2,1)S(1)}, u32[]{:S(2)}, u32[]{:S(2)}) collective-permute-start(bf16[160,1024]{1,0:T(8,128)(2,1)S(1)} %collective-permute-done.12.refs_1_), channel_id=1, source_target_pairs={{0,1},{1,0},{2,3},{3,2},{4,5},{5,4},{6,7},{7,6},{8,9},{9,8},{10,11... | collective-permute-start | bytes 983048 | tf_op jit(solution)/shard_map/ppermute | solution.py:692
  95.6 5.6 %collective-permute-done.16.refs_10_ = bf16[640,256]{1,0:T(8,128)(2,1)S(1)} collective-permute-done((bf16[640,256]{1,0:T(8,128)(2,1)S(1)}, bf16[640,256]{1,0:T(8,128)(2,1)S(1)}, u32[]{:S(2)}, u32[]{:S(2)}) %collective-permute-start.16) | collective-permute-done | bytes 327712 | tf_op jit(solution)/shard_map/ppermute | solution.py:683
  102.9 3.3 %self_weight.1 = (bf16[144,1024]{1,0:T(8,128)(2,1)S(1)}, bf16[144,1024]{1,0:T(8,128)(2,1)S(1)}) custom-call(s32[2]{0:T(128)S(1)} %copy-done.7, bf16[320,1024]{1,0:T(8,128)(2,1)S(1)} %get-tuple-element.120.refs_0_.grad_ref, bf16[160,1024]{1,0:T(8,128)(2,1)S(1)} %collective-permute-done.12.refs_1_, bf16[160,1024]{1,0:T(8,128)(2,1)S(1)} %collective-permute-done.13.refs_2_, ...), custom_call_target="tpu_custom_call" | custom-call | flops 671088640 | bytes 4194304 | tf_op jit(solution)/shard_map/self_weight/pallas_call | solution.py:43
  106.2 1.4 collective-permute-start.20
  107.5 8.4 %row_grad.1 = (bf16[640,512]{1,0:T(8,128)(2,1)S(1)}, bf16[320,512]{1,0:T(8,128)(2,1)S(1)}, bf16[320,512]{1,0:T(8,128)(2,1)S(1)}, bf16[528,512]{1,0:T(8,128)(2,1)S(1)}, bf16[528,512]{1,0:T(8,128)(2,1)S(1)}) custom-call(s32[2]{0:T(128)S(1)} %copy-done.7, f32[1280,8]{1,0:T(8,128)S(1)} %copy-done.8, bf16[1280,1280]{1,0:T(8,128)(2,1)} %get-tuple-element.92.matrix_in, ...), custom_call_target="tpu_custom_call" | custom-call | flops 4362076160 | bytes 16457728 | tf_op jit(solution)/shard_map/row_grad/pallas_call | solution.py:43
  115.9 1.3 collective-permute-start.21
  118.3 1.3 collective-permute-start.25
  120.2 1.4 collective-permute-start.23
  121.6 2.9 %collective-permute-done.21.came_ref = bf16[528,512]{1,0:T(8,128)(2,1)S(1)} collective-permute-done((bf16[528,512]{1,0:T(8,128)(2,1)S(1)}, bf16[528,512]{1,0:T(8,128)(2,1)S(1)}, u32[]{:S(2)}, u32[]{:S(2)}) %collective-permute-start.21) | collective-permute-done | bytes 540704 | tf_op jit(solution)/shard_map/ppermute | solution.py:683
  125.9 13.1 %collective-permute-done.23 = bf16[144,1024]{1,0:T(8,128)(2,1)S(1)} collective-permute-done((bf16[144,1024]{1,0:T(8,128)(2,1)S(1)}, bf16[144,1024]{1,0:T(8,128)(2,1)S(1)}, u32[]{:S(2)}, u32[]{:S(2)}) %collective-permute-start.23) | collective-permute-done | bytes 294944 | tf_op jit(solution)/shard_map/ppermute | solution.py:683
  140.6 2.3 %collective-permute-start.26 = (bf16[272,512]{1,0:T(8,128)(2,1)S(1)}, bf16[272,512]{1,0:T(8,128)(2,1)S(1)}, u32[]{:S(2)}, u32[]{:S(2)}) collective-permute-start(bf16[272,512]{1,0:T(8,128)(2,1)S(1)} %merge.4.keep_ref), channel_id=1, source_target_pairs={{0,8},{1,17},{2,10},{3,19},{4,12},{5,21},{6,14},{7,23},{8,0},{9,25... | collective-permute-start | bytes 835592 | tf_op jit(solution)/shard_map/ppermute | solution.py:683
  144.5 4.5 %collective-permute-done.29.refs_4_ = bf16[128,1024]{1,0:T(8,128)(2,1)S(1)} collective-permute-done((bf16[128,1024]{1,0:T(8,128)(2,1)S(1)}, bf16[128,1024]{1,0:T(8,128)(2,1)S(1)}, u32[]{:S(2)}, u32[]{:S(2)}) %collective-permute-start.29) | collective-permute-done | bytes 262176 | tf_op jit(solution)/shard_map/ppermute | solution.py:683
  150.3 5.4 %collective-permute-done.27.refs_1_ = bf16[128,1024]{1,0:T(8,128)(2,1)S(1)} collective-permute-done((bf16[128,1024]{1,0:T(8,128)(2,1)S(1)}, bf16[128,1024]{1,0:T(8,128)(2,1)S(1)}, u32[]{:S(2)}, u32[]{:S(2)}) %collective-permute-start.27) | collective-permute-done | bytes 262176 | tf_op jit(solution)/shard_map/ppermute | solution.py:683
  156.5 1.5 collective-permute-start.33
  158.7 3.3 %collective-permute-done.31.refs_6_ = bf16[128,1024]{1,0:T(8,128)(2,1)S(1)} collective-permute-done((bf16[128,1024]{1,0:T(8,128)(2,1)S(1)}, bf16[128,1024]{1,0:T(8,128)(2,1)S(1)}, u32[]{:S(2)}, u32[]{:S(2)}) %collective-permute-start.31) | collective-permute-done | bytes 262176 | tf_op jit(solution)/shard_map/ppermute | solution.py:683
  162.1 3.9 %collective-permute-done.33.refs_5_ = bf16[128,1024]{1,0:T(8,128)(2,1)S(1)} collective-permute-done((bf16[128,1024]{1,0:T(8,128)(2,1)S(1)}, bf16[128,1024]{1,0:T(8,128)(2,1)S(1)}, u32[]{:S(2)}, u32[]{:S(2)}) %collective-permute-start.33) | collective-permute-done | bytes 262176 | tf_op jit(solution)/shard_map/ppermute | solution.py:683
  166.1 2.1 %collective-permute-start.37 = (bf16[320,512]{1,0:T(8,128)(2,1)S(1)}, bf16[320,512]{1,0:T(8,128)(2,1)S(1)}, u32[]{:S(2)}, u32[]{:S(2)}) collective-permute-start(bf16[320,512]{1,0:T(8,128)(2,1)S(1)} %add_convert_fusion), channel_id=1, source_target_pairs={{0,16},{1,9},{2,18},{3,11},{4,20},{5,13},{6,22},{7,15},{8,24},{9,1... | collective-permute-start | bytes 983048 | tf_op jit(solution)/shard_map/ppermute | solution.py:683
  168.2 1.5 collective-permute-start.35
  169.8 3.6 %collective-permute-done.36.refs_7_ = bf16[128,1024]{1,0:T(8,128)(2,1)S(1)} collective-permute-done((bf16[128,1024]{1,0:T(8,128)(2,1)S(1)}, bf16[128,1024]{1,0:T(8,128)(2,1)S(1)}, u32[]{:S(2)}, u32[]{:S(2)}) %collective-permute-start.36) | collective-permute-done | bytes 262176 | tf_op jit(solution)/shard_map/ppermute | solution.py:683
  173.4 3.1 %collective-permute-done.35.refs_2_ = bf16[256,512]{1,0:T(8,128)(2,1)S(1)} collective-permute-done((bf16[256,512]{1,0:T(8,128)(2,1)S(1)}, bf16[256,512]{1,0:T(8,128)(2,1)S(1)}, u32[]{:S(2)}, u32[]{:S(2)}) %collective-permute-start.35) | collective-permute-done | bytes 262176 | tf_op jit(solution)/shard_map/ppermute | solution.py:683
  177.2 4.8 %collective-permute-start.43 = (bf16[320,512]{1,0:T(8,128)(2,1)S(1)}, bf16[320,512]{1,0:T(8,128)(2,1)S(1)}, u32[]{:S(2)}, u32[]{:S(2)}) collective-permute-start(bf16[320,512]{1,0:T(8,128)(2,1)S(1)} %row_sums.1.mine_ref), channel_id=1, source_target_pairs={{0,1},{1,0},{2,3},{3,2},{4,5},{5,4},{6,7},{7,6},{8,9},{9,8},{10,11... | collective-permute-start | bytes 983048 | tf_op jit(solution)/shard_map/ppermute | solution.py:692
  183.8 2.9 %unpack.2 = f32[1024,1024]{1,0:T(8,128)} custom-call(s32[2]{0:T(128)S(1)} %copy-done.7, bf16[128,1024]{1,0:T(8,128)(2,1)S(1)} %slice.58.refs_0_, bf16[128,1024]{1,0:T(8,128)(2,1)S(1)} %collective-permute-done.27.refs_1_, bf16[128,1024]{1,0:T(8,128)(2,1)S(1)} %collective-permute-done.28.refs_2_, bf16[128,1024]{1,0:T(8,128)(2,1)S(1)} %collective-permute-done.32.refs_3_, ...), custom_call_target="tpu_custom_call" | custom-call | bytes 6291456 | tf_op jit(solution)/shard_map/unpack/pallas_call | solution.py:43
  187.3 1.5 collective-permute-done.38.refs_3_
  190.1 3.9 %feature_step.1 = f32[320,512]{1,0:T(8,128)} custom-call(s32[2]{0:T(128)S(1)} %copy-done.7, bf16[320,1024]{1,0:T(8,128)(2,1)S(1)} %copy-done.5, bf16[320,512]{1,0:T(8,128)(2,1)S(1)} %row_sums.1.mine_ref, bf16[320,512]{1,0:T(8,128)(2,1)S(1)} %collective-permute-done.43.other_ref, bf16[1024,1024]{1,0:T(8,128)(2,1)S(1)} %copy-done.1, ...), custom_call_target="tpu_custom_call" | custom-call | flops 671088640 | bytes 8257536 | tf_op jit(solution)/shard_map/feature_step/pallas_call | solution.py:43
  194.1 3.5 %unpack.3 = f32[1024,1024]{1,0:T(8,128)} custom-call(s32[2]{0:T(128)S(1)} %copy-done.7, bf16[256,512]{1,0:T(8,128)(2,1)S(1)} %slice.57.refs_0_, bf16[256,512]{1,0:T(8,128)(2,1)S(1)} %collective-permute-done.34.refs_1_, bf16[256,512]{1,0:T(8,128)(2,1)S(1)} %collective-permute-done.35.refs_2_, bf16[256,512]{1,0:T(8,128)(2,1)} %collective-permute-done.38.refs_3_, ...), custom_call_target="tpu_custom_call" | custom-call | bytes 6291456 | tf_op jit(solution)/shard_map/unpack/pallas_call | solution.py:43
  (106 shorter events, 31.6 us)
Async XLA Ops:
  2.4 13.3 %collective-permute-start.2 = (bf16[160,1024]{1,0:T(8,128)(2,1)}, bf16[160,1024]{1,0:T(8,128)(2,1)}, u32[]{:S(2)}, u32[]{:S(2)}) collective-permute-start(bf16[160,1024]{1,0:T(8,128)(2,1)} %constant_dynamic-slice_fusion), channel_id=1, source_target_pairs={{0,16},{1,9},{2,18},{3,11},{4,20},{5,13},{6,22},{7,15},{8,24},{9,1... | collective-permute-start | bytes 983048 | tf_op jit(solution)/shard_map/ppermute | solution.py:683
  7.3 3.1 %collective-permute-start = (s32[32,320]{1,0:T(8,128)}, s32[32,320]{1,0:T(8,128)S(1)}, u32[]{:S(2)}, u32[]{:S(2)}) collective-permute-start(s32[32,320]{1,0:T(8,128)} %sort_slots.1), channel_id=1, source_target_pairs={{0,1},{1,0},{2,3},{3,2},{4,5},{5,4},{6,7},{7,6},{8,9},{9,8},{10,11... | collective-permute-start | bytes 122888 | tf_op jit(solution)/shard_map/ppermute | solution.py:692
  11.9 3.8 %collective-permute-start.1 = (s32[64,320]{1,0:T(8,128)S(1)}, s32[64,320]{1,0:T(8,128)S(1)}, u32[]{:S(2)}, u32[]{:S(2)}) collective-permute-start(s32[64,320]{1,0:T(8,128)S(1)} %pad_add_fusion.1.own_ref), channel_id=1, source_target_pairs={{0,4},{1,3},{2,6},{3,1},{4,0},{5,7},{6,2},{7,5},{8,12},{9,11},{10,... | collective-permute-start | bytes 245768 | tf_op jit(solution)/shard_map/ppermute | solution.py:683
  17.6 16.7 %collective-permute-start.4 = (bf16[320,1024]{1,0:T(8,128)(2,1)}, bf16[320,1024]{1,0:T(8,128)(2,1)}, u32[]{:S(2)}, u32[]{:S(2)}) collective-permute-start(bf16[320,1024]{1,0:T(8,128)(2,1)} %pad_maximum_fusion), channel_id=1, source_target_pairs={{0,8},{1,17},{2,10},{3,19},{4,12},{5,21},{6,14},{7,23},{8,0},{9,25... | collective-permute-start | bytes 1966088 | tf_op jit(solution)/shard_map/ppermute | solution.py:683
  18.4 5.0 %collective-permute-start.3 = (s32[128,320]{1,0:T(8,128)S(1)}, s32[128,320]{1,0:T(8,128)}, u32[]{:S(2)}, u32[]{:S(2)}) collective-permute-start(s32[128,320]{1,0:T(8,128)S(1)} %pad_add_fusion), channel_id=1, source_target_pairs={{0,2},{1,5},{2,0},{3,7},{4,6},{5,1},{6,4},{7,3},{8,10},{9,13},{10,... | collective-permute-start | bytes 491528 | tf_op jit(solution)/shard_map/ppermute | solution.py:683
  34.4 4.2 %collective-permute-start.6 = (bf16[320,1024]{1,0:T(8,128)(2,1)}, bf16[320,1024]{1,0:T(8,128)(2,1)}, u32[]{:S(2)}, u32[]{:S(2)}) collective-permute-start(bf16[320,1024]{1,0:T(8,128)(2,1)} %collective-permute-done.4.refs_2_.refs_9_), channel_id=1, source_target_pairs={{0,1},{1,0},{2,3},{3,2},{4,5},{5,4},{6,7},{7,6},{8,9},{9,8},{10,11... | collective-permute-start | bytes 1966088 | tf_op jit(solution)/shard_map/ppermute | solution.py:692
  36.0 2.5 %collective-permute-start.5 = (bf16[160,1024]{1,0:T(8,128)(2,1)}, bf16[160,1024]{1,0:T(8,128)(2,1)}, u32[]{:S(2)}, u32[]{:S(2)}) collective-permute-start(bf16[160,1024]{1,0:T(8,128)(2,1)} %collective-permute-done.2.refs_1_.refs_8_), channel_id=1, source_target_pairs={{0,1},{1,0},{2,3},{3,2},{4,5},{5,4},{6,7},{7,6},{8,9},{9,8},{10,11... | collective-permute-start | bytes 983048 | tf_op jit(solution)/shard_map/ppermute | solution.py:692
  45.7 21.8 %collective-permute-start.10 = (bf16[1024,1024]{1,0:T(8,128)(2,1)}, bf16[1024,1024]{1,0:T(8,128)(2,1)}, u32[]{:S(2)}, u32[]{:S(2)}) collective-permute-start(bf16[1024,1024]{1,0:T(8,128)(2,1)} %w_in.7), channel_id=1, source_target_pairs={{0,1},{1,0},{2,3},{3,2},{4,5},{5,4},{6,7},{7,6},{8,9},{9,8},{10,11... | collective-permute-start | bytes 6291464 | tf_op jit(solution)/shard_map/ppermute | solution.py:692
  46.1 10.0 %collective-permute-start.7 = (f32[320,512]{1,0:T(8,128)}, f32[320,512]{1,0:T(8,128)}, u32[]{:S(2)}, u32[]{:S(2)}) collective-permute-start(f32[320,512]{1,0:T(8,128)} %get-tuple-element.98), channel_id=1, source_target_pairs={{0,2},{1,5},{2,0},{3,7},{4,6},{5,1},{6,4},{7,3},{8,10},{9,13},{10,... | collective-permute-start | bytes 1966088 | tf_op jit(solution)/shard_map/ppermute | solution.py:683
  54.6 12.8 %copy-start = (bf16[1024,1024]{1,0:T(8,128)(2,1)S(1)}, bf16[1024,1024]{1,0:T(8,128)(2,1)}, u32[]{:S(2)}) copy-start(bf16[1024,1024]{1,0:T(8,128)(2,1)} %w_in.7) | copy-start | bytes 6291460
  54.6 12.8 %copy-start.7 = (s32[2]{0:T(128)S(1)}, s32[2]{0:T(128)}, u32[]{:S(2)}) copy-start(s32[2]{0:T(128)} %pad_add_fusion.2.place_ref) | copy-start | bytes 28
  54.6 12.8 %collective-permute-start.9 = (f32[320,512]{1,0:T(8,128)}, f32[320,512]{1,0:T(8,128)S(1)}, u32[]{:S(2)}, u32[]{:S(2)}) collective-permute-start(f32[320,512]{1,0:T(8,128)} %get-tuple-element.99), channel_id=1, source_target_pairs={{0,2},{1,5},{2,0},{3,7},{4,6},{5,1},{6,4},{7,3},{8,10},{9,13},{10,... | collective-permute-start | bytes 1966088 | tf_op jit(solution)/shard_map/ppermute | solution.py:683
  57.6 14.7 %collective-permute-start.8 = (f32[320,512]{1,0:T(8,128)S(1)}, f32[320,512]{1,0:T(8,128)S(1)}, u32[]{:S(2)}, u32[]{:S(2)}) collective-permute-start(f32[320,512]{1,0:T(8,128)S(1)} %add.34), channel_id=1, source_target_pairs={{0,4},{1,3},{2,6},{3,1},{4,0},{5,7},{6,2},{7,5},{8,12},{9,11},{10,... | collective-permute-start | bytes 1966088 | tf_op jit(solution)/shard_map/ppermute | solution.py:683
  72.4 2.8 %collective-permute-start.11 = (bf16[320,512]{1,0:T(8,128)(2,1)S(1)}, bf16[320,512]{1,0:T(8,128)(2,1)S(1)}, u32[]{:S(2)}, u32[]{:S(2)}) collective-permute-start(bf16[320,512]{1,0:T(8,128)(2,1)S(1)} %divide_convert_fusion.mine_ref), channel_id=1, source_target_pairs={{0,1},{1,0},{2,3},{3,2},{4,5},{5,4},{6,7},{7,6},{8,9},{9,8},{10,11... | collective-permute-start | bytes 983048 | tf_op jit(solution)/shard_map/ppermute | solution.py:692
  78.8 27.4 %copy-start.4 = (bf16[320,1024]{1,0:T(8,128)(2,1)}, bf16[320,1024]{1,0:T(8,128)(2,1)S(1)}, u32[]{:S(2)}) copy-start(bf16[320,1024]{1,0:T(8,128)(2,1)S(1)} %get-tuple-element.120.refs_0_.grad_ref) | copy-start | bytes 1966084
  78.8 7.4 %collective-permute-start.13 = (bf16[160,1024]{1,0:T(8,128)(2,1)S(1)}, bf16[160,1024]{1,0:T(8,128)(2,1)S(1)}, u32[]{:S(2)}, u32[]{:S(2)}) collective-permute-start(bf16[160,1024]{1,0:T(8,128)(2,1)S(1)} %get-tuple-element.110), channel_id=1, source_target_pairs={{0,2},{1,5},{2,0},{3,7},{4,6},{5,1},{6,4},{7,3},{8,10},{9,13},{10,... | collective-permute-start | bytes 983048 | tf_op jit(solution)/shard_map/ppermute | solution.py:683
  80.1 8.7 %collective-permute-start.12 = (bf16[160,1024]{1,0:T(8,128)(2,1)S(1)}, bf16[160,1024]{1,0:T(8,128)(2,1)S(1)}, u32[]{:S(2)}, u32[]{:S(2)}) collective-permute-start(bf16[160,1024]{1,0:T(8,128)(2,1)S(1)} %get-tuple-element.110), channel_id=1, source_target_pairs={{0,4},{1,3},{2,6},{3,1},{4,0},{5,7},{6,2},{7,5},{8,12},{9,11},{10,... | collective-permute-start | bytes 983048 | tf_op jit(solution)/shard_map/ppermute | solution.py:683
  80.9 11.2 %collective-permute-start.15 = (bf16[640,256]{1,0:T(8,128)(2,1)S(1)}, bf16[640,256]{1,0:T(8,128)(2,1)S(1)}, u32[]{:S(2)}, u32[]{:S(2)}) collective-permute-start(bf16[640,256]{1,0:T(8,128)(2,1)S(1)} %get-tuple-element.114), channel_id=1, source_target_pairs={{0,2},{1,5},{2,0},{3,7},{4,6},{5,1},{6,4},{7,3},{8,10},{9,13},{10,... | collective-permute-start | bytes 983048 | tf_op jit(solution)/shard_map/ppermute | solution.py:683
  88.8 6.8 %collective-permute-start.14 = (bf16[160,1024]{1,0:T(8,128)(2,1)S(1)}, bf16[160,1024]{1,0:T(8,128)(2,1)S(1)}, u32[]{:S(2)}, u32[]{:S(2)}) collective-permute-start(bf16[160,1024]{1,0:T(8,128)(2,1)S(1)} %collective-permute-done.12.refs_1_), channel_id=1, source_target_pairs={{0,2},{1,5},{2,0},{3,7},{4,6},{5,1},{6,4},{7,3},{8,10},{9,13},{10,... | collective-permute-start | bytes 983048 | tf_op jit(solution)/shard_map/ppermute | solution.py:683
  92.1 9.1 %collective-permute-start.16 = (bf16[640,256]{1,0:T(8,128)(2,1)S(1)}, bf16[640,256]{1,0:T(8,128)(2,1)S(1)}, u32[]{:S(2)}, u32[]{:S(2)}) collective-permute-start(bf16[640,256]{1,0:T(8,128)(2,1)S(1)} %pad_maximum_fusion.1), channel_id=1, source_target_pairs={{0,4},{1,3},{2,6},{3,1},{4,0},{5,7},{6,2},{7,5},{8,12},{9,11},{10,... | collective-permute-start | bytes 983048 | tf_op jit(solution)/shard_map/ppermute | solution.py:683
  92.2 9.4 %collective-permute-start.17 = (bf16[160,1024]{1,0:T(8,128)(2,1)S(1)}, bf16[160,1024]{1,0:T(8,128)(2,1)S(1)}, u32[]{:S(2)}, u32[]{:S(2)}) collective-permute-start(bf16[160,1024]{1,0:T(8,128)(2,1)S(1)} %collective-permute-done.12.refs_1_), channel_id=1, source_target_pairs={{0,1},{1,0},{2,3},{3,2},{4,5},{5,4},{6,7},{7,6},{8,9},{9,8},{10,11... | collective-permute-start | bytes 983048 | tf_op jit(solution)/shard_map/ppermute | solution.py:692
  94.5 7.1 %collective-permute-start.18 = (bf16[160,1024]{1,0:T(8,128)(2,1)S(1)}, bf16[160,1024]{1,0:T(8,128)(2,1)S(1)}, u32[]{:S(2)}, u32[]{:S(2)}) collective-permute-start(bf16[160,1024]{1,0:T(8,128)(2,1)S(1)} %collective-permute-done.13.refs_2_), channel_id=1, source_target_pairs={{0,1},{1,0},{2,3},{3,2},{4,5},{5,4},{6,7},{7,6},{8,9},{9,8},{10,11... | collective-permute-start | bytes 983048 | tf_op jit(solution)/shard_map/ppermute | solution.py:692
  101.2 1.6 collective-permute-start.19
  106.2 9.7 %collective-permute-start.20 = (bf16[144,1024]{1,0:T(8,128)(2,1)S(1)}, bf16[144,1024]{1,0:T(8,128)(2,1)S(1)}, u32[]{:S(2)}, u32[]{:S(2)}) collective-permute-start(bf16[144,1024]{1,0:T(8,128)(2,1)S(1)} %get-tuple-element.133), channel_id=1, source_target_pairs={{0,8},{1,17},{2,10},{3,19},{4,12},{5,21},{6,14},{7,23},{8,0},{9,25... | collective-permute-start | bytes 884744 | tf_op jit(solution)/shard_map/ppermute | solution.py:683
  115.9 8.6 %collective-permute-start.21 = (bf16[528,512]{1,0:T(8,128)(2,1)S(1)}, bf16[528,512]{1,0:T(8,128)(2,1)S(1)}, u32[]{:S(2)}, u32[]{:S(2)}) collective-permute-start(bf16[528,512]{1,0:T(8,128)(2,1)S(1)} %get-tuple-element.135), channel_id=1, source_target_pairs={{0,2},{1,5},{2,0},{3,7},{4,6},{5,1},{6,4},{7,3},{8,10},{9,13},{10,... | collective-permute-start | bytes 1622024 | tf_op jit(solution)/shard_map/ppermute | solution.py:683
  117.2 21.8 %collective-permute-start.24 = (bf16[320,512]{1,0:T(8,128)(2,1)S(1)}, bf16[320,512]{1,0:T(8,128)(2,1)S(1)}, u32[]{:S(2)}, u32[]{:S(2)}) collective-permute-start(bf16[320,512]{1,0:T(8,128)(2,1)S(1)} %get-tuple-element.140), channel_id=1, source_target_pairs={{0,8},{1,17},{2,10},{3,19},{4,12},{5,21},{6,14},{7,23},{8,0},{9,25... | collective-permute-start | bytes 983048 | tf_op jit(solution)/shard_map/ppermute | solution.py:683
  118.3 21.7 %collective-permute-start.25 = (bf16[320,512]{1,0:T(8,128)(2,1)S(1)}, bf16[320,512]{1,0:T(8,128)(2,1)S(1)}, u32[]{:S(2)}, u32[]{:S(2)}) collective-permute-start(bf16[320,512]{1,0:T(8,128)(2,1)S(1)} %get-tuple-element.141), channel_id=1, source_target_pairs={{0,8},{1,17},{2,10},{3,19},{4,12},{5,21},{6,14},{7,23},{8,0},{9,25... | collective-permute-start | bytes 983048 | tf_op jit(solution)/shard_map/ppermute | solution.py:683
  120.2 18.8 %collective-permute-start.23 = (bf16[144,1024]{1,0:T(8,128)(2,1)S(1)}, bf16[144,1024]{1,0:T(8,128)(2,1)S(1)}, u32[]{:S(2)}, u32[]{:S(2)}) collective-permute-start(bf16[144,1024]{1,0:T(8,128)(2,1)S(1)} %merge.3), channel_id=1, source_target_pairs={{0,16},{1,9},{2,18},{3,11},{4,20},{5,13},{6,22},{7,15},{8,24},{9,1... | collective-permute-start | bytes 884744 | tf_op jit(solution)/shard_map/ppermute | solution.py:683
  125.2 14.9 %collective-permute-start.22 = (bf16[272,512]{1,0:T(8,128)(2,1)S(1)}, bf16[272,512]{1,0:T(8,128)(2,1)S(1)}, u32[]{:S(2)}, u32[]{:S(2)}) collective-permute-start(bf16[272,512]{1,0:T(8,128)(2,1)S(1)} %get-tuple-element.136), channel_id=1, source_target_pairs={{0,4},{1,3},{2,6},{3,1},{4,0},{5,7},{6,2},{7,5},{8,12},{9,11},{10,... | collective-permute-start | bytes 835592 | tf_op jit(solution)/shard_map/ppermute | solution.py:683
  140.6 15.0 %collective-permute-start.26 = (bf16[272,512]{1,0:T(8,128)(2,1)S(1)}, bf16[272,512]{1,0:T(8,128)(2,1)S(1)}, u32[]{:S(2)}, u32[]{:S(2)}) collective-permute-start(bf16[272,512]{1,0:T(8,128)(2,1)S(1)} %merge.4.keep_ref), channel_id=1, source_target_pairs={{0,8},{1,17},{2,10},{3,19},{4,12},{5,21},{6,14},{7,23},{8,0},{9,25... | collective-permute-start | bytes 835592 | tf_op jit(solution)/shard_map/ppermute | solution.py:683
  143.1 6.0 %collective-permute-start.29 = (bf16[128,1024]{1,0:T(8,128)(2,1)S(1)}, bf16[128,1024]{1,0:T(8,128)(2,1)S(1)}, u32[]{:S(2)}, u32[]{:S(2)}) collective-permute-start(bf16[128,1024]{1,0:T(8,128)(2,1)S(1)} %slice.58.refs_0_), channel_id=1, source_target_pairs={{0,2},{1,5},{2,0},{3,7},{4,6},{5,1},{6,4},{7,3},{8,10},{9,13},{10,... | collective-permute-start | bytes 786440 | tf_op jit(solution)/shard_map/ppermute | solution.py:683
  143.1 7.1 %collective-permute-start.28 = (bf16[128,1024]{1,0:T(8,128)(2,1)S(1)}, bf16[128,1024]{1,0:T(8,128)(2,1)S(1)}, u32[]{:S(2)}, u32[]{:S(2)}) collective-permute-start(bf16[128,1024]{1,0:T(8,128)(2,1)S(1)} %slice.58.refs_0_), channel_id=1, source_target_pairs={{0,4},{1,3},{2,6},{3,1},{4,0},{5,7},{6,2},{7,5},{8,12},{9,11},{10,... | collective-permute-start | bytes 786440 | tf_op jit(solution)/shard_map/ppermute | solution.py:683
  143.9 11.7 %collective-permute-start.27 = (bf16[128,1024]{1,0:T(8,128)(2,1)S(1)}, bf16[128,1024]{1,0:T(8,128)(2,1)S(1)}, u32[]{:S(2)}, u32[]{:S(2)}) collective-permute-start(bf16[128,1024]{1,0:T(8,128)(2,1)S(1)} %slice.58.refs_0_), channel_id=1, source_target_pairs={{0,8},{1,17},{2,10},{3,19},{4,12},{5,21},{6,14},{7,23},{8,0},{9,25... | collective-permute-start | bytes 786440 | tf_op jit(solution)/shard_map/ppermute | solution.py:683
  156.2 9.7 %collective-permute-start.30 = (bf16[272,512]{1,0:T(8,128)(2,1)S(1)}, bf16[272,512]{1,0:T(8,128)(2,1)S(1)}, u32[]{:S(2)}, u32[]{:S(2)}) collective-permute-start(bf16[272,512]{1,0:T(8,128)(2,1)S(1)} %merge.5), channel_id=1, source_target_pairs={{0,16},{1,9},{2,18},{3,11},{4,20},{5,13},{6,22},{7,15},{8,24},{9,1... | collective-permute-start | bytes 835592 | tf_op jit(solution)/shard_map/ppermute | solution.py:683
  156.5 5.5 %collective-permute-start.31 = (bf16[128,1024]{1,0:T(8,128)(2,1)S(1)}, bf16[128,1024]{1,0:T(8,128)(2,1)S(1)}, u32[]{:S(2)}, u32[]{:S(2)}) collective-permute-start(bf16[128,1024]{1,0:T(8,128)(2,1)S(1)} %collective-permute-done.28.refs_2_), channel_id=1, source_target_pairs={{0,2},{1,5},{2,0},{3,7},{4,6},{5,1},{6,4},{7,3},{8,10},{9,13},{10,... | collective-permute-start | bytes 786440 | tf_op jit(solution)/shard_map/ppermute | solution.py:683
  156.5 9.4 %collective-permute-start.33 = (bf16[128,1024]{1,0:T(8,128)(2,1)S(1)}, bf16[128,1024]{1,0:T(8,128)(2,1)S(1)}, u32[]{:S(2)}, u32[]{:S(2)}) collective-permute-start(bf16[128,1024]{1,0:T(8,128)(2,1)S(1)} %collective-permute-done.27.refs_1_), channel_id=1, source_target_pairs={{0,2},{1,5},{2,0},{3,7},{4,6},{5,1},{6,4},{7,3},{8,10},{9,13},{10,... | collective-permute-start | bytes 786440 | tf_op jit(solution)/shard_map/ppermute | solution.py:683
  158.0 8.0 %collective-permute-start.32 = (bf16[128,1024]{1,0:T(8,128)(2,1)S(1)}, bf16[128,1024]{1,0:T(8,128)(2,1)S(1)}, u32[]{:S(2)}, u32[]{:S(2)}) collective-permute-start(bf16[128,1024]{1,0:T(8,128)(2,1)S(1)} %collective-permute-done.27.refs_1_), channel_id=1, source_target_pairs={{0,4},{1,3},{2,6},{3,1},{4,0},{5,7},{6,2},{7,5},{8,12},{9,11},{10,... | collective-permute-start | bytes 786440 | tf_op jit(solution)/shard_map/ppermute | solution.py:683
  166.1 10.4 %collective-permute-start.37 = (bf16[320,512]{1,0:T(8,128)(2,1)S(1)}, bf16[320,512]{1,0:T(8,128)(2,1)S(1)}, u32[]{:S(2)}, u32[]{:S(2)}) collective-permute-start(bf16[320,512]{1,0:T(8,128)(2,1)S(1)} %add_convert_fusion), channel_id=1, source_target_pairs={{0,16},{1,9},{2,18},{3,11},{4,20},{5,13},{6,22},{7,15},{8,24},{9,1... | collective-permute-start | bytes 983048 | tf_op jit(solution)/shard_map/ppermute | solution.py:683
  168.2 5.2 %collective-permute-start.36 = (bf16[128,1024]{1,0:T(8,128)(2,1)S(1)}, bf16[128,1024]{1,0:T(8,128)(2,1)S(1)}, u32[]{:S(2)}, u32[]{:S(2)}) collective-permute-start(bf16[128,1024]{1,0:T(8,128)(2,1)S(1)} %collective-permute-done.32.refs_3_), channel_id=1, source_target_pairs={{0,2},{1,5},{2,0},{3,7},{4,6},{5,1},{6,4},{7,3},{8,10},{9,13},{10,... | collective-permute-start | bytes 786440 | tf_op jit(solution)/shard_map/ppermute | solution.py:683
  168.2 8.3 %collective-permute-start.35 = (bf16[256,512]{1,0:T(8,128)(2,1)S(1)}, bf16[256,512]{1,0:T(8,128)(2,1)S(1)}, u32[]{:S(2)}, u32[]{:S(2)}) collective-permute-start(bf16[256,512]{1,0:T(8,128)(2,1)S(1)} %slice.57.refs_0_), channel_id=1, source_target_pairs={{0,2},{1,5},{2,0},{3,7},{4,6},{5,1},{6,4},{7,3},{8,10},{9,13},{10,... | collective-permute-start | bytes 786440 | tf_op jit(solution)/shard_map/ppermute | solution.py:683
  169.6 6.9 %collective-permute-start.34 = (bf16[256,512]{1,0:T(8,128)(2,1)S(1)}, bf16[256,512]{1,0:T(8,128)(2,1)S(1)}, u32[]{:S(2)}, u32[]{:S(2)}) collective-permute-start(bf16[256,512]{1,0:T(8,128)(2,1)S(1)} %slice.57.refs_0_), channel_id=1, source_target_pairs={{0,4},{1,3},{2,6},{3,1},{4,0},{5,7},{6,2},{7,5},{8,12},{9,11},{10,... | collective-permute-start | bytes 786440 | tf_op jit(solution)/shard_map/ppermute | solution.py:683
  177.2 11.7 %collective-permute-start.43 = (bf16[320,512]{1,0:T(8,128)(2,1)S(1)}, bf16[320,512]{1,0:T(8,128)(2,1)S(1)}, u32[]{:S(2)}, u32[]{:S(2)}) collective-permute-start(bf16[320,512]{1,0:T(8,128)(2,1)S(1)} %row_sums.1.mine_ref), channel_id=1, source_target_pairs={{0,1},{1,0},{2,3},{3,2},{4,5},{5,4},{6,7},{7,6},{8,9},{9,8},{10,11... | collective-permute-start | bytes 983048 | tf_op jit(solution)/shard_map/ppermute | solution.py:692
  182.0 1.3 collective-permute-start.42
  182.1 5.3 %collective-permute-start.39 = (bf16[256,512]{1,0:T(8,128)(2,1)S(1)}, bf16[256,512]{1,0:T(8,128)(2,1)}, u32[]{:S(2)}, u32[]{:S(2)}) collective-permute-start(bf16[256,512]{1,0:T(8,128)(2,1)S(1)} %slice.57.refs_0_), channel_id=1, source_target_pairs={{0,1},{1,0},{2,3},{3,2},{4,5},{5,4},{6,7},{7,6},{8,9},{9,8},{10,11... | collective-permute-start | bytes 786440 | tf_op jit(solution)/shard_map/ppermute | solution.py:692
  182.5 4.8 %collective-permute-start.41 = (bf16[256,512]{1,0:T(8,128)(2,1)S(1)}, bf16[256,512]{1,0:T(8,128)(2,1)}, u32[]{:S(2)}, u32[]{:S(2)}) collective-permute-start(bf16[256,512]{1,0:T(8,128)(2,1)S(1)} %collective-permute-done.35.refs_2_), channel_id=1, source_target_pairs={{0,1},{1,0},{2,3},{3,2},{4,5},{5,4},{6,7},{7,6},{8,9},{9,8},{10,11... | collective-permute-start | bytes 786440 | tf_op jit(solution)/shard_map/ppermute | solution.py:692
  182.6 4.7 %collective-permute-start.40 = (bf16[256,512]{1,0:T(8,128)(2,1)S(1)}, bf16[256,512]{1,0:T(8,128)(2,1)}, u32[]{:S(2)}, u32[]{:S(2)}) collective-permute-start(bf16[256,512]{1,0:T(8,128)(2,1)S(1)} %collective-permute-done.34.refs_1_), channel_id=1, source_target_pairs={{0,1},{1,0},{2,3},{3,2},{4,5},{5,4},{6,7},{7,6},{8,9},{9,8},{10,11... | collective-permute-start | bytes 786440 | tf_op jit(solution)/shard_map/ppermute | solution.py:692
  183.3 5.6 %collective-permute-start.38 = (bf16[256,512]{1,0:T(8,128)(2,1)S(1)}, bf16[256,512]{1,0:T(8,128)(2,1)}, u32[]{:S(2)}, u32[]{:S(2)}) collective-permute-start(bf16[256,512]{1,0:T(8,128)(2,1)S(1)} %collective-permute-done.34.refs_1_), channel_id=1, source_target_pairs={{0,2},{1,5},{2,0},{3,7},{4,6},{5,1},{6,4},{7,3},{8,10},{9,13},{10,... | collective-permute-start | bytes 786440 | tf_op jit(solution)/shard_map/ppermute | solution.py:683
  188.9 5.2 %collective-permute-start.44 = (bf16[256,512]{1,0:T(8,128)(2,1)}, bf16[256,512]{1,0:T(8,128)(2,1)S(1)}, u32[]{:S(2)}, u32[]{:S(2)}) collective-permute-start(bf16[256,512]{1,0:T(8,128)(2,1)} %collective-permute-done.38.refs_3_), channel_id=1, source_target_pairs={{0,1},{1,0},{2,3},{3,2},{4,5},{5,4},{6,7},{7,6},{8,9},{9,8},{10,11... | collective-permute-start | bytes 786440 | tf_op jit(solution)/shard_map/ppermute | solution.py:692
  (11 other events, 60.5 us)

commit v4 on v3

--- a/solution.py
+++ b/solution.py
@@ -35,7 +35,7 @@
 
 
 def call(kernel, name, outs, place, near, far=(), scratch=(), flops=0, far_outs=0,
-         limit=VMEM_BYTES, light=False):
+         limit=VMEM_BYTES, light=False, aliases={}):
     operands = list(near) + list(far)
     moved = sum(a.size * a.dtype.itemsize for a in operands + list(outs))
     if light:
@@ -48,6 +48,7 @@
         out_specs=spaced(pltpu.VMEM, outs[: len(outs) - far_outs])
         + spaced(pltpu.HBM, outs[len(outs) - far_outs :]),
         scratch_shapes=list(scratch),
+        input_output_aliases=aliases,
         compiler_params=pltpu.CompilerParams(vmem_limit_bytes=limit),
         cost_estimate=pl.CostEstimate(
             flops=int(flops), bytes_accessed=int(moved), transcendentals=0
@@ -354,30 +355,50 @@
     return out
 
 
-def feature_step(place, grad_linear, mine, other, w_weight, w_other, q_weight):
+def self_feature(place, grad_linear, w_weight, w_other):
     rows, dim = grad_linear.shape
     half = dim // 2
 
+    def kernel(place_ref, grad_ref, w_in, w_other_in, out_ref, w_ref, sem):
+        core = place_ref[1]
+        pick_copy(core, w_in, w_other_in, w_ref, sem, aligned(core * half, half)).wait()
+        out_ref[...] = times_t(grad_ref[...], w_ref[...])
+
+    (out,) = call(
+        kernel, "self_feature", [array((rows, half), F32)], place, [grad_linear],
+        [w_weight, w_other], [pltpu.VMEM((half, dim), BF16), pltpu.SemaphoreType.DMA(())],
+        flops=2 * rows * dim * half,
+    )
+    return out
+
+
+def feature_step(place, self_grad, mine, other, q_weight, bias_mine, bias_other):
+    rows, half = mine.shape
+    dim = 2 * half
+
     def kernel(
-        place_ref, grad_ref, mine_ref, other_ref, w_in, w_other_in, q_in, out_ref, w_ref, q_ref, sem
+        place_ref, self_ref, mine_ref, other_ref, bias_mine_ref, bias_other_ref, q_in,
+        out_ref, bias_ref, q_ref, sem,
     ):
         core = place_ref[1]
-        span = aligned(core * half, half)
-        q_copy = pltpu.make_async_copy(q_in.at[span, :], q_ref, sem.at[1])
+        spans = [aligned(core * half, half), aligned((1 - core) * half, half)]
+        q_copy = pltpu.make_async_copy(q_in.at[spans[0], :], q_ref, sem)
         q_copy.start()
-        pick_copy(core, w_in, w_other_in, w_ref, sem.at[0], span).wait()
-        total = times_t(grad_ref[...], w_ref[...])
+        bias_ref[:, spans[0]] = bias_mine_ref[...]
+        bias_ref[:, spans[1]] = bias_other_ref[...]
         q_copy.wait()
-        total += times_t(mine_ref[...], q_ref[:, span])
-        out_ref[...] = total + times_t(other_ref[...], q_ref[:, aligned((1 - core) * half, half)])
-
-    (out,) = call(
-        kernel, "feature_step", [array((rows, half), F32)], place, [grad_linear, mine, other],
-        [w_weight, w_other, q_weight],
-        [pltpu.VMEM((half, dim), BF16)] * 2 + [pltpu.SemaphoreType.DMA((2,))],
-        flops=4 * rows * dim * half,
-    )
-    return out
+        out_ref[...] = (
+            self_ref[...]
+            + times_t(mine_ref[...], q_ref[:, spans[0]])
+            + times_t(other_ref[...], q_ref[:, spans[1]])
+        )
+
+    return call(
+        kernel, "feature_step", [array((rows, half), F32), array((1, dim), F32)], place,
+        [self_grad, mine, other, bias_mine, bias_other], [q_weight],
+        [pltpu.VMEM((half, dim), BF16), pltpu.SemaphoreType.DMA(())],
+        flops=2 * rows * dim * half,
+    )
 
 
 def plane_slices(place, features, mine, other):
@@ -617,14 +638,14 @@
     return out
 
 
-def unpack(place, sides, lines=0):
+def unpack(place, blocks, spots, lines=0, sides=1, onto=None):
     parts = 2 if lines else 1
-    height, width = sides[0][0].shape
-    blocks = [block for side in sides for block in side]
+    height, width = blocks[0].shape
     count = len(blocks)
 
     def kernel(place_ref, *refs):
-        sources, (out_ref, block_ref, wide_ref, sem, out_sem) = refs[:count], refs[count:]
+        sources, refs = refs[:count], refs[count + (onto is not None) :]
+        out_ref, block_ref, wide_ref, sem, out_sem = refs
         spot = place_ref[0] % PLANE
         copies = [
             pltpu.make_async_copy(source, block_ref.at[index], sem.at[index])
@@ -633,12 +654,12 @@
         start_all(copies)
         outs = []
         for index, copy in enumerate(copies):
-            side, slot, at = index // (PLANE * parts), index // parts % PLANE, index % parts
+            side, slot, at = spots[index]
             core = place_ref[1] ^ side
             row = (spot ^ away(core, slot, 2)) * parts
             if lines:
                 row = row + (line_side(place_ref, lines) ^ at)
-            cols = aligned(core * width, width) if len(sides) > 1 else pl.ds(0, width)
+            cols = aligned(core * width, width) if sides > 1 else pl.ds(0, width)
             copy.wait()
             wide_ref[index] = block_ref[index].astype(F32)
             outs.append(
@@ -651,13 +672,13 @@
         wait_all(outs)
 
     (out,) = call(
-        kernel, "unpack", [array((PLANE * parts * height, width * len(sides)), F32)], place, [],
-        blocks,
+        kernel, "unpack", [array((PLANE * parts * height, width * sides), F32)], place, [],
+        list(blocks) + ([] if onto is None else [onto]),
         [
             pltpu.VMEM((count, height, width), BF16), pltpu.VMEM((count, height, width), F32),
             pltpu.SemaphoreType.DMA((count,)), pltpu.SemaphoreType.DMA((count,)),
         ],
-        far_outs=1,
+        far_outs=1, aliases={} if onto is None else {count + 1: 0},
     )
     return out
 
@@ -713,7 +734,7 @@
     lists.append(plane_swap(jnp.concatenate(lists, 0), 0))
     traded = [trade(stage) for stage in stages[:-1]]
     matrix, weight_sums = slot_matrix(place, lists, count)
-    matrix, stages[-1] = fence((matrix, stages[-1]))
+    matrix, stages[-1], traded = fence((matrix, stages[-1], traded))
     line_parts = [features] + stages + traded + [trade(stages[-1])]
     send, high, low = first_sums(place, line_parts, q_weight, q_bias[None], matrix)
     send, w_sent = fence((send, w_weight))
@@ -777,7 +798,10 @@
     w_near, biases["w"] = last_sum(w_sum, w_came)
     w_far = line_swap(w_near, 0)
     near_one, near_two = plane_swap(w_near, 1), plane_swap(w_near, 0)
-    q_came, w_far, near_one, near_two, biases = fence((q_came, w_far, near_one, near_two, biases))
+    self_grad = self_feature(place, grad_linear, w_weight, w_other)
+    q_came, w_far, near_one, near_two, biases, self_grad = fence(
+        (q_came, w_far, near_one, near_two, biases, self_grad)
+    )
     for step in range(1, line_bits):
         q_sum = merge(place, q_sum, q_came)
         q_came = line_swap(q_sum, step)
@@ -791,12 +815,17 @@
     rows_next = line_swap(upper, 1)
     q_one, q_two = plane_swap(q_own, 1), plane_swap(q_own, 0)
     far_three = plane_swap(far_one, 0)
-    q_one, q_two, far_three, rows_next, biases = fence((q_one, q_two, far_three, rows_next, biases))
+    w_all = [w_near, w_far, near_one, far_one, near_two, far_two, near_three]
+    w_part = unpack(
+        place, w_all, [(0, at // 2, at % 2) for at in range(2 * PLANE - 1)], lines
+    )
+    bias_other = trade(biases["q"][None])
+    q_one, q_two, far_three, rows_next, biases, w_part, bias_other = fence(
+        (q_one, q_two, far_three, rows_next, biases, w_part, bias_other)
+    )
     q_three = plane_swap(q_one, 0)
-    w_all = [w_near, w_far, near_one, far_one, near_two, far_two, near_three, far_three]
-    w_grad = unpack(place, [w_all], lines)
-    w_bias_grad, q_bias_half = biases["w"], biases["q"]
-    q_bias_grad = joined(q_bias_half, trade(q_bias_half), 0)
+    w_grad = unpack(place, [far_three], [(0, 3, 1)], lines, 1, w_part)
+    w_bias_grad, q_bias_half = biases["w"], biases["q"][None]
 
     stay = stay[: stay.shape[0] // 2]
     for step in range(2, line_bits):
@@ -808,14 +837,19 @@
     row_other = trade(row_half)
     q_mine = [q_own, q_one, q_two]
     q_other = [trade(block) for block in q_mine]
-    q_three, q_other, w_grad, q_bias_grad, row_other = fence(
-        (q_three, q_other, w_grad, q_bias_grad, row_other)
-    )
-    feature_grad = feature_step(
-        place, grad_linear, row_half, row_other, w_weight, w_other, q_weight
-    )
-    q_grad = unpack(place, [q_mine + [q_three], q_other + [trade(q_three)]])
-    return (embeddings, feature_grad, q_grad, q_bias_grad, w_grad, w_bias_grad)
+    feature_grad, q_bias_grad = feature_step(
+        place, self_grad, row_half, row_other, q_weight, q_bias_half, bias_other
+    )
+    q_three, q_other, w_grad, q_bias_grad, feature_grad = fence(
+        (q_three, q_other, w_grad, q_bias_grad, feature_grad)
+    )
+    last_other = trade(q_three)
+    q_part = unpack(place, q_mine + [q_three], [(0, at, 0) for at in range(PLANE)], 0, 2)
+    q_part, last_other = fence((q_part, last_other))
+    q_grad = unpack(
+        place, q_other + [last_other], [(1, at, 0) for at in range(PLANE)], 0, 2, q_part
+    )
+    return (embeddings, feature_grad, q_grad, q_bias_grad[0], w_grad, w_bias_grad)
 
 
 def solution(mesh):

time: 198 us -> 194 us (0.980)
  waiting for transfers between devices: 87.3 us -> 74.2 us
  starting transfers between devices: 42.2 us -> 48.2 us
  Pallas kernels: 56 us -> 58.2 us
    ppermute x31, waiting for transfers between devices: 80.9 us -> 68.5 us  [swap(): return lax.ppermute(value, ('nodes', 'stream'), pairs)]
    ppermute x14, starting transfers between devices: 15.4 us -> 20.7 us  [trade(): return lax.ppermute(value, 'stream', [(0, 1), (1, 0)])]
    pallas_call x17 -> x20, Pallas kernels: 56 us -> 58.2 us  [call(): pl.pallas_call(kernel, name=name, out_shape=list(outs), in_specs=spaced(p...]
  transfers between devices with their start and end apart: 45 -> 45, of which waited for: 27 -> 24; matrix products, arithmetic and copies ran while one was open for 3% -> 3% of each run, Pallas kernels for 19% -> 21%
where the time goes in v4:
time: 194 us; the launch traced here: 193 us
  waiting for transfers between devices  74.2 us (38%)
  Pallas kernels  58.2 us (30%)
  starting transfers between devices  48.2 us (25%)
  other arithmetic  6.61 us (3%)
  local copies, waits for them, and re-layouts  4.66 us (2%)
    ppermute x31, waiting for transfers between devices, swap(): return lax.ppermute(value, ('nodes', 'stream'), pairs)  68.5 us
    pallas_call x20, Pallas kernels, call(): pl.pallas_call(kernel, name=name, out_shape=list(outs), in_specs=spaced(p...  58.2 us
    ppermute x31, starting transfers between devices, swap(): return lax.ppermute(value, ('nodes', 'stream'), pairs)  27.5 us
    ppermute x14, starting transfers between devices, trade(): return lax.ppermute(value, 'stream', [(0, 1), (1, 0)])  20.7 us
    ppermute x14, waiting for transfers between devices, trade(): return lax.ppermute(value, 'stream', [(0, 1), (1, 0)])  5.7 us
  transfers between devices with their start and end apart: 45, of which 24 were waited for; matrix products, arithmetic and copies ran while one was open for 3% of the time, Pallas kernels for 21%

profile of v4, /device:TPU:1, one launch (start us, length us, event | category | flops | bytes accessed | tf_op | source)
XLA Modules:
  0.0 193.2 jit_solution(13043659858360669179)
XLA Ops:
  0.6 1.7 constant_dynamic-slice_fusion
  2.4 2.1 %collective-permute-start.2 = (bf16[160,1024]{1,0:T(8,128)(2,1)}, bf16[160,1024]{1,0:T(8,128)(2,1)}, u32[]{:S(2)}, u32[]{:S(2)}) collective-permute-start(bf16[160,1024]{1,0:T(8,128)(2,1)} %constant_dynamic-slice_fusion), channel_id=1, source_target_pairs={{0,16},{1,9},{2,18},{3,11},{4,20},{5,13},{6,22},{7,15},{8,24},{9,1... | collective-permute-start | bytes 983048 | tf_op jit(solution)/shard_map/ppermute | solution.py:704
  5.1 2.2 %sort_slots.1 = s32[32,320]{1,0:T(8,128)} custom-call(s32[2]{0:T(128)} %pad_add_fusion.2.place_ref, s32[25,320]{1,0:T(8,128)} %bitcast.12, s32[25,320]{1,0:T(8,128)} %bitcast.13, s32[25,320]{1,0:T(8,128)} %bitcast.14), custom_call_target="tpu_custom_call" | custom-call | bytes 136960 | tf_op jit(solution)/shard_map/sort_slots/pallas_call | solution.py:43
  7.3 2.0 %collective-permute-start = (s32[32,320]{1,0:T(8,128)}, s32[32,320]{1,0:T(8,128)S(1)}, u32[]{:S(2)}, u32[]{:S(2)}) collective-permute-start(s32[32,320]{1,0:T(8,128)} %sort_slots.1), channel_id=1, source_target_pairs={{0,1},{1,0},{2,3},{3,2},{4,5},{5,4},{6,7},{7,6},{8,9},{9,8},{10,11... | collective-permute-start | bytes 122888 | tf_op jit(solution)/shard_map/ppermute | solution.py:713
  13.1 2.6 %collective-permute-done.1.next_ref = s32[64,320]{1,0:T(8,128)S(1)} collective-permute-done((s32[64,320]{1,0:T(8,128)S(1)}, s32[64,320]{1,0:T(8,128)S(1)}, u32[]{:S(2)}, u32[]{:S(2)}) %collective-permute-start.1) | collective-permute-done | bytes 81952 | tf_op jit(solution)/shard_map/ppermute | solution.py:704
  15.6 2.0 %pad_maximum_fusion = bf16[320,1024]{1,0:T(8,128)(2,1)} fusion(bf16[160,1024]{1,0:T(8,128)(2,1)} %collective-permute-done.2.refs_1_.refs_8_, bf16[160,1024]{1,0:T(8,128)(2,1)} %constant_dynamic-slice_fusion), kind=kLoop, calls=%fused_computation | loop fusion | flops 1310720 | bytes 1310720 | tf_op jit(solution)/shard_map/concatenate | solution.py:733
  18.3 2.1 %collective-permute-start.5 = (bf16[160,1024]{1,0:T(8,128)(2,1)}, bf16[160,1024]{1,0:T(8,128)(2,1)}, u32[]{:S(2)}, u32[]{:S(2)}) collective-permute-start(bf16[160,1024]{1,0:T(8,128)(2,1)} %collective-permute-done.2.refs_1_.refs_8_), channel_id=1, source_target_pairs={{0,1},{1,0},{2,3},{3,2},{4,5},{5,4},{6,7},{7,6},{8,9},{9,8},{10,11... | collective-permute-start | bytes 983048 | tf_op jit(solution)/shard_map/ppermute | solution.py:713
  21.2 1.3 collective-permute-start.3
  22.5 3.7 %collective-permute-done.3.rest_ref = s32[128,320]{1,0:T(8,128)} collective-permute-done((s32[128,320]{1,0:T(8,128)S(1)}, s32[128,320]{1,0:T(8,128)}, u32[]{:S(2)}, u32[]{:S(2)}) %collective-permute-start.3) | collective-permute-done | bytes 163872 | tf_op jit(solution)/shard_map/ppermute | solution.py:704
  26.2 6.9 %slot_matrix.1 = (f32[1280,8]{1,0:T(8,128)}, bf16[1280,1280]{1,0:T(8,128)(2,1)}) custom-call(s32[2]{0:T(128)} %pad_add_fusion.2.place_ref, s32[64,320]{1,0:T(8,128)} %copy-done.12, s32[64,320]{1,0:T(8,128)} %copy-done.13, s32[128,320]{1,0:T(8,128)} %collective-permute-done.3.rest_ref), custom_call_target="tpu_custom_call" | custom-call | flops 1 | bytes 1 | tf_op jit(solution)/shard_map/slot_matrix/pallas_call | solution.py:43
  34.4 1.6 collective-permute-start.6
  36.0 2.1 %collective-permute-done.6.refs_4_.refs_11_ = bf16[320,1024]{1,0:T(8,128)(2,1)} collective-permute-done((bf16[320,1024]{1,0:T(8,128)(2,1)}, bf16[320,1024]{1,0:T(8,128)(2,1)}, u32[]{:S(2)}, u32[]{:S(2)}) %collective-permute-start.6) | collective-permute-done | bytes 655392 | tf_op jit(solution)/shard_map/ppermute | solution.py:713
  38.1 7.1 %first_sums.1 = (f32[320,512]{1,0:T(8,128)}, bf16[1280,512]{1,0:T(8,128)(2,1)}, bf16[1280,512]{1,0:T(8,128)(2,1)}) custom-call(s32[2]{0:T(128)} %pad_add_fusion.2.place_ref, f32[1,1024]{1,0:T(1,128)} %bitcast.16, bf16[1024,1024]{1,0:T(8,128)(2,1)} %q_in.3, bf16[1280,1280]{1,0:T(8,128)(2,1)} %get-tuple-element.100.matrix_in, bf16[320,1024]{1,0:T(8,128)(2,1)} %refs_7_.1, ...), custom_call_target="tpu_custom_call" | custom-call | flops 2181038080 | bytes 11276288 | tf_op jit(solution)/shard_map/first_sums/pallas_call | solution.py:43
  46.9 7.2 %more_sums.1 = (f32[320,512]{1,0:T(8,128)}, f32[320,512]{1,0:T(8,128)}, f32[320,512]{1,0:T(8,128)}) custom-call(s32[2]{0:T(128)} %pad_add_fusion.2.place_ref, bf16[1280,1280]{1,0:T(8,128)(2,1)} %get-tuple-element.100.matrix_in, bf16[1280,512]{1,0:T(8,128)(2,1)} %get-tuple-element.103.refs_0_.high_in, bf16[1280,512]{1,0:T(8,128)(2,1)} %get-tuple-element.104.refs_1_), custom_call_target="tpu_custom_call" | custom-call | flops 2516582400 | bytes 7864320 | tf_op jit(solution)/shard_map/more_sums/pallas_call | solution.py:43
  55.7 1.4 add.35
  59.4 7.5 %collective-permute-done.9 = f32[320,512]{1,0:T(8,128)S(1)} collective-permute-done((f32[320,512]{1,0:T(8,128)}, f32[320,512]{1,0:T(8,128)S(1)}, u32[]{:S(2)}, u32[]{:S(2)}) %collective-permute-start.9) | collective-permute-done | bytes 655392 | tf_op jit(solution)/shard_map/ppermute | solution.py:704
  68.0 3.0 %self_product.1.self_ref = f32[320,1024]{1,0:T(8,128)S(1)} custom-call(s32[2]{0:T(128)S(1)} %copy-done.8, bf16[320,1024]{1,0:T(8,128)(2,1)S(1)} %copy-done.2, f32[1,1024]{1,0:T(1,128)S(1)} %bitcast.11, bf16[1024,1024]{1,0:T(8,128)(2,1)S(1)} %copy-done, bf16[1024,1024]{1,0:T(8,128)(2,1)} %collective-permute-done.10.w_other_in), custom_call_target="tpu_custom_call" | custom-call | flops 671088640 | bytes 6164480 | tf_op jit(solution)/shard_map/self_product/pallas_call | solution.py:43
  71.9 1.5 collective-permute-start.11
  74.7 3.5 %node_step.1 = (f32[320,1024]{1,0:T(8,128)}, bf16[320,1024]{1,0:T(8,128)(2,1)S(1)}, bf16[160,1024]{1,0:T(8,128)(2,1)S(1)}) custom-call(s32[2]{0:T(128)S(1)} %copy-done.8, bf16[320,512]{1,0:T(8,128)(2,1)S(1)} %divide_convert_fusion.mine_ref, bf16[320,512]{1,0:T(8,128)(2,1)S(1)} %collective-permute-done.11.other_ref, f32[320,1024]{1,0:T(8,128)S(1)} %self_product.1.self_ref, ...), custom_call_target="tpu_custom_call" | custom-call | flops 671088640 | bytes 9109504 | tf_op jit(solution)/shard_map/node_step/pallas_call | solution.py:43
  78.3 1.3 collective-permute-start.13
  80.7 5.0 %collective-permute-done.13.refs_2_ = bf16[160,1024]{1,0:T(8,128)(2,1)S(1)} collective-permute-done((bf16[160,1024]{1,0:T(8,128)(2,1)S(1)}, bf16[160,1024]{1,0:T(8,128)(2,1)S(1)}, u32[]{:S(2)}, u32[]{:S(2)}) %collective-permute-start.13) | collective-permute-done | bytes 327712 | tf_op jit(solution)/shard_map/ppermute | solution.py:704
  85.7 2.6 %collective-permute-done.12.refs_1_ = bf16[160,1024]{1,0:T(8,128)(2,1)S(1)} collective-permute-done((bf16[160,1024]{1,0:T(8,128)(2,1)S(1)}, bf16[160,1024]{1,0:T(8,128)(2,1)S(1)}, u32[]{:S(2)}, u32[]{:S(2)}) %collective-permute-start.12) | collective-permute-done | bytes 327712 | tf_op jit(solution)/shard_map/ppermute | solution.py:704
  88.3 3.3 %collective-permute-done.15.refs_8_ = bf16[640,256]{1,0:T(8,128)(2,1)S(1)} collective-permute-done((bf16[640,256]{1,0:T(8,128)(2,1)S(1)}, bf16[640,256]{1,0:T(8,128)(2,1)S(1)}, u32[]{:S(2)}, u32[]{:S(2)}) %collective-permute-start.15) | collective-permute-done | bytes 327712 | tf_op jit(solution)/shard_map/ppermute | solution.py:704
  91.7 2.3 %collective-permute-start.17 = (bf16[160,1024]{1,0:T(8,128)(2,1)S(1)}, bf16[160,1024]{1,0:T(8,128)(2,1)S(1)}, u32[]{:S(2)}, u32[]{:S(2)}) collective-permute-start(bf16[160,1024]{1,0:T(8,128)(2,1)S(1)} %collective-permute-done.12.refs_1_), channel_id=1, source_target_pairs={{0,1},{1,0},{2,3},{3,2},{4,5},{5,4},{6,7},{7,6},{8,9},{9,8},{10,11... | collective-permute-start | bytes 983048 | tf_op jit(solution)/shard_map/ppermute | solution.py:713
  95.1 5.6 %collective-permute-done.16.refs_10_ = bf16[640,256]{1,0:T(8,128)(2,1)S(1)} collective-permute-done((bf16[640,256]{1,0:T(8,128)(2,1)S(1)}, bf16[640,256]{1,0:T(8,128)(2,1)S(1)}, u32[]{:S(2)}, u32[]{:S(2)}) %collective-permute-start.16) | collective-permute-done | bytes 327712 | tf_op jit(solution)/shard_map/ppermute | solution.py:704
  102.3 3.3 %self_weight.1 = (bf16[144,1024]{1,0:T(8,128)(2,1)S(1)}, bf16[144,1024]{1,0:T(8,128)(2,1)S(1)}) custom-call(s32[2]{0:T(128)S(1)} %copy-done.8, bf16[320,1024]{1,0:T(8,128)(2,1)S(1)} %get-tuple-element.129.refs_0_.grad_ref, bf16[160,1024]{1,0:T(8,128)(2,1)S(1)} %collective-permute-done.12.refs_1_, bf16[160,1024]{1,0:T(8,128)(2,1)S(1)} %collective-permute-done.13.refs_2_, ...), custom_call_target="tpu_custom_call" | custom-call | flops 671088640 | bytes 4194304 | tf_op jit(solution)/shard_map/self_weight/pallas_call | solution.py:43
  105.7 1.3 collective-permute-start.20
  107.0 8.4 %row_grad.1 = (bf16[640,512]{1,0:T(8,128)(2,1)S(1)}, bf16[320,512]{1,0:T(8,128)(2,1)S(1)}, bf16[320,512]{1,0:T(8,128)(2,1)S(1)}, bf16[528,512]{1,0:T(8,128)(2,1)S(1)}, bf16[528,512]{1,0:T(8,128)(2,1)S(1)}) custom-call(s32[2]{0:T(128)S(1)} %copy-done.8, f32[1280,8]{1,0:T(8,128)S(1)} %copy-done.9, bf16[1280,1280]{1,0:T(8,128)(2,1)} %get-tuple-element.100.matrix_in, ...), custom_call_target="tpu_custom_call" | custom-call | flops 4362076160 | bytes 16457728 | tf_op jit(solution)/shard_map/row_grad/pallas_call | solution.py:43
  119.7 1.4 collective-permute-start.23
  121.1 2.9 %collective-permute-done.21.came_ref = bf16[528,512]{1,0:T(8,128)(2,1)S(1)} collective-permute-done((bf16[528,512]{1,0:T(8,128)(2,1)S(1)}, bf16[528,512]{1,0:T(8,128)(2,1)S(1)}, u32[]{:S(2)}, u32[]{:S(2)}) %collective-permute-start.21) | collective-permute-done | bytes 540704 | tf_op jit(solution)/shard_map/ppermute | solution.py:704
  125.5 13.1 %collective-permute-done.23 = bf16[144,1024]{1,0:T(8,128)(2,1)S(1)} collective-permute-done((bf16[144,1024]{1,0:T(8,128)(2,1)S(1)}, bf16[144,1024]{1,0:T(8,128)(2,1)S(1)}, u32[]{:S(2)}, u32[]{:S(2)}) %collective-permute-start.23) | collective-permute-done | bytes 294944 | tf_op jit(solution)/shard_map/ppermute | solution.py:704
  140.1 2.4 %collective-permute-start.26 = (bf16[272,512]{1,0:T(8,128)(2,1)S(1)}, bf16[272,512]{1,0:T(8,128)(2,1)S(1)}, u32[]{:S(2)}, u32[]{:S(2)}) collective-permute-start(bf16[272,512]{1,0:T(8,128)(2,1)S(1)} %merge.4.keep_ref), channel_id=1, source_target_pairs={{0,8},{1,17},{2,10},{3,19},{4,12},{5,21},{6,14},{7,23},{8,0},{9,25... | collective-permute-start | bytes 835592 | tf_op jit(solution)/shard_map/ppermute | solution.py:704
  143.5 2.3 %self_feature.1.self_ref = f32[320,512]{1,0:T(8,128)S(1)} custom-call(s32[2]{0:T(128)S(1)} %copy-done.8, bf16[320,1024]{1,0:T(8,128)(2,1)S(1)} %copy-done.5, bf16[1024,1024]{1,0:T(8,128)(2,1)S(1)} %copy-done.1, bf16[1024,1024]{1,0:T(8,128)(2,1)} %collective-permute-done.10.w_other_in), custom_call_target="tpu_custom_call" | custom-call | flops 335544320 | bytes 5505024 | tf_op jit(solution)/shard_map/self_feature/pallas_call | solution.py:43
  146.4 2.1 %collective-permute-done.29.refs_4_ = bf16[128,1024]{1,0:T(8,128)(2,1)S(1)} collective-permute-done((bf16[128,1024]{1,0:T(8,128)(2,1)S(1)}, bf16[128,1024]{1,0:T(8,128)(2,1)S(1)}, u32[]{:S(2)}, u32[]{:S(2)}) %collective-permute-start.29) | collective-permute-done | bytes 262176 | tf_op jit(solution)/shard_map/ppermute | solution.py:704
  149.7 5.2 %collective-permute-done.27.refs_1_ = bf16[128,1024]{1,0:T(8,128)(2,1)S(1)} collective-permute-done((bf16[128,1024]{1,0:T(8,128)(2,1)S(1)}, bf16[128,1024]{1,0:T(8,128)(2,1)S(1)}, u32[]{:S(2)}, u32[]{:S(2)}) %collective-permute-start.27) | collective-permute-done | bytes 262176 | tf_op jit(solution)/shard_map/ppermute | solution.py:704
  156.1 1.5 collective-permute-start.33
  158.3 3.3 %collective-permute-done.31.refs_6_ = bf16[128,1024]{1,0:T(8,128)(2,1)S(1)} collective-permute-done((bf16[128,1024]{1,0:T(8,128)(2,1)S(1)}, bf16[128,1024]{1,0:T(8,128)(2,1)S(1)}, u32[]{:S(2)}, u32[]{:S(2)}) %collective-permute-start.31) | collective-permute-done | bytes 262176 | tf_op jit(solution)/shard_map/ppermute | solution.py:704
  161.6 3.9 %collective-permute-done.33.refs_5_ = bf16[128,1024]{1,0:T(8,128)(2,1)S(1)} collective-permute-done((bf16[128,1024]{1,0:T(8,128)(2,1)S(1)}, bf16[128,1024]{1,0:T(8,128)(2,1)S(1)}, u32[]{:S(2)}, u32[]{:S(2)}) %collective-permute-start.33) | collective-permute-done | bytes 262176 | tf_op jit(solution)/shard_map/ppermute | solution.py:704
  165.7 1.6 collective-permute-start.37
  167.3 1.5 collective-permute-start.35
  169.6 4.8 %collective-permute-start.38 = (f32[1,512]{1,0:T(1,128)S(1)}, f32[1,512]{1,0:T(1,128)S(1)}, u32[]{:S(2)}, u32[]{:S(2)}) collective-permute-start(f32[1,512]{1,0:T(1,128)S(1)} %slice_add_fusion.1), channel_id=1, source_target_pairs={{0,1},{1,0},{2,3},{3,2},{4,5},{5,4},{6,7},{7,6},{8,9},{9,8},{10,11... | collective-permute-start | bytes 6152 | tf_op jit(solution)/shard_map/ppermute | solution.py:713
  174.5 2.7 %unpack.4.refs_1_ = f32[1024,1024]{1,0:T(8,128)} custom-call(s32[2]{0:T(128)S(1)} %copy-done.8, bf16[128,1024]{1,0:T(8,128)(2,1)S(1)} %slice.58.refs_0_, bf16[128,1024]{1,0:T(8,128)(2,1)S(1)} %collective-permute-done.27.refs_1_, bf16[128,1024]{1,0:T(8,128)(2,1)S(1)} %collective-permute-done.28.refs_2_, ...), custom_call_target="tpu_custom_call" | custom-call | bytes 6029312 | tf_op jit(solution)/shard_map/unpack/pallas_call | solution.py:43
  177.9 3.6 %collective-permute-start.43 = (bf16[320,512]{1,0:T(8,128)(2,1)S(1)}, bf16[320,512]{1,0:T(8,128)(2,1)S(1)}, u32[]{:S(2)}, u32[]{:S(2)}) collective-permute-start(bf16[320,512]{1,0:T(8,128)(2,1)S(1)} %row_sums.1.mine_ref), channel_id=1, source_target_pairs={{0,1},{1,0},{2,3},{3,2},{4,5},{5,4},{6,7},{7,6},{8,9},{9,8},{10,11... | collective-permute-start | bytes 983048 | tf_op jit(solution)/shard_map/ppermute | solution.py:713
  182.7 1.4 unpack.5
  184.1 2.0 %feature_step.1 = (f32[320,512]{1,0:T(8,128)}, f32[1,1024]{1,0:T(1,128)}) custom-call(s32[2]{0:T(128)S(1)} %copy-done.8, f32[320,512]{1,0:T(8,128)S(1)} %self_feature.1.self_ref, bf16[320,512]{1,0:T(8,128)(2,1)S(1)} %row_sums.1.mine_ref, bf16[320,512]{1,0:T(8,128)(2,1)S(1)} %collective-permute-done.43.other_ref, f32[1,512]{1,0:T(1,128)S(1)} %slice_add_fusion.1, ...), custom_call_target="tpu_custom_call" | custom-call | flops 335544320 | bytes 4071424 | tf_op jit(solution)/shard_map/feature_step/pallas_call | solution.py:43
  186.2 1.4 collective-permute-done.39.refs_3_
  188.9 2.0 %unpack.6.refs_4_ = f32[1024,1024]{1,0:T(8,128)} custom-call(s32[2]{0:T(128)S(1)} %copy-done.8, bf16[256,512]{1,0:T(8,128)(2,1)S(1)} %slice.57.refs_0_, bf16[256,512]{1,0:T(8,128)(2,1)S(1)} %collective-permute-done.34.refs_1_, bf16[256,512]{1,0:T(8,128)(2,1)S(1)} %collective-permute-done.35.refs_2_, bf16[256,512]{1,0:T(8,128)(2,1)S(1)} %collective-permute-done.39.refs_3_), custom_call_target="tpu_custom_call" | custom-call | bytes 5242880 | tf_op jit(solution)/shard_map/unpack/pallas_call | solution.py:43
  191.0 2.0 %unpack.7 = f32[1024,1024]{1,0:T(8,128)} custom-call(s32[2]{0:T(128)S(1)} %copy-done.8, bf16[256,512]{1,0:T(8,128)(2,1)S(1)} %collective-permute-done.40.refs_0_, bf16[256,512]{1,0:T(8,128)(2,1)S(1)} %collective-permute-done.41.refs_1_, bf16[256,512]{1,0:T(8,128)(2,1)S(1)} %collective-permute-done.42.refs_2_, ...), custom_call_target="tpu_custom_call", output_to_operand_aliasing={{}: (5, {})} | custom-call | bytes 9437184 | tf_op jit(solution)/shard_map/unpack/pallas_call | solution.py:43
  (108 shorter events, 35.9 us)
Async XLA Ops:
  2.4 13.3 %collective-permute-start.2 = (bf16[160,1024]{1,0:T(8,128)(2,1)}, bf16[160,1024]{1,0:T(8,128)(2,1)}, u32[]{:S(2)}, u32[]{:S(2)}) collective-permute-start(bf16[160,1024]{1,0:T(8,128)(2,1)} %constant_dynamic-slice_fusion), channel_id=1, source_target_pairs={{0,16},{1,9},{2,18},{3,11},{4,20},{5,13},{6,22},{7,15},{8,24},{9,1... | collective-permute-start | bytes 983048 | tf_op jit(solution)/shard_map/ppermute | solution.py:704
  7.3 3.1 %collective-permute-start = (s32[32,320]{1,0:T(8,128)}, s32[32,320]{1,0:T(8,128)S(1)}, u32[]{:S(2)}, u32[]{:S(2)}) collective-permute-start(s32[32,320]{1,0:T(8,128)} %sort_slots.1), channel_id=1, source_target_pairs={{0,1},{1,0},{2,3},{3,2},{4,5},{5,4},{6,7},{7,6},{8,9},{9,8},{10,11... | collective-permute-start | bytes 122888 | tf_op jit(solution)/shard_map/ppermute | solution.py:713
  11.9 3.8 %collective-permute-start.1 = (s32[64,320]{1,0:T(8,128)S(1)}, s32[64,320]{1,0:T(8,128)S(1)}, u32[]{:S(2)}, u32[]{:S(2)}) collective-permute-start(s32[64,320]{1,0:T(8,128)S(1)} %pad_add_fusion.1.own_ref), channel_id=1, source_target_pairs={{0,4},{1,3},{2,6},{3,1},{4,0},{5,7},{6,2},{7,5},{8,12},{9,11},{10,... | collective-permute-start | bytes 245768 | tf_op jit(solution)/shard_map/ppermute | solution.py:704
  17.6 16.7 %collective-permute-start.4 = (bf16[320,1024]{1,0:T(8,128)(2,1)}, bf16[320,1024]{1,0:T(8,128)(2,1)}, u32[]{:S(2)}, u32[]{:S(2)}) collective-permute-start(bf16[320,1024]{1,0:T(8,128)(2,1)} %pad_maximum_fusion), channel_id=1, source_target_pairs={{0,8},{1,17},{2,10},{3,19},{4,12},{5,21},{6,14},{7,23},{8,0},{9,25... | collective-permute-start | bytes 1966088 | tf_op jit(solution)/shard_map/ppermute | solution.py:704
  18.3 14.8 %collective-permute-start.5 = (bf16[160,1024]{1,0:T(8,128)(2,1)}, bf16[160,1024]{1,0:T(8,128)(2,1)}, u32[]{:S(2)}, u32[]{:S(2)}) collective-permute-start(bf16[160,1024]{1,0:T(8,128)(2,1)} %collective-permute-done.2.refs_1_.refs_8_), channel_id=1, source_target_pairs={{0,1},{1,0},{2,3},{3,2},{4,5},{5,4},{6,7},{7,6},{8,9},{9,8},{10,11... | collective-permute-start | bytes 983048 | tf_op jit(solution)/shard_map/ppermute | solution.py:713
  21.2 5.0 %collective-permute-start.3 = (s32[128,320]{1,0:T(8,128)S(1)}, s32[128,320]{1,0:T(8,128)}, u32[]{:S(2)}, u32[]{:S(2)}) collective-permute-start(s32[128,320]{1,0:T(8,128)S(1)} %pad_add_fusion), channel_id=1, source_target_pairs={{0,2},{1,5},{2,0},{3,7},{4,6},{5,1},{6,4},{7,3},{8,10},{9,13},{10,... | collective-permute-start | bytes 491528 | tf_op jit(solution)/shard_map/ppermute | solution.py:704
  34.4 3.7 %collective-permute-start.6 = (bf16[320,1024]{1,0:T(8,128)(2,1)}, bf16[320,1024]{1,0:T(8,128)(2,1)}, u32[]{:S(2)}, u32[]{:S(2)}) collective-permute-start(bf16[320,1024]{1,0:T(8,128)(2,1)} %collective-permute-done.4.refs_2_.refs_9_), channel_id=1, source_target_pairs={{0,1},{1,0},{2,3},{3,2},{4,5},{5,4},{6,7},{7,6},{8,9},{9,8},{10,11... | collective-permute-start | bytes 1966088 | tf_op jit(solution)/shard_map/ppermute | solution.py:713
  45.2 21.7 %collective-permute-start.10 = (bf16[1024,1024]{1,0:T(8,128)(2,1)}, bf16[1024,1024]{1,0:T(8,128)(2,1)}, u32[]{:S(2)}, u32[]{:S(2)}) collective-permute-start(bf16[1024,1024]{1,0:T(8,128)(2,1)} %w_in.7), channel_id=1, source_target_pairs={{0,1},{1,0},{2,3},{3,2},{4,5},{5,4},{6,7},{7,6},{8,9},{9,8},{10,11... | collective-permute-start | bytes 6291464 | tf_op jit(solution)/shard_map/ppermute | solution.py:713
  45.6 10.0 %collective-permute-start.7 = (f32[320,512]{1,0:T(8,128)}, f32[320,512]{1,0:T(8,128)}, u32[]{:S(2)}, u32[]{:S(2)}) collective-permute-start(f32[320,512]{1,0:T(8,128)} %get-tuple-element.107), channel_id=1, source_target_pairs={{0,2},{1,5},{2,0},{3,7},{4,6},{5,1},{6,4},{7,3},{8,10},{9,13},{10,... | collective-permute-start | bytes 1966088 | tf_op jit(solution)/shard_map/ppermute | solution.py:704
  54.1 12.8 %collective-permute-start.9 = (f32[320,512]{1,0:T(8,128)}, f32[320,512]{1,0:T(8,128)S(1)}, u32[]{:S(2)}, u32[]{:S(2)}) collective-permute-start(f32[320,512]{1,0:T(8,128)} %get-tuple-element.108), channel_id=1, source_target_pairs={{0,2},{1,5},{2,0},{3,7},{4,6},{5,1},{6,4},{7,3},{8,10},{9,13},{10,... | collective-permute-start | bytes 1966088 | tf_op jit(solution)/shard_map/ppermute | solution.py:704
  57.1 14.6 %collective-permute-start.8 = (f32[320,512]{1,0:T(8,128)S(1)}, f32[320,512]{1,0:T(8,128)S(1)}, u32[]{:S(2)}, u32[]{:S(2)}) collective-permute-start(f32[320,512]{1,0:T(8,128)S(1)} %add.35), channel_id=1, source_target_pairs={{0,4},{1,3},{2,6},{3,1},{4,0},{5,7},{6,2},{7,5},{8,12},{9,11},{10,... | collective-permute-start | bytes 1966088 | tf_op jit(solution)/shard_map/ppermute | solution.py:704
  71.9 2.8 %collective-permute-start.11 = (bf16[320,512]{1,0:T(8,128)(2,1)S(1)}, bf16[320,512]{1,0:T(8,128)(2,1)S(1)}, u32[]{:S(2)}, u32[]{:S(2)}) collective-permute-start(bf16[320,512]{1,0:T(8,128)(2,1)S(1)} %divide_convert_fusion.mine_ref), channel_id=1, source_target_pairs={{0,1},{1,0},{2,3},{3,2},{4,5},{5,4},{6,7},{7,6},{8,9},{9,8},{10,11... | collective-permute-start | bytes 983048 | tf_op jit(solution)/shard_map/ppermute | solution.py:713
  78.2 27.4 %copy-start.4 = (bf16[320,1024]{1,0:T(8,128)(2,1)}, bf16[320,1024]{1,0:T(8,128)(2,1)S(1)}, u32[]{:S(2)}) copy-start(bf16[320,1024]{1,0:T(8,128)(2,1)S(1)} %get-tuple-element.129.refs_0_.grad_ref) | copy-start | bytes 1966084
  78.3 7.4 %collective-permute-start.13 = (bf16[160,1024]{1,0:T(8,128)(2,1)S(1)}, bf16[160,1024]{1,0:T(8,128)(2,1)S(1)}, u32[]{:S(2)}, u32[]{:S(2)}) collective-permute-start(bf16[160,1024]{1,0:T(8,128)(2,1)S(1)} %get-tuple-element.119), channel_id=1, source_target_pairs={{0,2},{1,5},{2,0},{3,7},{4,6},{5,1},{6,4},{7,3},{8,10},{9,13},{10,... | collective-permute-start | bytes 983048 | tf_op jit(solution)/shard_map/ppermute | solution.py:704
  79.6 8.7 %collective-permute-start.12 = (bf16[160,1024]{1,0:T(8,128)(2,1)S(1)}, bf16[160,1024]{1,0:T(8,128)(2,1)S(1)}, u32[]{:S(2)}, u32[]{:S(2)}) collective-permute-start(bf16[160,1024]{1,0:T(8,128)(2,1)S(1)} %get-tuple-element.119), channel_id=1, source_target_pairs={{0,4},{1,3},{2,6},{3,1},{4,0},{5,7},{6,2},{7,5},{8,12},{9,11},{10,... | collective-permute-start | bytes 983048 | tf_op jit(solution)/shard_map/ppermute | solution.py:704
  80.4 11.2 %collective-permute-start.15 = (bf16[640,256]{1,0:T(8,128)(2,1)S(1)}, bf16[640,256]{1,0:T(8,128)(2,1)S(1)}, u32[]{:S(2)}, u32[]{:S(2)}) collective-permute-start(bf16[640,256]{1,0:T(8,128)(2,1)S(1)} %get-tuple-element.123), channel_id=1, source_target_pairs={{0,2},{1,5},{2,0},{3,7},{4,6},{5,1},{6,4},{7,3},{8,10},{9,13},{10,... | collective-permute-start | bytes 983048 | tf_op jit(solution)/shard_map/ppermute | solution.py:704
  88.3 6.8 %collective-permute-start.14 = (bf16[160,1024]{1,0:T(8,128)(2,1)S(1)}, bf16[160,1024]{1,0:T(8,128)(2,1)S(1)}, u32[]{:S(2)}, u32[]{:S(2)}) collective-permute-start(bf16[160,1024]{1,0:T(8,128)(2,1)S(1)} %collective-permute-done.12.refs_1_), channel_id=1, source_target_pairs={{0,2},{1,5},{2,0},{3,7},{4,6},{5,1},{6,4},{7,3},{8,10},{9,13},{10,... | collective-permute-start | bytes 983048 | tf_op jit(solution)/shard_map/ppermute | solution.py:704
  91.6 9.1 %collective-permute-start.16 = (bf16[640,256]{1,0:T(8,128)(2,1)S(1)}, bf16[640,256]{1,0:T(8,128)(2,1)S(1)}, u32[]{:S(2)}, u32[]{:S(2)}) collective-permute-start(bf16[640,256]{1,0:T(8,128)(2,1)S(1)} %pad_maximum_fusion.1), channel_id=1, source_target_pairs={{0,4},{1,3},{2,6},{3,1},{4,0},{5,7},{6,2},{7,5},{8,12},{9,11},{10,... | collective-permute-start | bytes 983048 | tf_op jit(solution)/shard_map/ppermute | solution.py:704
  91.7 9.4 %collective-permute-start.17 = (bf16[160,1024]{1,0:T(8,128)(2,1)S(1)}, bf16[160,1024]{1,0:T(8,128)(2,1)S(1)}, u32[]{:S(2)}, u32[]{:S(2)}) collective-permute-start(bf16[160,1024]{1,0:T(8,128)(2,1)S(1)} %collective-permute-done.12.refs_1_), channel_id=1, source_target_pairs={{0,1},{1,0},{2,3},{3,2},{4,5},{5,4},{6,7},{7,6},{8,9},{9,8},{10,11... | collective-permute-start | bytes 983048 | tf_op jit(solution)/shard_map/ppermute | solution.py:713
  94.0 7.1 %collective-permute-start.18 = (bf16[160,1024]{1,0:T(8,128)(2,1)S(1)}, bf16[160,1024]{1,0:T(8,128)(2,1)S(1)}, u32[]{:S(2)}, u32[]{:S(2)}) collective-permute-start(bf16[160,1024]{1,0:T(8,128)(2,1)S(1)} %collective-permute-done.13.refs_2_), channel_id=1, source_target_pairs={{0,1},{1,0},{2,3},{3,2},{4,5},{5,4},{6,7},{7,6},{8,9},{9,8},{10,11... | collective-permute-start | bytes 983048 | tf_op jit(solution)/shard_map/ppermute | solution.py:713
  100.7 1.6 collective-permute-start.19
  105.7 9.7 %collective-permute-start.20 = (bf16[144,1024]{1,0:T(8,128)(2,1)S(1)}, bf16[144,1024]{1,0:T(8,128)(2,1)S(1)}, u32[]{:S(2)}, u32[]{:S(2)}) collective-permute-start(bf16[144,1024]{1,0:T(8,128)(2,1)S(1)} %get-tuple-element.142), channel_id=1, source_target_pairs={{0,8},{1,17},{2,10},{3,19},{4,12},{5,21},{6,14},{7,23},{8,0},{9,25... | collective-permute-start | bytes 884744 | tf_op jit(solution)/shard_map/ppermute | solution.py:704
  115.4 28.1 %copy-start.1 = (bf16[1024,1024]{1,0:T(8,128)(2,1)S(1)}, bf16[1024,1024]{1,0:T(8,128)(2,1)}, u32[]{:S(2)}) copy-start(bf16[1024,1024]{1,0:T(8,128)(2,1)} %w_in.7) | copy-start | bytes 6291460
  115.4 28.1 %copy-start.5 = (bf16[320,1024]{1,0:T(8,128)(2,1)S(1)}, bf16[320,1024]{1,0:T(8,128)(2,1)}, u32[]{:S(2)}) copy-start(bf16[320,1024]{1,0:T(8,128)(2,1)} %copy-done.4) | copy-start | bytes 1966084
  115.4 8.6 %collective-permute-start.21 = (bf16[528,512]{1,0:T(8,128)(2,1)S(1)}, bf16[528,512]{1,0:T(8,128)(2,1)S(1)}, u32[]{:S(2)}, u32[]{:S(2)}) collective-permute-start(bf16[528,512]{1,0:T(8,128)(2,1)S(1)} %get-tuple-element.144), channel_id=1, source_target_pairs={{0,2},{1,5},{2,0},{3,7},{4,6},{5,1},{6,4},{7,3},{8,10},{9,13},{10,... | collective-permute-start | bytes 1622024 | tf_op jit(solution)/shard_map/ppermute | solution.py:704
  116.7 21.8 %collective-permute-start.24 = (bf16[320,512]{1,0:T(8,128)(2,1)S(1)}, bf16[320,512]{1,0:T(8,128)(2,1)S(1)}, u32[]{:S(2)}, u32[]{:S(2)}) collective-permute-start(bf16[320,512]{1,0:T(8,128)(2,1)S(1)} %get-tuple-element.150), channel_id=1, source_target_pairs={{0,8},{1,17},{2,10},{3,19},{4,12},{5,21},{6,14},{7,23},{8,0},{9,25... | collective-permute-start | bytes 983048 | tf_op jit(solution)/shard_map/ppermute | solution.py:704
  117.8 21.7 %collective-permute-start.25 = (bf16[320,512]{1,0:T(8,128)(2,1)S(1)}, bf16[320,512]{1,0:T(8,128)(2,1)S(1)}, u32[]{:S(2)}, u32[]{:S(2)}) collective-permute-start(bf16[320,512]{1,0:T(8,128)(2,1)S(1)} %get-tuple-element.151), channel_id=1, source_target_pairs={{0,8},{1,17},{2,10},{3,19},{4,12},{5,21},{6,14},{7,23},{8,0},{9,25... | collective-permute-start | bytes 983048 | tf_op jit(solution)/shard_map/ppermute | solution.py:704
  119.7 18.8 %collective-permute-start.23 = (bf16[144,1024]{1,0:T(8,128)(2,1)S(1)}, bf16[144,1024]{1,0:T(8,128)(2,1)S(1)}, u32[]{:S(2)}, u32[]{:S(2)}) collective-permute-start(bf16[144,1024]{1,0:T(8,128)(2,1)S(1)} %merge.3), channel_id=1, source_target_pairs={{0,16},{1,9},{2,18},{3,11},{4,20},{5,13},{6,22},{7,15},{8,24},{9,1... | collective-permute-start | bytes 884744 | tf_op jit(solution)/shard_map/ppermute | solution.py:704
  124.6 14.8 %collective-permute-start.22 = (bf16[272,512]{1,0:T(8,128)(2,1)S(1)}, bf16[272,512]{1,0:T(8,128)(2,1)S(1)}, u32[]{:S(2)}, u32[]{:S(2)}) collective-permute-start(bf16[272,512]{1,0:T(8,128)(2,1)S(1)} %get-tuple-element.146), channel_id=1, source_target_pairs={{0,4},{1,3},{2,6},{3,1},{4,0},{5,7},{6,2},{7,5},{8,12},{9,11},{10,... | collective-permute-start | bytes 835592 | tf_op jit(solution)/shard_map/ppermute | solution.py:704
  140.1 14.9 %collective-permute-start.26 = (bf16[272,512]{1,0:T(8,128)(2,1)S(1)}, bf16[272,512]{1,0:T(8,128)(2,1)S(1)}, u32[]{:S(2)}, u32[]{:S(2)}) collective-permute-start(bf16[272,512]{1,0:T(8,128)(2,1)S(1)} %merge.4.keep_ref), channel_id=1, source_target_pairs={{0,8},{1,17},{2,10},{3,19},{4,12},{5,21},{6,14},{7,23},{8,0},{9,25... | collective-permute-start | bytes 835592 | tf_op jit(solution)/shard_map/ppermute | solution.py:704
  142.6 6.0 %collective-permute-start.29 = (bf16[128,1024]{1,0:T(8,128)(2,1)S(1)}, bf16[128,1024]{1,0:T(8,128)(2,1)S(1)}, u32[]{:S(2)}, u32[]{:S(2)}) collective-permute-start(bf16[128,1024]{1,0:T(8,128)(2,1)S(1)} %slice.58.refs_0_), channel_id=1, source_target_pairs={{0,2},{1,5},{2,0},{3,7},{4,6},{5,1},{6,4},{7,3},{8,10},{9,13},{10,... | collective-permute-start | bytes 786440 | tf_op jit(solution)/shard_map/ppermute | solution.py:704
  142.6 7.1 %collective-permute-start.28 = (bf16[128,1024]{1,0:T(8,128)(2,1)S(1)}, bf16[128,1024]{1,0:T(8,128)(2,1)S(1)}, u32[]{:S(2)}, u32[]{:S(2)}) collective-permute-start(bf16[128,1024]{1,0:T(8,128)(2,1)S(1)} %slice.58.refs_0_), channel_id=1, source_target_pairs={{0,4},{1,3},{2,6},{3,1},{4,0},{5,7},{6,2},{7,5},{8,12},{9,11},{10,... | collective-permute-start | bytes 786440 | tf_op jit(solution)/shard_map/ppermute | solution.py:704
  143.4 11.5 %collective-permute-start.27 = (bf16[128,1024]{1,0:T(8,128)(2,1)S(1)}, bf16[128,1024]{1,0:T(8,128)(2,1)S(1)}, u32[]{:S(2)}, u32[]{:S(2)}) collective-permute-start(bf16[128,1024]{1,0:T(8,128)(2,1)S(1)} %slice.58.refs_0_), channel_id=1, source_target_pairs={{0,8},{1,17},{2,10},{3,19},{4,12},{5,21},{6,14},{7,23},{8,0},{9,25... | collective-permute-start | bytes 786440 | tf_op jit(solution)/shard_map/ppermute | solution.py:704
  155.6 10.0 %collective-permute-start.30 = (bf16[272,512]{1,0:T(8,128)(2,1)S(1)}, bf16[272,512]{1,0:T(8,128)(2,1)S(1)}, u32[]{:S(2)}, u32[]{:S(2)}) collective-permute-start(bf16[272,512]{1,0:T(8,128)(2,1)S(1)} %merge.5), channel_id=1, source_target_pairs={{0,16},{1,9},{2,18},{3,11},{4,20},{5,13},{6,22},{7,15},{8,24},{9,1... | collective-permute-start | bytes 835592 | tf_op jit(solution)/shard_map/ppermute | solution.py:704
  156.1 5.5 %collective-permute-start.31 = (bf16[128,1024]{1,0:T(8,128)(2,1)S(1)}, bf16[128,1024]{1,0:T(8,128)(2,1)S(1)}, u32[]{:S(2)}, u32[]{:S(2)}) collective-permute-start(bf16[128,1024]{1,0:T(8,128)(2,1)S(1)} %collective-permute-done.28.refs_2_), channel_id=1, source_target_pairs={{0,2},{1,5},{2,0},{3,7},{4,6},{5,1},{6,4},{7,3},{8,10},{9,13},{10,... | collective-permute-start | bytes 786440 | tf_op jit(solution)/shard_map/ppermute | solution.py:704
  156.1 9.5 %collective-permute-start.33 = (bf16[128,1024]{1,0:T(8,128)(2,1)S(1)}, bf16[128,1024]{1,0:T(8,128)(2,1)S(1)}, u32[]{:S(2)}, u32[]{:S(2)}) collective-permute-start(bf16[128,1024]{1,0:T(8,128)(2,1)S(1)} %collective-permute-done.27.refs_1_), channel_id=1, source_target_pairs={{0,2},{1,5},{2,0},{3,7},{4,6},{5,1},{6,4},{7,3},{8,10},{9,13},{10,... | collective-permute-start | bytes 786440 | tf_op jit(solution)/shard_map/ppermute | solution.py:704
  157.6 8.0 %collective-permute-start.32 = (bf16[128,1024]{1,0:T(8,128)(2,1)S(1)}, bf16[128,1024]{1,0:T(8,128)(2,1)S(1)}, u32[]{:S(2)}, u32[]{:S(2)}) collective-permute-start(bf16[128,1024]{1,0:T(8,128)(2,1)S(1)} %collective-permute-done.27.refs_1_), channel_id=1, source_target_pairs={{0,4},{1,3},{2,6},{3,1},{4,0},{5,7},{6,2},{7,5},{8,12},{9,11},{10,... | collective-permute-start | bytes 786440 | tf_op jit(solution)/shard_map/ppermute | solution.py:704
  165.7 11.5 %collective-permute-start.37 = (bf16[320,512]{1,0:T(8,128)(2,1)S(1)}, bf16[320,512]{1,0:T(8,128)(2,1)S(1)}, u32[]{:S(2)}, u32[]{:S(2)}) collective-permute-start(bf16[320,512]{1,0:T(8,128)(2,1)S(1)} %add_convert_fusion), channel_id=1, source_target_pairs={{0,16},{1,9},{2,18},{3,11},{4,20},{5,13},{6,22},{7,15},{8,24},{9,1... | collective-permute-start | bytes 983048 | tf_op jit(solution)/shard_map/ppermute | solution.py:704
  167.3 9.9 %collective-permute-start.36 = (bf16[128,1024]{1,0:T(8,128)(2,1)S(1)}, bf16[128,1024]{1,0:T(8,128)(2,1)S(1)}, u32[]{:S(2)}, u32[]{:S(2)}) collective-permute-start(bf16[128,1024]{1,0:T(8,128)(2,1)S(1)} %collective-permute-done.32.refs_3_), channel_id=1, source_target_pairs={{0,2},{1,5},{2,0},{3,7},{4,6},{5,1},{6,4},{7,3},{8,10},{9,13},{10,... | collective-permute-start | bytes 786440 | tf_op jit(solution)/shard_map/ppermute | solution.py:704
  167.3 9.9 %collective-permute-start.35 = (bf16[256,512]{1,0:T(8,128)(2,1)S(1)}, bf16[256,512]{1,0:T(8,128)(2,1)S(1)}, u32[]{:S(2)}, u32[]{:S(2)}) collective-permute-start(bf16[256,512]{1,0:T(8,128)(2,1)S(1)} %slice.57.refs_0_), channel_id=1, source_target_pairs={{0,2},{1,5},{2,0},{3,7},{4,6},{5,1},{6,4},{7,3},{8,10},{9,13},{10,... | collective-permute-start | bytes 786440 | tf_op jit(solution)/shard_map/ppermute | solution.py:704
  168.8 8.4 %collective-permute-start.34 = (bf16[256,512]{1,0:T(8,128)(2,1)S(1)}, bf16[256,512]{1,0:T(8,128)(2,1)S(1)}, u32[]{:S(2)}, u32[]{:S(2)}) collective-permute-start(bf16[256,512]{1,0:T(8,128)(2,1)S(1)} %slice.57.refs_0_), channel_id=1, source_target_pairs={{0,4},{1,3},{2,6},{3,1},{4,0},{5,7},{6,2},{7,5},{8,12},{9,11},{10,... | collective-permute-start | bytes 786440 | tf_op jit(solution)/shard_map/ppermute | solution.py:704
  169.6 7.6 %collective-permute-start.38 = (f32[1,512]{1,0:T(1,128)S(1)}, f32[1,512]{1,0:T(1,128)S(1)}, u32[]{:S(2)}, u32[]{:S(2)}) collective-permute-start(f32[1,512]{1,0:T(1,128)S(1)} %slice_add_fusion.1), channel_id=1, source_target_pairs={{0,1},{1,0},{2,3},{3,2},{4,5},{5,4},{6,7},{7,6},{8,9},{9,8},{10,11... | collective-permute-start | bytes 6152 | tf_op jit(solution)/shard_map/ppermute | solution.py:713
  177.9 6.2 %collective-permute-start.43 = (bf16[320,512]{1,0:T(8,128)(2,1)S(1)}, bf16[320,512]{1,0:T(8,128)(2,1)S(1)}, u32[]{:S(2)}, u32[]{:S(2)}) collective-permute-start(bf16[320,512]{1,0:T(8,128)(2,1)S(1)} %row_sums.1.mine_ref), channel_id=1, source_target_pairs={{0,1},{1,0},{2,3},{3,2},{4,5},{5,4},{6,7},{7,6},{8,9},{9,8},{10,11... | collective-permute-start | bytes 983048 | tf_op jit(solution)/shard_map/ppermute | solution.py:713
  181.5 4.6 %collective-permute-start.40 = (bf16[256,512]{1,0:T(8,128)(2,1)S(1)}, bf16[256,512]{1,0:T(8,128)(2,1)S(1)}, u32[]{:S(2)}, u32[]{:S(2)}) collective-permute-start(bf16[256,512]{1,0:T(8,128)(2,1)S(1)} %slice.57.refs_0_), channel_id=1, source_target_pairs={{0,1},{1,0},{2,3},{3,2},{4,5},{5,4},{6,7},{7,6},{8,9},{9,8},{10,11... | collective-permute-start | bytes 786440 | tf_op jit(solution)/shard_map/ppermute | solution.py:713
  181.6 4.6 %collective-permute-start.42 = (bf16[256,512]{1,0:T(8,128)(2,1)S(1)}, bf16[256,512]{1,0:T(8,128)(2,1)S(1)}, u32[]{:S(2)}, u32[]{:S(2)}) collective-permute-start(bf16[256,512]{1,0:T(8,128)(2,1)S(1)} %collective-permute-done.35.refs_2_), channel_id=1, source_target_pairs={{0,1},{1,0},{2,3},{3,2},{4,5},{5,4},{6,7},{7,6},{8,9},{9,8},{10,11... | collective-permute-start | bytes 786440 | tf_op jit(solution)/shard_map/ppermute | solution.py:713
  182.0 4.1 %collective-permute-start.41 = (bf16[256,512]{1,0:T(8,128)(2,1)S(1)}, bf16[256,512]{1,0:T(8,128)(2,1)S(1)}, u32[]{:S(2)}, u32[]{:S(2)}) collective-permute-start(bf16[256,512]{1,0:T(8,128)(2,1)S(1)} %collective-permute-done.34.refs_1_), channel_id=1, source_target_pairs={{0,1},{1,0},{2,3},{3,2},{4,5},{5,4},{6,7},{7,6},{8,9},{9,8},{10,11... | collective-permute-start | bytes 786440 | tf_op jit(solution)/shard_map/ppermute | solution.py:713
  182.1 5.5 %collective-permute-start.39 = (bf16[256,512]{1,0:T(8,128)(2,1)S(1)}, bf16[256,512]{1,0:T(8,128)(2,1)S(1)}, u32[]{:S(2)}, u32[]{:S(2)}) collective-permute-start(bf16[256,512]{1,0:T(8,128)(2,1)S(1)} %collective-permute-done.34.refs_1_), channel_id=1, source_target_pairs={{0,2},{1,5},{2,0},{3,7},{4,6},{5,1},{6,4},{7,3},{8,10},{9,13},{10,... | collective-permute-start | bytes 786440 | tf_op jit(solution)/shard_map/ppermute | solution.py:704
  187.6 3.3 %collective-permute-start.44 = (bf16[256,512]{1,0:T(8,128)(2,1)S(1)}, bf16[256,512]{1,0:T(8,128)(2,1)S(1)}, u32[]{:S(2)}, u32[]{:S(2)}) collective-permute-start(bf16[256,512]{1,0:T(8,128)(2,1)S(1)} %collective-permute-done.39.refs_3_), channel_id=1, source_target_pairs={{0,1},{1,0},{2,3},{3,2},{4,5},{5,4},{6,7},{7,6},{8,9},{9,8},{10,11... | collective-permute-start | bytes 786440 | tf_op jit(solution)/shard_map/ppermute | solution.py:713
  (11 other events, 81.6 us)

commit v5 on v4

--- a/solution.py
+++ b/solution.py
@@ -744,10 +744,9 @@
     keep, middle, own_send = more_sums(place, [high], [low], matrix, 0, 3)
     came_own = plane_swap(own_send, 0)
     last = plane_swap(middle + came, 1)
-    came_own, w_other = fence((came_own, w_other))
     self_part = self_product(place, features, w_weight, w_other, w_bias[None])
-    last, self_part, keep = fence((last, self_part, keep))
-    mean_half = ((keep + came_own + last) / weight_sums[:rows, 0:1]).astype(BF16)
+    came_own, self_part, keep, weight_sum = fence((came_own, self_part, keep, weight_sums[:rows, 0]))
+    mean_half = ((keep + came_own + last) / weight_sum[:, None]).astype(BF16)
 
     mean_other = trade(mean_half)
     own_slice, next_slice, send_slices = plane_slices(place, features, mean_half, mean_other)

time: 194 us -> 193 us (level)
  no operation moved by 1% of the time
where the time goes in v5:
time: 193 us
  waiting for transfers between devices  73.7 us (38%)
  Pallas kernels  58.2 us (30%)
  starting transfers between devices  48 us (25%)
  other arithmetic  6.61 us (3%)
  local copies, waits for them, and re-layouts  4.66 us (2%)
    ppermute x31, waiting for transfers between devices, swap(): return lax.ppermute(value, ('nodes', 'stream'), pairs)  67.7 us
    pallas_call x20, Pallas kernels, call(): pl.pallas_call(kernel, name=name, out_shape=list(outs), in_specs=spaced(p...  58.2 us
    ppermute x31, starting transfers between devices, swap(): return lax.ppermute(value, ('nodes', 'stream'), pairs)  26.7 us
    ppermute x14, starting transfers between devices, trade(): return lax.ppermute(value, 'stream', [(0, 1), (1, 0)])  21.3 us
    ppermute x14, waiting for transfers between devices, trade(): return lax.ppermute(value, 'stream', [(0, 1), (1, 0)])  6.05 us
  transfers between devices with their start and end apart: 45, of which 24 were waited for; matrix products, arithmetic and copies ran while one was open for 3% of the time, Pallas kernels for 21%

profile of v5, /device:TPU:1, one launch (start us, length us, event | category | flops | bytes accessed | tf_op | source)
XLA Modules:
  0.0 192.6 jit_solution(13826121209634041280)
XLA Ops:
  0.6 1.7 constant_dynamic-slice_fusion
  2.4 2.1 %collective-permute-start.2 = (bf16[160,1024]{1,0:T(8,128)(2,1)}, bf16[160,1024]{1,0:T(8,128)(2,1)}, u32[]{:S(2)}, u32[]{:S(2)}) collective-permute-start(bf16[160,1024]{1,0:T(8,128)(2,1)} %constant_dynamic-slice_fusion), channel_id=1, source_target_pairs={{0,16},{1,9},{2,18},{3,11},{4,20},{5,13},{6,22},{7,15},{8,24},{9,1... | collective-permute-start | bytes 983048 | tf_op jit(solution)/shard_map/ppermute | solution.py:704
  5.1 2.2 %sort_slots.1 = s32[32,320]{1,0:T(8,128)} custom-call(s32[2]{0:T(128)} %pad_add_fusion.2.place_ref, s32[25,320]{1,0:T(8,128)} %bitcast.12, s32[25,320]{1,0:T(8,128)} %bitcast.13, s32[25,320]{1,0:T(8,128)} %bitcast.14), custom_call_target="tpu_custom_call" | custom-call | bytes 136960 | tf_op jit(solution)/shard_map/sort_slots/pallas_call | solution.py:43
  7.3 2.0 %collective-permute-start = (s32[32,320]{1,0:T(8,128)}, s32[32,320]{1,0:T(8,128)S(1)}, u32[]{:S(2)}, u32[]{:S(2)}) collective-permute-start(s32[32,320]{1,0:T(8,128)} %sort_slots.1), channel_id=1, source_target_pairs={{0,1},{1,0},{2,3},{3,2},{4,5},{5,4},{6,7},{7,6},{8,9},{9,8},{10,11... | collective-permute-start | bytes 122888 | tf_op jit(solution)/shard_map/ppermute | solution.py:713
  13.1 2.6 %collective-permute-done.1.next_ref = s32[64,320]{1,0:T(8,128)S(1)} collective-permute-done((s32[64,320]{1,0:T(8,128)S(1)}, s32[64,320]{1,0:T(8,128)S(1)}, u32[]{:S(2)}, u32[]{:S(2)}) %collective-permute-start.1) | collective-permute-done | bytes 81952 | tf_op jit(solution)/shard_map/ppermute | solution.py:704
  15.6 2.0 %pad_maximum_fusion = bf16[320,1024]{1,0:T(8,128)(2,1)} fusion(bf16[160,1024]{1,0:T(8,128)(2,1)} %collective-permute-done.2.refs_1_.refs_8_, bf16[160,1024]{1,0:T(8,128)(2,1)} %constant_dynamic-slice_fusion), kind=kLoop, calls=%fused_computation | loop fusion | flops 1310720 | bytes 1310720 | tf_op jit(solution)/shard_map/concatenate | solution.py:733
  18.3 2.1 %collective-permute-start.5 = (bf16[160,1024]{1,0:T(8,128)(2,1)}, bf16[160,1024]{1,0:T(8,128)(2,1)}, u32[]{:S(2)}, u32[]{:S(2)}) collective-permute-start(bf16[160,1024]{1,0:T(8,128)(2,1)} %collective-permute-done.2.refs_1_.refs_8_), channel_id=1, source_target_pairs={{0,1},{1,0},{2,3},{3,2},{4,5},{5,4},{6,7},{7,6},{8,9},{9,8},{10,11... | collective-permute-start | bytes 983048 | tf_op jit(solution)/shard_map/ppermute | solution.py:713
  21.2 1.3 collective-permute-start.3
  22.5 3.7 %collective-permute-done.3.rest_ref = s32[128,320]{1,0:T(8,128)} collective-permute-done((s32[128,320]{1,0:T(8,128)S(1)}, s32[128,320]{1,0:T(8,128)}, u32[]{:S(2)}, u32[]{:S(2)}) %collective-permute-start.3) | collective-permute-done | bytes 163872 | tf_op jit(solution)/shard_map/ppermute | solution.py:704
  26.2 6.9 %slot_matrix.1 = (f32[1280,8]{1,0:T(8,128)}, bf16[1280,1280]{1,0:T(8,128)(2,1)}) custom-call(s32[2]{0:T(128)} %pad_add_fusion.2.place_ref, s32[64,320]{1,0:T(8,128)} %copy-done.12, s32[64,320]{1,0:T(8,128)} %copy-done.13, s32[128,320]{1,0:T(8,128)} %collective-permute-done.3.rest_ref), custom_call_target="tpu_custom_call" | custom-call | flops 1 | bytes 1 | tf_op jit(solution)/shard_map/slot_matrix/pallas_call | solution.py:43
  34.4 1.6 collective-permute-start.6
  36.0 2.1 %collective-permute-done.6.refs_4_.refs_11_ = bf16[320,1024]{1,0:T(8,128)(2,1)} collective-permute-done((bf16[320,1024]{1,0:T(8,128)(2,1)}, bf16[320,1024]{1,0:T(8,128)(2,1)}, u32[]{:S(2)}, u32[]{:S(2)}) %collective-permute-start.6) | collective-permute-done | bytes 655392 | tf_op jit(solution)/shard_map/ppermute | solution.py:713
  38.1 7.1 %first_sums.1 = (f32[320,512]{1,0:T(8,128)}, bf16[1280,512]{1,0:T(8,128)(2,1)}, bf16[1280,512]{1,0:T(8,128)(2,1)}) custom-call(s32[2]{0:T(128)} %pad_add_fusion.2.place_ref, f32[1,1024]{1,0:T(1,128)} %bitcast.16, bf16[1024,1024]{1,0:T(8,128)(2,1)} %q_in.3, bf16[1280,1280]{1,0:T(8,128)(2,1)} %get-tuple-element.99.matrix_in, bf16[320,1024]{1,0:T(8,128)(2,1)} %refs_7_.1, ...), custom_call_target="tpu_custom_call" | custom-call | flops 2181038080 | bytes 11276288 | tf_op jit(solution)/shard_map/first_sums/pallas_call | solution.py:43
  46.9 7.2 %more_sums.1 = (f32[320,512]{1,0:T(8,128)}, f32[320,512]{1,0:T(8,128)}, f32[320,512]{1,0:T(8,128)}) custom-call(s32[2]{0:T(128)} %pad_add_fusion.2.place_ref, bf16[1280,1280]{1,0:T(8,128)(2,1)} %get-tuple-element.99.matrix_in, bf16[1280,512]{1,0:T(8,128)(2,1)} %get-tuple-element.102.refs_0_.high_in, bf16[1280,512]{1,0:T(8,128)(2,1)} %get-tuple-element.103.refs_1_), custom_call_target="tpu_custom_call" | custom-call | flops 2516582400 | bytes 7864320 | tf_op jit(solution)/shard_map/more_sums/pallas_call | solution.py:43
  55.7 1.4 add.36
  60.5 3.0 %self_product.1.self_ref = f32[320,1024]{1,0:T(8,128)S(1)} custom-call(s32[2]{0:T(128)S(1)} %copy-done.8, bf16[320,1024]{1,0:T(8,128)(2,1)S(1)} %copy-done.2, f32[1,1024]{1,0:T(1,128)S(1)} %bitcast.11, bf16[1024,1024]{1,0:T(8,128)(2,1)S(1)} %copy-done, bf16[1024,1024]{1,0:T(8,128)(2,1)} %collective-permute-done.8.w_other_in), custom_call_target="tpu_custom_call" | custom-call | flops 671088640 | bytes 6164480 | tf_op jit(solution)/shard_map/self_product/pallas_call | solution.py:43
  63.6 3.4 %collective-permute-done.7 = f32[320,512]{1,0:T(8,128)S(1)} collective-permute-done((f32[320,512]{1,0:T(8,128)}, f32[320,512]{1,0:T(8,128)S(1)}, u32[]{:S(2)}, u32[]{:S(2)}) %collective-permute-start.7) | collective-permute-done | bytes 655392 | tf_op jit(solution)/shard_map/ppermute | solution.py:704
  66.9 4.8 %collective-permute-done.10 = f32[320,512]{1,0:T(8,128)S(1)} collective-permute-done((f32[320,512]{1,0:T(8,128)S(1)}, f32[320,512]{1,0:T(8,128)S(1)}, u32[]{:S(2)}, u32[]{:S(2)}) %collective-permute-start.10) | collective-permute-done | bytes 655392 | tf_op jit(solution)/shard_map/ppermute | solution.py:704
  72.0 1.6 collective-permute-done.11.other_ref
  73.6 3.5 %node_step.1 = (f32[320,1024]{1,0:T(8,128)}, bf16[320,1024]{1,0:T(8,128)(2,1)S(1)}, bf16[160,1024]{1,0:T(8,128)(2,1)S(1)}) custom-call(s32[2]{0:T(128)S(1)} %copy-done.8, bf16[320,512]{1,0:T(8,128)(2,1)S(1)} %divide_convert_fusion.mine_ref, bf16[320,512]{1,0:T(8,128)(2,1)S(1)} %collective-permute-done.11.other_ref, f32[320,1024]{1,0:T(8,128)S(1)} %self_product.1.self_ref, ...), custom_call_target="tpu_custom_call" | custom-call | flops 671088640 | bytes 9109504 | tf_op jit(solution)/shard_map/node_step/pallas_call | solution.py:43
  77.2 1.3 collective-permute-start.13
  80.3 3.4 %collective-permute-done.13.refs_2_ = bf16[160,1024]{1,0:T(8,128)(2,1)S(1)} collective-permute-done((bf16[160,1024]{1,0:T(8,128)(2,1)S(1)}, bf16[160,1024]{1,0:T(8,128)(2,1)S(1)}, u32[]{:S(2)}, u32[]{:S(2)}) %collective-permute-start.13) | collective-permute-done | bytes 327712 | tf_op jit(solution)/shard_map/ppermute | solution.py:704
  83.7 3.8 %collective-permute-done.12.refs_1_ = bf16[160,1024]{1,0:T(8,128)(2,1)S(1)} collective-permute-done((bf16[160,1024]{1,0:T(8,128)(2,1)S(1)}, bf16[160,1024]{1,0:T(8,128)(2,1)S(1)}, u32[]{:S(2)}, u32[]{:S(2)}) %collective-permute-start.12) | collective-permute-done | bytes 327712 | tf_op jit(solution)/shard_map/ppermute | solution.py:704
  87.5 3.0 %collective-permute-done.15.refs_8_ = bf16[640,256]{1,0:T(8,128)(2,1)S(1)} collective-permute-done((bf16[640,256]{1,0:T(8,128)(2,1)S(1)}, bf16[640,256]{1,0:T(8,128)(2,1)S(1)}, u32[]{:S(2)}, u32[]{:S(2)}) %collective-permute-start.15) | collective-permute-done | bytes 327712 | tf_op jit(solution)/shard_map/ppermute | solution.py:704
  91.3 1.8 collective-permute-start.17
  94.0 5.9 %collective-permute-done.16.refs_10_ = bf16[640,256]{1,0:T(8,128)(2,1)S(1)} collective-permute-done((bf16[640,256]{1,0:T(8,128)(2,1)S(1)}, bf16[640,256]{1,0:T(8,128)(2,1)S(1)}, u32[]{:S(2)}, u32[]{:S(2)}) %collective-permute-start.16) | collective-permute-done | bytes 327712 | tf_op jit(solution)/shard_map/ppermute | solution.py:704
  102.0 3.3 %self_weight.1 = (bf16[144,1024]{1,0:T(8,128)(2,1)S(1)}, bf16[144,1024]{1,0:T(8,128)(2,1)S(1)}) custom-call(s32[2]{0:T(128)S(1)} %copy-done.8, bf16[320,1024]{1,0:T(8,128)(2,1)S(1)} %get-tuple-element.127.refs_0_.grad_ref, bf16[160,1024]{1,0:T(8,128)(2,1)S(1)} %collective-permute-done.12.refs_1_, bf16[160,1024]{1,0:T(8,128)(2,1)S(1)} %collective-permute-done.13.refs_2_, ...), custom_call_target="tpu_custom_call" | custom-call | flops 671088640 | bytes 4194304 | tf_op jit(solution)/shard_map/self_weight/pallas_call | solution.py:43
  105.3 1.4 collective-permute-start.20
  106.7 8.4 %row_grad.1 = (bf16[640,512]{1,0:T(8,128)(2,1)S(1)}, bf16[320,512]{1,0:T(8,128)(2,1)S(1)}, bf16[320,512]{1,0:T(8,128)(2,1)S(1)}, bf16[528,512]{1,0:T(8,128)(2,1)S(1)}, bf16[528,512]{1,0:T(8,128)(2,1)S(1)}) custom-call(s32[2]{0:T(128)S(1)} %copy-done.8, f32[1280,8]{1,0:T(8,128)S(1)} %copy-done.9, bf16[1280,1280]{1,0:T(8,128)(2,1)} %get-tuple-element.99.matrix_in, ...), custom_call_target="tpu_custom_call" | custom-call | flops 4362076160 | bytes 16457728 | tf_op jit(solution)/shard_map/row_grad/pallas_call | solution.py:43
  117.0 1.3 collective-permute-start.25
  119.0 1.4 collective-permute-start.23
  120.4 3.3 %collective-permute-done.21.came_ref = bf16[528,512]{1,0:T(8,128)(2,1)S(1)} collective-permute-done((bf16[528,512]{1,0:T(8,128)(2,1)S(1)}, bf16[528,512]{1,0:T(8,128)(2,1)S(1)}, u32[]{:S(2)}, u32[]{:S(2)}) %collective-permute-start.21) | collective-permute-done | bytes 540704 | tf_op jit(solution)/shard_map/ppermute | solution.py:704
  125.1 12.5 %collective-permute-done.23 = bf16[144,1024]{1,0:T(8,128)(2,1)S(1)} collective-permute-done((bf16[144,1024]{1,0:T(8,128)(2,1)S(1)}, bf16[144,1024]{1,0:T(8,128)(2,1)S(1)}, u32[]{:S(2)}, u32[]{:S(2)}) %collective-permute-start.23) | collective-permute-done | bytes 294944 | tf_op jit(solution)/shard_map/ppermute | solution.py:704
  139.0 2.6 %collective-permute-start.26 = (bf16[272,512]{1,0:T(8,128)(2,1)S(1)}, bf16[272,512]{1,0:T(8,128)(2,1)S(1)}, u32[]{:S(2)}, u32[]{:S(2)}) collective-permute-start(bf16[272,512]{1,0:T(8,128)(2,1)S(1)} %merge.4.keep_ref), channel_id=1, source_target_pairs={{0,8},{1,17},{2,10},{3,19},{4,12},{5,21},{6,14},{7,23},{8,0},{9,25... | collective-permute-start | bytes 835592 | tf_op jit(solution)/shard_map/ppermute | solution.py:704
  142.8 2.3 %self_feature.1.self_ref = f32[320,512]{1,0:T(8,128)S(1)} custom-call(s32[2]{0:T(128)S(1)} %copy-done.8, bf16[320,1024]{1,0:T(8,128)(2,1)S(1)} %copy-done.5, bf16[1024,1024]{1,0:T(8,128)(2,1)S(1)} %copy-done.1, bf16[1024,1024]{1,0:T(8,128)(2,1)} %collective-permute-done.8.w_other_in), custom_call_target="tpu_custom_call" | custom-call | flops 335544320 | bytes 5505024 | tf_op jit(solution)/shard_map/self_feature/pallas_call | solution.py:43
  145.8 2.0 %collective-permute-done.29.refs_4_ = bf16[128,1024]{1,0:T(8,128)(2,1)S(1)} collective-permute-done((bf16[128,1024]{1,0:T(8,128)(2,1)S(1)}, bf16[128,1024]{1,0:T(8,128)(2,1)S(1)}, u32[]{:S(2)}, u32[]{:S(2)}) %collective-permute-start.29) | collective-permute-done | bytes 262176 | tf_op jit(solution)/shard_map/ppermute | solution.py:704
  147.7 2.1 %collective-permute-done.28.refs_2_ = bf16[128,1024]{1,0:T(8,128)(2,1)S(1)} collective-permute-done((bf16[128,1024]{1,0:T(8,128)(2,1)S(1)}, bf16[128,1024]{1,0:T(8,128)(2,1)S(1)}, u32[]{:S(2)}, u32[]{:S(2)}) %collective-permute-start.28) | collective-permute-done | bytes 262176 | tf_op jit(solution)/shard_map/ppermute | solution.py:704
  149.8 4.5 %collective-permute-done.27.refs_1_ = bf16[128,1024]{1,0:T(8,128)(2,1)S(1)} collective-permute-done((bf16[128,1024]{1,0:T(8,128)(2,1)S(1)}, bf16[128,1024]{1,0:T(8,128)(2,1)S(1)}, u32[]{:S(2)}, u32[]{:S(2)}) %collective-permute-start.27) | collective-permute-done | bytes 262176 | tf_op jit(solution)/shard_map/ppermute | solution.py:704
  157.0 3.5 %collective-permute-done.31.refs_6_ = bf16[128,1024]{1,0:T(8,128)(2,1)S(1)} collective-permute-done((bf16[128,1024]{1,0:T(8,128)(2,1)S(1)}, bf16[128,1024]{1,0:T(8,128)(2,1)S(1)}, u32[]{:S(2)}, u32[]{:S(2)}) %collective-permute-start.31) | collective-permute-done | bytes 262176 | tf_op jit(solution)/shard_map/ppermute | solution.py:704
  160.6 3.9 %collective-permute-done.33.refs_5_ = bf16[128,1024]{1,0:T(8,128)(2,1)S(1)} collective-permute-done((bf16[128,1024]{1,0:T(8,128)(2,1)S(1)}, bf16[128,1024]{1,0:T(8,128)(2,1)S(1)}, u32[]{:S(2)}, u32[]{:S(2)}) %collective-permute-start.33) | collective-permute-done | bytes 262176 | tf_op jit(solution)/shard_map/ppermute | solution.py:704
  166.9 7.2 %collective-permute-start.38 = (f32[1,512]{1,0:T(1,128)S(1)}, f32[1,512]{1,0:T(1,128)S(1)}, u32[]{:S(2)}, u32[]{:S(2)}) collective-permute-start(f32[1,512]{1,0:T(1,128)S(1)} %slice_add_fusion.1), channel_id=1, source_target_pairs={{0,1},{1,0},{2,3},{3,2},{4,5},{5,4},{6,7},{7,6},{8,9},{9,8},{10,11... | collective-permute-start | bytes 6152 | tf_op jit(solution)/shard_map/ppermute | solution.py:713
  174.1 2.7 %unpack.4.refs_1_ = f32[1024,1024]{1,0:T(8,128)} custom-call(s32[2]{0:T(128)S(1)} %copy-done.8, bf16[128,1024]{1,0:T(8,128)(2,1)S(1)} %slice.58.refs_0_, bf16[128,1024]{1,0:T(8,128)(2,1)S(1)} %collective-permute-done.27.refs_1_, bf16[128,1024]{1,0:T(8,128)(2,1)S(1)} %collective-permute-done.28.refs_2_, ...), custom_call_target="tpu_custom_call" | custom-call | bytes 6029312 | tf_op jit(solution)/shard_map/unpack/pallas_call | solution.py:43
  177.5 3.4 %collective-permute-start.43 = (bf16[320,512]{1,0:T(8,128)(2,1)S(1)}, bf16[320,512]{1,0:T(8,128)(2,1)S(1)}, u32[]{:S(2)}, u32[]{:S(2)}) collective-permute-start(bf16[320,512]{1,0:T(8,128)(2,1)S(1)} %row_sums.1.mine_ref), channel_id=1, source_target_pairs={{0,1},{1,0},{2,3},{3,2},{4,5},{5,4},{6,7},{7,6},{8,9},{9,8},{10,11... | collective-permute-start | bytes 983048 | tf_op jit(solution)/shard_map/ppermute | solution.py:713
  182.3 1.4 unpack.5
  183.7 2.0 %feature_step.1 = (f32[320,512]{1,0:T(8,128)}, f32[1,1024]{1,0:T(1,128)}) custom-call(s32[2]{0:T(128)S(1)} %copy-done.8, f32[320,512]{1,0:T(8,128)S(1)} %self_feature.1.self_ref, bf16[320,512]{1,0:T(8,128)(2,1)S(1)} %row_sums.1.mine_ref, bf16[320,512]{1,0:T(8,128)(2,1)S(1)} %collective-permute-done.43.other_ref, f32[1,512]{1,0:T(1,128)S(1)} %slice_add_fusion.1, ...), custom_call_target="tpu_custom_call" | custom-call | flops 335544320 | bytes 4071424 | tf_op jit(solution)/shard_map/feature_step/pallas_call | solution.py:43
  187.0 1.3 collective-permute-start.44
  188.3 2.0 %unpack.6.refs_4_ = f32[1024,1024]{1,0:T(8,128)} custom-call(s32[2]{0:T(128)S(1)} %copy-done.8, bf16[256,512]{1,0:T(8,128)(2,1)S(1)} %slice.57.refs_0_, bf16[256,512]{1,0:T(8,128)(2,1)S(1)} %collective-permute-done.34.refs_1_, bf16[256,512]{1,0:T(8,128)(2,1)S(1)} %collective-permute-done.35.refs_2_, bf16[256,512]{1,0:T(8,128)(2,1)S(1)} %collective-permute-done.39.refs_3_), custom_call_target="tpu_custom_call" | custom-call | bytes 5242880 | tf_op jit(solution)/shard_map/unpack/pallas_call | solution.py:43
  190.4 2.0 %unpack.7 = f32[1024,1024]{1,0:T(8,128)} custom-call(s32[2]{0:T(128)S(1)} %copy-done.8, bf16[256,512]{1,0:T(8,128)(2,1)S(1)} %collective-permute-done.40.refs_0_, bf16[256,512]{1,0:T(8,128)(2,1)S(1)} %collective-permute-done.41.refs_1_, bf16[256,512]{1,0:T(8,128)(2,1)S(1)} %collective-permute-done.42.refs_2_, ...), custom_call_target="tpu_custom_call", output_to_operand_aliasing={{}: (5, {})} | custom-call | bytes 9437184 | tf_op jit(solution)/shard_map/unpack/pallas_call | solution.py:43
  (108 shorter events, 35.3 us)
Async XLA Ops:
  2.4 13.3 %collective-permute-start.2 = (bf16[160,1024]{1,0:T(8,128)(2,1)}, bf16[160,1024]{1,0:T(8,128)(2,1)}, u32[]{:S(2)}, u32[]{:S(2)}) collective-permute-start(bf16[160,1024]{1,0:T(8,128)(2,1)} %constant_dynamic-slice_fusion), channel_id=1, source_target_pairs={{0,16},{1,9},{2,18},{3,11},{4,20},{5,13},{6,22},{7,15},{8,24},{9,1... | collective-permute-start | bytes 983048 | tf_op jit(solution)/shard_map/ppermute | solution.py:704
  7.3 3.1 %collective-permute-start = (s32[32,320]{1,0:T(8,128)}, s32[32,320]{1,0:T(8,128)S(1)}, u32[]{:S(2)}, u32[]{:S(2)}) collective-permute-start(s32[32,320]{1,0:T(8,128)} %sort_slots.1), channel_id=1, source_target_pairs={{0,1},{1,0},{2,3},{3,2},{4,5},{5,4},{6,7},{7,6},{8,9},{9,8},{10,11... | collective-permute-start | bytes 122888 | tf_op jit(solution)/shard_map/ppermute | solution.py:713
  11.9 3.8 %collective-permute-start.1 = (s32[64,320]{1,0:T(8,128)S(1)}, s32[64,320]{1,0:T(8,128)S(1)}, u32[]{:S(2)}, u32[]{:S(2)}) collective-permute-start(s32[64,320]{1,0:T(8,128)S(1)} %pad_add_fusion.1.own_ref), channel_id=1, source_target_pairs={{0,4},{1,3},{2,6},{3,1},{4,0},{5,7},{6,2},{7,5},{8,12},{9,11},{10,... | collective-permute-start | bytes 245768 | tf_op jit(solution)/shard_map/ppermute | solution.py:704
  17.6 16.7 %collective-permute-start.4 = (bf16[320,1024]{1,0:T(8,128)(2,1)}, bf16[320,1024]{1,0:T(8,128)(2,1)}, u32[]{:S(2)}, u32[]{:S(2)}) collective-permute-start(bf16[320,1024]{1,0:T(8,128)(2,1)} %pad_maximum_fusion), channel_id=1, source_target_pairs={{0,8},{1,17},{2,10},{3,19},{4,12},{5,21},{6,14},{7,23},{8,0},{9,25... | collective-permute-start | bytes 1966088 | tf_op jit(solution)/shard_map/ppermute | solution.py:704
  18.3 14.8 %collective-permute-start.5 = (bf16[160,1024]{1,0:T(8,128)(2,1)}, bf16[160,1024]{1,0:T(8,128)(2,1)}, u32[]{:S(2)}, u32[]{:S(2)}) collective-permute-start(bf16[160,1024]{1,0:T(8,128)(2,1)} %collective-permute-done.2.refs_1_.refs_8_), channel_id=1, source_target_pairs={{0,1},{1,0},{2,3},{3,2},{4,5},{5,4},{6,7},{7,6},{8,9},{9,8},{10,11... | collective-permute-start | bytes 983048 | tf_op jit(solution)/shard_map/ppermute | solution.py:713
  21.2 5.0 %collective-permute-start.3 = (s32[128,320]{1,0:T(8,128)S(1)}, s32[128,320]{1,0:T(8,128)}, u32[]{:S(2)}, u32[]{:S(2)}) collective-permute-start(s32[128,320]{1,0:T(8,128)S(1)} %pad_add_fusion), channel_id=1, source_target_pairs={{0,2},{1,5},{2,0},{3,7},{4,6},{5,1},{6,4},{7,3},{8,10},{9,13},{10,... | collective-permute-start | bytes 491528 | tf_op jit(solution)/shard_map/ppermute | solution.py:704
  34.4 3.7 %collective-permute-start.6 = (bf16[320,1024]{1,0:T(8,128)(2,1)}, bf16[320,1024]{1,0:T(8,128)(2,1)}, u32[]{:S(2)}, u32[]{:S(2)}) collective-permute-start(bf16[320,1024]{1,0:T(8,128)(2,1)} %collective-permute-done.4.refs_2_.refs_9_), channel_id=1, source_target_pairs={{0,1},{1,0},{2,3},{3,2},{4,5},{5,4},{6,7},{7,6},{8,9},{9,8},{10,11... | collective-permute-start | bytes 1966088 | tf_op jit(solution)/shard_map/ppermute | solution.py:713
  45.2 14.2 %collective-permute-start.8 = (bf16[1024,1024]{1,0:T(8,128)(2,1)}, bf16[1024,1024]{1,0:T(8,128)(2,1)}, u32[]{:S(2)}, u32[]{:S(2)}) collective-permute-start(bf16[1024,1024]{1,0:T(8,128)(2,1)} %w_in.7), channel_id=1, source_target_pairs={{0,1},{1,0},{2,3},{3,2},{4,5},{5,4},{6,7},{7,6},{8,9},{9,8},{10,11... | collective-permute-start | bytes 6291464 | tf_op jit(solution)/shard_map/ppermute | solution.py:713
  45.6 10.0 %collective-permute-start.9 = (f32[320,512]{1,0:T(8,128)}, f32[320,512]{1,0:T(8,128)}, u32[]{:S(2)}, u32[]{:S(2)}) collective-permute-start(f32[320,512]{1,0:T(8,128)} %get-tuple-element.112), channel_id=1, source_target_pairs={{0,2},{1,5},{2,0},{3,7},{4,6},{5,1},{6,4},{7,3},{8,10},{9,13},{10,... | collective-permute-start | bytes 1966088 | tf_op jit(solution)/shard_map/ppermute | solution.py:704
  54.1 12.8 %collective-permute-start.7 = (f32[320,512]{1,0:T(8,128)}, f32[320,512]{1,0:T(8,128)S(1)}, u32[]{:S(2)}, u32[]{:S(2)}) collective-permute-start(f32[320,512]{1,0:T(8,128)} %get-tuple-element.104), channel_id=1, source_target_pairs={{0,2},{1,5},{2,0},{3,7},{4,6},{5,1},{6,4},{7,3},{8,10},{9,13},{10,... | collective-permute-start | bytes 1966088 | tf_op jit(solution)/shard_map/ppermute | solution.py:704
  57.1 14.6 %collective-permute-start.10 = (f32[320,512]{1,0:T(8,128)S(1)}, f32[320,512]{1,0:T(8,128)S(1)}, u32[]{:S(2)}, u32[]{:S(2)}) collective-permute-start(f32[320,512]{1,0:T(8,128)S(1)} %add.36), channel_id=1, source_target_pairs={{0,4},{1,3},{2,6},{3,1},{4,0},{5,7},{6,2},{7,5},{8,12},{9,11},{10,... | collective-permute-start | bytes 1966088 | tf_op jit(solution)/shard_map/ppermute | solution.py:704
  71.9 1.7 collective-permute-start.11
  77.2 28.1 %copy-start.4 = (bf16[320,1024]{1,0:T(8,128)(2,1)}, bf16[320,1024]{1,0:T(8,128)(2,1)S(1)}, u32[]{:S(2)}) copy-start(bf16[320,1024]{1,0:T(8,128)(2,1)S(1)} %get-tuple-element.127.refs_0_.grad_ref) | copy-start | bytes 1966084
  77.2 6.5 %collective-permute-start.13 = (bf16[160,1024]{1,0:T(8,128)(2,1)S(1)}, bf16[160,1024]{1,0:T(8,128)(2,1)S(1)}, u32[]{:S(2)}, u32[]{:S(2)}) collective-permute-start(bf16[160,1024]{1,0:T(8,128)(2,1)S(1)} %get-tuple-element.117), channel_id=1, source_target_pairs={{0,2},{1,5},{2,0},{3,7},{4,6},{5,1},{6,4},{7,3},{8,10},{9,13},{10,... | collective-permute-start | bytes 983048 | tf_op jit(solution)/shard_map/ppermute | solution.py:704
  78.5 9.0 %collective-permute-start.12 = (bf16[160,1024]{1,0:T(8,128)(2,1)S(1)}, bf16[160,1024]{1,0:T(8,128)(2,1)S(1)}, u32[]{:S(2)}, u32[]{:S(2)}) collective-permute-start(bf16[160,1024]{1,0:T(8,128)(2,1)S(1)} %get-tuple-element.117), channel_id=1, source_target_pairs={{0,4},{1,3},{2,6},{3,1},{4,0},{5,7},{6,2},{7,5},{8,12},{9,11},{10,... | collective-permute-start | bytes 983048 | tf_op jit(solution)/shard_map/ppermute | solution.py:704
  79.6 10.9 %collective-permute-start.15 = (bf16[640,256]{1,0:T(8,128)(2,1)S(1)}, bf16[640,256]{1,0:T(8,128)(2,1)S(1)}, u32[]{:S(2)}, u32[]{:S(2)}) collective-permute-start(bf16[640,256]{1,0:T(8,128)(2,1)S(1)} %get-tuple-element.121), channel_id=1, source_target_pairs={{0,2},{1,5},{2,0},{3,7},{4,6},{5,1},{6,4},{7,3},{8,10},{9,13},{10,... | collective-permute-start | bytes 983048 | tf_op jit(solution)/shard_map/ppermute | solution.py:704
  87.5 6.5 %collective-permute-start.14 = (bf16[160,1024]{1,0:T(8,128)(2,1)S(1)}, bf16[160,1024]{1,0:T(8,128)(2,1)S(1)}, u32[]{:S(2)}, u32[]{:S(2)}) collective-permute-start(bf16[160,1024]{1,0:T(8,128)(2,1)S(1)} %collective-permute-done.12.refs_1_), channel_id=1, source_target_pairs={{0,2},{1,5},{2,0},{3,7},{4,6},{5,1},{6,4},{7,3},{8,10},{9,13},{10,... | collective-permute-start | bytes 983048 | tf_op jit(solution)/shard_map/ppermute | solution.py:704
  90.5 9.4 %collective-permute-start.16 = (bf16[640,256]{1,0:T(8,128)(2,1)S(1)}, bf16[640,256]{1,0:T(8,128)(2,1)S(1)}, u32[]{:S(2)}, u32[]{:S(2)}) collective-permute-start(bf16[640,256]{1,0:T(8,128)(2,1)S(1)} %pad_maximum_fusion.1), channel_id=1, source_target_pairs={{0,4},{1,3},{2,6},{3,1},{4,0},{5,7},{6,2},{7,5},{8,12},{9,11},{10,... | collective-permute-start | bytes 983048 | tf_op jit(solution)/shard_map/ppermute | solution.py:704
  91.3 9.5 %collective-permute-start.17 = (bf16[160,1024]{1,0:T(8,128)(2,1)S(1)}, bf16[160,1024]{1,0:T(8,128)(2,1)S(1)}, u32[]{:S(2)}, u32[]{:S(2)}) collective-permute-start(bf16[160,1024]{1,0:T(8,128)(2,1)S(1)} %collective-permute-done.12.refs_1_), channel_id=1, source_target_pairs={{0,1},{1,0},{2,3},{3,2},{4,5},{5,4},{6,7},{7,6},{8,9},{9,8},{10,11... | collective-permute-start | bytes 983048 | tf_op jit(solution)/shard_map/ppermute | solution.py:713
  93.1 7.6 %collective-permute-start.18 = (bf16[160,1024]{1,0:T(8,128)(2,1)S(1)}, bf16[160,1024]{1,0:T(8,128)(2,1)S(1)}, u32[]{:S(2)}, u32[]{:S(2)}) collective-permute-start(bf16[160,1024]{1,0:T(8,128)(2,1)S(1)} %collective-permute-done.13.refs_2_), channel_id=1, source_target_pairs={{0,1},{1,0},{2,3},{3,2},{4,5},{5,4},{6,7},{7,6},{8,9},{9,8},{10,11... | collective-permute-start | bytes 983048 | tf_op jit(solution)/shard_map/ppermute | solution.py:713
  100.0 2.1 %collective-permute-start.19 = (bf16[160,1024]{1,0:T(8,128)(2,1)S(1)}, bf16[160,1024]{1,0:T(8,128)(2,1)S(1)}, u32[]{:S(2)}, u32[]{:S(2)}) collective-permute-start(bf16[160,1024]{1,0:T(8,128)(2,1)S(1)} %collective-permute-done.14.refs_3_), channel_id=1, source_target_pairs={{0,1},{1,0},{2,3},{3,2},{4,5},{5,4},{6,7},{7,6},{8,9},{9,8},{10,11... | collective-permute-start | bytes 983048 | tf_op jit(solution)/shard_map/ppermute | solution.py:713
  105.3 9.7 %collective-permute-start.20 = (bf16[144,1024]{1,0:T(8,128)(2,1)S(1)}, bf16[144,1024]{1,0:T(8,128)(2,1)S(1)}, u32[]{:S(2)}, u32[]{:S(2)}) collective-permute-start(bf16[144,1024]{1,0:T(8,128)(2,1)S(1)} %get-tuple-element.140), channel_id=1, source_target_pairs={{0,8},{1,17},{2,10},{3,19},{4,12},{5,21},{6,14},{7,23},{8,0},{9,25... | collective-permute-start | bytes 884744 | tf_op jit(solution)/shard_map/ppermute | solution.py:704
  115.0 27.8 %copy-start.1 = (bf16[1024,1024]{1,0:T(8,128)(2,1)S(1)}, bf16[1024,1024]{1,0:T(8,128)(2,1)}, u32[]{:S(2)}) copy-start(bf16[1024,1024]{1,0:T(8,128)(2,1)} %w_in.7) | copy-start | bytes 6291460
  115.1 27.8 %copy-start.5 = (bf16[320,1024]{1,0:T(8,128)(2,1)S(1)}, bf16[320,1024]{1,0:T(8,128)(2,1)}, u32[]{:S(2)}) copy-start(bf16[320,1024]{1,0:T(8,128)(2,1)} %copy-done.4) | copy-start | bytes 1966084
  115.1 8.6 %collective-permute-start.21 = (bf16[528,512]{1,0:T(8,128)(2,1)S(1)}, bf16[528,512]{1,0:T(8,128)(2,1)S(1)}, u32[]{:S(2)}, u32[]{:S(2)}) collective-permute-start(bf16[528,512]{1,0:T(8,128)(2,1)S(1)} %get-tuple-element.142), channel_id=1, source_target_pairs={{0,2},{1,5},{2,0},{3,7},{4,6},{5,1},{6,4},{7,3},{8,10},{9,13},{10,... | collective-permute-start | bytes 1622024 | tf_op jit(solution)/shard_map/ppermute | solution.py:704
  116.0 21.5 %collective-permute-start.24 = (bf16[320,512]{1,0:T(8,128)(2,1)S(1)}, bf16[320,512]{1,0:T(8,128)(2,1)S(1)}, u32[]{:S(2)}, u32[]{:S(2)}) collective-permute-start(bf16[320,512]{1,0:T(8,128)(2,1)S(1)} %get-tuple-element.148), channel_id=1, source_target_pairs={{0,8},{1,17},{2,10},{3,19},{4,12},{5,21},{6,14},{7,23},{8,0},{9,25... | collective-permute-start | bytes 983048 | tf_op jit(solution)/shard_map/ppermute | solution.py:704
  117.0 21.3 %collective-permute-start.25 = (bf16[320,512]{1,0:T(8,128)(2,1)S(1)}, bf16[320,512]{1,0:T(8,128)(2,1)S(1)}, u32[]{:S(2)}, u32[]{:S(2)}) collective-permute-start(bf16[320,512]{1,0:T(8,128)(2,1)S(1)} %get-tuple-element.149), channel_id=1, source_target_pairs={{0,8},{1,17},{2,10},{3,19},{4,12},{5,21},{6,14},{7,23},{8,0},{9,25... | collective-permute-start | bytes 983048 | tf_op jit(solution)/shard_map/ppermute | solution.py:704
  119.0 18.5 %collective-permute-start.23 = (bf16[144,1024]{1,0:T(8,128)(2,1)S(1)}, bf16[144,1024]{1,0:T(8,128)(2,1)S(1)}, u32[]{:S(2)}, u32[]{:S(2)}) collective-permute-start(bf16[144,1024]{1,0:T(8,128)(2,1)S(1)} %merge.3), channel_id=1, source_target_pairs={{0,16},{1,9},{2,18},{3,11},{4,20},{5,13},{6,22},{7,15},{8,24},{9,1... | collective-permute-start | bytes 884744 | tf_op jit(solution)/shard_map/ppermute | solution.py:704
  124.3 14.1 %collective-permute-start.22 = (bf16[272,512]{1,0:T(8,128)(2,1)S(1)}, bf16[272,512]{1,0:T(8,128)(2,1)S(1)}, u32[]{:S(2)}, u32[]{:S(2)}) collective-permute-start(bf16[272,512]{1,0:T(8,128)(2,1)S(1)} %get-tuple-element.144), channel_id=1, source_target_pairs={{0,4},{1,3},{2,6},{3,1},{4,0},{5,7},{6,2},{7,5},{8,12},{9,11},{10,... | collective-permute-start | bytes 835592 | tf_op jit(solution)/shard_map/ppermute | solution.py:704
  139.0 15.3 %collective-permute-start.26 = (bf16[272,512]{1,0:T(8,128)(2,1)S(1)}, bf16[272,512]{1,0:T(8,128)(2,1)S(1)}, u32[]{:S(2)}, u32[]{:S(2)}) collective-permute-start(bf16[272,512]{1,0:T(8,128)(2,1)S(1)} %merge.4.keep_ref), channel_id=1, source_target_pairs={{0,8},{1,17},{2,10},{3,19},{4,12},{5,21},{6,14},{7,23},{8,0},{9,25... | collective-permute-start | bytes 835592 | tf_op jit(solution)/shard_map/ppermute | solution.py:704
  141.7 6.0 %collective-permute-start.29 = (bf16[128,1024]{1,0:T(8,128)(2,1)S(1)}, bf16[128,1024]{1,0:T(8,128)(2,1)S(1)}, u32[]{:S(2)}, u32[]{:S(2)}) collective-permute-start(bf16[128,1024]{1,0:T(8,128)(2,1)S(1)} %slice.58.refs_0_), channel_id=1, source_target_pairs={{0,2},{1,5},{2,0},{3,7},{4,6},{5,1},{6,4},{7,3},{8,10},{9,13},{10,... | collective-permute-start | bytes 786440 | tf_op jit(solution)/shard_map/ppermute | solution.py:704
  142.4 7.4 %collective-permute-start.28 = (bf16[128,1024]{1,0:T(8,128)(2,1)S(1)}, bf16[128,1024]{1,0:T(8,128)(2,1)S(1)}, u32[]{:S(2)}, u32[]{:S(2)}) collective-permute-start(bf16[128,1024]{1,0:T(8,128)(2,1)S(1)} %slice.58.refs_0_), channel_id=1, source_target_pairs={{0,4},{1,3},{2,6},{3,1},{4,0},{5,7},{6,2},{7,5},{8,12},{9,11},{10,... | collective-permute-start | bytes 786440 | tf_op jit(solution)/shard_map/ppermute | solution.py:704
  142.8 11.5 %collective-permute-start.27 = (bf16[128,1024]{1,0:T(8,128)(2,1)S(1)}, bf16[128,1024]{1,0:T(8,128)(2,1)S(1)}, u32[]{:S(2)}, u32[]{:S(2)}) collective-permute-start(bf16[128,1024]{1,0:T(8,128)(2,1)S(1)} %slice.58.refs_0_), channel_id=1, source_target_pairs={{0,8},{1,17},{2,10},{3,19},{4,12},{5,21},{6,14},{7,23},{8,0},{9,25... | collective-permute-start | bytes 786440 | tf_op jit(solution)/shard_map/ppermute | solution.py:704
  154.9 9.6 %collective-permute-start.30 = (bf16[272,512]{1,0:T(8,128)(2,1)S(1)}, bf16[272,512]{1,0:T(8,128)(2,1)S(1)}, u32[]{:S(2)}, u32[]{:S(2)}) collective-permute-start(bf16[272,512]{1,0:T(8,128)(2,1)S(1)} %merge.5), channel_id=1, source_target_pairs={{0,16},{1,9},{2,18},{3,11},{4,20},{5,13},{6,22},{7,15},{8,24},{9,1... | collective-permute-start | bytes 835592 | tf_op jit(solution)/shard_map/ppermute | solution.py:704
  155.0 5.6 %collective-permute-start.31 = (bf16[128,1024]{1,0:T(8,128)(2,1)S(1)}, bf16[128,1024]{1,0:T(8,128)(2,1)S(1)}, u32[]{:S(2)}, u32[]{:S(2)}) collective-permute-start(bf16[128,1024]{1,0:T(8,128)(2,1)S(1)} %collective-permute-done.28.refs_2_), channel_id=1, source_target_pairs={{0,2},{1,5},{2,0},{3,7},{4,6},{5,1},{6,4},{7,3},{8,10},{9,13},{10,... | collective-permute-start | bytes 786440 | tf_op jit(solution)/shard_map/ppermute | solution.py:704
  155.6 8.8 %collective-permute-start.33 = (bf16[128,1024]{1,0:T(8,128)(2,1)S(1)}, bf16[128,1024]{1,0:T(8,128)(2,1)S(1)}, u32[]{:S(2)}, u32[]{:S(2)}) collective-permute-start(bf16[128,1024]{1,0:T(8,128)(2,1)S(1)} %collective-permute-done.27.refs_1_), channel_id=1, source_target_pairs={{0,2},{1,5},{2,0},{3,7},{4,6},{5,1},{6,4},{7,3},{8,10},{9,13},{10,... | collective-permute-start | bytes 786440 | tf_op jit(solution)/shard_map/ppermute | solution.py:704
  156.5 7.9 %collective-permute-start.32 = (bf16[128,1024]{1,0:T(8,128)(2,1)S(1)}, bf16[128,1024]{1,0:T(8,128)(2,1)S(1)}, u32[]{:S(2)}, u32[]{:S(2)}) collective-permute-start(bf16[128,1024]{1,0:T(8,128)(2,1)S(1)} %collective-permute-done.27.refs_1_), channel_id=1, source_target_pairs={{0,4},{1,3},{2,6},{3,1},{4,0},{5,7},{6,2},{7,5},{8,12},{9,11},{10,... | collective-permute-start | bytes 786440 | tf_op jit(solution)/shard_map/ppermute | solution.py:704
  164.6 12.2 %collective-permute-start.37 = (bf16[320,512]{1,0:T(8,128)(2,1)S(1)}, bf16[320,512]{1,0:T(8,128)(2,1)S(1)}, u32[]{:S(2)}, u32[]{:S(2)}) collective-permute-start(bf16[320,512]{1,0:T(8,128)(2,1)S(1)} %add_convert_fusion), channel_id=1, source_target_pairs={{0,16},{1,9},{2,18},{3,11},{4,20},{5,13},{6,22},{7,15},{8,24},{9,1... | collective-permute-start | bytes 983048 | tf_op jit(solution)/shard_map/ppermute | solution.py:704
  165.4 11.4 %collective-permute-start.36 = (bf16[128,1024]{1,0:T(8,128)(2,1)S(1)}, bf16[128,1024]{1,0:T(8,128)(2,1)S(1)}, u32[]{:S(2)}, u32[]{:S(2)}) collective-permute-start(bf16[128,1024]{1,0:T(8,128)(2,1)S(1)} %collective-permute-done.32.refs_3_), channel_id=1, source_target_pairs={{0,2},{1,5},{2,0},{3,7},{4,6},{5,1},{6,4},{7,3},{8,10},{9,13},{10,... | collective-permute-start | bytes 786440 | tf_op jit(solution)/shard_map/ppermute | solution.py:704
  165.7 11.1 %collective-permute-start.35 = (bf16[256,512]{1,0:T(8,128)(2,1)S(1)}, bf16[256,512]{1,0:T(8,128)(2,1)S(1)}, u32[]{:S(2)}, u32[]{:S(2)}) collective-permute-start(bf16[256,512]{1,0:T(8,128)(2,1)S(1)} %slice.57.refs_0_), channel_id=1, source_target_pairs={{0,2},{1,5},{2,0},{3,7},{4,6},{5,1},{6,4},{7,3},{8,10},{9,13},{10,... | collective-permute-start | bytes 786440 | tf_op jit(solution)/shard_map/ppermute | solution.py:704
  166.9 9.9 %collective-permute-start.34 = (bf16[256,512]{1,0:T(8,128)(2,1)S(1)}, bf16[256,512]{1,0:T(8,128)(2,1)S(1)}, u32[]{:S(2)}, u32[]{:S(2)}) collective-permute-start(bf16[256,512]{1,0:T(8,128)(2,1)S(1)} %slice.57.refs_0_), channel_id=1, source_target_pairs={{0,4},{1,3},{2,6},{3,1},{4,0},{5,7},{6,2},{7,5},{8,12},{9,11},{10,... | collective-permute-start | bytes 786440 | tf_op jit(solution)/shard_map/ppermute | solution.py:704
  166.9 9.9 %collective-permute-start.38 = (f32[1,512]{1,0:T(1,128)S(1)}, f32[1,512]{1,0:T(1,128)S(1)}, u32[]{:S(2)}, u32[]{:S(2)}) collective-permute-start(f32[1,512]{1,0:T(1,128)S(1)} %slice_add_fusion.1), channel_id=1, source_target_pairs={{0,1},{1,0},{2,3},{3,2},{4,5},{5,4},{6,7},{7,6},{8,9},{9,8},{10,11... | collective-permute-start | bytes 6152 | tf_op jit(solution)/shard_map/ppermute | solution.py:713
  177.5 6.2 %collective-permute-start.43 = (bf16[320,512]{1,0:T(8,128)(2,1)S(1)}, bf16[320,512]{1,0:T(8,128)(2,1)S(1)}, u32[]{:S(2)}, u32[]{:S(2)}) collective-permute-start(bf16[320,512]{1,0:T(8,128)(2,1)S(1)} %row_sums.1.mine_ref), channel_id=1, source_target_pairs={{0,1},{1,0},{2,3},{3,2},{4,5},{5,4},{6,7},{7,6},{8,9},{9,8},{10,11... | collective-permute-start | bytes 983048 | tf_op jit(solution)/shard_map/ppermute | solution.py:713
  180.9 4.8 %collective-permute-start.40 = (bf16[256,512]{1,0:T(8,128)(2,1)S(1)}, bf16[256,512]{1,0:T(8,128)(2,1)S(1)}, u32[]{:S(2)}, u32[]{:S(2)}) collective-permute-start(bf16[256,512]{1,0:T(8,128)(2,1)S(1)} %slice.57.refs_0_), channel_id=1, source_target_pairs={{0,1},{1,0},{2,3},{3,2},{4,5},{5,4},{6,7},{7,6},{8,9},{9,8},{10,11... | collective-permute-start | bytes 786440 | tf_op jit(solution)/shard_map/ppermute | solution.py:713
  181.0 4.8 %collective-permute-start.42 = (bf16[256,512]{1,0:T(8,128)(2,1)S(1)}, bf16[256,512]{1,0:T(8,128)(2,1)S(1)}, u32[]{:S(2)}, u32[]{:S(2)}) collective-permute-start(bf16[256,512]{1,0:T(8,128)(2,1)S(1)} %collective-permute-done.35.refs_2_), channel_id=1, source_target_pairs={{0,1},{1,0},{2,3},{3,2},{4,5},{5,4},{6,7},{7,6},{8,9},{9,8},{10,11... | collective-permute-start | bytes 786440 | tf_op jit(solution)/shard_map/ppermute | solution.py:713
  181.4 4.3 %collective-permute-start.41 = (bf16[256,512]{1,0:T(8,128)(2,1)S(1)}, bf16[256,512]{1,0:T(8,128)(2,1)S(1)}, u32[]{:S(2)}, u32[]{:S(2)}) collective-permute-start(bf16[256,512]{1,0:T(8,128)(2,1)S(1)} %collective-permute-done.34.refs_1_), channel_id=1, source_target_pairs={{0,1},{1,0},{2,3},{3,2},{4,5},{5,4},{6,7},{7,6},{8,9},{9,8},{10,11... | collective-permute-start | bytes 786440 | tf_op jit(solution)/shard_map/ppermute | solution.py:713
  181.5 5.5 %collective-permute-start.39 = (bf16[256,512]{1,0:T(8,128)(2,1)S(1)}, bf16[256,512]{1,0:T(8,128)(2,1)S(1)}, u32[]{:S(2)}, u32[]{:S(2)}) collective-permute-start(bf16[256,512]{1,0:T(8,128)(2,1)S(1)} %collective-permute-done.34.refs_1_), channel_id=1, source_target_pairs={{0,2},{1,5},{2,0},{3,7},{4,6},{5,1},{6,4},{7,3},{8,10},{9,13},{10,... | collective-permute-start | bytes 786440 | tf_op jit(solution)/shard_map/ppermute | solution.py:704
  187.0 3.3 %collective-permute-start.44 = (bf16[256,512]{1,0:T(8,128)(2,1)S(1)}, bf16[256,512]{1,0:T(8,128)(2,1)S(1)}, u32[]{:S(2)}, u32[]{:S(2)}) collective-permute-start(bf16[256,512]{1,0:T(8,128)(2,1)S(1)} %collective-permute-done.39.refs_3_), channel_id=1, source_target_pairs={{0,1},{1,0},{2,3},{3,2},{4,5},{5,4},{6,7},{7,6},{8,9},{9,8},{10,11... | collective-permute-start | bytes 786440 | tf_op jit(solution)/shard_map/ppermute | solution.py:713
  (11 other events, 72.9 us)

commit v6 on v5

--- a/solution.py
+++ b/solution.py
@@ -757,7 +757,7 @@
 
     one, two = plane_swap(grad_half, 1), plane_swap(grad_half, 0)
     last_slices = plane_swap(jnp.concatenate([next_slice, far_slices[rows:]], 0), 1)
-    one, two = fence((one, two))
+    one = fence(one)
     three = plane_swap(one, 0)
     three, last_slices = fence((three, last_slices))
     pieces = [grad_linear, one, two, three, trade(one), trade(two), trade(three)]
@@ -819,8 +819,8 @@
         place, w_all, [(0, at // 2, at % 2) for at in range(2 * PLANE - 1)], lines
     )
     bias_other = trade(biases["q"][None])
-    q_one, q_two, far_three, rows_next, biases, w_part, bias_other = fence(
-        (q_one, q_two, far_three, rows_next, biases, w_part, bias_other)
+    q_one, far_three, rows_next, biases, w_part, bias_other = fence(
+        (q_one, far_three, rows_next, biases, w_part, bias_other)
     )
     q_three = plane_swap(q_one, 0)
     w_grad = unpack(place, [far_three], [(0, 3, 1)], lines, 1, w_part)

time: 193 us -> 191 us (0.990)
  waiting for transfers between devices: 73.7 us -> 67.8 us
  starting transfers between devices: 48 us -> 52.2 us
    ppermute x31, waiting for transfers between devices: 67.7 us -> 61.8 us  [swap(): return lax.ppermute(value, ('nodes', 'stream'), pairs)]
    ppermute x31, starting transfers between devices: 26.7 us -> 30.7 us  [swap(): return lax.ppermute(value, ('nodes', 'stream'), pairs)]
where the time goes in v6:
time: 191 us
  waiting for transfers between devices  67.8 us (35%)
  Pallas kernels  58.2 us (30%)
  starting transfers between devices  52.2 us (27%)
  other arithmetic  6.61 us (3%)
  local copies, waits for them, and re-layouts  4.66 us (2%)
    ppermute x31, waiting for transfers between devices, swap(): return lax.ppermute(value, ('nodes', 'stream'), pairs)  61.8 us
    pallas_call x20, Pallas kernels, call(): pl.pallas_call(kernel, name=name, out_shape=list(outs), in_specs=spaced(p...  58.2 us
    ppermute x31, starting transfers between devices, swap(): return lax.ppermute(value, ('nodes', 'stream'), pairs)  30.7 us
    ppermute x14, starting transfers between devices, trade(): return lax.ppermute(value, 'stream', [(0, 1), (1, 0)])  21.5 us
    ppermute x14, waiting for transfers between devices, trade(): return lax.ppermute(value, 'stream', [(0, 1), (1, 0)])  6.05 us
  transfers between devices with their start and end apart: 45, of which 24 were waited for; matrix products, arithmetic and copies ran while one was open for 3% of the time, Pallas kernels for 21%

profile of v6, /device:TPU:1, one launch (start us, length us, event | category | flops | bytes accessed | tf_op | source)
XLA Modules:
  0.0 190.8 jit_solution(3753565747494580748)
XLA Ops:
  0.6 1.7 constant_dynamic-slice_fusion
  2.4 2.1 %collective-permute-start.2 = (bf16[160,1024]{1,0:T(8,128)(2,1)}, bf16[160,1024]{1,0:T(8,128)(2,1)}, u32[]{:S(2)}, u32[]{:S(2)}) collective-permute-start(bf16[160,1024]{1,0:T(8,128)(2,1)} %constant_dynamic-slice_fusion), channel_id=1, source_target_pairs={{0,16},{1,9},{2,18},{3,11},{4,20},{5,13},{6,22},{7,15},{8,24},{9,1... | collective-permute-start | bytes 983048 | tf_op jit(solution)/shard_map/ppermute | solution.py:704
  5.1 2.2 %sort_slots.1 = s32[32,320]{1,0:T(8,128)} custom-call(s32[2]{0:T(128)} %pad_add_fusion.2.place_ref, s32[25,320]{1,0:T(8,128)} %bitcast.12, s32[25,320]{1,0:T(8,128)} %bitcast.13, s32[25,320]{1,0:T(8,128)} %bitcast.14), custom_call_target="tpu_custom_call" | custom-call | bytes 136960 | tf_op jit(solution)/shard_map/sort_slots/pallas_call | solution.py:43
  7.3 2.0 %collective-permute-start = (s32[32,320]{1,0:T(8,128)}, s32[32,320]{1,0:T(8,128)S(1)}, u32[]{:S(2)}, u32[]{:S(2)}) collective-permute-start(s32[32,320]{1,0:T(8,128)} %sort_slots.1), channel_id=1, source_target_pairs={{0,1},{1,0},{2,3},{3,2},{4,5},{5,4},{6,7},{7,6},{8,9},{9,8},{10,11... | collective-permute-start | bytes 122888 | tf_op jit(solution)/shard_map/ppermute | solution.py:713
  13.1 2.6 %collective-permute-done.1.next_ref = s32[64,320]{1,0:T(8,128)S(1)} collective-permute-done((s32[64,320]{1,0:T(8,128)S(1)}, s32[64,320]{1,0:T(8,128)S(1)}, u32[]{:S(2)}, u32[]{:S(2)}) %collective-permute-start.1) | collective-permute-done | bytes 81952 | tf_op jit(solution)/shard_map/ppermute | solution.py:704
  15.6 2.0 %pad_maximum_fusion = bf16[320,1024]{1,0:T(8,128)(2,1)} fusion(bf16[160,1024]{1,0:T(8,128)(2,1)} %collective-permute-done.2.refs_1_.refs_8_, bf16[160,1024]{1,0:T(8,128)(2,1)} %constant_dynamic-slice_fusion), kind=kLoop, calls=%fused_computation | loop fusion | flops 1310720 | bytes 1310720 | tf_op jit(solution)/shard_map/concatenate | solution.py:733
  18.3 2.1 %collective-permute-start.5 = (bf16[160,1024]{1,0:T(8,128)(2,1)}, bf16[160,1024]{1,0:T(8,128)(2,1)}, u32[]{:S(2)}, u32[]{:S(2)}) collective-permute-start(bf16[160,1024]{1,0:T(8,128)(2,1)} %collective-permute-done.2.refs_1_.refs_8_), channel_id=1, source_target_pairs={{0,1},{1,0},{2,3},{3,2},{4,5},{5,4},{6,7},{7,6},{8,9},{9,8},{10,11... | collective-permute-start | bytes 983048 | tf_op jit(solution)/shard_map/ppermute | solution.py:713
  21.2 1.3 collective-permute-start.3
  22.5 3.7 %collective-permute-done.3.rest_ref = s32[128,320]{1,0:T(8,128)} collective-permute-done((s32[128,320]{1,0:T(8,128)S(1)}, s32[128,320]{1,0:T(8,128)}, u32[]{:S(2)}, u32[]{:S(2)}) %collective-permute-start.3) | collective-permute-done | bytes 163872 | tf_op jit(solution)/shard_map/ppermute | solution.py:704
  26.2 6.9 %slot_matrix.1 = (f32[1280,8]{1,0:T(8,128)}, bf16[1280,1280]{1,0:T(8,128)(2,1)}) custom-call(s32[2]{0:T(128)} %pad_add_fusion.2.place_ref, s32[64,320]{1,0:T(8,128)} %copy-done.12, s32[64,320]{1,0:T(8,128)} %copy-done.13, s32[128,320]{1,0:T(8,128)} %collective-permute-done.3.rest_ref), custom_call_target="tpu_custom_call" | custom-call | flops 1 | bytes 1 | tf_op jit(solution)/shard_map/slot_matrix/pallas_call | solution.py:43
  34.4 1.6 collective-permute-start.6
  36.0 2.1 %collective-permute-done.6.refs_4_.refs_11_ = bf16[320,1024]{1,0:T(8,128)(2,1)} collective-permute-done((bf16[320,1024]{1,0:T(8,128)(2,1)}, bf16[320,1024]{1,0:T(8,128)(2,1)}, u32[]{:S(2)}, u32[]{:S(2)}) %collective-permute-start.6) | collective-permute-done | bytes 655392 | tf_op jit(solution)/shard_map/ppermute | solution.py:713
  38.1 7.1 %first_sums.1 = (f32[320,512]{1,0:T(8,128)}, bf16[1280,512]{1,0:T(8,128)(2,1)}, bf16[1280,512]{1,0:T(8,128)(2,1)}) custom-call(s32[2]{0:T(128)} %pad_add_fusion.2.place_ref, f32[1,1024]{1,0:T(1,128)} %bitcast.16, bf16[1024,1024]{1,0:T(8,128)(2,1)} %q_in.3, bf16[1280,1280]{1,0:T(8,128)(2,1)} %get-tuple-element.96.matrix_in, bf16[320,1024]{1,0:T(8,128)(2,1)} %refs_7_.1, ...), custom_call_target="tpu_custom_call" | custom-call | flops 2181038080 | bytes 11276288 | tf_op jit(solution)/shard_map/first_sums/pallas_call | solution.py:43
  46.9 7.2 %more_sums.1 = (f32[320,512]{1,0:T(8,128)}, f32[320,512]{1,0:T(8,128)}, f32[320,512]{1,0:T(8,128)}) custom-call(s32[2]{0:T(128)} %pad_add_fusion.2.place_ref, bf16[1280,1280]{1,0:T(8,128)(2,1)} %get-tuple-element.96.matrix_in, bf16[1280,512]{1,0:T(8,128)(2,1)} %get-tuple-element.99.refs_0_.high_in, bf16[1280,512]{1,0:T(8,128)(2,1)} %get-tuple-element.100.refs_1_), custom_call_target="tpu_custom_call" | custom-call | flops 2516582400 | bytes 7864320 | tf_op jit(solution)/shard_map/more_sums/pallas_call | solution.py:43
  55.7 1.4 add.36
  60.5 3.0 %self_product.1.self_ref = f32[320,1024]{1,0:T(8,128)S(1)} custom-call(s32[2]{0:T(128)S(1)} %copy-done.8, bf16[320,1024]{1,0:T(8,128)(2,1)S(1)} %copy-done.2, f32[1,1024]{1,0:T(1,128)S(1)} %bitcast.11, bf16[1024,1024]{1,0:T(8,128)(2,1)S(1)} %copy-done, bf16[1024,1024]{1,0:T(8,128)(2,1)} %collective-permute-done.8.w_other_in), custom_call_target="tpu_custom_call" | custom-call | flops 671088640 | bytes 6164480 | tf_op jit(solution)/shard_map/self_product/pallas_call | solution.py:43
  63.6 3.4 %collective-permute-done.7 = f32[320,512]{1,0:T(8,128)S(1)} collective-permute-done((f32[320,512]{1,0:T(8,128)}, f32[320,512]{1,0:T(8,128)S(1)}, u32[]{:S(2)}, u32[]{:S(2)}) %collective-permute-start.7) | collective-permute-done | bytes 655392 | tf_op jit(solution)/shard_map/ppermute | solution.py:704
  66.9 4.8 %collective-permute-done.10 = f32[320,512]{1,0:T(8,128)S(1)} collective-permute-done((f32[320,512]{1,0:T(8,128)S(1)}, f32[320,512]{1,0:T(8,128)S(1)}, u32[]{:S(2)}, u32[]{:S(2)}) %collective-permute-start.10) | collective-permute-done | bytes 655392 | tf_op jit(solution)/shard_map/ppermute | solution.py:704
  72.0 1.6 collective-permute-done.11.other_ref
  73.6 3.5 %node_step.1 = (f32[320,1024]{1,0:T(8,128)}, bf16[320,1024]{1,0:T(8,128)(2,1)S(1)}, bf16[160,1024]{1,0:T(8,128)(2,1)S(1)}) custom-call(s32[2]{0:T(128)S(1)} %copy-done.8, bf16[320,512]{1,0:T(8,128)(2,1)S(1)} %divide_convert_fusion.mine_ref, bf16[320,512]{1,0:T(8,128)(2,1)S(1)} %collective-permute-done.11.other_ref, f32[320,1024]{1,0:T(8,128)S(1)} %self_product.1.self_ref, ...), custom_call_target="tpu_custom_call" | custom-call | flops 671088640 | bytes 9109504 | tf_op jit(solution)/shard_map/node_step/pallas_call | solution.py:43
  80.3 3.2 %collective-permute-done.12.refs_1_ = bf16[160,1024]{1,0:T(8,128)(2,1)S(1)} collective-permute-done((bf16[160,1024]{1,0:T(8,128)(2,1)S(1)}, bf16[160,1024]{1,0:T(8,128)(2,1)S(1)}, u32[]{:S(2)}, u32[]{:S(2)}) %collective-permute-start.12) | collective-permute-done | bytes 327712 | tf_op jit(solution)/shard_map/ppermute | solution.py:704
  84.7 3.5 %collective-permute-done.15.refs_8_ = bf16[640,256]{1,0:T(8,128)(2,1)S(1)} collective-permute-done((bf16[640,256]{1,0:T(8,128)(2,1)S(1)}, bf16[640,256]{1,0:T(8,128)(2,1)S(1)}, u32[]{:S(2)}, u32[]{:S(2)}) %collective-permute-start.15) | collective-permute-done | bytes 327712 | tf_op jit(solution)/shard_map/ppermute | solution.py:704
  89.0 2.4 %collective-permute-start.17 = (bf16[160,1024]{1,0:T(8,128)(2,1)S(1)}, bf16[160,1024]{1,0:T(8,128)(2,1)S(1)}, u32[]{:S(2)}, u32[]{:S(2)}) collective-permute-start(bf16[160,1024]{1,0:T(8,128)(2,1)S(1)} %collective-permute-done.12.refs_1_), channel_id=1, source_target_pairs={{0,1},{1,0},{2,3},{3,2},{4,5},{5,4},{6,7},{7,6},{8,9},{9,8},{10,11... | collective-permute-start | bytes 983048 | tf_op jit(solution)/shard_map/ppermute | solution.py:713
  92.1 5.2 %collective-permute-done.14.refs_3_ = bf16[160,1024]{1,0:T(8,128)(2,1)S(1)} collective-permute-done((bf16[160,1024]{1,0:T(8,128)(2,1)S(1)}, bf16[160,1024]{1,0:T(8,128)(2,1)S(1)}, u32[]{:S(2)}, u32[]{:S(2)}) %collective-permute-start.14) | collective-permute-done | bytes 327712 | tf_op jit(solution)/shard_map/ppermute | solution.py:704
  97.4 2.1 %collective-permute-start.19 = (bf16[160,1024]{1,0:T(8,128)(2,1)S(1)}, bf16[160,1024]{1,0:T(8,128)(2,1)S(1)}, u32[]{:S(2)}, u32[]{:S(2)}) collective-permute-start(bf16[160,1024]{1,0:T(8,128)(2,1)S(1)} %collective-permute-done.14.refs_3_), channel_id=1, source_target_pairs={{0,1},{1,0},{2,3},{3,2},{4,5},{5,4},{6,7},{7,6},{8,9},{9,8},{10,11... | collective-permute-start | bytes 983048 | tf_op jit(solution)/shard_map/ppermute | solution.py:713
  100.7 3.3 %self_weight.1 = (bf16[144,1024]{1,0:T(8,128)(2,1)S(1)}, bf16[144,1024]{1,0:T(8,128)(2,1)S(1)}) custom-call(s32[2]{0:T(128)S(1)} %copy-done.8, bf16[320,1024]{1,0:T(8,128)(2,1)S(1)} %get-tuple-element.122.refs_0_.grad_ref, bf16[160,1024]{1,0:T(8,128)(2,1)S(1)} %collective-permute-done.12.refs_1_, bf16[160,1024]{1,0:T(8,128)(2,1)S(1)} %collective-permute-done.13.refs_2_, ...), custom_call_target="tpu_custom_call" | custom-call | flops 671088640 | bytes 4194304 | tf_op jit(solution)/shard_map/self_weight/pallas_call | solution.py:43
  104.1 1.4 collective-permute-start.20
  105.4 8.4 %row_grad.1 = (bf16[640,512]{1,0:T(8,128)(2,1)S(1)}, bf16[320,512]{1,0:T(8,128)(2,1)S(1)}, bf16[320,512]{1,0:T(8,128)(2,1)S(1)}, bf16[528,512]{1,0:T(8,128)(2,1)S(1)}, bf16[528,512]{1,0:T(8,128)(2,1)S(1)}) custom-call(s32[2]{0:T(128)S(1)} %copy-done.8, f32[1280,8]{1,0:T(8,128)S(1)} %copy-done.9, bf16[1280,1280]{1,0:T(8,128)(2,1)} %get-tuple-element.96.matrix_in, ...), custom_call_target="tpu_custom_call" | custom-call | flops 4362076160 | bytes 16457728 | tf_op jit(solution)/shard_map/row_grad/pallas_call | solution.py:43
  117.7 1.4 collective-permute-start.23
  119.1 3.3 %collective-permute-done.21.came_ref = bf16[528,512]{1,0:T(8,128)(2,1)S(1)} collective-permute-done((bf16[528,512]{1,0:T(8,128)(2,1)S(1)}, bf16[528,512]{1,0:T(8,128)(2,1)S(1)}, u32[]{:S(2)}, u32[]{:S(2)}) %collective-permute-start.21) | collective-permute-done | bytes 540704 | tf_op jit(solution)/shard_map/ppermute | solution.py:704
  123.9 12.1 %collective-permute-done.23 = bf16[144,1024]{1,0:T(8,128)(2,1)S(1)} collective-permute-done((bf16[144,1024]{1,0:T(8,128)(2,1)S(1)}, bf16[144,1024]{1,0:T(8,128)(2,1)S(1)}, u32[]{:S(2)}, u32[]{:S(2)}) %collective-permute-start.23) | collective-permute-done | bytes 294944 | tf_op jit(solution)/shard_map/ppermute | solution.py:704
  137.5 2.7 %collective-permute-start.26 = (bf16[272,512]{1,0:T(8,128)(2,1)S(1)}, bf16[272,512]{1,0:T(8,128)(2,1)S(1)}, u32[]{:S(2)}, u32[]{:S(2)}) collective-permute-start(bf16[272,512]{1,0:T(8,128)(2,1)S(1)} %merge.4.keep_ref), channel_id=1, source_target_pairs={{0,8},{1,17},{2,10},{3,19},{4,12},{5,21},{6,14},{7,23},{8,0},{9,25... | collective-permute-start | bytes 835592 | tf_op jit(solution)/shard_map/ppermute | solution.py:704
  141.9 2.3 %self_feature.1.self_ref = f32[320,512]{1,0:T(8,128)S(1)} custom-call(s32[2]{0:T(128)S(1)} %copy-done.8, bf16[320,1024]{1,0:T(8,128)(2,1)S(1)} %copy-done.5, bf16[1024,1024]{1,0:T(8,128)(2,1)S(1)} %copy-done.1, bf16[1024,1024]{1,0:T(8,128)(2,1)} %collective-permute-done.8.w_other_in), custom_call_target="tpu_custom_call" | custom-call | flops 335544320 | bytes 5505024 | tf_op jit(solution)/shard_map/self_feature/pallas_call | solution.py:43
  146.0 1.5 collective-permute-done.28.refs_2_
  147.5 5.4 %collective-permute-done.27.refs_1_ = bf16[128,1024]{1,0:T(8,128)(2,1)S(1)} collective-permute-done((bf16[128,1024]{1,0:T(8,128)(2,1)S(1)}, bf16[128,1024]{1,0:T(8,128)(2,1)S(1)}, u32[]{:S(2)}, u32[]{:S(2)}) %collective-permute-start.27) | collective-permute-done | bytes 262176 | tf_op jit(solution)/shard_map/ppermute | solution.py:704
  153.8 1.3 collective-permute-start.33
  156.5 2.7 %collective-permute-done.31.refs_6_ = bf16[128,1024]{1,0:T(8,128)(2,1)S(1)} collective-permute-done((bf16[128,1024]{1,0:T(8,128)(2,1)S(1)}, bf16[128,1024]{1,0:T(8,128)(2,1)S(1)}, u32[]{:S(2)}, u32[]{:S(2)}) %collective-permute-start.31) | collective-permute-done | bytes 262176 | tf_op jit(solution)/shard_map/ppermute | solution.py:704
  159.2 3.7 %collective-permute-done.33.refs_5_ = bf16[128,1024]{1,0:T(8,128)(2,1)S(1)} collective-permute-done((bf16[128,1024]{1,0:T(8,128)(2,1)S(1)}, bf16[128,1024]{1,0:T(8,128)(2,1)S(1)}, u32[]{:S(2)}, u32[]{:S(2)}) %collective-permute-start.33) | collective-permute-done | bytes 262176 | tf_op jit(solution)/shard_map/ppermute | solution.py:704
  163.7 2.0 %collective-permute-start.34 = (bf16[256,512]{1,0:T(8,128)(2,1)S(1)}, bf16[256,512]{1,0:T(8,128)(2,1)S(1)}, u32[]{:S(2)}, u32[]{:S(2)}) collective-permute-start(bf16[256,512]{1,0:T(8,128)(2,1)S(1)} %slice.57.refs_0_), channel_id=1, source_target_pairs={{0,4},{1,3},{2,6},{3,1},{4,0},{5,7},{6,2},{7,5},{8,12},{9,11},{10,... | collective-permute-start | bytes 786440 | tf_op jit(solution)/shard_map/ppermute | solution.py:704
  165.7 1.5 collective-permute-start.41
  167.2 5.2 %collective-permute-start.37 = (f32[1,512]{1,0:T(1,128)S(1)}, f32[1,512]{1,0:T(1,128)S(1)}, u32[]{:S(2)}, u32[]{:S(2)}) collective-permute-start(f32[1,512]{1,0:T(1,128)S(1)} %slice_add_fusion.1), channel_id=1, source_target_pairs={{0,1},{1,0},{2,3},{3,2},{4,5},{5,4},{6,7},{7,6},{8,9},{9,8},{10,11... | collective-permute-start | bytes 6152 | tf_op jit(solution)/shard_map/ppermute | solution.py:713
  172.4 2.7 %unpack.4.refs_1_ = f32[1024,1024]{1,0:T(8,128)} custom-call(s32[2]{0:T(128)S(1)} %copy-done.8, bf16[128,1024]{1,0:T(8,128)(2,1)S(1)} %slice.58.refs_0_, bf16[128,1024]{1,0:T(8,128)(2,1)S(1)} %collective-permute-done.27.refs_1_, bf16[128,1024]{1,0:T(8,128)(2,1)S(1)} %collective-permute-done.28.refs_2_, ...), custom_call_target="tpu_custom_call" | custom-call | bytes 6029312 | tf_op jit(solution)/shard_map/unpack/pallas_call | solution.py:43
  175.9 3.3 %collective-permute-start.43 = (bf16[320,512]{1,0:T(8,128)(2,1)S(1)}, bf16[320,512]{1,0:T(8,128)(2,1)S(1)}, u32[]{:S(2)}, u32[]{:S(2)}) collective-permute-start(bf16[320,512]{1,0:T(8,128)(2,1)S(1)} %row_sums.1.mine_ref), channel_id=1, source_target_pairs={{0,1},{1,0},{2,3},{3,2},{4,5},{5,4},{6,7},{7,6},{8,9},{9,8},{10,11... | collective-permute-start | bytes 983048 | tf_op jit(solution)/shard_map/ppermute | solution.py:713
  180.0 1.4 unpack.5
  181.5 2.0 %feature_step.1 = (f32[320,512]{1,0:T(8,128)}, f32[1,1024]{1,0:T(1,128)}) custom-call(s32[2]{0:T(128)S(1)} %copy-done.8, f32[320,512]{1,0:T(8,128)S(1)} %self_feature.1.self_ref, bf16[320,512]{1,0:T(8,128)(2,1)S(1)} %row_sums.1.mine_ref, bf16[320,512]{1,0:T(8,128)(2,1)S(1)} %collective-permute-done.43.other_ref, f32[1,512]{1,0:T(1,128)S(1)} %slice_add_fusion.1, ...), custom_call_target="tpu_custom_call" | custom-call | flops 335544320 | bytes 4071424 | tf_op jit(solution)/shard_map/feature_step/pallas_call | solution.py:43
  183.5 1.7 collective-permute-done.38.refs_3_
  186.5 2.0 %unpack.6.refs_4_ = f32[1024,1024]{1,0:T(8,128)} custom-call(s32[2]{0:T(128)S(1)} %copy-done.8, bf16[256,512]{1,0:T(8,128)(2,1)S(1)} %slice.57.refs_0_, bf16[256,512]{1,0:T(8,128)(2,1)S(1)} %collective-permute-done.34.refs_1_, bf16[256,512]{1,0:T(8,128)(2,1)S(1)} %collective-permute-done.41.refs_2_, bf16[256,512]{1,0:T(8,128)(2,1)S(1)} %collective-permute-done.38.refs_3_), custom_call_target="tpu_custom_call" | custom-call | bytes 5242880 | tf_op jit(solution)/shard_map/unpack/pallas_call | solution.py:43
  188.6 2.0 %unpack.7 = f32[1024,1024]{1,0:T(8,128)} custom-call(s32[2]{0:T(128)S(1)} %copy-done.8, bf16[256,512]{1,0:T(8,128)(2,1)S(1)} %collective-permute-done.39.refs_0_, bf16[256,512]{1,0:T(8,128)(2,1)S(1)} %collective-permute-done.40.refs_1_, bf16[256,512]{1,0:T(8,128)(2,1)S(1)} %collective-permute-done.42.refs_2_, ...), custom_call_target="tpu_custom_call", output_to_operand_aliasing={{}: (5, {})} | custom-call | bytes 9437184 | tf_op jit(solution)/shard_map/unpack/pallas_call | solution.py:43
  (108 shorter events, 37.3 us)
Async XLA Ops:
  2.4 13.3 %collective-permute-start.2 = (bf16[160,1024]{1,0:T(8,128)(2,1)}, bf16[160,1024]{1,0:T(8,128)(2,1)}, u32[]{:S(2)}, u32[]{:S(2)}) collective-permute-start(bf16[160,1024]{1,0:T(8,128)(2,1)} %constant_dynamic-slice_fusion), channel_id=1, source_target_pairs={{0,16},{1,9},{2,18},{3,11},{4,20},{5,13},{6,22},{7,15},{8,24},{9,1... | collective-permute-start | bytes 983048 | tf_op jit(solution)/shard_map/ppermute | solution.py:704
  7.3 3.1 %collective-permute-start = (s32[32,320]{1,0:T(8,128)}, s32[32,320]{1,0:T(8,128)S(1)}, u32[]{:S(2)}, u32[]{:S(2)}) collective-permute-start(s32[32,320]{1,0:T(8,128)} %sort_slots.1), channel_id=1, source_target_pairs={{0,1},{1,0},{2,3},{3,2},{4,5},{5,4},{6,7},{7,6},{8,9},{9,8},{10,11... | collective-permute-start | bytes 122888 | tf_op jit(solution)/shard_map/ppermute | solution.py:713
  11.9 3.8 %collective-permute-start.1 = (s32[64,320]{1,0:T(8,128)S(1)}, s32[64,320]{1,0:T(8,128)S(1)}, u32[]{:S(2)}, u32[]{:S(2)}) collective-permute-start(s32[64,320]{1,0:T(8,128)S(1)} %pad_add_fusion.1.own_ref), channel_id=1, source_target_pairs={{0,4},{1,3},{2,6},{3,1},{4,0},{5,7},{6,2},{7,5},{8,12},{9,11},{10,... | collective-permute-start | bytes 245768 | tf_op jit(solution)/shard_map/ppermute | solution.py:704
  17.6 16.7 %collective-permute-start.4 = (bf16[320,1024]{1,0:T(8,128)(2,1)}, bf16[320,1024]{1,0:T(8,128)(2,1)}, u32[]{:S(2)}, u32[]{:S(2)}) collective-permute-start(bf16[320,1024]{1,0:T(8,128)(2,1)} %pad_maximum_fusion), channel_id=1, source_target_pairs={{0,8},{1,17},{2,10},{3,19},{4,12},{5,21},{6,14},{7,23},{8,0},{9,25... | collective-permute-start | bytes 1966088 | tf_op jit(solution)/shard_map/ppermute | solution.py:704
  18.3 14.8 %collective-permute-start.5 = (bf16[160,1024]{1,0:T(8,128)(2,1)}, bf16[160,1024]{1,0:T(8,128)(2,1)}, u32[]{:S(2)}, u32[]{:S(2)}) collective-permute-start(bf16[160,1024]{1,0:T(8,128)(2,1)} %collective-permute-done.2.refs_1_.refs_8_), channel_id=1, source_target_pairs={{0,1},{1,0},{2,3},{3,2},{4,5},{5,4},{6,7},{7,6},{8,9},{9,8},{10,11... | collective-permute-start | bytes 983048 | tf_op jit(solution)/shard_map/ppermute | solution.py:713
  21.2 5.0 %collective-permute-start.3 = (s32[128,320]{1,0:T(8,128)S(1)}, s32[128,320]{1,0:T(8,128)}, u32[]{:S(2)}, u32[]{:S(2)}) collective-permute-start(s32[128,320]{1,0:T(8,128)S(1)} %pad_add_fusion), channel_id=1, source_target_pairs={{0,2},{1,5},{2,0},{3,7},{4,6},{5,1},{6,4},{7,3},{8,10},{9,13},{10,... | collective-permute-start | bytes 491528 | tf_op jit(solution)/shard_map/ppermute | solution.py:704
  34.4 3.7 %collective-permute-start.6 = (bf16[320,1024]{1,0:T(8,128)(2,1)}, bf16[320,1024]{1,0:T(8,128)(2,1)}, u32[]{:S(2)}, u32[]{:S(2)}) collective-permute-start(bf16[320,1024]{1,0:T(8,128)(2,1)} %collective-permute-done.4.refs_2_.refs_9_), channel_id=1, source_target_pairs={{0,1},{1,0},{2,3},{3,2},{4,5},{5,4},{6,7},{7,6},{8,9},{9,8},{10,11... | collective-permute-start | bytes 1966088 | tf_op jit(solution)/shard_map/ppermute | solution.py:713
  45.2 14.2 %collective-permute-start.8 = (bf16[1024,1024]{1,0:T(8,128)(2,1)}, bf16[1024,1024]{1,0:T(8,128)(2,1)}, u32[]{:S(2)}, u32[]{:S(2)}) collective-permute-start(bf16[1024,1024]{1,0:T(8,128)(2,1)} %w_in.7), channel_id=1, source_target_pairs={{0,1},{1,0},{2,3},{3,2},{4,5},{5,4},{6,7},{7,6},{8,9},{9,8},{10,11... | collective-permute-start | bytes 6291464 | tf_op jit(solution)/shard_map/ppermute | solution.py:713
  45.6 10.0 %collective-permute-start.9 = (f32[320,512]{1,0:T(8,128)}, f32[320,512]{1,0:T(8,128)}, u32[]{:S(2)}, u32[]{:S(2)}) collective-permute-start(f32[320,512]{1,0:T(8,128)} %get-tuple-element.109), channel_id=1, source_target_pairs={{0,2},{1,5},{2,0},{3,7},{4,6},{5,1},{6,4},{7,3},{8,10},{9,13},{10,... | collective-permute-start | bytes 1966088 | tf_op jit(solution)/shard_map/ppermute | solution.py:704
  54.1 12.8 %collective-permute-start.7 = (f32[320,512]{1,0:T(8,128)}, f32[320,512]{1,0:T(8,128)S(1)}, u32[]{:S(2)}, u32[]{:S(2)}) collective-permute-start(f32[320,512]{1,0:T(8,128)} %get-tuple-element.101), channel_id=1, source_target_pairs={{0,2},{1,5},{2,0},{3,7},{4,6},{5,1},{6,4},{7,3},{8,10},{9,13},{10,... | collective-permute-start | bytes 1966088 | tf_op jit(solution)/shard_map/ppermute | solution.py:704
  57.1 14.6 %collective-permute-start.10 = (f32[320,512]{1,0:T(8,128)S(1)}, f32[320,512]{1,0:T(8,128)S(1)}, u32[]{:S(2)}, u32[]{:S(2)}) collective-permute-start(f32[320,512]{1,0:T(8,128)S(1)} %add.36), channel_id=1, source_target_pairs={{0,4},{1,3},{2,6},{3,1},{4,0},{5,7},{6,2},{7,5},{8,12},{9,11},{10,... | collective-permute-start | bytes 1966088 | tf_op jit(solution)/shard_map/ppermute | solution.py:704
  71.9 1.7 collective-permute-start.11
  77.2 26.9 %copy-start.4 = (bf16[320,1024]{1,0:T(8,128)(2,1)}, bf16[320,1024]{1,0:T(8,128)(2,1)S(1)}, u32[]{:S(2)}) copy-start(bf16[320,1024]{1,0:T(8,128)(2,1)S(1)} %get-tuple-element.122.refs_0_.grad_ref) | copy-start | bytes 1966084
  77.2 6.3 %collective-permute-start.12 = (bf16[160,1024]{1,0:T(8,128)(2,1)S(1)}, bf16[160,1024]{1,0:T(8,128)(2,1)S(1)}, u32[]{:S(2)}, u32[]{:S(2)}) collective-permute-start(bf16[160,1024]{1,0:T(8,128)(2,1)S(1)} %get-tuple-element.114), channel_id=1, source_target_pairs={{0,4},{1,3},{2,6},{3,1},{4,0},{5,7},{6,2},{7,5},{8,12},{9,11},{10,... | collective-permute-start | bytes 983048 | tf_op jit(solution)/shard_map/ppermute | solution.py:704
  78.8 9.5 %collective-permute-start.15 = (bf16[640,256]{1,0:T(8,128)(2,1)S(1)}, bf16[640,256]{1,0:T(8,128)(2,1)S(1)}, u32[]{:S(2)}, u32[]{:S(2)}) collective-permute-start(bf16[640,256]{1,0:T(8,128)(2,1)S(1)} %get-tuple-element.116), channel_id=1, source_target_pairs={{0,2},{1,5},{2,0},{3,7},{4,6},{5,1},{6,4},{7,3},{8,10},{9,13},{10,... | collective-permute-start | bytes 983048 | tf_op jit(solution)/shard_map/ppermute | solution.py:704
  79.6 12.1 %collective-permute-start.13 = (bf16[160,1024]{1,0:T(8,128)(2,1)S(1)}, bf16[160,1024]{1,0:T(8,128)(2,1)S(1)}, u32[]{:S(2)}, u32[]{:S(2)}) collective-permute-start(bf16[160,1024]{1,0:T(8,128)(2,1)S(1)} %get-tuple-element.114), channel_id=1, source_target_pairs={{0,2},{1,5},{2,0},{3,7},{4,6},{5,1},{6,4},{7,3},{8,10},{9,13},{10,... | collective-permute-start | bytes 983048 | tf_op jit(solution)/shard_map/ppermute | solution.py:704
  83.5 13.8 %collective-permute-start.14 = (bf16[160,1024]{1,0:T(8,128)(2,1)S(1)}, bf16[160,1024]{1,0:T(8,128)(2,1)S(1)}, u32[]{:S(2)}, u32[]{:S(2)}) collective-permute-start(bf16[160,1024]{1,0:T(8,128)(2,1)S(1)} %collective-permute-done.12.refs_1_), channel_id=1, source_target_pairs={{0,2},{1,5},{2,0},{3,7},{4,6},{5,1},{6,4},{7,3},{8,10},{9,13},{10,... | collective-permute-start | bytes 983048 | tf_op jit(solution)/shard_map/ppermute | solution.py:704
  88.3 9.1 %collective-permute-start.16 = (bf16[640,256]{1,0:T(8,128)(2,1)S(1)}, bf16[640,256]{1,0:T(8,128)(2,1)S(1)}, u32[]{:S(2)}, u32[]{:S(2)}) collective-permute-start(bf16[640,256]{1,0:T(8,128)(2,1)S(1)} %pad_maximum_fusion.1), channel_id=1, source_target_pairs={{0,4},{1,3},{2,6},{3,1},{4,0},{5,7},{6,2},{7,5},{8,12},{9,11},{10,... | collective-permute-start | bytes 983048 | tf_op jit(solution)/shard_map/ppermute | solution.py:704
  89.0 10.5 %collective-permute-start.17 = (bf16[160,1024]{1,0:T(8,128)(2,1)S(1)}, bf16[160,1024]{1,0:T(8,128)(2,1)S(1)}, u32[]{:S(2)}, u32[]{:S(2)}) collective-permute-start(bf16[160,1024]{1,0:T(8,128)(2,1)S(1)} %collective-permute-done.12.refs_1_), channel_id=1, source_target_pairs={{0,1},{1,0},{2,3},{3,2},{4,5},{5,4},{6,7},{7,6},{8,9},{9,8},{10,11... | collective-permute-start | bytes 983048 | tf_op jit(solution)/shard_map/ppermute | solution.py:713
  91.8 7.7 %collective-permute-start.18 = (bf16[160,1024]{1,0:T(8,128)(2,1)S(1)}, bf16[160,1024]{1,0:T(8,128)(2,1)S(1)}, u32[]{:S(2)}, u32[]{:S(2)}) collective-permute-start(bf16[160,1024]{1,0:T(8,128)(2,1)S(1)} %collective-permute-done.13.refs_2_), channel_id=1, source_target_pairs={{0,1},{1,0},{2,3},{3,2},{4,5},{5,4},{6,7},{7,6},{8,9},{9,8},{10,11... | collective-permute-start | bytes 983048 | tf_op jit(solution)/shard_map/ppermute | solution.py:713
  97.4 3.3 %collective-permute-start.19 = (bf16[160,1024]{1,0:T(8,128)(2,1)S(1)}, bf16[160,1024]{1,0:T(8,128)(2,1)S(1)}, u32[]{:S(2)}, u32[]{:S(2)}) collective-permute-start(bf16[160,1024]{1,0:T(8,128)(2,1)S(1)} %collective-permute-done.14.refs_3_), channel_id=1, source_target_pairs={{0,1},{1,0},{2,3},{3,2},{4,5},{5,4},{6,7},{7,6},{8,9},{9,8},{10,11... | collective-permute-start | bytes 983048 | tf_op jit(solution)/shard_map/ppermute | solution.py:713
  104.1 9.7 %collective-permute-start.20 = (bf16[144,1024]{1,0:T(8,128)(2,1)S(1)}, bf16[144,1024]{1,0:T(8,128)(2,1)S(1)}, u32[]{:S(2)}, u32[]{:S(2)}) collective-permute-start(bf16[144,1024]{1,0:T(8,128)(2,1)S(1)} %get-tuple-element.135), channel_id=1, source_target_pairs={{0,8},{1,17},{2,10},{3,19},{4,12},{5,21},{6,14},{7,23},{8,0},{9,25... | collective-permute-start | bytes 884744 | tf_op jit(solution)/shard_map/ppermute | solution.py:704
  113.8 28.1 %copy-start.1 = (bf16[1024,1024]{1,0:T(8,128)(2,1)S(1)}, bf16[1024,1024]{1,0:T(8,128)(2,1)}, u32[]{:S(2)}) copy-start(bf16[1024,1024]{1,0:T(8,128)(2,1)} %w_in.7) | copy-start | bytes 6291460
  113.8 28.1 %copy-start.5 = (bf16[320,1024]{1,0:T(8,128)(2,1)S(1)}, bf16[320,1024]{1,0:T(8,128)(2,1)}, u32[]{:S(2)}) copy-start(bf16[320,1024]{1,0:T(8,128)(2,1)} %copy-done.4) | copy-start | bytes 1966084
  113.8 8.6 %collective-permute-start.21 = (bf16[528,512]{1,0:T(8,128)(2,1)S(1)}, bf16[528,512]{1,0:T(8,128)(2,1)S(1)}, u32[]{:S(2)}, u32[]{:S(2)}) collective-permute-start(bf16[528,512]{1,0:T(8,128)(2,1)S(1)} %get-tuple-element.137), channel_id=1, source_target_pairs={{0,2},{1,5},{2,0},{3,7},{4,6},{5,1},{6,4},{7,3},{8,10},{9,13},{10,... | collective-permute-start | bytes 1622024 | tf_op jit(solution)/shard_map/ppermute | solution.py:704
  114.7 21.4 %collective-permute-start.24 = (bf16[320,512]{1,0:T(8,128)(2,1)S(1)}, bf16[320,512]{1,0:T(8,128)(2,1)S(1)}, u32[]{:S(2)}, u32[]{:S(2)}) collective-permute-start(bf16[320,512]{1,0:T(8,128)(2,1)S(1)} %get-tuple-element.143), channel_id=1, source_target_pairs={{0,8},{1,17},{2,10},{3,19},{4,12},{5,21},{6,14},{7,23},{8,0},{9,25... | collective-permute-start | bytes 983048 | tf_op jit(solution)/shard_map/ppermute | solution.py:704
  115.8 21.2 %collective-permute-start.25 = (bf16[320,512]{1,0:T(8,128)(2,1)S(1)}, bf16[320,512]{1,0:T(8,128)(2,1)S(1)}, u32[]{:S(2)}, u32[]{:S(2)}) collective-permute-start(bf16[320,512]{1,0:T(8,128)(2,1)S(1)} %get-tuple-element.144), channel_id=1, source_target_pairs={{0,8},{1,17},{2,10},{3,19},{4,12},{5,21},{6,14},{7,23},{8,0},{9,25... | collective-permute-start | bytes 983048 | tf_op jit(solution)/shard_map/ppermute | solution.py:704
  117.7 18.4 %collective-permute-start.23 = (bf16[144,1024]{1,0:T(8,128)(2,1)S(1)}, bf16[144,1024]{1,0:T(8,128)(2,1)S(1)}, u32[]{:S(2)}, u32[]{:S(2)}) collective-permute-start(bf16[144,1024]{1,0:T(8,128)(2,1)S(1)} %merge.3), channel_id=1, source_target_pairs={{0,16},{1,9},{2,18},{3,11},{4,20},{5,13},{6,22},{7,15},{8,24},{9,1... | collective-permute-start | bytes 884744 | tf_op jit(solution)/shard_map/ppermute | solution.py:704
  123.1 13.9 %collective-permute-start.22 = (bf16[272,512]{1,0:T(8,128)(2,1)S(1)}, bf16[272,512]{1,0:T(8,128)(2,1)S(1)}, u32[]{:S(2)}, u32[]{:S(2)}) collective-permute-start(bf16[272,512]{1,0:T(8,128)(2,1)S(1)} %get-tuple-element.139), channel_id=1, source_target_pairs={{0,4},{1,3},{2,6},{3,1},{4,0},{5,7},{6,2},{7,5},{8,12},{9,11},{10,... | collective-permute-start | bytes 835592 | tf_op jit(solution)/shard_map/ppermute | solution.py:704
  137.5 15.4 %collective-permute-start.26 = (bf16[272,512]{1,0:T(8,128)(2,1)S(1)}, bf16[272,512]{1,0:T(8,128)(2,1)S(1)}, u32[]{:S(2)}, u32[]{:S(2)}) collective-permute-start(bf16[272,512]{1,0:T(8,128)(2,1)S(1)} %merge.4.keep_ref), channel_id=1, source_target_pairs={{0,8},{1,17},{2,10},{3,19},{4,12},{5,21},{6,14},{7,23},{8,0},{9,25... | collective-permute-start | bytes 835592 | tf_op jit(solution)/shard_map/ppermute | solution.py:704
  140.4 5.6 %collective-permute-start.29 = (bf16[128,1024]{1,0:T(8,128)(2,1)S(1)}, bf16[128,1024]{1,0:T(8,128)(2,1)S(1)}, u32[]{:S(2)}, u32[]{:S(2)}) collective-permute-start(bf16[128,1024]{1,0:T(8,128)(2,1)S(1)} %slice.58.refs_0_), channel_id=1, source_target_pairs={{0,2},{1,5},{2,0},{3,7},{4,6},{5,1},{6,4},{7,3},{8,10},{9,13},{10,... | collective-permute-start | bytes 786440 | tf_op jit(solution)/shard_map/ppermute | solution.py:704
  140.6 6.9 %collective-permute-start.28 = (bf16[128,1024]{1,0:T(8,128)(2,1)S(1)}, bf16[128,1024]{1,0:T(8,128)(2,1)S(1)}, u32[]{:S(2)}, u32[]{:S(2)}) collective-permute-start(bf16[128,1024]{1,0:T(8,128)(2,1)S(1)} %slice.58.refs_0_), channel_id=1, source_target_pairs={{0,4},{1,3},{2,6},{3,1},{4,0},{5,7},{6,2},{7,5},{8,12},{9,11},{10,... | collective-permute-start | bytes 786440 | tf_op jit(solution)/shard_map/ppermute | solution.py:704
  141.8 11.1 %collective-permute-start.27 = (bf16[128,1024]{1,0:T(8,128)(2,1)S(1)}, bf16[128,1024]{1,0:T(8,128)(2,1)S(1)}, u32[]{:S(2)}, u32[]{:S(2)}) collective-permute-start(bf16[128,1024]{1,0:T(8,128)(2,1)S(1)} %slice.58.refs_0_), channel_id=1, source_target_pairs={{0,8},{1,17},{2,10},{3,19},{4,12},{5,21},{6,14},{7,23},{8,0},{9,25... | collective-permute-start | bytes 786440 | tf_op jit(solution)/shard_map/ppermute | solution.py:704
  153.5 9.4 %collective-permute-start.30 = (bf16[272,512]{1,0:T(8,128)(2,1)S(1)}, bf16[272,512]{1,0:T(8,128)(2,1)S(1)}, u32[]{:S(2)}, u32[]{:S(2)}) collective-permute-start(bf16[272,512]{1,0:T(8,128)(2,1)S(1)} %merge.5), channel_id=1, source_target_pairs={{0,16},{1,9},{2,18},{3,11},{4,20},{5,13},{6,22},{7,15},{8,24},{9,1... | collective-permute-start | bytes 835592 | tf_op jit(solution)/shard_map/ppermute | solution.py:704
  153.6 5.6 %collective-permute-start.31 = (bf16[128,1024]{1,0:T(8,128)(2,1)S(1)}, bf16[128,1024]{1,0:T(8,128)(2,1)S(1)}, u32[]{:S(2)}, u32[]{:S(2)}) collective-permute-start(bf16[128,1024]{1,0:T(8,128)(2,1)S(1)} %collective-permute-done.28.refs_2_), channel_id=1, source_target_pairs={{0,2},{1,5},{2,0},{3,7},{4,6},{5,1},{6,4},{7,3},{8,10},{9,13},{10,... | collective-permute-start | bytes 786440 | tf_op jit(solution)/shard_map/ppermute | solution.py:704
  153.8 9.1 %collective-permute-start.33 = (bf16[128,1024]{1,0:T(8,128)(2,1)S(1)}, bf16[128,1024]{1,0:T(8,128)(2,1)S(1)}, u32[]{:S(2)}, u32[]{:S(2)}) collective-permute-start(bf16[128,1024]{1,0:T(8,128)(2,1)S(1)} %collective-permute-done.27.refs_1_), channel_id=1, source_target_pairs={{0,2},{1,5},{2,0},{3,7},{4,6},{5,1},{6,4},{7,3},{8,10},{9,13},{10,... | collective-permute-start | bytes 786440 | tf_op jit(solution)/shard_map/ppermute | solution.py:704
  155.1 7.8 %collective-permute-start.32 = (bf16[128,1024]{1,0:T(8,128)(2,1)S(1)}, bf16[128,1024]{1,0:T(8,128)(2,1)S(1)}, u32[]{:S(2)}, u32[]{:S(2)}) collective-permute-start(bf16[128,1024]{1,0:T(8,128)(2,1)S(1)} %collective-permute-done.27.refs_1_), channel_id=1, source_target_pairs={{0,4},{1,3},{2,6},{3,1},{4,0},{5,7},{6,2},{7,5},{8,12},{9,11},{10,... | collective-permute-start | bytes 786440 | tf_op jit(solution)/shard_map/ppermute | solution.py:704
  163.0 12.1 %collective-permute-start.36 = (bf16[320,512]{1,0:T(8,128)(2,1)S(1)}, bf16[320,512]{1,0:T(8,128)(2,1)S(1)}, u32[]{:S(2)}, u32[]{:S(2)}) collective-permute-start(bf16[320,512]{1,0:T(8,128)(2,1)S(1)} %add_convert_fusion), channel_id=1, source_target_pairs={{0,16},{1,9},{2,18},{3,11},{4,20},{5,13},{6,22},{7,15},{8,24},{9,1... | collective-permute-start | bytes 983048 | tf_op jit(solution)/shard_map/ppermute | solution.py:704
  163.7 11.4 %collective-permute-start.35 = (bf16[128,1024]{1,0:T(8,128)(2,1)S(1)}, bf16[128,1024]{1,0:T(8,128)(2,1)S(1)}, u32[]{:S(2)}, u32[]{:S(2)}) collective-permute-start(bf16[128,1024]{1,0:T(8,128)(2,1)S(1)} %collective-permute-done.32.refs_3_), channel_id=1, source_target_pairs={{0,2},{1,5},{2,0},{3,7},{4,6},{5,1},{6,4},{7,3},{8,10},{9,13},{10,... | collective-permute-start | bytes 786440 | tf_op jit(solution)/shard_map/ppermute | solution.py:704
  163.7 11.4 %collective-permute-start.34 = (bf16[256,512]{1,0:T(8,128)(2,1)S(1)}, bf16[256,512]{1,0:T(8,128)(2,1)S(1)}, u32[]{:S(2)}, u32[]{:S(2)}) collective-permute-start(bf16[256,512]{1,0:T(8,128)(2,1)S(1)} %slice.57.refs_0_), channel_id=1, source_target_pairs={{0,4},{1,3},{2,6},{3,1},{4,0},{5,7},{6,2},{7,5},{8,12},{9,11},{10,... | collective-permute-start | bytes 786440 | tf_op jit(solution)/shard_map/ppermute | solution.py:704
  165.7 13.5 %collective-permute-start.41 = (bf16[256,512]{1,0:T(8,128)(2,1)S(1)}, bf16[256,512]{1,0:T(8,128)(2,1)S(1)}, u32[]{:S(2)}, u32[]{:S(2)}) collective-permute-start(bf16[256,512]{1,0:T(8,128)(2,1)S(1)} %slice.57.refs_0_), channel_id=1, source_target_pairs={{0,2},{1,5},{2,0},{3,7},{4,6},{5,1},{6,4},{7,3},{8,10},{9,13},{10,... | collective-permute-start | bytes 786440 | tf_op jit(solution)/shard_map/ppermute | solution.py:704
  167.2 7.9 %collective-permute-start.37 = (f32[1,512]{1,0:T(1,128)S(1)}, f32[1,512]{1,0:T(1,128)S(1)}, u32[]{:S(2)}, u32[]{:S(2)}) collective-permute-start(f32[1,512]{1,0:T(1,128)S(1)} %slice_add_fusion.1), channel_id=1, source_target_pairs={{0,1},{1,0},{2,3},{3,2},{4,5},{5,4},{6,7},{7,6},{8,9},{9,8},{10,11... | collective-permute-start | bytes 6152 | tf_op jit(solution)/shard_map/ppermute | solution.py:713
  175.9 5.6 %collective-permute-start.43 = (bf16[320,512]{1,0:T(8,128)(2,1)S(1)}, bf16[320,512]{1,0:T(8,128)(2,1)S(1)}, u32[]{:S(2)}, u32[]{:S(2)}) collective-permute-start(bf16[320,512]{1,0:T(8,128)(2,1)S(1)} %row_sums.1.mine_ref), channel_id=1, source_target_pairs={{0,1},{1,0},{2,3},{3,2},{4,5},{5,4},{6,7},{7,6},{8,9},{9,8},{10,11... | collective-permute-start | bytes 983048 | tf_op jit(solution)/shard_map/ppermute | solution.py:713
  179.1 4.4 %collective-permute-start.39 = (bf16[256,512]{1,0:T(8,128)(2,1)S(1)}, bf16[256,512]{1,0:T(8,128)(2,1)S(1)}, u32[]{:S(2)}, u32[]{:S(2)}) collective-permute-start(bf16[256,512]{1,0:T(8,128)(2,1)S(1)} %slice.57.refs_0_), channel_id=1, source_target_pairs={{0,1},{1,0},{2,3},{3,2},{4,5},{5,4},{6,7},{7,6},{8,9},{9,8},{10,11... | collective-permute-start | bytes 786440 | tf_op jit(solution)/shard_map/ppermute | solution.py:713
  179.2 4.3 %collective-permute-start.42 = (bf16[256,512]{1,0:T(8,128)(2,1)S(1)}, bf16[256,512]{1,0:T(8,128)(2,1)S(1)}, u32[]{:S(2)}, u32[]{:S(2)}) collective-permute-start(bf16[256,512]{1,0:T(8,128)(2,1)S(1)} %collective-permute-done.41.refs_2_), channel_id=1, source_target_pairs={{0,1},{1,0},{2,3},{3,2},{4,5},{5,4},{6,7},{7,6},{8,9},{9,8},{10,11... | collective-permute-start | bytes 786440 | tf_op jit(solution)/shard_map/ppermute | solution.py:713
  179.6 3.9 %collective-permute-start.40 = (bf16[256,512]{1,0:T(8,128)(2,1)S(1)}, bf16[256,512]{1,0:T(8,128)(2,1)S(1)}, u32[]{:S(2)}, u32[]{:S(2)}) collective-permute-start(bf16[256,512]{1,0:T(8,128)(2,1)S(1)} %collective-permute-done.34.refs_1_), channel_id=1, source_target_pairs={{0,1},{1,0},{2,3},{3,2},{4,5},{5,4},{6,7},{7,6},{8,9},{9,8},{10,11... | collective-permute-start | bytes 786440 | tf_op jit(solution)/shard_map/ppermute | solution.py:713
  179.7 5.5 %collective-permute-start.38 = (bf16[256,512]{1,0:T(8,128)(2,1)S(1)}, bf16[256,512]{1,0:T(8,128)(2,1)S(1)}, u32[]{:S(2)}, u32[]{:S(2)}) collective-permute-start(bf16[256,512]{1,0:T(8,128)(2,1)S(1)} %collective-permute-done.34.refs_1_), channel_id=1, source_target_pairs={{0,2},{1,5},{2,0},{3,7},{4,6},{5,1},{6,4},{7,3},{8,10},{9,13},{10,... | collective-permute-start | bytes 786440 | tf_op jit(solution)/shard_map/ppermute | solution.py:704
  185.2 3.3 %collective-permute-start.44 = (bf16[256,512]{1,0:T(8,128)(2,1)S(1)}, bf16[256,512]{1,0:T(8,128)(2,1)S(1)}, u32[]{:S(2)}, u32[]{:S(2)}) collective-permute-start(bf16[256,512]{1,0:T(8,128)(2,1)S(1)} %collective-permute-done.38.refs_3_), channel_id=1, source_target_pairs={{0,1},{1,0},{2,3},{3,2},{4,5},{5,4},{6,7},{7,6},{8,9},{9,8},{10,11... | collective-permute-start | bytes 786440 | tf_op jit(solution)/shard_map/ppermute | solution.py:713
  (11 other events, 72.5 us)

commit v7 on v6

--- a/solution.py
+++ b/solution.py
@@ -786,9 +786,7 @@
     w_came = line_swap(w_sum, 1)
     q_came = fence(q_came)
     q_keep, q_send = fold(place, q_keep, q_came)
-    q_came, w_came, stay, rows_go, rows_late = fence(
-        (plane_swap(q_send, 1), w_came, stay, rows_go, rows_late)
-    )
+    q_came, w_came, stay, rows_go = fence((plane_swap(q_send, 1), w_came, stay, rows_go))
     for step in range(2, line_bits):
         w_sum = merge(place, w_sum, w_came)
         w_came = line_swap(w_sum, step)
@@ -798,8 +796,8 @@
     w_far = line_swap(w_near, 0)
     near_one, near_two = plane_swap(w_near, 1), plane_swap(w_near, 0)
     self_grad = self_feature(place, grad_linear, w_weight, w_other)
-    q_came, w_far, near_one, near_two, biases, self_grad = fence(
-        (q_came, w_far, near_one, near_two, biases, self_grad)
+    q_came, w_far, near_one, near_two, biases, self_grad, rows_late = fence(
+        (q_came, w_far, near_one, near_two, biases, self_grad, rows_late)
     )
     for step in range(1, line_bits):
         q_sum = merge(place, q_sum, q_came)

time: 191 us -> 189 us (0.990)
  waiting for transfers between devices: 67.8 us -> 65.4 us
    ppermute x31, waiting for transfers between devices: 61.8 us -> 59.3 us  [swap(): return lax.ppermute(value, ('nodes', 'stream'), pairs)]
  transfers between devices with their start and end apart: 45 -> 45, of which waited for: 24 -> 22; matrix products, arithmetic and copies ran while one was open for 3% -> 3% of each run, Pallas kernels for 21% -> 22%
where the time goes in v7:
time: 189 us
  waiting for transfers between devices  65.4 us (35%)
  Pallas kernels  58.2 us (31%)
  starting transfers between devices  52.4 us (28%)
  other arithmetic  6.61 us (3%)
  local copies, waits for them, and re-layouts  4.66 us (2%)
    ppermute x31, waiting for transfers between devices, swap(): return lax.ppermute(value, ('nodes', 'stream'), pairs)  59.3 us
    pallas_call x20, Pallas kernels, call(): pl.pallas_call(kernel, name=name, out_shape=list(outs), in_specs=spaced(p...  58.2 us
    ppermute x31, starting transfers between devices, swap(): return lax.ppermute(value, ('nodes', 'stream'), pairs)  31 us
    ppermute x14, starting transfers between devices, trade(): return lax.ppermute(value, 'stream', [(0, 1), (1, 0)])  21.4 us
    ppermute x14, waiting for transfers between devices, trade(): return lax.ppermute(value, 'stream', [(0, 1), (1, 0)])  6.05 us
  transfers between devices with their start and end apart: 45, of which 22 were waited for; matrix products, arithmetic and copies ran while one was open for 3% of the time, Pallas kernels for 22%

profile of v7, /device:TPU:1, one launch (start us, length us, event | category | flops | bytes accessed | tf_op | source)
XLA Modules:
  0.0 188.6 jit_solution(16545390333558880619)
XLA Ops:
  0.6 1.7 constant_dynamic-slice_fusion
  2.4 2.1 %collective-permute-start.2 = (bf16[160,1024]{1,0:T(8,128)(2,1)}, bf16[160,1024]{1,0:T(8,128)(2,1)}, u32[]{:S(2)}, u32[]{:S(2)}) collective-permute-start(bf16[160,1024]{1,0:T(8,128)(2,1)} %constant_dynamic-slice_fusion), channel_id=1, source_target_pairs={{0,16},{1,9},{2,18},{3,11},{4,20},{5,13},{6,22},{7,15},{8,24},{9,1... | collective-permute-start | bytes 983048 | tf_op jit(solution)/shard_map/ppermute | solution.py:704
  5.1 2.2 %sort_slots.1 = s32[32,320]{1,0:T(8,128)} custom-call(s32[2]{0:T(128)} %pad_add_fusion.2.place_ref, s32[25,320]{1,0:T(8,128)} %bitcast.12, s32[25,320]{1,0:T(8,128)} %bitcast.13, s32[25,320]{1,0:T(8,128)} %bitcast.14), custom_call_target="tpu_custom_call" | custom-call | bytes 136960 | tf_op jit(solution)/shard_map/sort_slots/pallas_call | solution.py:43
  7.3 2.0 %collective-permute-start = (s32[32,320]{1,0:T(8,128)}, s32[32,320]{1,0:T(8,128)S(1)}, u32[]{:S(2)}, u32[]{:S(2)}) collective-permute-start(s32[32,320]{1,0:T(8,128)} %sort_slots.1), channel_id=1, source_target_pairs={{0,1},{1,0},{2,3},{3,2},{4,5},{5,4},{6,7},{7,6},{8,9},{9,8},{10,11... | collective-permute-start | bytes 122888 | tf_op jit(solution)/shard_map/ppermute | solution.py:713
  13.1 2.6 %collective-permute-done.1.next_ref = s32[64,320]{1,0:T(8,128)S(1)} collective-permute-done((s32[64,320]{1,0:T(8,128)S(1)}, s32[64,320]{1,0:T(8,128)S(1)}, u32[]{:S(2)}, u32[]{:S(2)}) %collective-permute-start.1) | collective-permute-done | bytes 81952 | tf_op jit(solution)/shard_map/ppermute | solution.py:704
  15.6 2.0 %pad_maximum_fusion = bf16[320,1024]{1,0:T(8,128)(2,1)} fusion(bf16[160,1024]{1,0:T(8,128)(2,1)} %collective-permute-done.2.refs_1_.refs_8_, bf16[160,1024]{1,0:T(8,128)(2,1)} %constant_dynamic-slice_fusion), kind=kLoop, calls=%fused_computation | loop fusion | flops 1310720 | bytes 1310720 | tf_op jit(solution)/shard_map/concatenate | solution.py:733
  18.3 2.1 %collective-permute-start.5 = (bf16[160,1024]{1,0:T(8,128)(2,1)}, bf16[160,1024]{1,0:T(8,128)(2,1)}, u32[]{:S(2)}, u32[]{:S(2)}) collective-permute-start(bf16[160,1024]{1,0:T(8,128)(2,1)} %collective-permute-done.2.refs_1_.refs_8_), channel_id=1, source_target_pairs={{0,1},{1,0},{2,3},{3,2},{4,5},{5,4},{6,7},{7,6},{8,9},{9,8},{10,11... | collective-permute-start | bytes 983048 | tf_op jit(solution)/shard_map/ppermute | solution.py:713
  21.2 1.3 collective-permute-start.3
  22.5 3.7 %collective-permute-done.3.rest_ref = s32[128,320]{1,0:T(8,128)} collective-permute-done((s32[128,320]{1,0:T(8,128)S(1)}, s32[128,320]{1,0:T(8,128)}, u32[]{:S(2)}, u32[]{:S(2)}) %collective-permute-start.3) | collective-permute-done | bytes 163872 | tf_op jit(solution)/shard_map/ppermute | solution.py:704
  26.2 6.9 %slot_matrix.1 = (f32[1280,8]{1,0:T(8,128)}, bf16[1280,1280]{1,0:T(8,128)(2,1)}) custom-call(s32[2]{0:T(128)} %pad_add_fusion.2.place_ref, s32[64,320]{1,0:T(8,128)} %copy-done.12, s32[64,320]{1,0:T(8,128)} %copy-done.13, s32[128,320]{1,0:T(8,128)} %collective-permute-done.3.rest_ref), custom_call_target="tpu_custom_call" | custom-call | flops 1 | bytes 1 | tf_op jit(solution)/shard_map/slot_matrix/pallas_call | solution.py:43
  34.4 1.6 collective-permute-start.6
  36.0 2.1 %collective-permute-done.6.refs_4_.refs_11_ = bf16[320,1024]{1,0:T(8,128)(2,1)} collective-permute-done((bf16[320,1024]{1,0:T(8,128)(2,1)}, bf16[320,1024]{1,0:T(8,128)(2,1)}, u32[]{:S(2)}, u32[]{:S(2)}) %collective-permute-start.6) | collective-permute-done | bytes 655392 | tf_op jit(solution)/shard_map/ppermute | solution.py:713
  38.1 7.1 %first_sums.1 = (f32[320,512]{1,0:T(8,128)}, bf16[1280,512]{1,0:T(8,128)(2,1)}, bf16[1280,512]{1,0:T(8,128)(2,1)}) custom-call(s32[2]{0:T(128)} %pad_add_fusion.2.place_ref, f32[1,1024]{1,0:T(1,128)} %bitcast.16, bf16[1024,1024]{1,0:T(8,128)(2,1)} %q_in.3, bf16[1280,1280]{1,0:T(8,128)(2,1)} %get-tuple-element.96.matrix_in, bf16[320,1024]{1,0:T(8,128)(2,1)} %refs_7_.1, ...), custom_call_target="tpu_custom_call" | custom-call | flops 2181038080 | bytes 11276288 | tf_op jit(solution)/shard_map/first_sums/pallas_call | solution.py:43
  46.9 7.2 %more_sums.1 = (f32[320,512]{1,0:T(8,128)}, f32[320,512]{1,0:T(8,128)}, f32[320,512]{1,0:T(8,128)}) custom-call(s32[2]{0:T(128)} %pad_add_fusion.2.place_ref, bf16[1280,1280]{1,0:T(8,128)(2,1)} %get-tuple-element.96.matrix_in, bf16[1280,512]{1,0:T(8,128)(2,1)} %get-tuple-element.99.refs_0_.high_in, bf16[1280,512]{1,0:T(8,128)(2,1)} %get-tuple-element.100.refs_1_), custom_call_target="tpu_custom_call" | custom-call | flops 2516582400 | bytes 7864320 | tf_op jit(solution)/shard_map/more_sums/pallas_call | solution.py:43
  55.7 1.4 add.36
  60.5 3.0 %self_product.1.self_ref = f32[320,1024]{1,0:T(8,128)S(1)} custom-call(s32[2]{0:T(128)S(1)} %copy-done.8, bf16[320,1024]{1,0:T(8,128)(2,1)S(1)} %copy-done.2, f32[1,1024]{1,0:T(1,128)S(1)} %bitcast.11, bf16[1024,1024]{1,0:T(8,128)(2,1)S(1)} %copy-done, bf16[1024,1024]{1,0:T(8,128)(2,1)} %collective-permute-done.8.w_other_in), custom_call_target="tpu_custom_call" | custom-call | flops 671088640 | bytes 6164480 | tf_op jit(solution)/shard_map/self_product/pallas_call | solution.py:43
  63.6 3.4 %collective-permute-done.7 = f32[320,512]{1,0:T(8,128)S(1)} collective-permute-done((f32[320,512]{1,0:T(8,128)}, f32[320,512]{1,0:T(8,128)S(1)}, u32[]{:S(2)}, u32[]{:S(2)}) %collective-permute-start.7) | collective-permute-done | bytes 655392 | tf_op jit(solution)/shard_map/ppermute | solution.py:704
  66.9 4.8 %collective-permute-done.10 = f32[320,512]{1,0:T(8,128)S(1)} collective-permute-done((f32[320,512]{1,0:T(8,128)S(1)}, f32[320,512]{1,0:T(8,128)S(1)}, u32[]{:S(2)}, u32[]{:S(2)}) %collective-permute-start.10) | collective-permute-done | bytes 655392 | tf_op jit(solution)/shard_map/ppermute | solution.py:704
  72.0 1.6 collective-permute-done.11.other_ref
  73.6 3.5 %node_step.1 = (f32[320,1024]{1,0:T(8,128)}, bf16[320,1024]{1,0:T(8,128)(2,1)S(1)}, bf16[160,1024]{1,0:T(8,128)(2,1)S(1)}) custom-call(s32[2]{0:T(128)S(1)} %copy-done.8, bf16[320,512]{1,0:T(8,128)(2,1)S(1)} %divide_convert_fusion.mine_ref, bf16[320,512]{1,0:T(8,128)(2,1)S(1)} %collective-permute-done.11.other_ref, f32[320,1024]{1,0:T(8,128)S(1)} %self_product.1.self_ref, ...), custom_call_target="tpu_custom_call" | custom-call | flops 671088640 | bytes 9109504 | tf_op jit(solution)/shard_map/node_step/pallas_call | solution.py:43
  80.3 3.2 %collective-permute-done.12.refs_1_ = bf16[160,1024]{1,0:T(8,128)(2,1)S(1)} collective-permute-done((bf16[160,1024]{1,0:T(8,128)(2,1)S(1)}, bf16[160,1024]{1,0:T(8,128)(2,1)S(1)}, u32[]{:S(2)}, u32[]{:S(2)}) %collective-permute-start.12) | collective-permute-done | bytes 327712 | tf_op jit(solution)/shard_map/ppermute | solution.py:704
  84.7 3.5 %collective-permute-done.15.refs_8_ = bf16[640,256]{1,0:T(8,128)(2,1)S(1)} collective-permute-done((bf16[640,256]{1,0:T(8,128)(2,1)S(1)}, bf16[640,256]{1,0:T(8,128)(2,1)S(1)}, u32[]{:S(2)}, u32[]{:S(2)}) %collective-permute-start.15) | collective-permute-done | bytes 327712 | tf_op jit(solution)/shard_map/ppermute | solution.py:704
  89.0 2.4 %collective-permute-start.17 = (bf16[160,1024]{1,0:T(8,128)(2,1)S(1)}, bf16[160,1024]{1,0:T(8,128)(2,1)S(1)}, u32[]{:S(2)}, u32[]{:S(2)}) collective-permute-start(bf16[160,1024]{1,0:T(8,128)(2,1)S(1)} %collective-permute-done.12.refs_1_), channel_id=1, source_target_pairs={{0,1},{1,0},{2,3},{3,2},{4,5},{5,4},{6,7},{7,6},{8,9},{9,8},{10,11... | collective-permute-start | bytes 983048 | tf_op jit(solution)/shard_map/ppermute | solution.py:713
  92.1 5.2 %collective-permute-done.14.refs_3_ = bf16[160,1024]{1,0:T(8,128)(2,1)S(1)} collective-permute-done((bf16[160,1024]{1,0:T(8,128)(2,1)S(1)}, bf16[160,1024]{1,0:T(8,128)(2,1)S(1)}, u32[]{:S(2)}, u32[]{:S(2)}) %collective-permute-start.14) | collective-permute-done | bytes 327712 | tf_op jit(solution)/shard_map/ppermute | solution.py:704
  97.4 2.1 %collective-permute-start.19 = (bf16[160,1024]{1,0:T(8,128)(2,1)S(1)}, bf16[160,1024]{1,0:T(8,128)(2,1)S(1)}, u32[]{:S(2)}, u32[]{:S(2)}) collective-permute-start(bf16[160,1024]{1,0:T(8,128)(2,1)S(1)} %collective-permute-done.14.refs_3_), channel_id=1, source_target_pairs={{0,1},{1,0},{2,3},{3,2},{4,5},{5,4},{6,7},{7,6},{8,9},{9,8},{10,11... | collective-permute-start | bytes 983048 | tf_op jit(solution)/shard_map/ppermute | solution.py:713
  100.7 3.3 %self_weight.1 = (bf16[144,1024]{1,0:T(8,128)(2,1)S(1)}, bf16[144,1024]{1,0:T(8,128)(2,1)S(1)}) custom-call(s32[2]{0:T(128)S(1)} %copy-done.8, bf16[320,1024]{1,0:T(8,128)(2,1)S(1)} %get-tuple-element.122.refs_0_.grad_ref, bf16[160,1024]{1,0:T(8,128)(2,1)S(1)} %collective-permute-done.12.refs_1_, bf16[160,1024]{1,0:T(8,128)(2,1)S(1)} %collective-permute-done.13.refs_2_, ...), custom_call_target="tpu_custom_call" | custom-call | flops 671088640 | bytes 4194304 | tf_op jit(solution)/shard_map/self_weight/pallas_call | solution.py:43
  104.1 1.4 collective-permute-start.20
  105.4 8.4 %row_grad.1 = (bf16[640,512]{1,0:T(8,128)(2,1)S(1)}, bf16[320,512]{1,0:T(8,128)(2,1)S(1)}, bf16[320,512]{1,0:T(8,128)(2,1)S(1)}, bf16[528,512]{1,0:T(8,128)(2,1)S(1)}, bf16[528,512]{1,0:T(8,128)(2,1)S(1)}) custom-call(s32[2]{0:T(128)S(1)} %copy-done.8, f32[1280,8]{1,0:T(8,128)S(1)} %copy-done.9, bf16[1280,1280]{1,0:T(8,128)(2,1)} %get-tuple-element.96.matrix_in, ...), custom_call_target="tpu_custom_call" | custom-call | flops 4362076160 | bytes 16457728 | tf_op jit(solution)/shard_map/row_grad/pallas_call | solution.py:43
  116.4 1.4 collective-permute-start.23
  117.8 4.6 %collective-permute-done.21.came_ref = bf16[528,512]{1,0:T(8,128)(2,1)S(1)} collective-permute-done((bf16[528,512]{1,0:T(8,128)(2,1)S(1)}, bf16[528,512]{1,0:T(8,128)(2,1)S(1)}, u32[]{:S(2)}, u32[]{:S(2)}) %collective-permute-start.21) | collective-permute-done | bytes 540704 | tf_op jit(solution)/shard_map/ppermute | solution.py:704
  125.0 7.5 %collective-permute-done.23 = bf16[144,1024]{1,0:T(8,128)(2,1)S(1)} collective-permute-done((bf16[144,1024]{1,0:T(8,128)(2,1)S(1)}, bf16[144,1024]{1,0:T(8,128)(2,1)S(1)}, u32[]{:S(2)}, u32[]{:S(2)}) %collective-permute-start.23) | collective-permute-done | bytes 294944 | tf_op jit(solution)/shard_map/ppermute | solution.py:704
  134.9 2.2 %collective-permute-start.26 = (bf16[128,1024]{1,0:T(8,128)(2,1)S(1)}, bf16[128,1024]{1,0:T(8,128)(2,1)S(1)}, u32[]{:S(2)}, u32[]{:S(2)}) collective-permute-start(bf16[128,1024]{1,0:T(8,128)(2,1)S(1)} %slice.58.refs_0_), channel_id=1, source_target_pairs={{0,8},{1,17},{2,10},{3,19},{4,12},{5,21},{6,14},{7,23},{8,0},{9,25... | collective-permute-start | bytes 786440 | tf_op jit(solution)/shard_map/ppermute | solution.py:704
  137.1 2.3 %self_feature.1.self_ref = f32[320,512]{1,0:T(8,128)S(1)} custom-call(s32[2]{0:T(128)S(1)} %copy-done.8, bf16[320,1024]{1,0:T(8,128)(2,1)S(1)} %copy-done.5, bf16[1024,1024]{1,0:T(8,128)(2,1)S(1)} %copy-done.1, bf16[1024,1024]{1,0:T(8,128)(2,1)} %collective-permute-done.8.w_other_in), custom_call_target="tpu_custom_call" | custom-call | flops 335544320 | bytes 5505024 | tf_op jit(solution)/shard_map/self_feature/pallas_call | solution.py:43
  140.9 8.4 %collective-permute-done.26.refs_1_ = bf16[128,1024]{1,0:T(8,128)(2,1)S(1)} collective-permute-done((bf16[128,1024]{1,0:T(8,128)(2,1)S(1)}, bf16[128,1024]{1,0:T(8,128)(2,1)S(1)}, u32[]{:S(2)}, u32[]{:S(2)}) %collective-permute-start.26) | collective-permute-done | bytes 262176 | tf_op jit(solution)/shard_map/ppermute | solution.py:704
  149.9 1.6 collective-permute-start.30
  153.0 1.4 collective-permute-start.32
  154.5 2.6 %collective-permute-done.31.refs_6_ = bf16[128,1024]{1,0:T(8,128)(2,1)S(1)} collective-permute-done((bf16[128,1024]{1,0:T(8,128)(2,1)S(1)}, bf16[128,1024]{1,0:T(8,128)(2,1)S(1)}, u32[]{:S(2)}, u32[]{:S(2)}) %collective-permute-start.31) | collective-permute-done | bytes 262176 | tf_op jit(solution)/shard_map/ppermute | solution.py:704
  157.1 4.5 %collective-permute-done.33.refs_5_ = bf16[128,1024]{1,0:T(8,128)(2,1)S(1)} collective-permute-done((bf16[128,1024]{1,0:T(8,128)(2,1)S(1)}, bf16[128,1024]{1,0:T(8,128)(2,1)S(1)}, u32[]{:S(2)}, u32[]{:S(2)}) %collective-permute-start.33) | collective-permute-done | bytes 262176 | tf_op jit(solution)/shard_map/ppermute | solution.py:704
  161.8 1.8 collective-permute-start.34
  163.6 1.4 collective-permute-start.41
  165.0 4.4 %collective-permute-start.37 = (f32[1,512]{1,0:T(1,128)S(1)}, f32[1,512]{1,0:T(1,128)S(1)}, u32[]{:S(2)}, u32[]{:S(2)}) collective-permute-start(f32[1,512]{1,0:T(1,128)S(1)} %slice_add_fusion.1), channel_id=1, source_target_pairs={{0,1},{1,0},{2,3},{3,2},{4,5},{5,4},{6,7},{7,6},{8,9},{9,8},{10,11... | collective-permute-start | bytes 6152 | tf_op jit(solution)/shard_map/ppermute | solution.py:713
  169.4 2.7 %unpack.4.refs_1_ = f32[1024,1024]{1,0:T(8,128)} custom-call(s32[2]{0:T(128)S(1)} %copy-done.8, bf16[128,1024]{1,0:T(8,128)(2,1)S(1)} %slice.58.refs_0_, bf16[128,1024]{1,0:T(8,128)(2,1)S(1)} %collective-permute-done.26.refs_1_, bf16[128,1024]{1,0:T(8,128)(2,1)S(1)} %collective-permute-done.27.refs_2_, ...), custom_call_target="tpu_custom_call" | custom-call | bytes 6029312 | tf_op jit(solution)/shard_map/unpack/pallas_call | solution.py:43
  172.8 4.0 %collective-permute-start.43 = (bf16[320,512]{1,0:T(8,128)(2,1)S(1)}, bf16[320,512]{1,0:T(8,128)(2,1)S(1)}, u32[]{:S(2)}, u32[]{:S(2)}) collective-permute-start(bf16[320,512]{1,0:T(8,128)(2,1)S(1)} %row_sums.1.mine_ref), channel_id=1, source_target_pairs={{0,1},{1,0},{2,3},{3,2},{4,5},{5,4},{6,7},{7,6},{8,9},{9,8},{10,11... | collective-permute-start | bytes 983048 | tf_op jit(solution)/shard_map/ppermute | solution.py:713
  177.8 1.4 unpack.5
  179.2 2.0 %feature_step.1 = (f32[320,512]{1,0:T(8,128)}, f32[1,1024]{1,0:T(1,128)}) custom-call(s32[2]{0:T(128)S(1)} %copy-done.8, f32[320,512]{1,0:T(8,128)S(1)} %self_feature.1.self_ref, bf16[320,512]{1,0:T(8,128)(2,1)S(1)} %row_sums.1.mine_ref, bf16[320,512]{1,0:T(8,128)(2,1)S(1)} %collective-permute-done.43.other_ref, f32[1,512]{1,0:T(1,128)S(1)} %slice_add_fusion.1, ...), custom_call_target="tpu_custom_call" | custom-call | flops 335544320 | bytes 4071424 | tf_op jit(solution)/shard_map/feature_step/pallas_call | solution.py:43
  181.3 1.7 collective-permute-done.38.refs_3_
  184.3 2.0 %unpack.6.refs_4_ = f32[1024,1024]{1,0:T(8,128)} custom-call(s32[2]{0:T(128)S(1)} %copy-done.8, bf16[256,512]{1,0:T(8,128)(2,1)S(1)} %slice.57.refs_0_, bf16[256,512]{1,0:T(8,128)(2,1)S(1)} %collective-permute-done.34.refs_1_, bf16[256,512]{1,0:T(8,128)(2,1)S(1)} %collective-permute-done.41.refs_2_, bf16[256,512]{1,0:T(8,128)(2,1)S(1)} %collective-permute-done.38.refs_3_), custom_call_target="tpu_custom_call" | custom-call | bytes 5242880 | tf_op jit(solution)/shard_map/unpack/pallas_call | solution.py:43
  186.3 2.0 %unpack.7 = f32[1024,1024]{1,0:T(8,128)} custom-call(s32[2]{0:T(128)S(1)} %copy-done.8, bf16[256,512]{1,0:T(8,128)(2,1)S(1)} %collective-permute-done.39.refs_0_, bf16[256,512]{1,0:T(8,128)(2,1)S(1)} %collective-permute-done.40.refs_1_, bf16[256,512]{1,0:T(8,128)(2,1)S(1)} %collective-permute-done.42.refs_2_, ...), custom_call_target="tpu_custom_call", output_to_operand_aliasing={{}: (5, {})} | custom-call | bytes 9437184 | tf_op jit(solution)/shard_map/unpack/pallas_call | solution.py:43
  (108 shorter events, 35.4 us)
Async XLA Ops:
  2.4 13.3 %collective-permute-start.2 = (bf16[160,1024]{1,0:T(8,128)(2,1)}, bf16[160,1024]{1,0:T(8,128)(2,1)}, u32[]{:S(2)}, u32[]{:S(2)}) collective-permute-start(bf16[160,1024]{1,0:T(8,128)(2,1)} %constant_dynamic-slice_fusion), channel_id=1, source_target_pairs={{0,16},{1,9},{2,18},{3,11},{4,20},{5,13},{6,22},{7,15},{8,24},{9,1... | collective-permute-start | bytes 983048 | tf_op jit(solution)/shard_map/ppermute | solution.py:704
  7.3 3.1 %collective-permute-start = (s32[32,320]{1,0:T(8,128)}, s32[32,320]{1,0:T(8,128)S(1)}, u32[]{:S(2)}, u32[]{:S(2)}) collective-permute-start(s32[32,320]{1,0:T(8,128)} %sort_slots.1), channel_id=1, source_target_pairs={{0,1},{1,0},{2,3},{3,2},{4,5},{5,4},{6,7},{7,6},{8,9},{9,8},{10,11... | collective-permute-start | bytes 122888 | tf_op jit(solution)/shard_map/ppermute | solution.py:713
  11.9 3.8 %collective-permute-start.1 = (s32[64,320]{1,0:T(8,128)S(1)}, s32[64,320]{1,0:T(8,128)S(1)}, u32[]{:S(2)}, u32[]{:S(2)}) collective-permute-start(s32[64,320]{1,0:T(8,128)S(1)} %pad_add_fusion.1.own_ref), channel_id=1, source_target_pairs={{0,4},{1,3},{2,6},{3,1},{4,0},{5,7},{6,2},{7,5},{8,12},{9,11},{10,... | collective-permute-start | bytes 245768 | tf_op jit(solution)/shard_map/ppermute | solution.py:704
  17.6 16.7 %collective-permute-start.4 = (bf16[320,1024]{1,0:T(8,128)(2,1)}, bf16[320,1024]{1,0:T(8,128)(2,1)}, u32[]{:S(2)}, u32[]{:S(2)}) collective-permute-start(bf16[320,1024]{1,0:T(8,128)(2,1)} %pad_maximum_fusion), channel_id=1, source_target_pairs={{0,8},{1,17},{2,10},{3,19},{4,12},{5,21},{6,14},{7,23},{8,0},{9,25... | collective-permute-start | bytes 1966088 | tf_op jit(solution)/shard_map/ppermute | solution.py:704
  18.3 14.8 %collective-permute-start.5 = (bf16[160,1024]{1,0:T(8,128)(2,1)}, bf16[160,1024]{1,0:T(8,128)(2,1)}, u32[]{:S(2)}, u32[]{:S(2)}) collective-permute-start(bf16[160,1024]{1,0:T(8,128)(2,1)} %collective-permute-done.2.refs_1_.refs_8_), channel_id=1, source_target_pairs={{0,1},{1,0},{2,3},{3,2},{4,5},{5,4},{6,7},{7,6},{8,9},{9,8},{10,11... | collective-permute-start | bytes 983048 | tf_op jit(solution)/shard_map/ppermute | solution.py:713
  21.2 5.0 %collective-permute-start.3 = (s32[128,320]{1,0:T(8,128)S(1)}, s32[128,320]{1,0:T(8,128)}, u32[]{:S(2)}, u32[]{:S(2)}) collective-permute-start(s32[128,320]{1,0:T(8,128)S(1)} %pad_add_fusion), channel_id=1, source_target_pairs={{0,2},{1,5},{2,0},{3,7},{4,6},{5,1},{6,4},{7,3},{8,10},{9,13},{10,... | collective-permute-start | bytes 491528 | tf_op jit(solution)/shard_map/ppermute | solution.py:704
  34.4 3.7 %collective-permute-start.6 = (bf16[320,1024]{1,0:T(8,128)(2,1)}, bf16[320,1024]{1,0:T(8,128)(2,1)}, u32[]{:S(2)}, u32[]{:S(2)}) collective-permute-start(bf16[320,1024]{1,0:T(8,128)(2,1)} %collective-permute-done.4.refs_2_.refs_9_), channel_id=1, source_target_pairs={{0,1},{1,0},{2,3},{3,2},{4,5},{5,4},{6,7},{7,6},{8,9},{9,8},{10,11... | collective-permute-start | bytes 1966088 | tf_op jit(solution)/shard_map/ppermute | solution.py:713
  45.2 14.2 %collective-permute-start.8 = (bf16[1024,1024]{1,0:T(8,128)(2,1)}, bf16[1024,1024]{1,0:T(8,128)(2,1)}, u32[]{:S(2)}, u32[]{:S(2)}) collective-permute-start(bf16[1024,1024]{1,0:T(8,128)(2,1)} %w_in.7), channel_id=1, source_target_pairs={{0,1},{1,0},{2,3},{3,2},{4,5},{5,4},{6,7},{7,6},{8,9},{9,8},{10,11... | collective-permute-start | bytes 6291464 | tf_op jit(solution)/shard_map/ppermute | solution.py:713
  45.6 10.0 %collective-permute-start.9 = (f32[320,512]{1,0:T(8,128)}, f32[320,512]{1,0:T(8,128)}, u32[]{:S(2)}, u32[]{:S(2)}) collective-permute-start(f32[320,512]{1,0:T(8,128)} %get-tuple-element.109), channel_id=1, source_target_pairs={{0,2},{1,5},{2,0},{3,7},{4,6},{5,1},{6,4},{7,3},{8,10},{9,13},{10,... | collective-permute-start | bytes 1966088 | tf_op jit(solution)/shard_map/ppermute | solution.py:704
  54.1 12.8 %collective-permute-start.7 = (f32[320,512]{1,0:T(8,128)}, f32[320,512]{1,0:T(8,128)S(1)}, u32[]{:S(2)}, u32[]{:S(2)}) collective-permute-start(f32[320,512]{1,0:T(8,128)} %get-tuple-element.101), channel_id=1, source_target_pairs={{0,2},{1,5},{2,0},{3,7},{4,6},{5,1},{6,4},{7,3},{8,10},{9,13},{10,... | collective-permute-start | bytes 1966088 | tf_op jit(solution)/shard_map/ppermute | solution.py:704
  57.1 14.6 %collective-permute-start.10 = (f32[320,512]{1,0:T(8,128)S(1)}, f32[320,512]{1,0:T(8,128)S(1)}, u32[]{:S(2)}, u32[]{:S(2)}) collective-permute-start(f32[320,512]{1,0:T(8,128)S(1)} %add.36), channel_id=1, source_target_pairs={{0,4},{1,3},{2,6},{3,1},{4,0},{5,7},{6,2},{7,5},{8,12},{9,11},{10,... | collective-permute-start | bytes 1966088 | tf_op jit(solution)/shard_map/ppermute | solution.py:704
  71.9 1.7 collective-permute-start.11
  77.2 26.9 %copy-start.4 = (bf16[320,1024]{1,0:T(8,128)(2,1)}, bf16[320,1024]{1,0:T(8,128)(2,1)S(1)}, u32[]{:S(2)}) copy-start(bf16[320,1024]{1,0:T(8,128)(2,1)S(1)} %get-tuple-element.122.refs_0_.grad_ref) | copy-start | bytes 1966084
  77.2 6.3 %collective-permute-start.12 = (bf16[160,1024]{1,0:T(8,128)(2,1)S(1)}, bf16[160,1024]{1,0:T(8,128)(2,1)S(1)}, u32[]{:S(2)}, u32[]{:S(2)}) collective-permute-start(bf16[160,1024]{1,0:T(8,128)(2,1)S(1)} %get-tuple-element.114), channel_id=1, source_target_pairs={{0,4},{1,3},{2,6},{3,1},{4,0},{5,7},{6,2},{7,5},{8,12},{9,11},{10,... | collective-permute-start | bytes 983048 | tf_op jit(solution)/shard_map/ppermute | solution.py:704
  78.8 9.5 %collective-permute-start.15 = (bf16[640,256]{1,0:T(8,128)(2,1)S(1)}, bf16[640,256]{1,0:T(8,128)(2,1)S(1)}, u32[]{:S(2)}, u32[]{:S(2)}) collective-permute-start(bf16[640,256]{1,0:T(8,128)(2,1)S(1)} %get-tuple-element.116), channel_id=1, source_target_pairs={{0,2},{1,5},{2,0},{3,7},{4,6},{5,1},{6,4},{7,3},{8,10},{9,13},{10,... | collective-permute-start | bytes 983048 | tf_op jit(solution)/shard_map/ppermute | solution.py:704
  79.6 12.1 %collective-permute-start.13 = (bf16[160,1024]{1,0:T(8,128)(2,1)S(1)}, bf16[160,1024]{1,0:T(8,128)(2,1)S(1)}, u32[]{:S(2)}, u32[]{:S(2)}) collective-permute-start(bf16[160,1024]{1,0:T(8,128)(2,1)S(1)} %get-tuple-element.114), channel_id=1, source_target_pairs={{0,2},{1,5},{2,0},{3,7},{4,6},{5,1},{6,4},{7,3},{8,10},{9,13},{10,... | collective-permute-start | bytes 983048 | tf_op jit(solution)/shard_map/ppermute | solution.py:704
  83.5 13.8 %collective-permute-start.14 = (bf16[160,1024]{1,0:T(8,128)(2,1)S(1)}, bf16[160,1024]{1,0:T(8,128)(2,1)S(1)}, u32[]{:S(2)}, u32[]{:S(2)}) collective-permute-start(bf16[160,1024]{1,0:T(8,128)(2,1)S(1)} %collective-permute-done.12.refs_1_), channel_id=1, source_target_pairs={{0,2},{1,5},{2,0},{3,7},{4,6},{5,1},{6,4},{7,3},{8,10},{9,13},{10,... | collective-permute-start | bytes 983048 | tf_op jit(solution)/shard_map/ppermute | solution.py:704
  88.3 9.1 %collective-permute-start.16 = (bf16[640,256]{1,0:T(8,128)(2,1)S(1)}, bf16[640,256]{1,0:T(8,128)(2,1)S(1)}, u32[]{:S(2)}, u32[]{:S(2)}) collective-permute-start(bf16[640,256]{1,0:T(8,128)(2,1)S(1)} %pad_maximum_fusion.1), channel_id=1, source_target_pairs={{0,4},{1,3},{2,6},{3,1},{4,0},{5,7},{6,2},{7,5},{8,12},{9,11},{10,... | collective-permute-start | bytes 983048 | tf_op jit(solution)/shard_map/ppermute | solution.py:704
  89.0 10.5 %collective-permute-start.17 = (bf16[160,1024]{1,0:T(8,128)(2,1)S(1)}, bf16[160,1024]{1,0:T(8,128)(2,1)S(1)}, u32[]{:S(2)}, u32[]{:S(2)}) collective-permute-start(bf16[160,1024]{1,0:T(8,128)(2,1)S(1)} %collective-permute-done.12.refs_1_), channel_id=1, source_target_pairs={{0,1},{1,0},{2,3},{3,2},{4,5},{5,4},{6,7},{7,6},{8,9},{9,8},{10,11... | collective-permute-start | bytes 983048 | tf_op jit(solution)/shard_map/ppermute | solution.py:713
  91.8 7.7 %collective-permute-start.18 = (bf16[160,1024]{1,0:T(8,128)(2,1)S(1)}, bf16[160,1024]{1,0:T(8,128)(2,1)S(1)}, u32[]{:S(2)}, u32[]{:S(2)}) collective-permute-start(bf16[160,1024]{1,0:T(8,128)(2,1)S(1)} %collective-permute-done.13.refs_2_), channel_id=1, source_target_pairs={{0,1},{1,0},{2,3},{3,2},{4,5},{5,4},{6,7},{7,6},{8,9},{9,8},{10,11... | collective-permute-start | bytes 983048 | tf_op jit(solution)/shard_map/ppermute | solution.py:713
  97.4 3.3 %collective-permute-start.19 = (bf16[160,1024]{1,0:T(8,128)(2,1)S(1)}, bf16[160,1024]{1,0:T(8,128)(2,1)S(1)}, u32[]{:S(2)}, u32[]{:S(2)}) collective-permute-start(bf16[160,1024]{1,0:T(8,128)(2,1)S(1)} %collective-permute-done.14.refs_3_), channel_id=1, source_target_pairs={{0,1},{1,0},{2,3},{3,2},{4,5},{5,4},{6,7},{7,6},{8,9},{9,8},{10,11... | collective-permute-start | bytes 983048 | tf_op jit(solution)/shard_map/ppermute | solution.py:713
  104.1 9.7 %collective-permute-start.20 = (bf16[144,1024]{1,0:T(8,128)(2,1)S(1)}, bf16[144,1024]{1,0:T(8,128)(2,1)S(1)}, u32[]{:S(2)}, u32[]{:S(2)}) collective-permute-start(bf16[144,1024]{1,0:T(8,128)(2,1)S(1)} %get-tuple-element.135), channel_id=1, source_target_pairs={{0,8},{1,17},{2,10},{3,19},{4,12},{5,21},{6,14},{7,23},{8,0},{9,25... | collective-permute-start | bytes 884744 | tf_op jit(solution)/shard_map/ppermute | solution.py:704
  113.8 23.3 %copy-start.1 = (bf16[1024,1024]{1,0:T(8,128)(2,1)S(1)}, bf16[1024,1024]{1,0:T(8,128)(2,1)}, u32[]{:S(2)}) copy-start(bf16[1024,1024]{1,0:T(8,128)(2,1)} %w_in.7) | copy-start | bytes 6291460
  113.8 23.3 %copy-start.5 = (bf16[320,1024]{1,0:T(8,128)(2,1)S(1)}, bf16[320,1024]{1,0:T(8,128)(2,1)}, u32[]{:S(2)}) copy-start(bf16[320,1024]{1,0:T(8,128)(2,1)} %copy-done.4) | copy-start | bytes 1966084
  113.8 8.6 %collective-permute-start.21 = (bf16[528,512]{1,0:T(8,128)(2,1)S(1)}, bf16[528,512]{1,0:T(8,128)(2,1)S(1)}, u32[]{:S(2)}, u32[]{:S(2)}) collective-permute-start(bf16[528,512]{1,0:T(8,128)(2,1)S(1)} %get-tuple-element.137), channel_id=1, source_target_pairs={{0,2},{1,5},{2,0},{3,7},{4,6},{5,1},{6,4},{7,3},{8,10},{9,13},{10,... | collective-permute-start | bytes 1622024 | tf_op jit(solution)/shard_map/ppermute | solution.py:704
  114.7 17.8 %collective-permute-start.24 = (bf16[320,512]{1,0:T(8,128)(2,1)S(1)}, bf16[320,512]{1,0:T(8,128)(2,1)S(1)}, u32[]{:S(2)}, u32[]{:S(2)}) collective-permute-start(bf16[320,512]{1,0:T(8,128)(2,1)S(1)} %get-tuple-element.143), channel_id=1, source_target_pairs={{0,8},{1,17},{2,10},{3,19},{4,12},{5,21},{6,14},{7,23},{8,0},{9,25... | collective-permute-start | bytes 983048 | tf_op jit(solution)/shard_map/ppermute | solution.py:704
  116.4 16.1 %collective-permute-start.23 = (bf16[144,1024]{1,0:T(8,128)(2,1)S(1)}, bf16[144,1024]{1,0:T(8,128)(2,1)S(1)}, u32[]{:S(2)}, u32[]{:S(2)}) collective-permute-start(bf16[144,1024]{1,0:T(8,128)(2,1)S(1)} %merge.3), channel_id=1, source_target_pairs={{0,16},{1,9},{2,18},{3,11},{4,20},{5,13},{6,22},{7,15},{8,24},{9,1... | collective-permute-start | bytes 884744 | tf_op jit(solution)/shard_map/ppermute | solution.py:704
  123.1 9.4 %collective-permute-start.22 = (bf16[272,512]{1,0:T(8,128)(2,1)S(1)}, bf16[272,512]{1,0:T(8,128)(2,1)S(1)}, u32[]{:S(2)}, u32[]{:S(2)}) collective-permute-start(bf16[272,512]{1,0:T(8,128)(2,1)S(1)} %get-tuple-element.139), channel_id=1, source_target_pairs={{0,4},{1,3},{2,6},{3,1},{4,0},{5,7},{6,2},{7,5},{8,12},{9,11},{10,... | collective-permute-start | bytes 835592 | tf_op jit(solution)/shard_map/ppermute | solution.py:704
  123.9 16.1 %collective-permute-start.29 = (bf16[320,512]{1,0:T(8,128)(2,1)S(1)}, bf16[320,512]{1,0:T(8,128)(2,1)S(1)}, u32[]{:S(2)}, u32[]{:S(2)}) collective-permute-start(bf16[320,512]{1,0:T(8,128)(2,1)S(1)} %get-tuple-element.146), channel_id=1, source_target_pairs={{0,8},{1,17},{2,10},{3,19},{4,12},{5,21},{6,14},{7,23},{8,0},{9,25... | collective-permute-start | bytes 983048 | tf_op jit(solution)/shard_map/ppermute | solution.py:704
  133.1 16.2 %collective-permute-start.25 = (bf16[272,512]{1,0:T(8,128)(2,1)S(1)}, bf16[272,512]{1,0:T(8,128)(2,1)S(1)}, u32[]{:S(2)}, u32[]{:S(2)}) collective-permute-start(bf16[272,512]{1,0:T(8,128)(2,1)S(1)} %merge.4.keep_ref), channel_id=1, source_target_pairs={{0,8},{1,17},{2,10},{3,19},{4,12},{5,21},{6,14},{7,23},{8,0},{9,25... | collective-permute-start | bytes 835592 | tf_op jit(solution)/shard_map/ppermute | solution.py:704
  133.3 6.7 %collective-permute-start.28 = (bf16[128,1024]{1,0:T(8,128)(2,1)S(1)}, bf16[128,1024]{1,0:T(8,128)(2,1)S(1)}, u32[]{:S(2)}, u32[]{:S(2)}) collective-permute-start(bf16[128,1024]{1,0:T(8,128)(2,1)S(1)} %slice.58.refs_0_), channel_id=1, source_target_pairs={{0,2},{1,5},{2,0},{3,7},{4,6},{5,1},{6,4},{7,3},{8,10},{9,13},{10,... | collective-permute-start | bytes 786440 | tf_op jit(solution)/shard_map/ppermute | solution.py:704
  134.0 6.9 %collective-permute-start.27 = (bf16[128,1024]{1,0:T(8,128)(2,1)S(1)}, bf16[128,1024]{1,0:T(8,128)(2,1)S(1)}, u32[]{:S(2)}, u32[]{:S(2)}) collective-permute-start(bf16[128,1024]{1,0:T(8,128)(2,1)S(1)} %slice.58.refs_0_), channel_id=1, source_target_pairs={{0,4},{1,3},{2,6},{3,1},{4,0},{5,7},{6,2},{7,5},{8,12},{9,11},{10,... | collective-permute-start | bytes 786440 | tf_op jit(solution)/shard_map/ppermute | solution.py:704
  134.9 14.4 %collective-permute-start.26 = (bf16[128,1024]{1,0:T(8,128)(2,1)S(1)}, bf16[128,1024]{1,0:T(8,128)(2,1)S(1)}, u32[]{:S(2)}, u32[]{:S(2)}) collective-permute-start(bf16[128,1024]{1,0:T(8,128)(2,1)S(1)} %slice.58.refs_0_), channel_id=1, source_target_pairs={{0,8},{1,17},{2,10},{3,19},{4,12},{5,21},{6,14},{7,23},{8,0},{9,25... | collective-permute-start | bytes 786440 | tf_op jit(solution)/shard_map/ppermute | solution.py:704
  149.9 11.6 %collective-permute-start.30 = (bf16[272,512]{1,0:T(8,128)(2,1)S(1)}, bf16[272,512]{1,0:T(8,128)(2,1)S(1)}, u32[]{:S(2)}, u32[]{:S(2)}) collective-permute-start(bf16[272,512]{1,0:T(8,128)(2,1)S(1)} %merge.5), channel_id=1, source_target_pairs={{0,16},{1,9},{2,18},{3,11},{4,20},{5,13},{6,22},{7,15},{8,24},{9,1... | collective-permute-start | bytes 835592 | tf_op jit(solution)/shard_map/ppermute | solution.py:704
  151.5 5.5 %collective-permute-start.31 = (bf16[128,1024]{1,0:T(8,128)(2,1)S(1)}, bf16[128,1024]{1,0:T(8,128)(2,1)S(1)}, u32[]{:S(2)}, u32[]{:S(2)}) collective-permute-start(bf16[128,1024]{1,0:T(8,128)(2,1)S(1)} %collective-permute-done.27.refs_2_), channel_id=1, source_target_pairs={{0,2},{1,5},{2,0},{3,7},{4,6},{5,1},{6,4},{7,3},{8,10},{9,13},{10,... | collective-permute-start | bytes 786440 | tf_op jit(solution)/shard_map/ppermute | solution.py:704
  151.8 9.8 %collective-permute-start.33 = (bf16[128,1024]{1,0:T(8,128)(2,1)S(1)}, bf16[128,1024]{1,0:T(8,128)(2,1)S(1)}, u32[]{:S(2)}, u32[]{:S(2)}) collective-permute-start(bf16[128,1024]{1,0:T(8,128)(2,1)S(1)} %collective-permute-done.26.refs_1_), channel_id=1, source_target_pairs={{0,2},{1,5},{2,0},{3,7},{4,6},{5,1},{6,4},{7,3},{8,10},{9,13},{10,... | collective-permute-start | bytes 786440 | tf_op jit(solution)/shard_map/ppermute | solution.py:704
  153.0 8.5 %collective-permute-start.32 = (bf16[128,1024]{1,0:T(8,128)(2,1)S(1)}, bf16[128,1024]{1,0:T(8,128)(2,1)S(1)}, u32[]{:S(2)}, u32[]{:S(2)}) collective-permute-start(bf16[128,1024]{1,0:T(8,128)(2,1)S(1)} %collective-permute-done.26.refs_1_), channel_id=1, source_target_pairs={{0,4},{1,3},{2,6},{3,1},{4,0},{5,7},{6,2},{7,5},{8,12},{9,11},{10,... | collective-permute-start | bytes 786440 | tf_op jit(solution)/shard_map/ppermute | solution.py:704
  161.7 10.5 %collective-permute-start.36 = (bf16[320,512]{1,0:T(8,128)(2,1)S(1)}, bf16[320,512]{1,0:T(8,128)(2,1)S(1)}, u32[]{:S(2)}, u32[]{:S(2)}) collective-permute-start(bf16[320,512]{1,0:T(8,128)(2,1)S(1)} %add_convert_fusion), channel_id=1, source_target_pairs={{0,16},{1,9},{2,18},{3,11},{4,20},{5,13},{6,22},{7,15},{8,24},{9,1... | collective-permute-start | bytes 983048 | tf_op jit(solution)/shard_map/ppermute | solution.py:704
  161.8 10.4 %collective-permute-start.35 = (bf16[128,1024]{1,0:T(8,128)(2,1)S(1)}, bf16[128,1024]{1,0:T(8,128)(2,1)S(1)}, u32[]{:S(2)}, u32[]{:S(2)}) collective-permute-start(bf16[128,1024]{1,0:T(8,128)(2,1)S(1)} %collective-permute-done.32.refs_3_), channel_id=1, source_target_pairs={{0,2},{1,5},{2,0},{3,7},{4,6},{5,1},{6,4},{7,3},{8,10},{9,13},{10,... | collective-permute-start | bytes 786440 | tf_op jit(solution)/shard_map/ppermute | solution.py:704
  161.8 10.3 %collective-permute-start.34 = (bf16[256,512]{1,0:T(8,128)(2,1)S(1)}, bf16[256,512]{1,0:T(8,128)(2,1)S(1)}, u32[]{:S(2)}, u32[]{:S(2)}) collective-permute-start(bf16[256,512]{1,0:T(8,128)(2,1)S(1)} %slice.57.refs_0_), channel_id=1, source_target_pairs={{0,4},{1,3},{2,6},{3,1},{4,0},{5,7},{6,2},{7,5},{8,12},{9,11},{10,... | collective-permute-start | bytes 786440 | tf_op jit(solution)/shard_map/ppermute | solution.py:704
  163.6 13.4 %collective-permute-start.41 = (bf16[256,512]{1,0:T(8,128)(2,1)S(1)}, bf16[256,512]{1,0:T(8,128)(2,1)S(1)}, u32[]{:S(2)}, u32[]{:S(2)}) collective-permute-start(bf16[256,512]{1,0:T(8,128)(2,1)S(1)} %slice.57.refs_0_), channel_id=1, source_target_pairs={{0,2},{1,5},{2,0},{3,7},{4,6},{5,1},{6,4},{7,3},{8,10},{9,13},{10,... | collective-permute-start | bytes 786440 | tf_op jit(solution)/shard_map/ppermute | solution.py:704
  165.0 7.1 %collective-permute-start.37 = (f32[1,512]{1,0:T(1,128)S(1)}, f32[1,512]{1,0:T(1,128)S(1)}, u32[]{:S(2)}, u32[]{:S(2)}) collective-permute-start(f32[1,512]{1,0:T(1,128)S(1)} %slice_add_fusion.1), channel_id=1, source_target_pairs={{0,1},{1,0},{2,3},{3,2},{4,5},{5,4},{6,7},{7,6},{8,9},{9,8},{10,11... | collective-permute-start | bytes 6152 | tf_op jit(solution)/shard_map/ppermute | solution.py:713
  172.8 6.4 %collective-permute-start.43 = (bf16[320,512]{1,0:T(8,128)(2,1)S(1)}, bf16[320,512]{1,0:T(8,128)(2,1)S(1)}, u32[]{:S(2)}, u32[]{:S(2)}) collective-permute-start(bf16[320,512]{1,0:T(8,128)(2,1)S(1)} %row_sums.1.mine_ref), channel_id=1, source_target_pairs={{0,1},{1,0},{2,3},{3,2},{4,5},{5,4},{6,7},{7,6},{8,9},{9,8},{10,11... | collective-permute-start | bytes 983048 | tf_op jit(solution)/shard_map/ppermute | solution.py:713
  176.9 4.3 %collective-permute-start.39 = (bf16[256,512]{1,0:T(8,128)(2,1)S(1)}, bf16[256,512]{1,0:T(8,128)(2,1)S(1)}, u32[]{:S(2)}, u32[]{:S(2)}) collective-permute-start(bf16[256,512]{1,0:T(8,128)(2,1)S(1)} %slice.57.refs_0_), channel_id=1, source_target_pairs={{0,1},{1,0},{2,3},{3,2},{4,5},{5,4},{6,7},{7,6},{8,9},{9,8},{10,11... | collective-permute-start | bytes 786440 | tf_op jit(solution)/shard_map/ppermute | solution.py:713
  177.0 4.3 %collective-permute-start.42 = (bf16[256,512]{1,0:T(8,128)(2,1)S(1)}, bf16[256,512]{1,0:T(8,128)(2,1)S(1)}, u32[]{:S(2)}, u32[]{:S(2)}) collective-permute-start(bf16[256,512]{1,0:T(8,128)(2,1)S(1)} %collective-permute-done.41.refs_2_), channel_id=1, source_target_pairs={{0,1},{1,0},{2,3},{3,2},{4,5},{5,4},{6,7},{7,6},{8,9},{9,8},{10,11... | collective-permute-start | bytes 786440 | tf_op jit(solution)/shard_map/ppermute | solution.py:713
  177.4 3.9 %collective-permute-start.40 = (bf16[256,512]{1,0:T(8,128)(2,1)S(1)}, bf16[256,512]{1,0:T(8,128)(2,1)S(1)}, u32[]{:S(2)}, u32[]{:S(2)}) collective-permute-start(bf16[256,512]{1,0:T(8,128)(2,1)S(1)} %collective-permute-done.34.refs_1_), channel_id=1, source_target_pairs={{0,1},{1,0},{2,3},{3,2},{4,5},{5,4},{6,7},{7,6},{8,9},{9,8},{10,11... | collective-permute-start | bytes 786440 | tf_op jit(solution)/shard_map/ppermute | solution.py:713
  177.5 5.5 %collective-permute-start.38 = (bf16[256,512]{1,0:T(8,128)(2,1)S(1)}, bf16[256,512]{1,0:T(8,128)(2,1)S(1)}, u32[]{:S(2)}, u32[]{:S(2)}) collective-permute-start(bf16[256,512]{1,0:T(8,128)(2,1)S(1)} %collective-permute-done.34.refs_1_), channel_id=1, source_target_pairs={{0,2},{1,5},{2,0},{3,7},{4,6},{5,1},{6,4},{7,3},{8,10},{9,13},{10,... | collective-permute-start | bytes 786440 | tf_op jit(solution)/shard_map/ppermute | solution.py:704
  183.0 3.3 %collective-permute-start.44 = (bf16[256,512]{1,0:T(8,128)(2,1)S(1)}, bf16[256,512]{1,0:T(8,128)(2,1)S(1)}, u32[]{:S(2)}, u32[]{:S(2)}) collective-permute-start(bf16[256,512]{1,0:T(8,128)(2,1)S(1)} %collective-permute-done.38.refs_3_), channel_id=1, source_target_pairs={{0,1},{1,0},{2,3},{3,2},{4,5},{5,4},{6,7},{7,6},{8,9},{9,8},{10,11... | collective-permute-start | bytes 786440 | tf_op jit(solution)/shard_map/ppermute | solution.py:713
  (11 other events, 73.3 us)

commit v8 on v7

--- a/solution.py
+++ b/solution.py
@@ -804,7 +804,7 @@
         q_came = line_swap(q_sum, step)
     near_three = plane_swap(near_one, 0)
     far_one, far_two = plane_swap(w_far, 1), plane_swap(w_far, 0)
-    q_came, near_three, far_one, far_two = fence((q_came, near_three, far_one, far_two))
+    q_came, far_one = fence((q_came, far_one))
     q_own, biases["q"] = last_sum(q_sum, q_came)
     half = stay.shape[0] // 2
     upper = (stay[half:].astype(F32) + rows_go.astype(F32)).astype(BF16)

time: 189 us -> 187 us (0.989)
  no operation moved by 1% of the time
where the time goes in v8:
time: 187 us
  waiting for transfers between devices  63.9 us (34%)
  Pallas kernels  58.2 us (31%)
  starting transfers between devices  52.1 us (28%)
  other arithmetic  6.61 us (4%)
  local copies, waits for them, and re-layouts  4.66 us (2%)
    pallas_call x20, Pallas kernels, call(): pl.pallas_call(kernel, name=name, out_shape=list(outs), in_specs=spaced(p...  58.2 us
    ppermute x31, waiting for transfers between devices, swap(): return lax.ppermute(value, ('nodes', 'stream'), pairs)  57.9 us
    ppermute x31, starting transfers between devices, swap(): return lax.ppermute(value, ('nodes', 'stream'), pairs)  31.4 us
    ppermute x14, starting transfers between devices, trade(): return lax.ppermute(value, 'stream', [(0, 1), (1, 0)])  20.6 us
    ppermute x14, waiting for transfers between devices, trade(): return lax.ppermute(value, 'stream', [(0, 1), (1, 0)])  6.05 us
  transfers between devices with their start and end apart: 45, of which 22 were waited for; matrix products, arithmetic and copies ran while one was open for 3% of the time, Pallas kernels for 22%

profile of v8, /device:TPU:1, one launch (start us, length us, event | category | flops | bytes accessed | tf_op | source)
XLA Modules:
  0.0 186.8 jit_solution(11184301413230905816)
XLA Ops:
  0.6 1.7 constant_dynamic-slice_fusion
  2.4 2.1 %collective-permute-start.2 = (bf16[160,1024]{1,0:T(8,128)(2,1)}, bf16[160,1024]{1,0:T(8,128)(2,1)}, u32[]{:S(2)}, u32[]{:S(2)}) collective-permute-start(bf16[160,1024]{1,0:T(8,128)(2,1)} %constant_dynamic-slice_fusion), channel_id=1, source_target_pairs={{0,16},{1,9},{2,18},{3,11},{4,20},{5,13},{6,22},{7,15},{8,24},{9,1... | collective-permute-start | bytes 983048 | tf_op jit(solution)/shard_map/ppermute | solution.py:704
  5.1 2.2 %sort_slots.1 = s32[32,320]{1,0:T(8,128)} custom-call(s32[2]{0:T(128)} %pad_add_fusion.2.place_ref, s32[25,320]{1,0:T(8,128)} %bitcast.12, s32[25,320]{1,0:T(8,128)} %bitcast.13, s32[25,320]{1,0:T(8,128)} %bitcast.14), custom_call_target="tpu_custom_call" | custom-call | bytes 136960 | tf_op jit(solution)/shard_map/sort_slots/pallas_call | solution.py:43
  7.3 2.0 %collective-permute-start = (s32[32,320]{1,0:T(8,128)}, s32[32,320]{1,0:T(8,128)S(1)}, u32[]{:S(2)}, u32[]{:S(2)}) collective-permute-start(s32[32,320]{1,0:T(8,128)} %sort_slots.1), channel_id=1, source_target_pairs={{0,1},{1,0},{2,3},{3,2},{4,5},{5,4},{6,7},{7,6},{8,9},{9,8},{10,11... | collective-permute-start | bytes 122888 | tf_op jit(solution)/shard_map/ppermute | solution.py:713
  13.1 2.6 %collective-permute-done.1.next_ref = s32[64,320]{1,0:T(8,128)S(1)} collective-permute-done((s32[64,320]{1,0:T(8,128)S(1)}, s32[64,320]{1,0:T(8,128)S(1)}, u32[]{:S(2)}, u32[]{:S(2)}) %collective-permute-start.1) | collective-permute-done | bytes 81952 | tf_op jit(solution)/shard_map/ppermute | solution.py:704
  15.6 2.0 %pad_maximum_fusion = bf16[320,1024]{1,0:T(8,128)(2,1)} fusion(bf16[160,1024]{1,0:T(8,128)(2,1)} %collective-permute-done.2.refs_1_.refs_8_, bf16[160,1024]{1,0:T(8,128)(2,1)} %constant_dynamic-slice_fusion), kind=kLoop, calls=%fused_computation | loop fusion | flops 1310720 | bytes 1310720 | tf_op jit(solution)/shard_map/concatenate | solution.py:733
  18.3 2.1 %collective-permute-start.5 = (bf16[160,1024]{1,0:T(8,128)(2,1)}, bf16[160,1024]{1,0:T(8,128)(2,1)}, u32[]{:S(2)}, u32[]{:S(2)}) collective-permute-start(bf16[160,1024]{1,0:T(8,128)(2,1)} %collective-permute-done.2.refs_1_.refs_8_), channel_id=1, source_target_pairs={{0,1},{1,0},{2,3},{3,2},{4,5},{5,4},{6,7},{7,6},{8,9},{9,8},{10,11... | collective-permute-start | bytes 983048 | tf_op jit(solution)/shard_map/ppermute | solution.py:713
  22.5 3.7 %collective-permute-done.3.rest_ref = s32[128,320]{1,0:T(8,128)} collective-permute-done((s32[128,320]{1,0:T(8,128)S(1)}, s32[128,320]{1,0:T(8,128)}, u32[]{:S(2)}, u32[]{:S(2)}) %collective-permute-start.3) | collective-permute-done | bytes 163872 | tf_op jit(solution)/shard_map/ppermute | solution.py:704
  26.2 6.9 %slot_matrix.1 = (f32[1280,8]{1,0:T(8,128)}, bf16[1280,1280]{1,0:T(8,128)(2,1)}) custom-call(s32[2]{0:T(128)} %pad_add_fusion.2.place_ref, s32[64,320]{1,0:T(8,128)} %copy-done.12, s32[64,320]{1,0:T(8,128)} %copy-done.13, s32[128,320]{1,0:T(8,128)} %collective-permute-done.3.rest_ref), custom_call_target="tpu_custom_call" | custom-call | flops 1 | bytes 1 | tf_op jit(solution)/shard_map/slot_matrix/pallas_call | solution.py:43
  34.4 1.6 collective-permute-start.6
  36.0 2.1 %collective-permute-done.6.refs_4_.refs_11_ = bf16[320,1024]{1,0:T(8,128)(2,1)} collective-permute-done((bf16[320,1024]{1,0:T(8,128)(2,1)}, bf16[320,1024]{1,0:T(8,128)(2,1)}, u32[]{:S(2)}, u32[]{:S(2)}) %collective-permute-start.6) | collective-permute-done | bytes 655392 | tf_op jit(solution)/shard_map/ppermute | solution.py:713
  38.1 7.1 %first_sums.1 = (f32[320,512]{1,0:T(8,128)}, bf16[1280,512]{1,0:T(8,128)(2,1)}, bf16[1280,512]{1,0:T(8,128)(2,1)}) custom-call(s32[2]{0:T(128)} %pad_add_fusion.2.place_ref, f32[1,1024]{1,0:T(1,128)} %bitcast.16, bf16[1024,1024]{1,0:T(8,128)(2,1)} %q_in.3, bf16[1280,1280]{1,0:T(8,128)(2,1)} %get-tuple-element.94.matrix_in, bf16[320,1024]{1,0:T(8,128)(2,1)} %refs_7_.1, ...), custom_call_target="tpu_custom_call" | custom-call | flops 2181038080 | bytes 11276288 | tf_op jit(solution)/shard_map/first_sums/pallas_call | solution.py:43
  46.9 7.2 %more_sums.1 = (f32[320,512]{1,0:T(8,128)}, f32[320,512]{1,0:T(8,128)}, f32[320,512]{1,0:T(8,128)}) custom-call(s32[2]{0:T(128)} %pad_add_fusion.2.place_ref, bf16[1280,1280]{1,0:T(8,128)(2,1)} %get-tuple-element.94.matrix_in, bf16[1280,512]{1,0:T(8,128)(2,1)} %get-tuple-element.97.refs_0_.high_in, bf16[1280,512]{1,0:T(8,128)(2,1)} %get-tuple-element.98.refs_1_), custom_call_target="tpu_custom_call" | custom-call | flops 2516582400 | bytes 7864320 | tf_op jit(solution)/shard_map/more_sums/pallas_call | solution.py:43
  55.7 1.4 add.36
  60.5 3.0 %self_product.1.self_ref = f32[320,1024]{1,0:T(8,128)S(1)} custom-call(s32[2]{0:T(128)S(1)} %copy-done.8, bf16[320,1024]{1,0:T(8,128)(2,1)S(1)} %copy-done.2, f32[1,1024]{1,0:T(1,128)S(1)} %bitcast.11, bf16[1024,1024]{1,0:T(8,128)(2,1)S(1)} %copy-done, bf16[1024,1024]{1,0:T(8,128)(2,1)} %collective-permute-done.8.w_other_in), custom_call_target="tpu_custom_call" | custom-call | flops 671088640 | bytes 6164480 | tf_op jit(solution)/shard_map/self_product/pallas_call | solution.py:43
  63.6 3.4 %collective-permute-done.7 = f32[320,512]{1,0:T(8,128)S(1)} collective-permute-done((f32[320,512]{1,0:T(8,128)}, f32[320,512]{1,0:T(8,128)S(1)}, u32[]{:S(2)}, u32[]{:S(2)}) %collective-permute-start.7) | collective-permute-done | bytes 655392 | tf_op jit(solution)/shard_map/ppermute | solution.py:704
  66.9 4.8 %collective-permute-done.10 = f32[320,512]{1,0:T(8,128)S(1)} collective-permute-done((f32[320,512]{1,0:T(8,128)S(1)}, f32[320,512]{1,0:T(8,128)S(1)}, u32[]{:S(2)}, u32[]{:S(2)}) %collective-permute-start.10) | collective-permute-done | bytes 655392 | tf_op jit(solution)/shard_map/ppermute | solution.py:704
  72.0 1.6 collective-permute-done.11.other_ref
  73.6 3.5 %node_step.1 = (f32[320,1024]{1,0:T(8,128)}, bf16[320,1024]{1,0:T(8,128)(2,1)S(1)}, bf16[160,1024]{1,0:T(8,128)(2,1)S(1)}) custom-call(s32[2]{0:T(128)S(1)} %copy-done.8, bf16[320,512]{1,0:T(8,128)(2,1)S(1)} %divide_convert_fusion.mine_ref, bf16[320,512]{1,0:T(8,128)(2,1)S(1)} %collective-permute-done.11.other_ref, f32[320,1024]{1,0:T(8,128)S(1)} %self_product.1.self_ref, ...), custom_call_target="tpu_custom_call" | custom-call | flops 671088640 | bytes 9109504 | tf_op jit(solution)/shard_map/node_step/pallas_call | solution.py:43
  80.3 3.2 %collective-permute-done.12.refs_1_ = bf16[160,1024]{1,0:T(8,128)(2,1)S(1)} collective-permute-done((bf16[160,1024]{1,0:T(8,128)(2,1)S(1)}, bf16[160,1024]{1,0:T(8,128)(2,1)S(1)}, u32[]{:S(2)}, u32[]{:S(2)}) %collective-permute-start.12) | collective-permute-done | bytes 327712 | tf_op jit(solution)/shard_map/ppermute | solution.py:704
  84.7 3.5 %collective-permute-done.15.refs_8_ = bf16[640,256]{1,0:T(8,128)(2,1)S(1)} collective-permute-done((bf16[640,256]{1,0:T(8,128)(2,1)S(1)}, bf16[640,256]{1,0:T(8,128)(2,1)S(1)}, u32[]{:S(2)}, u32[]{:S(2)}) %collective-permute-start.15) | collective-permute-done | bytes 327712 | tf_op jit(solution)/shard_map/ppermute | solution.py:704
  89.0 2.4 %collective-permute-start.17 = (bf16[160,1024]{1,0:T(8,128)(2,1)S(1)}, bf16[160,1024]{1,0:T(8,128)(2,1)S(1)}, u32[]{:S(2)}, u32[]{:S(2)}) collective-permute-start(bf16[160,1024]{1,0:T(8,128)(2,1)S(1)} %collective-permute-done.12.refs_1_), channel_id=1, source_target_pairs={{0,1},{1,0},{2,3},{3,2},{4,5},{5,4},{6,7},{7,6},{8,9},{9,8},{10,11... | collective-permute-start | bytes 983048 | tf_op jit(solution)/shard_map/ppermute | solution.py:713
  92.1 5.2 %collective-permute-done.14.refs_3_ = bf16[160,1024]{1,0:T(8,128)(2,1)S(1)} collective-permute-done((bf16[160,1024]{1,0:T(8,128)(2,1)S(1)}, bf16[160,1024]{1,0:T(8,128)(2,1)S(1)}, u32[]{:S(2)}, u32[]{:S(2)}) %collective-permute-start.14) | collective-permute-done | bytes 327712 | tf_op jit(solution)/shard_map/ppermute | solution.py:704
  97.4 2.1 %collective-permute-start.19 = (bf16[160,1024]{1,0:T(8,128)(2,1)S(1)}, bf16[160,1024]{1,0:T(8,128)(2,1)S(1)}, u32[]{:S(2)}, u32[]{:S(2)}) collective-permute-start(bf16[160,1024]{1,0:T(8,128)(2,1)S(1)} %collective-permute-done.14.refs_3_), channel_id=1, source_target_pairs={{0,1},{1,0},{2,3},{3,2},{4,5},{5,4},{6,7},{7,6},{8,9},{9,8},{10,11... | collective-permute-start | bytes 983048 | tf_op jit(solution)/shard_map/ppermute | solution.py:713
  100.7 3.3 %self_weight.1 = (bf16[144,1024]{1,0:T(8,128)(2,1)S(1)}, bf16[144,1024]{1,0:T(8,128)(2,1)S(1)}) custom-call(s32[2]{0:T(128)S(1)} %copy-done.8, bf16[320,1024]{1,0:T(8,128)(2,1)S(1)} %get-tuple-element.120.refs_0_.grad_ref, bf16[160,1024]{1,0:T(8,128)(2,1)S(1)} %collective-permute-done.12.refs_1_, bf16[160,1024]{1,0:T(8,128)(2,1)S(1)} %collective-permute-done.13.refs_2_, ...), custom_call_target="tpu_custom_call" | custom-call | flops 671088640 | bytes 4194304 | tf_op jit(solution)/shard_map/self_weight/pallas_call | solution.py:43
  105.4 8.4 %row_grad.1 = (bf16[640,512]{1,0:T(8,128)(2,1)S(1)}, bf16[320,512]{1,0:T(8,128)(2,1)S(1)}, bf16[320,512]{1,0:T(8,128)(2,1)S(1)}, bf16[528,512]{1,0:T(8,128)(2,1)S(1)}, bf16[528,512]{1,0:T(8,128)(2,1)S(1)}) custom-call(s32[2]{0:T(128)S(1)} %copy-done.8, f32[1280,8]{1,0:T(8,128)S(1)} %copy-done.9, bf16[1280,1280]{1,0:T(8,128)(2,1)} %get-tuple-element.94.matrix_in, ...), custom_call_target="tpu_custom_call" | custom-call | flops 4362076160 | bytes 16457728 | tf_op jit(solution)/shard_map/row_grad/pallas_call | solution.py:43
  116.4 1.4 collective-permute-start.23
  117.8 4.6 %collective-permute-done.21.came_ref = bf16[528,512]{1,0:T(8,128)(2,1)S(1)} collective-permute-done((bf16[528,512]{1,0:T(8,128)(2,1)S(1)}, bf16[528,512]{1,0:T(8,128)(2,1)S(1)}, u32[]{:S(2)}, u32[]{:S(2)}) %collective-permute-start.21) | collective-permute-done | bytes 540704 | tf_op jit(solution)/shard_map/ppermute | solution.py:704
  125.0 7.5 %collective-permute-done.23 = bf16[144,1024]{1,0:T(8,128)(2,1)S(1)} collective-permute-done((bf16[144,1024]{1,0:T(8,128)(2,1)S(1)}, bf16[144,1024]{1,0:T(8,128)(2,1)S(1)}, u32[]{:S(2)}, u32[]{:S(2)}) %collective-permute-start.23) | collective-permute-done | bytes 294944 | tf_op jit(solution)/shard_map/ppermute | solution.py:704
  134.9 2.2 %collective-permute-start.26 = (bf16[128,1024]{1,0:T(8,128)(2,1)S(1)}, bf16[128,1024]{1,0:T(8,128)(2,1)S(1)}, u32[]{:S(2)}, u32[]{:S(2)}) collective-permute-start(bf16[128,1024]{1,0:T(8,128)(2,1)S(1)} %slice.58.refs_0_), channel_id=1, source_target_pairs={{0,8},{1,17},{2,10},{3,19},{4,12},{5,21},{6,14},{7,23},{8,0},{9,25... | collective-permute-start | bytes 786440 | tf_op jit(solution)/shard_map/ppermute | solution.py:704
  137.1 2.3 %self_feature.1.self_ref = f32[320,512]{1,0:T(8,128)S(1)} custom-call(s32[2]{0:T(128)S(1)} %copy-done.8, bf16[320,1024]{1,0:T(8,128)(2,1)S(1)} %copy-done.5, bf16[1024,1024]{1,0:T(8,128)(2,1)S(1)} %copy-done.1, bf16[1024,1024]{1,0:T(8,128)(2,1)} %collective-permute-done.8.w_other_in), custom_call_target="tpu_custom_call" | custom-call | flops 335544320 | bytes 5505024 | tf_op jit(solution)/shard_map/self_feature/pallas_call | solution.py:43
  140.9 8.4 %collective-permute-done.26.refs_1_ = bf16[128,1024]{1,0:T(8,128)(2,1)S(1)} collective-permute-done((bf16[128,1024]{1,0:T(8,128)(2,1)S(1)}, bf16[128,1024]{1,0:T(8,128)(2,1)S(1)}, u32[]{:S(2)}, u32[]{:S(2)}) %collective-permute-start.26) | collective-permute-done | bytes 262176 | tf_op jit(solution)/shard_map/ppermute | solution.py:704
  149.9 1.6 collective-permute-start.30
  151.5 1.4 collective-permute-start.31
  153.1 4.0 %collective-permute-done.31.refs_3_ = bf16[128,1024]{1,0:T(8,128)(2,1)S(1)} collective-permute-done((bf16[128,1024]{1,0:T(8,128)(2,1)S(1)}, bf16[128,1024]{1,0:T(8,128)(2,1)S(1)}, u32[]{:S(2)}, u32[]{:S(2)}) %collective-permute-start.31) | collective-permute-done | bytes 262176 | tf_op jit(solution)/shard_map/ppermute | solution.py:704
  157.2 1.6 collective-permute-start.34
  158.8 1.5 collective-permute-start.33
  160.3 1.7 collective-permute-start.32
  162.0 2.0 %collective-permute-done.35.refs_5_ = bf16[128,1024]{1,0:T(8,128)(2,1)S(1)} collective-permute-done((bf16[128,1024]{1,0:T(8,128)(2,1)S(1)}, bf16[128,1024]{1,0:T(8,128)(2,1)S(1)}, u32[]{:S(2)}, u32[]{:S(2)}) %collective-permute-start.35) | collective-permute-done | bytes 262176 | tf_op jit(solution)/shard_map/ppermute | solution.py:704
  164.0 6.0 %collective-permute-start.37 = (f32[1,512]{1,0:T(1,128)S(1)}, f32[1,512]{1,0:T(1,128)S(1)}, u32[]{:S(2)}, u32[]{:S(2)}) collective-permute-start(f32[1,512]{1,0:T(1,128)S(1)} %slice_add_fusion.1), channel_id=1, source_target_pairs={{0,1},{1,0},{2,3},{3,2},{4,5},{5,4},{6,7},{7,6},{8,9},{9,8},{10,11... | collective-permute-start | bytes 6152 | tf_op jit(solution)/shard_map/ppermute | solution.py:713
  170.0 2.7 %unpack.4.refs_1_ = f32[1024,1024]{1,0:T(8,128)} custom-call(s32[2]{0:T(128)S(1)} %copy-done.8, bf16[128,1024]{1,0:T(8,128)(2,1)S(1)} %slice.58.refs_0_, bf16[128,1024]{1,0:T(8,128)(2,1)S(1)} %collective-permute-done.26.refs_1_, bf16[128,1024]{1,0:T(8,128)(2,1)S(1)} %collective-permute-done.27.refs_2_, ...), custom_call_target="tpu_custom_call" | custom-call | bytes 6029312 | tf_op jit(solution)/shard_map/unpack/pallas_call | solution.py:43
  174.2 1.4 collective-permute-start.42
  176.2 1.4 unpack.5
  177.7 2.0 %feature_step.1 = (f32[320,512]{1,0:T(8,128)}, f32[1,1024]{1,0:T(1,128)}) custom-call(s32[2]{0:T(128)S(1)} %copy-done.8, f32[320,512]{1,0:T(8,128)S(1)} %self_feature.1.self_ref, bf16[320,512]{1,0:T(8,128)(2,1)S(1)} %row_sums.1.mine_ref, bf16[320,512]{1,0:T(8,128)(2,1)S(1)} %collective-permute-done.43.other_ref, f32[1,512]{1,0:T(1,128)S(1)} %slice_add_fusion.1, ...), custom_call_target="tpu_custom_call" | custom-call | flops 335544320 | bytes 4071424 | tf_op jit(solution)/shard_map/feature_step/pallas_call | solution.py:43
  179.7 1.4 collective-permute-done.38.refs_3_
  181.1 1.4 collective-permute-start.44
  182.5 2.0 %unpack.6.refs_4_ = f32[1024,1024]{1,0:T(8,128)} custom-call(s32[2]{0:T(128)S(1)} %copy-done.8, bf16[256,512]{1,0:T(8,128)(2,1)S(1)} %slice.57.refs_0_, bf16[256,512]{1,0:T(8,128)(2,1)S(1)} %collective-permute-done.32.refs_1_, bf16[256,512]{1,0:T(8,128)(2,1)S(1)} %collective-permute-done.41.refs_2_, bf16[256,512]{1,0:T(8,128)(2,1)S(1)} %collective-permute-done.38.refs_3_), custom_call_target="tpu_custom_call" | custom-call | bytes 5242880 | tf_op jit(solution)/shard_map/unpack/pallas_call | solution.py:43
  184.5 2.0 %unpack.7 = f32[1024,1024]{1,0:T(8,128)} custom-call(s32[2]{0:T(128)S(1)} %copy-done.8, bf16[256,512]{1,0:T(8,128)(2,1)S(1)} %collective-permute-done.39.refs_0_, bf16[256,512]{1,0:T(8,128)(2,1)S(1)} %collective-permute-done.40.refs_1_, bf16[256,512]{1,0:T(8,128)(2,1)S(1)} %collective-permute-done.42.refs_2_, ...), custom_call_target="tpu_custom_call", output_to_operand_aliasing={{}: (5, {})} | custom-call | bytes 9437184 | tf_op jit(solution)/shard_map/unpack/pallas_call | solution.py:43
  (108 shorter events, 35.7 us)
Async XLA Ops:
  2.4 13.3 %collective-permute-start.2 = (bf16[160,1024]{1,0:T(8,128)(2,1)}, bf16[160,1024]{1,0:T(8,128)(2,1)}, u32[]{:S(2)}, u32[]{:S(2)}) collective-permute-start(bf16[160,1024]{1,0:T(8,128)(2,1)} %constant_dynamic-slice_fusion), channel_id=1, source_target_pairs={{0,16},{1,9},{2,18},{3,11},{4,20},{5,13},{6,22},{7,15},{8,24},{9,1... | collective-permute-start | bytes 983048 | tf_op jit(solution)/shard_map/ppermute | solution.py:704
  7.3 3.1 %collective-permute-start = (s32[32,320]{1,0:T(8,128)}, s32[32,320]{1,0:T(8,128)S(1)}, u32[]{:S(2)}, u32[]{:S(2)}) collective-permute-start(s32[32,320]{1,0:T(8,128)} %sort_slots.1), channel_id=1, source_target_pairs={{0,1},{1,0},{2,3},{3,2},{4,5},{5,4},{6,7},{7,6},{8,9},{9,8},{10,11... | collective-permute-start | bytes 122888 | tf_op jit(solution)/shard_map/ppermute | solution.py:713
  11.9 3.8 %collective-permute-start.1 = (s32[64,320]{1,0:T(8,128)S(1)}, s32[64,320]{1,0:T(8,128)S(1)}, u32[]{:S(2)}, u32[]{:S(2)}) collective-permute-start(s32[64,320]{1,0:T(8,128)S(1)} %pad_add_fusion.1.own_ref), channel_id=1, source_target_pairs={{0,4},{1,3},{2,6},{3,1},{4,0},{5,7},{6,2},{7,5},{8,12},{9,11},{10,... | collective-permute-start | bytes 245768 | tf_op jit(solution)/shard_map/ppermute | solution.py:704
  17.6 16.7 %collective-permute-start.4 = (bf16[320,1024]{1,0:T(8,128)(2,1)}, bf16[320,1024]{1,0:T(8,128)(2,1)}, u32[]{:S(2)}, u32[]{:S(2)}) collective-permute-start(bf16[320,1024]{1,0:T(8,128)(2,1)} %pad_maximum_fusion), channel_id=1, source_target_pairs={{0,8},{1,17},{2,10},{3,19},{4,12},{5,21},{6,14},{7,23},{8,0},{9,25... | collective-permute-start | bytes 1966088 | tf_op jit(solution)/shard_map/ppermute | solution.py:704
  18.3 14.8 %collective-permute-start.5 = (bf16[160,1024]{1,0:T(8,128)(2,1)}, bf16[160,1024]{1,0:T(8,128)(2,1)}, u32[]{:S(2)}, u32[]{:S(2)}) collective-permute-start(bf16[160,1024]{1,0:T(8,128)(2,1)} %collective-permute-done.2.refs_1_.refs_8_), channel_id=1, source_target_pairs={{0,1},{1,0},{2,3},{3,2},{4,5},{5,4},{6,7},{7,6},{8,9},{9,8},{10,11... | collective-permute-start | bytes 983048 | tf_op jit(solution)/shard_map/ppermute | solution.py:713
  21.2 5.0 %collective-permute-start.3 = (s32[128,320]{1,0:T(8,128)S(1)}, s32[128,320]{1,0:T(8,128)}, u32[]{:S(2)}, u32[]{:S(2)}) collective-permute-start(s32[128,320]{1,0:T(8,128)S(1)} %pad_add_fusion), channel_id=1, source_target_pairs={{0,2},{1,5},{2,0},{3,7},{4,6},{5,1},{6,4},{7,3},{8,10},{9,13},{10,... | collective-permute-start | bytes 491528 | tf_op jit(solution)/shard_map/ppermute | solution.py:704
  34.4 3.7 %collective-permute-start.6 = (bf16[320,1024]{1,0:T(8,128)(2,1)}, bf16[320,1024]{1,0:T(8,128)(2,1)}, u32[]{:S(2)}, u32[]{:S(2)}) collective-permute-start(bf16[320,1024]{1,0:T(8,128)(2,1)} %collective-permute-done.4.refs_2_.refs_9_), channel_id=1, source_target_pairs={{0,1},{1,0},{2,3},{3,2},{4,5},{5,4},{6,7},{7,6},{8,9},{9,8},{10,11... | collective-permute-start | bytes 1966088 | tf_op jit(solution)/shard_map/ppermute | solution.py:713
  45.2 14.2 %collective-permute-start.8 = (bf16[1024,1024]{1,0:T(8,128)(2,1)}, bf16[1024,1024]{1,0:T(8,128)(2,1)}, u32[]{:S(2)}, u32[]{:S(2)}) collective-permute-start(bf16[1024,1024]{1,0:T(8,128)(2,1)} %w_in.7), channel_id=1, source_target_pairs={{0,1},{1,0},{2,3},{3,2},{4,5},{5,4},{6,7},{7,6},{8,9},{9,8},{10,11... | collective-permute-start | bytes 6291464 | tf_op jit(solution)/shard_map/ppermute | solution.py:713
  45.6 10.0 %collective-permute-start.9 = (f32[320,512]{1,0:T(8,128)}, f32[320,512]{1,0:T(8,128)}, u32[]{:S(2)}, u32[]{:S(2)}) collective-permute-start(f32[320,512]{1,0:T(8,128)} %get-tuple-element.107), channel_id=1, source_target_pairs={{0,2},{1,5},{2,0},{3,7},{4,6},{5,1},{6,4},{7,3},{8,10},{9,13},{10,... | collective-permute-start | bytes 1966088 | tf_op jit(solution)/shard_map/ppermute | solution.py:704
  54.1 12.8 %collective-permute-start.7 = (f32[320,512]{1,0:T(8,128)}, f32[320,512]{1,0:T(8,128)S(1)}, u32[]{:S(2)}, u32[]{:S(2)}) collective-permute-start(f32[320,512]{1,0:T(8,128)} %get-tuple-element.99), channel_id=1, source_target_pairs={{0,2},{1,5},{2,0},{3,7},{4,6},{5,1},{6,4},{7,3},{8,10},{9,13},{10,... | collective-permute-start | bytes 1966088 | tf_op jit(solution)/shard_map/ppermute | solution.py:704
  57.1 14.6 %collective-permute-start.10 = (f32[320,512]{1,0:T(8,128)S(1)}, f32[320,512]{1,0:T(8,128)S(1)}, u32[]{:S(2)}, u32[]{:S(2)}) collective-permute-start(f32[320,512]{1,0:T(8,128)S(1)} %add.36), channel_id=1, source_target_pairs={{0,4},{1,3},{2,6},{3,1},{4,0},{5,7},{6,2},{7,5},{8,12},{9,11},{10,... | collective-permute-start | bytes 1966088 | tf_op jit(solution)/shard_map/ppermute | solution.py:704
  71.9 1.7 collective-permute-start.11
  77.2 26.9 %copy-start.4 = (bf16[320,1024]{1,0:T(8,128)(2,1)}, bf16[320,1024]{1,0:T(8,128)(2,1)S(1)}, u32[]{:S(2)}) copy-start(bf16[320,1024]{1,0:T(8,128)(2,1)S(1)} %get-tuple-element.120.refs_0_.grad_ref) | copy-start | bytes 1966084
  77.2 6.3 %collective-permute-start.12 = (bf16[160,1024]{1,0:T(8,128)(2,1)S(1)}, bf16[160,1024]{1,0:T(8,128)(2,1)S(1)}, u32[]{:S(2)}, u32[]{:S(2)}) collective-permute-start(bf16[160,1024]{1,0:T(8,128)(2,1)S(1)} %get-tuple-element.112), channel_id=1, source_target_pairs={{0,4},{1,3},{2,6},{3,1},{4,0},{5,7},{6,2},{7,5},{8,12},{9,11},{10,... | collective-permute-start | bytes 983048 | tf_op jit(solution)/shard_map/ppermute | solution.py:704
  78.8 9.5 %collective-permute-start.15 = (bf16[640,256]{1,0:T(8,128)(2,1)S(1)}, bf16[640,256]{1,0:T(8,128)(2,1)S(1)}, u32[]{:S(2)}, u32[]{:S(2)}) collective-permute-start(bf16[640,256]{1,0:T(8,128)(2,1)S(1)} %get-tuple-element.114), channel_id=1, source_target_pairs={{0,2},{1,5},{2,0},{3,7},{4,6},{5,1},{6,4},{7,3},{8,10},{9,13},{10,... | collective-permute-start | bytes 983048 | tf_op jit(solution)/shard_map/ppermute | solution.py:704
  79.6 12.1 %collective-permute-start.13 = (bf16[160,1024]{1,0:T(8,128)(2,1)S(1)}, bf16[160,1024]{1,0:T(8,128)(2,1)S(1)}, u32[]{:S(2)}, u32[]{:S(2)}) collective-permute-start(bf16[160,1024]{1,0:T(8,128)(2,1)S(1)} %get-tuple-element.112), channel_id=1, source_target_pairs={{0,2},{1,5},{2,0},{3,7},{4,6},{5,1},{6,4},{7,3},{8,10},{9,13},{10,... | collective-permute-start | bytes 983048 | tf_op jit(solution)/shard_map/ppermute | solution.py:704
  83.5 13.8 %collective-permute-start.14 = (bf16[160,1024]{1,0:T(8,128)(2,1)S(1)}, bf16[160,1024]{1,0:T(8,128)(2,1)S(1)}, u32[]{:S(2)}, u32[]{:S(2)}) collective-permute-start(bf16[160,1024]{1,0:T(8,128)(2,1)S(1)} %collective-permute-done.12.refs_1_), channel_id=1, source_target_pairs={{0,2},{1,5},{2,0},{3,7},{4,6},{5,1},{6,4},{7,3},{8,10},{9,13},{10,... | collective-permute-start | bytes 983048 | tf_op jit(solution)/shard_map/ppermute | solution.py:704
  88.3 9.1 %collective-permute-start.16 = (bf16[640,256]{1,0:T(8,128)(2,1)S(1)}, bf16[640,256]{1,0:T(8,128)(2,1)S(1)}, u32[]{:S(2)}, u32[]{:S(2)}) collective-permute-start(bf16[640,256]{1,0:T(8,128)(2,1)S(1)} %pad_maximum_fusion.1), channel_id=1, source_target_pairs={{0,4},{1,3},{2,6},{3,1},{4,0},{5,7},{6,2},{7,5},{8,12},{9,11},{10,... | collective-permute-start | bytes 983048 | tf_op jit(solution)/shard_map/ppermute | solution.py:704
  89.0 10.5 %collective-permute-start.17 = (bf16[160,1024]{1,0:T(8,128)(2,1)S(1)}, bf16[160,1024]{1,0:T(8,128)(2,1)S(1)}, u32[]{:S(2)}, u32[]{:S(2)}) collective-permute-start(bf16[160,1024]{1,0:T(8,128)(2,1)S(1)} %collective-permute-done.12.refs_1_), channel_id=1, source_target_pairs={{0,1},{1,0},{2,3},{3,2},{4,5},{5,4},{6,7},{7,6},{8,9},{9,8},{10,11... | collective-permute-start | bytes 983048 | tf_op jit(solution)/shard_map/ppermute | solution.py:713
  91.8 7.7 %collective-permute-start.18 = (bf16[160,1024]{1,0:T(8,128)(2,1)S(1)}, bf16[160,1024]{1,0:T(8,128)(2,1)S(1)}, u32[]{:S(2)}, u32[]{:S(2)}) collective-permute-start(bf16[160,1024]{1,0:T(8,128)(2,1)S(1)} %collective-permute-done.13.refs_2_), channel_id=1, source_target_pairs={{0,1},{1,0},{2,3},{3,2},{4,5},{5,4},{6,7},{7,6},{8,9},{9,8},{10,11... | collective-permute-start | bytes 983048 | tf_op jit(solution)/shard_map/ppermute | solution.py:713
  97.4 3.3 %collective-permute-start.19 = (bf16[160,1024]{1,0:T(8,128)(2,1)S(1)}, bf16[160,1024]{1,0:T(8,128)(2,1)S(1)}, u32[]{:S(2)}, u32[]{:S(2)}) collective-permute-start(bf16[160,1024]{1,0:T(8,128)(2,1)S(1)} %collective-permute-done.14.refs_3_), channel_id=1, source_target_pairs={{0,1},{1,0},{2,3},{3,2},{4,5},{5,4},{6,7},{7,6},{8,9},{9,8},{10,11... | collective-permute-start | bytes 983048 | tf_op jit(solution)/shard_map/ppermute | solution.py:713
  104.1 9.7 %collective-permute-start.20 = (bf16[144,1024]{1,0:T(8,128)(2,1)S(1)}, bf16[144,1024]{1,0:T(8,128)(2,1)S(1)}, u32[]{:S(2)}, u32[]{:S(2)}) collective-permute-start(bf16[144,1024]{1,0:T(8,128)(2,1)S(1)} %get-tuple-element.133), channel_id=1, source_target_pairs={{0,8},{1,17},{2,10},{3,19},{4,12},{5,21},{6,14},{7,23},{8,0},{9,25... | collective-permute-start | bytes 884744 | tf_op jit(solution)/shard_map/ppermute | solution.py:704
  113.8 23.3 %copy-start.1 = (bf16[1024,1024]{1,0:T(8,128)(2,1)S(1)}, bf16[1024,1024]{1,0:T(8,128)(2,1)}, u32[]{:S(2)}) copy-start(bf16[1024,1024]{1,0:T(8,128)(2,1)} %w_in.7) | copy-start | bytes 6291460
  113.8 23.3 %copy-start.5 = (bf16[320,1024]{1,0:T(8,128)(2,1)S(1)}, bf16[320,1024]{1,0:T(8,128)(2,1)}, u32[]{:S(2)}) copy-start(bf16[320,1024]{1,0:T(8,128)(2,1)} %copy-done.4) | copy-start | bytes 1966084
  113.8 8.6 %collective-permute-start.21 = (bf16[528,512]{1,0:T(8,128)(2,1)S(1)}, bf16[528,512]{1,0:T(8,128)(2,1)S(1)}, u32[]{:S(2)}, u32[]{:S(2)}) collective-permute-start(bf16[528,512]{1,0:T(8,128)(2,1)S(1)} %get-tuple-element.135), channel_id=1, source_target_pairs={{0,2},{1,5},{2,0},{3,7},{4,6},{5,1},{6,4},{7,3},{8,10},{9,13},{10,... | collective-permute-start | bytes 1622024 | tf_op jit(solution)/shard_map/ppermute | solution.py:704
  114.7 17.8 %collective-permute-start.24 = (bf16[320,512]{1,0:T(8,128)(2,1)S(1)}, bf16[320,512]{1,0:T(8,128)(2,1)S(1)}, u32[]{:S(2)}, u32[]{:S(2)}) collective-permute-start(bf16[320,512]{1,0:T(8,128)(2,1)S(1)} %get-tuple-element.141), channel_id=1, source_target_pairs={{0,8},{1,17},{2,10},{3,19},{4,12},{5,21},{6,14},{7,23},{8,0},{9,25... | collective-permute-start | bytes 983048 | tf_op jit(solution)/shard_map/ppermute | solution.py:704
  116.4 16.1 %collective-permute-start.23 = (bf16[144,1024]{1,0:T(8,128)(2,1)S(1)}, bf16[144,1024]{1,0:T(8,128)(2,1)S(1)}, u32[]{:S(2)}, u32[]{:S(2)}) collective-permute-start(bf16[144,1024]{1,0:T(8,128)(2,1)S(1)} %merge.3), channel_id=1, source_target_pairs={{0,16},{1,9},{2,18},{3,11},{4,20},{5,13},{6,22},{7,15},{8,24},{9,1... | collective-permute-start | bytes 884744 | tf_op jit(solution)/shard_map/ppermute | solution.py:704
  123.1 9.4 %collective-permute-start.22 = (bf16[272,512]{1,0:T(8,128)(2,1)S(1)}, bf16[272,512]{1,0:T(8,128)(2,1)S(1)}, u32[]{:S(2)}, u32[]{:S(2)}) collective-permute-start(bf16[272,512]{1,0:T(8,128)(2,1)S(1)} %get-tuple-element.137), channel_id=1, source_target_pairs={{0,4},{1,3},{2,6},{3,1},{4,0},{5,7},{6,2},{7,5},{8,12},{9,11},{10,... | collective-permute-start | bytes 835592 | tf_op jit(solution)/shard_map/ppermute | solution.py:704
  123.9 16.1 %collective-permute-start.29 = (bf16[320,512]{1,0:T(8,128)(2,1)S(1)}, bf16[320,512]{1,0:T(8,128)(2,1)S(1)}, u32[]{:S(2)}, u32[]{:S(2)}) collective-permute-start(bf16[320,512]{1,0:T(8,128)(2,1)S(1)} %get-tuple-element.144), channel_id=1, source_target_pairs={{0,8},{1,17},{2,10},{3,19},{4,12},{5,21},{6,14},{7,23},{8,0},{9,25... | collective-permute-start | bytes 983048 | tf_op jit(solution)/shard_map/ppermute | solution.py:704
  133.1 16.2 %collective-permute-start.25 = (bf16[272,512]{1,0:T(8,128)(2,1)S(1)}, bf16[272,512]{1,0:T(8,128)(2,1)S(1)}, u32[]{:S(2)}, u32[]{:S(2)}) collective-permute-start(bf16[272,512]{1,0:T(8,128)(2,1)S(1)} %merge.4.keep_ref), channel_id=1, source_target_pairs={{0,8},{1,17},{2,10},{3,19},{4,12},{5,21},{6,14},{7,23},{8,0},{9,25... | collective-permute-start | bytes 835592 | tf_op jit(solution)/shard_map/ppermute | solution.py:704
  133.3 6.7 %collective-permute-start.28 = (bf16[128,1024]{1,0:T(8,128)(2,1)S(1)}, bf16[128,1024]{1,0:T(8,128)(2,1)S(1)}, u32[]{:S(2)}, u32[]{:S(2)}) collective-permute-start(bf16[128,1024]{1,0:T(8,128)(2,1)S(1)} %slice.58.refs_0_), channel_id=1, source_target_pairs={{0,2},{1,5},{2,0},{3,7},{4,6},{5,1},{6,4},{7,3},{8,10},{9,13},{10,... | collective-permute-start | bytes 786440 | tf_op jit(solution)/shard_map/ppermute | solution.py:704
  134.0 6.9 %collective-permute-start.27 = (bf16[128,1024]{1,0:T(8,128)(2,1)S(1)}, bf16[128,1024]{1,0:T(8,128)(2,1)S(1)}, u32[]{:S(2)}, u32[]{:S(2)}) collective-permute-start(bf16[128,1024]{1,0:T(8,128)(2,1)S(1)} %slice.58.refs_0_), channel_id=1, source_target_pairs={{0,4},{1,3},{2,6},{3,1},{4,0},{5,7},{6,2},{7,5},{8,12},{9,11},{10,... | collective-permute-start | bytes 786440 | tf_op jit(solution)/shard_map/ppermute | solution.py:704
  134.9 14.4 %collective-permute-start.26 = (bf16[128,1024]{1,0:T(8,128)(2,1)S(1)}, bf16[128,1024]{1,0:T(8,128)(2,1)S(1)}, u32[]{:S(2)}, u32[]{:S(2)}) collective-permute-start(bf16[128,1024]{1,0:T(8,128)(2,1)S(1)} %slice.58.refs_0_), channel_id=1, source_target_pairs={{0,8},{1,17},{2,10},{3,19},{4,12},{5,21},{6,14},{7,23},{8,0},{9,25... | collective-permute-start | bytes 786440 | tf_op jit(solution)/shard_map/ppermute | solution.py:704
  149.9 7.1 %collective-permute-start.30 = (bf16[272,512]{1,0:T(8,128)(2,1)S(1)}, bf16[272,512]{1,0:T(8,128)(2,1)S(1)}, u32[]{:S(2)}, u32[]{:S(2)}) collective-permute-start(bf16[272,512]{1,0:T(8,128)(2,1)S(1)} %merge.5), channel_id=1, source_target_pairs={{0,16},{1,9},{2,18},{3,11},{4,20},{5,13},{6,22},{7,15},{8,24},{9,1... | collective-permute-start | bytes 835592 | tf_op jit(solution)/shard_map/ppermute | solution.py:704
  151.5 5.5 %collective-permute-start.31 = (bf16[128,1024]{1,0:T(8,128)(2,1)S(1)}, bf16[128,1024]{1,0:T(8,128)(2,1)S(1)}, u32[]{:S(2)}, u32[]{:S(2)}) collective-permute-start(bf16[128,1024]{1,0:T(8,128)(2,1)S(1)} %collective-permute-done.26.refs_1_), channel_id=1, source_target_pairs={{0,4},{1,3},{2,6},{3,1},{4,0},{5,7},{6,2},{7,5},{8,12},{9,11},{10,... | collective-permute-start | bytes 786440 | tf_op jit(solution)/shard_map/ppermute | solution.py:704
  153.0 9.0 %collective-permute-start.36 = (bf16[128,1024]{1,0:T(8,128)(2,1)S(1)}, bf16[128,1024]{1,0:T(8,128)(2,1)S(1)}, u32[]{:S(2)}, u32[]{:S(2)}) collective-permute-start(bf16[128,1024]{1,0:T(8,128)(2,1)S(1)} %collective-permute-done.27.refs_2_), channel_id=1, source_target_pairs={{0,2},{1,5},{2,0},{3,7},{4,6},{5,1},{6,4},{7,3},{8,10},{9,13},{10,... | collective-permute-start | bytes 786440 | tf_op jit(solution)/shard_map/ppermute | solution.py:704
  157.2 15.6 %collective-permute-start.34 = (bf16[320,512]{1,0:T(8,128)(2,1)S(1)}, bf16[320,512]{1,0:T(8,128)(2,1)S(1)}, u32[]{:S(2)}, u32[]{:S(2)}) collective-permute-start(bf16[320,512]{1,0:T(8,128)(2,1)S(1)} %add_convert_fusion), channel_id=1, source_target_pairs={{0,16},{1,9},{2,18},{3,11},{4,20},{5,13},{6,22},{7,15},{8,24},{9,1... | collective-permute-start | bytes 983048 | tf_op jit(solution)/shard_map/ppermute | solution.py:704
  158.8 5.2 %collective-permute-start.35 = (bf16[128,1024]{1,0:T(8,128)(2,1)S(1)}, bf16[128,1024]{1,0:T(8,128)(2,1)S(1)}, u32[]{:S(2)}, u32[]{:S(2)}) collective-permute-start(bf16[128,1024]{1,0:T(8,128)(2,1)S(1)} %collective-permute-done.26.refs_1_), channel_id=1, source_target_pairs={{0,2},{1,5},{2,0},{3,7},{4,6},{5,1},{6,4},{7,3},{8,10},{9,13},{10,... | collective-permute-start | bytes 786440 | tf_op jit(solution)/shard_map/ppermute | solution.py:704
  158.8 13.9 %collective-permute-start.33 = (bf16[128,1024]{1,0:T(8,128)(2,1)S(1)}, bf16[128,1024]{1,0:T(8,128)(2,1)S(1)}, u32[]{:S(2)}, u32[]{:S(2)}) collective-permute-start(bf16[128,1024]{1,0:T(8,128)(2,1)S(1)} %collective-permute-done.31.refs_3_), channel_id=1, source_target_pairs={{0,2},{1,5},{2,0},{3,7},{4,6},{5,1},{6,4},{7,3},{8,10},{9,13},{10,... | collective-permute-start | bytes 786440 | tf_op jit(solution)/shard_map/ppermute | solution.py:704
  160.3 12.5 %collective-permute-start.32 = (bf16[256,512]{1,0:T(8,128)(2,1)S(1)}, bf16[256,512]{1,0:T(8,128)(2,1)S(1)}, u32[]{:S(2)}, u32[]{:S(2)}) collective-permute-start(bf16[256,512]{1,0:T(8,128)(2,1)S(1)} %slice.57.refs_0_), channel_id=1, source_target_pairs={{0,4},{1,3},{2,6},{3,1},{4,0},{5,7},{6,2},{7,5},{8,12},{9,11},{10,... | collective-permute-start | bytes 786440 | tf_op jit(solution)/shard_map/ppermute | solution.py:704
  162.0 12.2 %collective-permute-start.41 = (bf16[256,512]{1,0:T(8,128)(2,1)S(1)}, bf16[256,512]{1,0:T(8,128)(2,1)S(1)}, u32[]{:S(2)}, u32[]{:S(2)}) collective-permute-start(bf16[256,512]{1,0:T(8,128)(2,1)S(1)} %slice.57.refs_0_), channel_id=1, source_target_pairs={{0,2},{1,5},{2,0},{3,7},{4,6},{5,1},{6,4},{7,3},{8,10},{9,13},{10,... | collective-permute-start | bytes 786440 | tf_op jit(solution)/shard_map/ppermute | solution.py:704
  164.0 8.7 %collective-permute-start.37 = (f32[1,512]{1,0:T(1,128)S(1)}, f32[1,512]{1,0:T(1,128)S(1)}, u32[]{:S(2)}, u32[]{:S(2)}) collective-permute-start(f32[1,512]{1,0:T(1,128)S(1)} %slice_add_fusion.1), channel_id=1, source_target_pairs={{0,1},{1,0},{2,3},{3,2},{4,5},{5,4},{6,7},{7,6},{8,9},{9,8},{10,11... | collective-permute-start | bytes 6152 | tf_op jit(solution)/shard_map/ppermute | solution.py:713
  173.4 4.2 %collective-permute-start.43 = (bf16[320,512]{1,0:T(8,128)(2,1)S(1)}, bf16[320,512]{1,0:T(8,128)(2,1)S(1)}, u32[]{:S(2)}, u32[]{:S(2)}) collective-permute-start(bf16[320,512]{1,0:T(8,128)(2,1)S(1)} %row_sums.1.mine_ref), channel_id=1, source_target_pairs={{0,1},{1,0},{2,3},{3,2},{4,5},{5,4},{6,7},{7,6},{8,9},{9,8},{10,11... | collective-permute-start | bytes 983048 | tf_op jit(solution)/shard_map/ppermute | solution.py:713
  174.1 5.6 %collective-permute-start.39 = (bf16[256,512]{1,0:T(8,128)(2,1)S(1)}, bf16[256,512]{1,0:T(8,128)(2,1)S(1)}, u32[]{:S(2)}, u32[]{:S(2)}) collective-permute-start(bf16[256,512]{1,0:T(8,128)(2,1)S(1)} %slice.57.refs_0_), channel_id=1, source_target_pairs={{0,1},{1,0},{2,3},{3,2},{4,5},{5,4},{6,7},{7,6},{8,9},{9,8},{10,11... | collective-permute-start | bytes 786440 | tf_op jit(solution)/shard_map/ppermute | solution.py:713
  174.2 5.5 %collective-permute-start.42 = (bf16[256,512]{1,0:T(8,128)(2,1)S(1)}, bf16[256,512]{1,0:T(8,128)(2,1)S(1)}, u32[]{:S(2)}, u32[]{:S(2)}) collective-permute-start(bf16[256,512]{1,0:T(8,128)(2,1)S(1)} %collective-permute-done.41.refs_2_), channel_id=1, source_target_pairs={{0,1},{1,0},{2,3},{3,2},{4,5},{5,4},{6,7},{7,6},{8,9},{9,8},{10,11... | collective-permute-start | bytes 786440 | tf_op jit(solution)/shard_map/ppermute | solution.py:713
  175.6 4.1 %collective-permute-start.40 = (bf16[256,512]{1,0:T(8,128)(2,1)S(1)}, bf16[256,512]{1,0:T(8,128)(2,1)S(1)}, u32[]{:S(2)}, u32[]{:S(2)}) collective-permute-start(bf16[256,512]{1,0:T(8,128)(2,1)S(1)} %collective-permute-done.32.refs_1_), channel_id=1, source_target_pairs={{0,1},{1,0},{2,3},{3,2},{4,5},{5,4},{6,7},{7,6},{8,9},{9,8},{10,11... | collective-permute-start | bytes 786440 | tf_op jit(solution)/shard_map/ppermute | solution.py:713
  175.6 5.5 %collective-permute-start.38 = (bf16[256,512]{1,0:T(8,128)(2,1)S(1)}, bf16[256,512]{1,0:T(8,128)(2,1)S(1)}, u32[]{:S(2)}, u32[]{:S(2)}) collective-permute-start(bf16[256,512]{1,0:T(8,128)(2,1)S(1)} %collective-permute-done.32.refs_1_), channel_id=1, source_target_pairs={{0,2},{1,5},{2,0},{3,7},{4,6},{5,1},{6,4},{7,3},{8,10},{9,13},{10,... | collective-permute-start | bytes 786440 | tf_op jit(solution)/shard_map/ppermute | solution.py:704
  181.1 3.4 %collective-permute-start.44 = (bf16[256,512]{1,0:T(8,128)(2,1)S(1)}, bf16[256,512]{1,0:T(8,128)(2,1)S(1)}, u32[]{:S(2)}, u32[]{:S(2)}) collective-permute-start(bf16[256,512]{1,0:T(8,128)(2,1)S(1)} %collective-permute-done.38.refs_3_), channel_id=1, source_target_pairs={{0,1},{1,0},{2,3},{3,2},{4,5},{5,4},{6,7},{7,6},{8,9},{9,8},{10,11... | collective-permute-start | bytes 786440 | tf_op jit(solution)/shard_map/ppermute | solution.py:713
  (11 other events, 71.1 us)
